TPU v7x, 32 devices: a whole 2x2x4 slice. The times are simulated.
32 devices in a mesh: grid: 8 (over y, x, core), orb: 4 (over z).
Axes of the slice: x: 2, y: 2, z: 4, core: 2. Of those that a mesh axis runs over, the one named last changes fastest.
Arguments:
- orbitals: float32 [512, 32, 8, 128], P('orb', 'grid'), may hold values from -13 to 13, as said below
- potential: float32 [32, 8, 128], P('grid'), may hold values from -1 to 1
Outputs:
- orthonormal: float32 [512, 32, 8, 128], P('orb', 'grid')
Inputs may be any that keep to these rules, and one draw needn't show every extreme that they name: Trial orbitals, real-valued.
All inputs are finite; a program needn't handle non-finite values.
Results may differ from a plain program's by a relative error of at most 0.0003.
Values sent between devices are 32-bit elements; how exact they have to be, the bound alone decides.
No kernel may reach another device: no remote copies, remote signals or barrier semaphores. Data moves between devices by JAX's collectives and lax.ppermute only.
A program may use at most 64 MiB of HBM per device.

v0:
```python
import functools

import jax
import jax.numpy as jnp
from jax import lax
from jax.experimental import pallas as pl
from jax.experimental.pallas import tpu as pltpu
from jax.sharding import PartitionSpec as P


lap_weights = (-205.0 / 72.0, 8.0 / 5.0, -1.0 / 5.0, 8.0 / 315.0, -1.0 / 560.0)
lower_edge = 3.0
upper_edge = 11.0
center = 0.5 * (upper_edge + lower_edge)
half_width = 0.5 * (upper_edge - lower_edge)
bf16 = jnp.bfloat16
f32 = jnp.float32


whole_weights = {1: 8064.0, 2: -1008.0, 3: 128.0, 4: -9.0}
unit = 5040.0
vmem = pl.BlockSpec(memory_space=pltpu.VMEM)
smem = pl.BlockSpec(memory_space=pltpu.SMEM)
big = pltpu.CompilerParams(vmem_limit_bytes=56 << 20)


def split(value):
    high = value.astype(bf16)
    return high, (value - high.astype(f32)).astype(bf16)


def ring_weights(length, apart):
    total = jnp.zeros(apart.shape, f32)
    for m, weight in whole_weights.items():
        total = total + jnp.where(apart == m % length, weight, 0.0)
        total = total + jnp.where(apart == (-m) % length, weight, 0.0)
    return total


def plane_matrix(nx, ny):
    at = lax.broadcasted_iota(jnp.int32, (nx * ny, nx * ny), 0)
    to = lax.broadcasted_iota(jnp.int32, (nx * ny, nx * ny), 1)
    x0, y0, x1, y1 = at // ny, at % ny, to // ny, to % ny
    along_x = ring_weights(nx, (x0 - x1 + nx) % nx)
    along_y = ring_weights(ny, (y0 - y1 + ny) % ny)
    return (jnp.where(y0 == y1, along_x, 0.0) + jnp.where(x0 == x1, along_y, 0.0)).astype(bf16)


def line_matrix(nz, copies):
    at = lax.broadcasted_iota(jnp.int32, (copies * nz, copies * nz), 0)
    to = lax.broadcasted_iota(jnp.int32, (copies * nz, copies * nz), 1)
    along_z = ring_weights(nz, (at - to + copies * nz) % nz)
    return jnp.where(at // nz == to // nz, along_z, 0.0).astype(bf16)


def mm(a, b):
    return jnp.dot(a, b, preferred_element_type=f32)


def filter_kernel(orbs, place_ref, xy_ref, z_ref, pot_ref, *refs):
    *parts, out_ref, diag, level = refs
    planes, slabs, rows, _, cols = out_ref.shape
    pair = z_ref.shape[0] // cols
    flat = slabs * planes * rows
    pot = pot_ref[:, pot_ref.shape[1] - 1].reshape(flat, cols)
    pot = (pot - (1.5 * lap_weights[0] + center)) / half_width
    diag[...] = pot if pair == 1 else jnp.concatenate([pot] * pair, axis=1)
    scale = -0.5 / (unit * half_width)
    for s, part in enumerate(parts):
        height = part.shape[0] * planes * rows
        first = pl.multiple_of((place_ref[0] ^ s) * height, height) if len(parts) > 1 else 0
        for o in range(orbs):
            level[o, pl.ds(first, height), :] = part[:, o].reshape(height, cols)

    def apply(v):
        high, low = split(v)
        near = mm(xy_ref[...], high) + mm(xy_ref[...], low)
        near = near + (mm(high, z_ref[...]) + mm(low, z_ref[...]))
        return diag[...] * v + scale * near

    for q in range(0, orbs, pair):
        pieces = [level[q + e] for e in range(pair)]
        level0 = pieces[0] if pair == 1 else jnp.concatenate(pieces, axis=1)
        level1 = apply(level0)
        level2 = 2.0 * apply(level1) - level0
        level3 = 2.0 * apply(level2) - level1
        for e in range(pair):
            value = level3[:, e * cols : (e + 1) * cols].reshape(slabs, planes, rows, cols)
            for g in range(slabs):
                out_ref[:, g, :, q + e, :] = value[g]


def filter_orbitals(place, parts, with_pot, orbs, xy, z):
    slabs, _, planes, rows, cols = with_pot.shape
    flat = slabs * planes * rows
    return pl.pallas_call(
        functools.partial(filter_kernel, orbs),
        out_shape=jax.ShapeDtypeStruct((planes, slabs, rows, orbs, cols), f32),
        in_specs=[smem] + [vmem] * (3 + len(parts)),
        out_specs=vmem,
        scratch_shapes=[pltpu.VMEM((flat, z.shape[0]), f32), pltpu.VMEM((orbs, flat, cols), f32)],
        compiler_params=big,
        name="filter",
    )(place, xy, z, with_pot, *parts)


def block_list(count):
    return [(i, j) for i in range(count) for j in range(i, count)]


def margin_kernel(shape, place_ref, *refs):
    owners, slabs, chunks, pieces = shape
    parts = refs[:chunks]
    outs = refs[chunks : chunks + pieces]
    high, low, acc = refs[chunks + pieces :]
    _, rows, orbs, cols = parts[0].shape
    norb = chunks * parts[0].shape[0] * orbs
    span = slabs * orbs
    for z in range(owners):
        for c in range(chunks):
            at = pl.ds((z * chunks + c) * span, span)
            for r in range(rows):
                h, l = split(parts[c][z * slabs : (z + 1) * slabs, r].reshape(span, cols))
                high[at, r * cols : (r + 1) * cols] = h
                low[at, r * cols : (r + 1) * cols] = l
    size = acc.shape[-1]
    contract = (((1,), (1,)), ((), ()))
    at = 0
    for i in range(norb // size):
        mine = pl.ds(i * size, size)
        rest = pl.ds(i * size, norb - i * size)
        h, l = high[mine, :], low[mine, :]
        hr, lr = high[rest, :], low[rest, :]
        total = lax.dot_general(h, lr, contract, preferred_element_type=f32)
        total = total + lax.dot_general(l, hr, contract, preferred_element_type=f32)
        total = total + lax.dot_general(h, hr, contract, preferred_element_type=f32)
        for j in range(norb // size - i):
            acc[at] = total[:, j * size : (j + 1) * size]
            at += 1
    part = size // pieces
    for s in range(pieces):
        first = pl.multiple_of((place_ref[0] ^ s) * part, part)
        outs[s][...] = acc[:, pl.ds(first, part), :]


def margin_blocks(place, parts, owners, slabs, size, pieces):
    _, rows, orbs, cols = parts[0].shape
    norb = len(parts) * parts[0].shape[0] * orbs
    count = norb // size
    blocks = count * (count + 1) // 2
    wide = jax.ShapeDtypeStruct((norb, rows * cols), bf16)
    outs = [jax.ShapeDtypeStruct((blocks, size // pieces, size), f32)] * pieces + [wide, wide]
    return pl.pallas_call(
        functools.partial(margin_kernel, (owners, slabs, len(parts), pieces)),
        out_shape=outs,
        in_specs=[smem] + [vmem] * len(parts),
        out_specs=[vmem] * len(outs),
        scratch_shapes=[pltpu.VMEM((blocks, size, size), f32)],
        compiler_params=big,
        name="margin",
    )(place, *parts)


def split3(value):
    high = value.astype(bf16).astype(f32)
    rest = value - high
    mid = rest.astype(bf16).astype(f32)
    return high, mid, rest - mid


def tdot(a, b):
    return lax.dot_general(a, b, (((0,), (0,)), ((), ())), preferred_element_type=f32)


def eliminate(pd, pi, base, row):
    def spread(value, k):
        return jnp.broadcast_to(value[k : k + 1, :], value.shape)
    groups = len(pd)
    for t in range(groups):
        cols = []
        for j in range(8):
            at = jnp.full(pd[t].shape, base + (8 * t + j), jnp.int32)
            cols.append([jnp.take_along_axis(pd[v], at, axis=1) for v in range(t, groups)])
        diag = jnp.zeros_like(pd[t])
        for j in range(8):
            pivot = spread(cols[j][0], j)
            diag = jnp.where(row == j, pivot, diag)
            inv = pl.reciprocal(pivot, approx=True)
            inv = inv * (2.0 - pivot * inv)
            below = jnp.where(row > j, cols[j][0], 0.0)
            for k in range(j + 1, 8):
                over = spread(cols[j][0], k)
                cols[k][0] = cols[k][0] - (below * over) * inv
                if t + 1 < groups:
                    over = over * inv
                    for v in range(1, groups - t):
                        cols[k][v] = cols[k][v] - cols[j][v] * over
            for p in (pd, pi):
                over = spread(p[t], j)
                if j < 7:
                    p[t] = p[t] - (below * over) * inv
                if t + 1 < groups:
                    over = over * inv
                    for v in range(1, groups - t):
                        p[t + v] = p[t + v] - cols[j][v] * over
        scale = lax.rsqrt(diag)
        scale = scale * (1.5 - 0.5 * diag * scale * scale)
        pd[t] = pd[t] * scale
        pi[t] = pi[t] * scale
    return jnp.concatenate(pd, axis=0), jnp.concatenate(pi, axis=0)


def inverse_kernel(factor, place_ref, *refs):
    v_ref, work, w = refs[-3:]
    pieces = len(refs) - 3
    size = v_ref.shape[-1]
    blocks = {}
    count = 0
    while count * (count + 1) // 2 < v_ref.shape[0]:
        count += 1
    for at, pair in enumerate(block_list(count)):
        blocks[pair] = at
    part = size // pieces
    for s in range(pieces):
        first = pl.multiple_of((place_ref[0] ^ s) * part, part)
        work[:, pl.ds(first, part), :] = refs[s][...] * factor
    tall = min(32, size)
    row = lax.broadcasted_iota(jnp.int32, (8, size), 0)
    lane = lax.broadcasted_iota(jnp.int32, (tall, size), 1)
    def panel(s, carry):
        base = pl.multiple_of(s * tall, tall)
        pd = [w[pl.ds(base + 8 * t, 8), :size] for t in range(tall // 8)]
        pi = [w[pl.ds(base + 8 * t, 8), size:] for t in range(tall // 8)]
        pd, pi = eliminate(pd, pi, base, row)
        w[pl.ds(base, tall), size:] = pi
        left = jnp.where(lane >= base + tall, pd, 0.0)
        lh, lm, ll = split3(left)
        rh, rm, rl = split3(jnp.concatenate([pd, pi], axis=1))
        a = jnp.concatenate([lh, lh, lm, lm, lh, ll], axis=0).astype(bf16)
        b = jnp.concatenate([rh, rm, rh, rm, rl, rh], axis=0).astype(bf16)
        w[...] = w[...] - tdot(a, b)
        return carry
    r0 = lax.broadcasted_iota(jnp.int32, (size, size), 0)
    c0 = lax.broadcasted_iota(jnp.int32, (size, size), 1)
    for k in range(count):
        w[:, :size] = work[blocks[k, k]]
        w[:, size:] = jnp.where(r0 == c0, 1.0, 0.0)
        lax.fori_loop(0, size // tall, panel, 0)
        inv = w[:, size:]
        ih, il = split(inv)
        todo = [v_ref.at[blocks[j, k]] for j in range(k)] + [work.at[blocks[k, j]] for j in range(k + 1, count)]
        v_ref[blocks[k, k]] = inv
        if todo:
            wide = jnp.concatenate([t[...] for t in todo], axis=1)
            wh, wl = split(wide)
            out = mm(ih, wl) + mm(il, wh) + mm(ih, wh)
            for n in range(k):
                v_ref[blocks[n, k]] = out[:, n * size : (n + 1) * size]
            if k + 1 < count:
                oh, ol = split(out)
                front = [oh[:, : k * size]] if k else []
                oh = jnp.concatenate(front + [ih, oh[:, k * size :]], axis=1)
                front = [ol[:, : k * size]] if k else []
                ol = jnp.concatenate(front + [il, ol[:, k * size :]], axis=1)
                ah, al = oh[:, (k + 1) * size :], ol[:, (k + 1) * size :]
                for i in range(k + 1, count):
                    lo = slice((i - k - 1) * size, (i - k) * size)
                    term = tdot(ah[:, lo], ol) + tdot(al[:, lo], oh) + tdot(ah[:, lo], oh)
                    for j in range(k + 1):
                        t = term[:, j * size : (j + 1) * size]
                        v_ref[blocks[j, i]] = -t if j == k else v_ref[blocks[j, i]] - t
                    for j in range(i, count):
                        t = term[:, j * size : (j + 1) * size]
                        work[blocks[i, j]] = work[blocks[i, j]] - t


def inverse_blocks(place, pieces, factor):
    blocks, _, size = pieces[0].shape
    shape = (blocks, size, size)
    return pl.pallas_call(
        functools.partial(inverse_kernel, factor),
        out_shape=jax.ShapeDtypeStruct(shape, f32),
        in_specs=[smem] + [vmem] * len(pieces),
        out_specs=vmem,
        scratch_shapes=[pltpu.VMEM(shape, f32), pltpu.VMEM((size, 2 * size), f32)],
        compiler_params=big,
        name="inverse",
    )(place, *pieces)


def rotate_kernel(v_ref, high, low, out_ref):
    owners, local, rows, cols = out_ref.shape
    size = v_ref.shape[-1]
    norb = owners * local
    count = norb // size
    vs = {}
    for at, (j, i) in enumerate(block_list(count)):
        vs[i, j] = split(v_ref[at])
    for i in range(count):
        vh = jnp.concatenate([vs[i, j][0] for j in range(i + 1)], axis=1)
        vl = jnp.concatenate([vs[i, j][1] for j in range(i + 1)], axis=1)
        upto = pl.ds(0, (i + 1) * size)
        total = mm(vh, low[upto, :]) + mm(vl, high[upto, :]) + mm(vh, high[upto, :])
        step = min(size, local)
        for q in range(size // step):
            row0 = i * size + q * step
            own, off = row0 // local, row0 % local
            for r in range(rows):
                out_ref[own, pl.ds(off, step), r, :] = total[
                    q * step : (q + 1) * step, r * cols : (r + 1) * cols
                ]


def rotate(v, high, low, owners, rows):
    norb, wide = high.shape
    return pl.pallas_call(
        rotate_kernel,
        out_shape=jax.ShapeDtypeStruct((owners, norb // owners, rows, wide // rows), f32),
        in_specs=[vmem] * 3,
        out_specs=vmem,
        compiler_params=big,
        name="rotate",
    )(v, high, low)


def swap_all(pieces, axis):
    count = len(pieces)
    return [pieces[0]] + [
        lax.ppermute(pieces[s], axis, [(i, i ^ s) for i in range(count)]) for s in range(1, count)
    ]


def tree_sum(values):
    while len(values) > 1:
        values = [values[i] + values[i + 1] for i in range(0, len(values), 2)]
    return values[0]


def orthonormalized(orbitals, potential):
    local, planes, rows, cols = orbitals.shape
    slabs = lax.axis_size("grid")
    owners = lax.axis_size("orb")
    chunks = 2 if local % (16 * slabs) == 0 else 1
    orbs = local // slabs // chunks
    everyone = ("orb", "grid")
    nx = slabs * planes
    place = lax.axis_index("grid").astype(jnp.int32).reshape(1)

    xy = plane_matrix(nx, rows)
    z = line_matrix(cols, 2 if orbs % 2 == 0 else 1)

    spread = jnp.broadcast_to(potential, (slabs, 1, planes, rows, cols))
    parts = [
        orbitals[c * slabs * orbs : (c + 1) * slabs * orbs].reshape(slabs, orbs, planes, rows, cols)
        for c in range(chunks)
    ]
    first = jnp.concatenate([parts[0], spread], axis=1)
    with_pot = lax.all_to_all(first, "grid", split_axis=0, concat_axis=0, tiled=True)
    arrived = [[with_pot]]
    for part in parts[1:]:
        pieces = [
            lax.dynamic_slice_in_dim(part, place[0] ^ s, 1, axis=0) for s in range(slabs)
        ]
        arrived.append(swap_all(pieces, "grid"))

    cells = []
    for c in range(chunks):
        filtered = filter_orbitals(place, arrived[c], with_pot, orbs, xy, z)
        if planes >= owners:
            each = planes // owners
            part_rows = each * rows
            filtered = filtered.reshape(owners, each, slabs, rows, orbs, cols)
        else:
            each = owners // planes
            part_rows = rows // each
            filtered = filtered.reshape(planes, slabs, each, part_rows, orbs, cols)
        filtered = jnp.swapaxes(filtered, 1, 2).reshape(owners * slabs, part_rows, orbs, cols)
        cells.append(lax.all_to_all(filtered, everyone, split_axis=0, concat_axis=0, tiled=True))

    size = 128
    total_cells = float(nx * rows * cols)
    *pieces, high, low = margin_blocks(place, cells, owners, slabs, size, slabs)
    mine = tree_sum(swap_all(pieces, "grid"))
    mine = tree_sum(swap_all([mine] * owners, "orb"))
    margin = swap_all([mine] * slabs, "grid")
    inverse = inverse_blocks(place, margin, 1.0 / total_cells)
    rotated = rotate(inverse, high, low, owners, part_rows)
    back = lax.all_to_all(rotated, "orb", split_axis=0, concat_axis=0, tiled=True)
    return jnp.swapaxes(back, 0, 1).reshape(local, planes, rows, cols)


def solution(mesh):
    in_specs = (P("orb", "grid", None, None), P("grid", None, None))
    out_specs = P("orb", "grid", None, None)
    return jax.shard_map(orthonormalized, mesh=mesh, in_specs=in_specs, out_specs=out_specs, check_vma=False)
```

profile of v0, /device:TPU:0, one launch (start us, length us, event | category | flops | bytes accessed | tf_op | source)
XLA Modules:
  0.0 223.1 jit_solution(6433945380554631693)
XLA Ops:
  0.0 1.7 fusion.12
  1.8 1.1 pad_maximum_fusion
  2.9 5.2 %all-to-all-start = ((f32[8,9,4,8,128]{4,3,2,1,0:T(8,128)}), f32[8,9,4,8,128]{4,3,2,1,0:T(8,128)S(1)}, u32[]{:S(2)}, u32[]{:S(2)}) async-start(f32[8,9,4,8,128]{4,3,2,1,0:T(8,128)} %pad_maximum_fusion), calls=%async_computation | async-start | bytes 2359296 | tf_op jit(solution)/shard_map/all_to_all | solution.py:358
  8.1 0.8 constant_dynamic-slice_fusion
  8.9 2.6 %collective-permute-start.6 = (f32[1,8,4,8,128]{4,3,2,1,0:T(8,128)S(1)}, f32[1,8,4,8,128]{4,3,2,1,0:T(8,128)S(1)}, u32[]{:S(2)}, u32[]{:S(2)}) collective-permute-start(f32[1,8,4,8,128]{4,3,2,1,0:T(8,128)S(1)} %get-tuple-element.27), channel_id=1, source_target_pairs={{0,28},{4,24},{8,20},{12,16},{16,12},{20,8},{24,4},{28,0},{1,29},{... | collective-permute-start | bytes 393224 | tf_op jit(solution)/shard_map/ppermute | solution.py:329
  11.5 0.4 collective-permute-start.5
  11.9 1.4 collective-permute-start.4
  13.5 1.5 collective-permute-start.2
  15.0 1.4 fusion.6.xy_ref
  16.4 10.8 %collective-permute-done.6.refs_7_ = f32[1,8,4,8,128]{4,3,2,1,0:T(8,128)S(1)} collective-permute-done((f32[1,8,4,8,128]{4,3,2,1,0:T(8,128)S(1)}, f32[1,8,4,8,128]{4,3,2,1,0:T(8,128)S(1)}, u32[]{:S(2)}, u32[]{:S(2)}) %collective-permute-start.6) | collective-permute-done | bytes 131104 | tf_op jit(solution)/shard_map/ppermute | solution.py:329
  27.2 0.6 collective-permute-start.1
  27.8 3.3 %collective-permute-done.5.refs_6_ = f32[1,8,4,8,128]{4,3,2,1,0:T(8,128)S(1)} collective-permute-done((f32[1,8,4,8,128]{4,3,2,1,0:T(8,128)S(1)}, f32[1,8,4,8,128]{4,3,2,1,0:T(8,128)S(1)}, u32[]{:S(2)}, u32[]{:S(2)}) %collective-permute-start.5) | collective-permute-done | bytes 131104 | tf_op jit(solution)/shard_map/ppermute | solution.py:329
  31.1 1.0 select_convert_fusion.z_ref
  32.1 3.1 %collective-permute-done.3.refs_4_ = f32[1,8,4,8,128]{4,3,2,1,0:T(8,128)S(1)} collective-permute-done((f32[1,8,4,8,128]{4,3,2,1,0:T(8,128)S(1)}, f32[1,8,4,8,128]{4,3,2,1,0:T(8,128)S(1)}, u32[]{:S(2)}, u32[]{:S(2)}) %collective-permute-start.3) | collective-permute-done | bytes 131104 | tf_op jit(solution)/shard_map/ppermute | solution.py:329
  35.3 0.5 copy-done.6
  36.3 6.3 %filter.3 = f32[4,8,8,8,128]{4,3,2,1,0:T(8,128)} custom-call(s32[1]{0:T(128)} %bitcast.place_ref, bf16[256,256]{1,0:T(8,128)(2,1)} %fusion.6.xy_ref, bf16[256,256]{1,0:T(8,128)(2,1)} %select_convert_fusion.z_ref, f32[8,9,4,8,128]{4,3,2,1,0:T(8,128)} %copy-done, f32[1,8,4,8,128]{4,3,2,1,0:T(8,128)} %get-tuple-element.34.refs_0_, ...), custom_call_target="tpu_custom_call" | custom-call | tf_op jit(solution)/shard_map/filter/pallas_call | solution.py:96
  42.6 4.9 %all-to-all-start.2 = ((f32[32,8,8,128]{3,2,1,0:T(8,128)}), f32[32,8,8,128]{3,2,1,0:T(8,128)S(1)}, u32[]{:S(2)}, u32[]{:S(2)}) async-start(f32[32,8,8,128]{3,2,1,0:T(8,128)} %bitcast.8), calls=%async_computation.2 | async-start | bytes 2097152 | tf_op jit(solution)/shard_map/all_to_all | solution.py:378
  47.5 6.2 %filter.2 = f32[4,8,8,8,128]{4,3,2,1,0:T(8,128)} custom-call(s32[1]{0:T(128)} %bitcast.place_ref, bf16[256,256]{1,0:T(8,128)(2,1)} %fusion.6.xy_ref, bf16[256,256]{1,0:T(8,128)(2,1)} %select_convert_fusion.z_ref, f32[8,9,4,8,128]{4,3,2,1,0:T(8,128)} %copy-done, f32[8,9,4,8,128]{4,3,2,1,0:T(8,128)} %copy-done), custom_call_target="tpu_custom_call" | custom-call | tf_op jit(solution)/shard_map/filter/pallas_call | solution.py:96
  53.7 20.0 %all-to-all-done.2.refs_1_ = f32[32,8,8,128]{3,2,1,0:T(8,128)S(1)} async-done(((f32[32,8,8,128]{3,2,1,0:T(8,128)}), f32[32,8,8,128]{3,2,1,0:T(8,128)S(1)}, u32[]{:S(2)}, u32[]{:S(2)}) %all-to-all-start.2) | async-done | bytes 1048608 | tf_op jit(solution)/shard_map/all_to_all | solution.py:378
  73.7 29.9 %all_to_all.20.refs_0_ = f32[32,8,8,128]{3,2,1,0:T(8,128)} all-to-all(f32[32,8,8,128]{3,2,1,0:T(8,128)} %bitcast.9), channel_id=1, replica_groups=mesh['grid'=8,'orb'=4] {'orb','grid'}, dimensions={0} | all-to-all | bytes 2097152 | tf_op jit(solution)/shard_map/all_to_all | solution.py:378
  103.7 5.4 %margin.1 = (f32[10,16,128]{2,1,0:T(8,128)}, f32[10,16,128]{2,1,0:T(8,128)}, f32[10,16,128]{2,1,0:T(8,128)}, f32[10,16,128]{2,1,0:T(8,128)}, f32[10,16,128]{2,1,...) custom-call(s32[1]{0:T(128)} %bitcast.place_ref, ...), custom_call_target="tpu_custom_call" | custom-call | tf_op jit(solution)/shard_map/margin/pallas_call | solution.py:153
  109.0 1.5 collective-permute-start.8
  110.9 1.5 collective-permute-start.10
  112.6 2.4 %collective-permute-start.12 = (f32[10,16,128]{2,1,0:T(8,128)}, f32[10,16,128]{2,1,0:T(8,128)S(1)}, u32[]{:S(2)}, u32[]{:S(2)}) collective-permute-start(f32[10,16,128]{2,1,0:T(8,128)} %get-tuple-element.21), channel_id=1, source_target_pairs={{0,24},{4,28},{8,16},{12,20},{16,8},{20,12},{24,0},{28,4},{1,25},{... | collective-permute-start | bytes 245768 | tf_op jit(solution)/shard_map/ppermute | solution.py:329
  115.0 0.7 collective-permute-start.13
  116.0 4.2 %collective-permute-done.11 = f32[10,16,128]{2,1,0:T(8,128)S(1)} collective-permute-done((f32[10,16,128]{2,1,0:T(8,128)}, f32[10,16,128]{2,1,0:T(8,128)S(1)}, u32[]{:S(2)}, u32[]{:S(2)}) %collective-permute-start.11) | collective-permute-done | bytes 81952 | tf_op jit(solution)/shard_map/ppermute | solution.py:329
  120.2 0.4 collective-permute-done.13
  120.6 0.9 add_add_fusion.2
  121.5 1.5 collective-permute-start.16
  123.0 0.9 collective-permute-start.15
  123.9 2.1 collective-permute-start.14
  126.0 2.8 %collective-permute-done.16 = f32[10,16,128]{2,1,0:T(8,128)S(1)} collective-permute-done((f32[10,16,128]{2,1,0:T(8,128)S(1)}, f32[10,16,128]{2,1,0:T(8,128)S(1)}, u32[]{:S(2)}, u32[]{:S(2)}) %collective-permute-start.16) | collective-permute-done | bytes 81952 | tf_op jit(solution)/shard_map/ppermute | solution.py:329
  128.8 3.0 %collective-permute-done.15 = f32[10,16,128]{2,1,0:T(8,128)S(1)} collective-permute-done((f32[10,16,128]{2,1,0:T(8,128)S(1)}, f32[10,16,128]{2,1,0:T(8,128)S(1)}, u32[]{:S(2)}, u32[]{:S(2)}) %collective-permute-start.15) | collective-permute-done | bytes 81952 | tf_op jit(solution)/shard_map/ppermute | solution.py:329
  131.9 1.8 collective-permute-start.23
  133.7 0.7 collective-permute-start.22
  134.4 1.1 collective-permute-start.21
  135.5 0.8 collective-permute-start.20
  136.3 1.1 collective-permute-start.19
  137.5 1.5 collective-permute-start.18
  139.0 0.4 collective-permute-done.22.refs_6_
  139.4 1.6 collective-permute-done.21.refs_5_
  141.0 1.8 collective-permute-done.20.refs_4_
  142.9 0.6 copy-done.13
  143.5 0.6 copy-done.16
  144.2 19.6 %inverse.1.v_ref = f32[10,128,128]{2,1,0:T(8,128)} custom-call(s32[1]{0:T(128)} %bitcast.place_ref, f32[10,16,128]{2,1,0:T(8,128)} %copy-done.2, f32[10,16,128]{2,1,0:T(8,128)} %copy-done.16, f32[10,16,128]{2,1,0:T(8,128)} %copy-done.15, f32[10,16,128]{2,1,0:T(8,128)} %copy-done.14, f32[10,16,128]{2,1,0:T(8,128)} %copy-done.13, f32[10,16,128]{2,1,0:T(8,128)} %copy-done.12, ...), custom_call_target="tpu_custom_call" | custom-call | tf_op jit(solution)/shard_map/inverse/pallas_call | solution.py:280
  163.7 5.5 %rotate.1 = f32[4,128,8,128]{3,2,1,0:T(8,128)} custom-call(f32[10,128,128]{2,1,0:T(8,128)} %inverse.1.v_ref, bf16[512,1024]{1,0:T(8,128)(2,1)} %get-tuple-element.23.high, bf16[512,1024]{1,0:T(8,128)(2,1)} %get-tuple-element.24.low), custom_call_target="tpu_custom_call" | custom-call | tf_op jit(solution)/shard_map/rotate/pallas_call | solution.py:316
  169.2 52.2 %all_to_all.21 = f32[4,128,8,128]{3,2,1,0:T(8,128)S(1)} all-to-all(f32[4,128,8,128]{3,2,1,0:T(8,128)} %rotate.1), channel_id=1, replica_groups=mesh['grid'=8,'orb'=4] {'orb'}, dimensions={0} | all-to-all | bytes 4194304 | tf_op jit(solution)/shard_map/all_to_all | solution.py:388
  221.4 1.6 copy.3
  (61 shorter events, 2.1 us)
Async XLA Ops:
  0.0 1.7 copy-start.17
  2.9 32.4 %all-to-all-start = ((f32[8,9,4,8,128]{4,3,2,1,0:T(8,128)}), f32[8,9,4,8,128]{4,3,2,1,0:T(8,128)S(1)}, u32[]{:S(2)}, u32[]{:S(2)}) async-start(f32[8,9,4,8,128]{4,3,2,1,0:T(8,128)} %pad_maximum_fusion), calls=%async_computation | async-start | bytes 2359296 | tf_op jit(solution)/shard_map/all_to_all | solution.py:358
  8.9 18.3 %collective-permute-start.6 = (f32[1,8,4,8,128]{4,3,2,1,0:T(8,128)S(1)}, f32[1,8,4,8,128]{4,3,2,1,0:T(8,128)S(1)}, u32[]{:S(2)}, u32[]{:S(2)}) collective-permute-start(f32[1,8,4,8,128]{4,3,2,1,0:T(8,128)S(1)} %get-tuple-element.27), channel_id=1, source_target_pairs={{0,28},{4,24},{8,20},{12,16},{16,12},{20,8},{24,4},{28,0},{1,29},{... | collective-permute-start | bytes 393224 | tf_op jit(solution)/shard_map/ppermute | solution.py:329
  11.5 19.6 %collective-permute-start.5 = (f32[1,8,4,8,128]{4,3,2,1,0:T(8,128)S(1)}, f32[1,8,4,8,128]{4,3,2,1,0:T(8,128)S(1)}, u32[]{:S(2)}, u32[]{:S(2)}) collective-permute-start(f32[1,8,4,8,128]{4,3,2,1,0:T(8,128)S(1)} %get-tuple-element.28), channel_id=1, source_target_pairs={{0,24},{4,28},{8,16},{12,20},{16,8},{20,12},{24,0},{28,4},{1,25},{... | collective-permute-start | bytes 393224 | tf_op jit(solution)/shard_map/ppermute | solution.py:329
  11.9 20.2 %collective-permute-start.4 = (f32[1,8,4,8,128]{4,3,2,1,0:T(8,128)S(1)}, f32[1,8,4,8,128]{4,3,2,1,0:T(8,128)S(1)}, u32[]{:S(2)}, u32[]{:S(2)}) collective-permute-start(f32[1,8,4,8,128]{4,3,2,1,0:T(8,128)S(1)} %get-tuple-element.29), channel_id=1, source_target_pairs={{0,20},{4,16},{8,28},{12,24},{16,4},{20,0},{24,12},{28,8},{1,21},{... | collective-permute-start | bytes 393224 | tf_op jit(solution)/shard_map/ppermute | solution.py:329
  13.2 21.9 %collective-permute-start.3 = (f32[1,8,4,8,128]{4,3,2,1,0:T(8,128)S(1)}, f32[1,8,4,8,128]{4,3,2,1,0:T(8,128)S(1)}, u32[]{:S(2)}, u32[]{:S(2)}) collective-permute-start(f32[1,8,4,8,128]{4,3,2,1,0:T(8,128)S(1)} %get-tuple-element.30), channel_id=1, source_target_pairs={{0,16},{4,20},{8,24},{12,28},{16,0},{20,4},{24,8},{28,12},{1,17},{... | collective-permute-start | bytes 393224 | tf_op jit(solution)/shard_map/ppermute | solution.py:329
  13.5 21.6 %collective-permute-start.2 = (f32[1,8,4,8,128]{4,3,2,1,0:T(8,128)S(1)}, f32[1,8,4,8,128]{4,3,2,1,0:T(8,128)S(1)}, u32[]{:S(2)}, u32[]{:S(2)}) collective-permute-start(f32[1,8,4,8,128]{4,3,2,1,0:T(8,128)S(1)} %get-tuple-element.31), channel_id=1, source_target_pairs={{0,12},{4,8},{8,4},{12,0},{16,28},{20,24},{24,20},{28,16},{1,13},{... | collective-permute-start | bytes 393224 | tf_op jit(solution)/shard_map/ppermute | solution.py:329
  27.2 8.1 %copy-start.3 = (f32[1,8,4,8,128]{4,3,2,1,0:T(8,128)}, f32[1,8,4,8,128]{4,3,2,1,0:T(8,128)S(1)}, u32[]{:S(2)}) copy-start(f32[1,8,4,8,128]{4,3,2,1,0:T(8,128)S(1)} %collective-permute-done.6.refs_7_) | copy-start | bytes 393220
  27.2 8.0 %collective-permute-start.1 = (f32[1,8,4,8,128]{4,3,2,1,0:T(8,128)S(1)}, f32[1,8,4,8,128]{4,3,2,1,0:T(8,128)S(1)}, u32[]{:S(2)}, u32[]{:S(2)}) collective-permute-start(f32[1,8,4,8,128]{4,3,2,1,0:T(8,128)S(1)} %get-tuple-element.32), channel_id=1, source_target_pairs={{0,8},{4,12},{8,0},{12,4},{16,24},{20,28},{24,16},{28,20},{1,9},{5... | collective-permute-start | bytes 393224 | tf_op jit(solution)/shard_map/ppermute | solution.py:329
  31.1 4.2 %copy-start.4 = (f32[1,8,4,8,128]{4,3,2,1,0:T(8,128)}, f32[1,8,4,8,128]{4,3,2,1,0:T(8,128)S(1)}, u32[]{:S(2)}) copy-start(f32[1,8,4,8,128]{4,3,2,1,0:T(8,128)S(1)} %collective-permute-done.5.refs_6_) | copy-start | bytes 393220
  31.1 4.1 %collective-permute-start = (f32[1,8,4,8,128]{4,3,2,1,0:T(8,128)S(1)}, f32[1,8,4,8,128]{4,3,2,1,0:T(8,128)S(1)}, u32[]{:S(2)}, u32[]{:S(2)}) collective-permute-start(f32[1,8,4,8,128]{4,3,2,1,0:T(8,128)S(1)} %get-tuple-element.33), channel_id=1, source_target_pairs={{0,4},{4,0},{8,12},{12,8},{16,20},{20,16},{24,28},{28,24},{1,5},{5... | collective-permute-start | bytes 393224 | tf_op jit(solution)/shard_map/ppermute | solution.py:329
  32.1 3.2 %copy-start.5 = (f32[1,8,4,8,128]{4,3,2,1,0:T(8,128)}, f32[1,8,4,8,128]{4,3,2,1,0:T(8,128)S(1)}, u32[]{:S(2)}) copy-start(f32[1,8,4,8,128]{4,3,2,1,0:T(8,128)S(1)} %collective-permute-done.4.refs_5_) | copy-start | bytes 393220
  35.1 0.7 copy-start.6
  35.2 0.7 copy-start.7
  35.2 0.7 copy-start.8
  35.2 0.7 copy-start.9
  35.2 1.1 copy-start
  42.6 31.1 %all-to-all-start.2 = ((f32[32,8,8,128]{3,2,1,0:T(8,128)}), f32[32,8,8,128]{3,2,1,0:T(8,128)S(1)}, u32[]{:S(2)}, u32[]{:S(2)}) async-start(f32[32,8,8,128]{3,2,1,0:T(8,128)} %bitcast.8), calls=%async_computation.2 | async-start | bytes 2097152 | tf_op jit(solution)/shard_map/all_to_all | solution.py:378
  73.7 29.9 %copy-start.1 = (f32[32,8,8,128]{3,2,1,0:T(8,128)}, f32[32,8,8,128]{3,2,1,0:T(8,128)S(1)}, u32[]{:S(2)}) copy-start(f32[32,8,8,128]{3,2,1,0:T(8,128)S(1)} %all-to-all-done.2.refs_1_) | copy-start | bytes 3145732
  109.0 3.6 %collective-permute-start.7 = (f32[10,16,128]{2,1,0:T(8,128)}, f32[10,16,128]{2,1,0:T(8,128)S(1)}, u32[]{:S(2)}, u32[]{:S(2)}) collective-permute-start(f32[10,16,128]{2,1,0:T(8,128)} %get-tuple-element.16), channel_id=1, source_target_pairs={{0,4},{4,0},{8,12},{12,8},{16,20},{20,16},{24,28},{28,24},{1,5},{5... | collective-permute-start | bytes 245768 | tf_op jit(solution)/shard_map/ppermute | solution.py:329
  109.0 6.0 %collective-permute-start.8 = (f32[10,16,128]{2,1,0:T(8,128)}, f32[10,16,128]{2,1,0:T(8,128)S(1)}, u32[]{:S(2)}, u32[]{:S(2)}) collective-permute-start(f32[10,16,128]{2,1,0:T(8,128)} %get-tuple-element.17), channel_id=1, source_target_pairs={{0,8},{4,12},{8,0},{12,4},{16,24},{20,28},{24,16},{28,20},{1,9},{5... | collective-permute-start | bytes 245768 | tf_op jit(solution)/shard_map/ppermute | solution.py:329
  110.6 5.1 %collective-permute-start.9 = (f32[10,16,128]{2,1,0:T(8,128)}, f32[10,16,128]{2,1,0:T(8,128)S(1)}, u32[]{:S(2)}, u32[]{:S(2)}) collective-permute-start(f32[10,16,128]{2,1,0:T(8,128)} %get-tuple-element.18), channel_id=1, source_target_pairs={{0,12},{4,8},{8,4},{12,0},{16,28},{20,24},{24,20},{28,16},{1,13},{... | collective-permute-start | bytes 245768 | tf_op jit(solution)/shard_map/ppermute | solution.py:329
  110.9 5.1 %collective-permute-start.10 = (f32[10,16,128]{2,1,0:T(8,128)}, f32[10,16,128]{2,1,0:T(8,128)S(1)}, u32[]{:S(2)}, u32[]{:S(2)}) collective-permute-start(f32[10,16,128]{2,1,0:T(8,128)} %get-tuple-element.19), channel_id=1, source_target_pairs={{0,16},{4,20},{8,24},{12,28},{16,0},{20,4},{24,8},{28,12},{1,17},{... | collective-permute-start | bytes 245768 | tf_op jit(solution)/shard_map/ppermute | solution.py:329
  112.4 7.8 %collective-permute-start.11 = (f32[10,16,128]{2,1,0:T(8,128)}, f32[10,16,128]{2,1,0:T(8,128)S(1)}, u32[]{:S(2)}, u32[]{:S(2)}) collective-permute-start(f32[10,16,128]{2,1,0:T(8,128)} %get-tuple-element.20), channel_id=1, source_target_pairs={{0,20},{4,16},{8,28},{12,24},{16,4},{20,0},{24,12},{28,8},{1,21},{... | collective-permute-start | bytes 245768 | tf_op jit(solution)/shard_map/ppermute | solution.py:329
  112.6 7.6 %collective-permute-start.12 = (f32[10,16,128]{2,1,0:T(8,128)}, f32[10,16,128]{2,1,0:T(8,128)S(1)}, u32[]{:S(2)}, u32[]{:S(2)}) collective-permute-start(f32[10,16,128]{2,1,0:T(8,128)} %get-tuple-element.21), channel_id=1, source_target_pairs={{0,24},{4,28},{8,16},{12,20},{16,8},{20,12},{24,0},{28,4},{1,25},{... | collective-permute-start | bytes 245768 | tf_op jit(solution)/shard_map/ppermute | solution.py:329
  115.0 5.6 %collective-permute-start.13 = (f32[10,16,128]{2,1,0:T(8,128)}, f32[10,16,128]{2,1,0:T(8,128)S(1)}, u32[]{:S(2)}, u32[]{:S(2)}) collective-permute-start(f32[10,16,128]{2,1,0:T(8,128)} %get-tuple-element.22), channel_id=1, source_target_pairs={{0,28},{4,24},{8,20},{12,16},{16,12},{20,8},{24,4},{28,0},{1,29},{... | collective-permute-start | bytes 245768 | tf_op jit(solution)/shard_map/ppermute | solution.py:329
  121.5 7.3 %collective-permute-start.16 = (f32[10,16,128]{2,1,0:T(8,128)S(1)}, f32[10,16,128]{2,1,0:T(8,128)S(1)}, u32[]{:S(2)}, u32[]{:S(2)}) collective-permute-start(f32[10,16,128]{2,1,0:T(8,128)S(1)} %add_add_fusion.2), channel_id=1, source_target_pairs={{0,3},{1,2},{2,1},{3,0},{4,7},{5,6},{6,5},{7,4},{8,11},{9,10},{10,... | collective-permute-start | bytes 245768 | tf_op jit(solution)/shard_map/ppermute | solution.py:329
  123.0 8.8 %collective-permute-start.15 = (f32[10,16,128]{2,1,0:T(8,128)S(1)}, f32[10,16,128]{2,1,0:T(8,128)S(1)}, u32[]{:S(2)}, u32[]{:S(2)}) collective-permute-start(f32[10,16,128]{2,1,0:T(8,128)S(1)} %add_add_fusion.2), channel_id=1, source_target_pairs={{0,2},{1,3},{2,0},{3,1},{4,6},{5,7},{6,4},{7,5},{8,10},{9,11},{10,... | collective-permute-start | bytes 245768 | tf_op jit(solution)/shard_map/ppermute | solution.py:329
  123.9 7.9 %collective-permute-start.14 = (f32[10,16,128]{2,1,0:T(8,128)S(1)}, f32[10,16,128]{2,1,0:T(8,128)S(1)}, u32[]{:S(2)}, u32[]{:S(2)}) collective-permute-start(f32[10,16,128]{2,1,0:T(8,128)S(1)} %add_add_fusion.2), channel_id=1, source_target_pairs={{0,1},{1,0},{2,3},{3,2},{4,5},{5,4},{6,7},{7,6},{8,9},{9,8},{10,11... | collective-permute-start | bytes 245768 | tf_op jit(solution)/shard_map/ppermute | solution.py:329
  131.9 11.0 %copy-start.2 = (f32[10,16,128]{2,1,0:T(8,128)}, f32[10,16,128]{2,1,0:T(8,128)S(1)}, u32[]{:S(2)}) copy-start(f32[10,16,128]{2,1,0:T(8,128)S(1)} %add_add_fusion.1.refs_0_) | copy-start | bytes 245764
  131.9 5.6 %collective-permute-start.23 = (f32[10,16,128]{2,1,0:T(8,128)S(1)}, f32[10,16,128]{2,1,0:T(8,128)S(1)}, u32[]{:S(2)}, u32[]{:S(2)}) collective-permute-start(f32[10,16,128]{2,1,0:T(8,128)S(1)} %add_add_fusion.1.refs_0_), channel_id=1, source_target_pairs={{0,28},{4,24},{8,20},{12,16},{16,12},{20,8},{24,4},{28,0},{1,29},{... | collective-permute-start | bytes 245768 | tf_op jit(solution)/shard_map/ppermute | solution.py:329
  133.7 5.8 %collective-permute-start.22 = (f32[10,16,128]{2,1,0:T(8,128)S(1)}, f32[10,16,128]{2,1,0:T(8,128)S(1)}, u32[]{:S(2)}, u32[]{:S(2)}) collective-permute-start(f32[10,16,128]{2,1,0:T(8,128)S(1)} %add_add_fusion.1.refs_0_), channel_id=1, source_target_pairs={{0,24},{4,28},{8,16},{12,20},{16,8},{20,12},{24,0},{28,4},{1,25},{... | collective-permute-start | bytes 245768 | tf_op jit(solution)/shard_map/ppermute | solution.py:329
  134.4 6.6 %collective-permute-start.21 = (f32[10,16,128]{2,1,0:T(8,128)S(1)}, f32[10,16,128]{2,1,0:T(8,128)S(1)}, u32[]{:S(2)}, u32[]{:S(2)}) collective-permute-start(f32[10,16,128]{2,1,0:T(8,128)S(1)} %add_add_fusion.1.refs_0_), channel_id=1, source_target_pairs={{0,20},{4,16},{8,28},{12,24},{16,4},{20,0},{24,12},{28,8},{1,21},{... | collective-permute-start | bytes 245768 | tf_op jit(solution)/shard_map/ppermute | solution.py:329
  135.5 7.4 %collective-permute-start.20 = (f32[10,16,128]{2,1,0:T(8,128)S(1)}, f32[10,16,128]{2,1,0:T(8,128)S(1)}, u32[]{:S(2)}, u32[]{:S(2)}) collective-permute-start(f32[10,16,128]{2,1,0:T(8,128)S(1)} %add_add_fusion.1.refs_0_), channel_id=1, source_target_pairs={{0,16},{4,20},{8,24},{12,28},{16,0},{20,4},{24,8},{28,12},{1,17},{... | collective-permute-start | bytes 245768 | tf_op jit(solution)/shard_map/ppermute | solution.py:329
  136.3 6.5 %collective-permute-start.19 = (f32[10,16,128]{2,1,0:T(8,128)S(1)}, f32[10,16,128]{2,1,0:T(8,128)S(1)}, u32[]{:S(2)}, u32[]{:S(2)}) collective-permute-start(f32[10,16,128]{2,1,0:T(8,128)S(1)} %add_add_fusion.1.refs_0_), channel_id=1, source_target_pairs={{0,12},{4,8},{8,4},{12,0},{16,28},{20,24},{24,20},{28,16},{1,13},{... | collective-permute-start | bytes 245768 | tf_op jit(solution)/shard_map/ppermute | solution.py:329
  137.5 5.4 %copy-start.10 = (f32[10,16,128]{2,1,0:T(8,128)}, f32[10,16,128]{2,1,0:T(8,128)S(1)}, u32[]{:S(2)}) copy-start(f32[10,16,128]{2,1,0:T(8,128)S(1)} %collective-permute-done.23.refs_7_) | copy-start | bytes 245764
  137.5 5.4 %collective-permute-start.18 = (f32[10,16,128]{2,1,0:T(8,128)S(1)}, f32[10,16,128]{2,1,0:T(8,128)S(1)}, u32[]{:S(2)}, u32[]{:S(2)}) collective-permute-start(f32[10,16,128]{2,1,0:T(8,128)S(1)} %add_add_fusion.1.refs_0_), channel_id=1, source_target_pairs={{0,8},{4,12},{8,0},{12,4},{16,24},{20,28},{24,16},{28,20},{1,9},{5... | collective-permute-start | bytes 245768 | tf_op jit(solution)/shard_map/ppermute | solution.py:329
  139.4 3.5 %copy-start.11 = (f32[10,16,128]{2,1,0:T(8,128)}, f32[10,16,128]{2,1,0:T(8,128)S(1)}, u32[]{:S(2)}) copy-start(f32[10,16,128]{2,1,0:T(8,128)S(1)} %collective-permute-done.22.refs_6_) | copy-start | bytes 245764
  139.4 3.4 %collective-permute-start.17 = (f32[10,16,128]{2,1,0:T(8,128)S(1)}, f32[10,16,128]{2,1,0:T(8,128)S(1)}, u32[]{:S(2)}, u32[]{:S(2)}) collective-permute-start(f32[10,16,128]{2,1,0:T(8,128)S(1)} %add_add_fusion.1.refs_0_), channel_id=1, source_target_pairs={{0,4},{4,0},{8,12},{12,8},{16,20},{20,16},{24,28},{28,24},{1,5},{5... | collective-permute-start | bytes 245768 | tf_op jit(solution)/shard_map/ppermute | solution.py:329
  141.0 1.9 copy-start.12
  142.8 0.6 copy-start.13
  142.9 0.7 copy-start.14
  142.9 0.7 copy-start.15
  143.5 0.6 copy-start.16
where the time goes:
time: 224 us; the launch traced here: 223 us
  blocking collectives  82.2 us (37%)
  waiting for transfers between devices  51.9 us (23%)
  Pallas kernels  42.9 us (19%)
  starting transfers between devices  35 us (16%)
  local copies, waits for them, and re-layouts  6.45 us (3%)
  other arithmetic  4.47 us (2%)
    all_to_all x1, blocking collectives, orthonormalized(): lax.all_to_all(rotated, 'orb', split_axis=0, concat_axis=0, tiled=True)  52.2 us
    ppermute x24, waiting for transfers between devices, swap_all(): lax.ppermute(pieces[s], axis, [(i, i ^ s) for i in range(count)])  31.9 us
    all_to_all x1, blocking collectives, orthonormalized(): lax.all_to_all(filtered, everyone, split_axis=0, concat_axis=0, tiled=True)  29.9 us
    ppermute x24, starting transfers between devices, swap_all(): lax.ppermute(pieces[s], axis, [(i, i ^ s) for i in range(count)])  24.9 us
    all_to_all x1, waiting for transfers between devices, orthonormalized(): lax.all_to_all(filtered, everyone, split_axis=0, concat_axis=0, tiled=True)  20 us
    pallas_call x1, Pallas kernels, inverse_blocks(): pl.pallas_call(functools.partial(inverse_kernel, factor), out_shape=jax.S...  19.6 us
    pallas_call x2, Pallas kernels, filter_orbitals(): pl.pallas_call(functools.partial(filter_kernel, orbs), out_shape=jax.Shap...  12.5 us
    pallas_call x1, Pallas kernels, rotate(): pl.pallas_call(rotate_kernel, out_shape=jax.ShapeDtypeStruct((owners, nor...  5.47 us
  transfers between devices with their start and end apart: 26, of which 14 were waited for; matrix products, arithmetic and copies ran while one was open for 1% of the time, Pallas kernels for 3%

commit v1 on v0

--- a/solution.py
+++ b/solution.py
@@ -113,16 +113,8 @@
     parts = refs[:chunks]
     outs = refs[chunks : chunks + pieces]
     high, low, acc = refs[chunks + pieces :]
-    _, rows, orbs, cols = parts[0].shape
-    norb = chunks * parts[0].shape[0] * orbs
-    span = slabs * orbs
-    for z in range(owners):
-        for c in range(chunks):
-            at = pl.ds((z * chunks + c) * span, span)
-            for r in range(rows):
-                h, l = split(parts[c][z * slabs : (z + 1) * slabs, r].reshape(span, cols))
-                high[at, r * cols : (r + 1) * cols] = h
-                low[at, r * cols : (r + 1) * cols] = l
+    norb = chunks * parts[0].shape[0] * parts[0].shape[2]
+    gather_cells(parts, owners, slabs, high, low)
     size = acc.shape[-1]
     contract = (((1,), (1,)), ((), ()))
     at = 0
@@ -175,6 +167,7 @@
 def eliminate(pd, pi, base, row):
     def spread(value, k):
         return jnp.broadcast_to(value[k : k + 1, :], value.shape)
+
     groups = len(pd)
     for t in range(groups):
         cols = []
@@ -213,13 +206,8 @@
 def inverse_kernel(factor, place_ref, *refs):
     v_ref, work, w = refs[-3:]
     pieces = len(refs) - 3
-    size = v_ref.shape[-1]
-    blocks = {}
-    count = 0
-    while count * (count + 1) // 2 < v_ref.shape[0]:
-        count += 1
-    for at, pair in enumerate(block_list(count)):
-        blocks[pair] = at
+    count, size, _ = v_ref.shape
+    blocks = {pair: at for at, pair in enumerate(block_list(count))}
     part = size // pieces
     for s in range(pieces):
         first = pl.multiple_of((place_ref[0] ^ s) * part, part)
@@ -227,6 +215,10 @@
     tall = min(32, size)
     row = lax.broadcasted_iota(jnp.int32, (8, size), 0)
     lane = lax.broadcasted_iota(jnp.int32, (tall, size), 1)
+
+    def cut(j):
+        return slice(j * size, (j + 1) * size)
+
     def panel(s, carry):
         base = pl.multiple_of(s * tall, tall)
         pd = [w[pl.ds(base + 8 * t, 8), :size] for t in range(tall // 8)]
@@ -240,6 +232,7 @@
         b = jnp.concatenate([rh, rm, rh, rm, rl, rh], axis=0).astype(bf16)
         w[...] = w[...] - tdot(a, b)
         return carry
+
     r0 = lax.broadcasted_iota(jnp.int32, (size, size), 0)
     c0 = lax.broadcasted_iota(jnp.int32, (size, size), 1)
     for k in range(count):
@@ -248,67 +241,81 @@
         lax.fori_loop(0, size // tall, panel, 0)
         inv = w[:, size:]
         ih, il = split(inv)
-        todo = [v_ref.at[blocks[j, k]] for j in range(k)] + [work.at[blocks[k, j]] for j in range(k + 1, count)]
-        v_ref[blocks[k, k]] = inv
-        if todo:
-            wide = jnp.concatenate([t[...] for t in todo], axis=1)
-            wh, wl = split(wide)
-            out = mm(ih, wl) + mm(il, wh) + mm(ih, wh)
-            for n in range(k):
-                v_ref[blocks[n, k]] = out[:, n * size : (n + 1) * size]
-            if k + 1 < count:
-                oh, ol = split(out)
-                front = [oh[:, : k * size]] if k else []
-                oh = jnp.concatenate(front + [ih, oh[:, k * size :]], axis=1)
-                front = [ol[:, : k * size]] if k else []
-                ol = jnp.concatenate(front + [il, ol[:, k * size :]], axis=1)
-                ah, al = oh[:, (k + 1) * size :], ol[:, (k + 1) * size :]
-                for i in range(k + 1, count):
-                    lo = slice((i - k - 1) * size, (i - k) * size)
-                    term = tdot(ah[:, lo], ol) + tdot(al[:, lo], oh) + tdot(ah[:, lo], oh)
-                    for j in range(k + 1):
-                        t = term[:, j * size : (j + 1) * size]
-                        v_ref[blocks[j, i]] = -t if j == k else v_ref[blocks[j, i]] - t
-                    for j in range(i, count):
-                        t = term[:, j * size : (j + 1) * size]
-                        work[blocks[i, j]] = work[blocks[i, j]] - t
-
-
-def inverse_blocks(place, pieces, factor):
+        if k + 1 < count:
+            v_ref[k, :, (k + 1) * size :] = jnp.zeros((size, (count - k - 1) * size), f32)
+        v_ref[k, :, cut(k)] = inv
+        todo = [v_ref[k, :, cut(j)] for j in range(k)] + [work[blocks[k, j]] for j in range(k + 1, count)]
+        if not todo:
+            continue
+        wh, wl = split(jnp.concatenate(todo, axis=1))
+        out = mm(ih, wl) + mm(il, wh) + mm(ih, wh)
+        if k:
+            v_ref[k, :, : k * size] = out[:, : k * size]
+        if k + 1 == count:
+            continue
+        oh, ol = split(out)
+        front = [oh[:, : k * size]] if k else []
+        oh = jnp.concatenate(front + [ih, oh[:, k * size :]], axis=1)
+        front = [ol[:, : k * size]] if k else []
+        ol = jnp.concatenate(front + [il, ol[:, k * size :]], axis=1)
+        ah, al = oh[:, (k + 1) * size :], ol[:, (k + 1) * size :]
+        for i in range(k + 1, count):
+            lo = cut(i - k - 1)
+            term = tdot(ah[:, lo], ol) + tdot(al[:, lo], oh) + tdot(ah[:, lo], oh)
+            for j in range(k + 1):
+                v_ref[i, :, cut(j)] = -term[:, cut(j)] if j == k else v_ref[i, :, cut(j)] - term[:, cut(j)]
+            for j in range(i, count):
+                work[blocks[i, j]] = work[blocks[i, j]] - term[:, cut(j)]
+
+
+def inverse_rows(place, pieces, factor):
     blocks, _, size = pieces[0].shape
-    shape = (blocks, size, size)
+    count = 1
+    while count * (count + 1) // 2 < blocks:
+        count += 1
     return pl.pallas_call(
         functools.partial(inverse_kernel, factor),
-        out_shape=jax.ShapeDtypeStruct(shape, f32),
+        out_shape=jax.ShapeDtypeStruct((count, size, count * size), f32),
         in_specs=[smem] + [vmem] * len(pieces),
         out_specs=vmem,
-        scratch_shapes=[pltpu.VMEM(shape, f32), pltpu.VMEM((size, 2 * size), f32)],
+        scratch_shapes=[pltpu.VMEM((blocks, size, size), f32), pltpu.VMEM((size, 2 * size), f32)],
         compiler_params=big,
         name="inverse",
     )(place, *pieces)
 
 
+def gather_cells(parts, owners, slabs, high, low):
+    _, rows, orbs, cols = parts[0].shape
+    span = slabs * orbs
+    for z in range(owners):
+        for c in range(len(parts)):
+            at = pl.ds((z * len(parts) + c) * span, span)
+            for r in range(rows):
+                h, l = split(parts[c][z * slabs : (z + 1) * slabs, r].reshape(span, cols))
+                high[at, r * cols : (r + 1) * cols] = h
+                low[at, r * cols : (r + 1) * cols] = l
+
+
+def product(weights, high, low):
+    h, l = split(weights)
+    return mm(h, low) + mm(l, high) + mm(h, high)
+
+
+def put_rows(out, value, rows, cols):
+    for r in range(rows):
+        out[:, r, :] = value[:, r * cols : (r + 1) * cols]
+
+
 def rotate_kernel(v_ref, high, low, out_ref):
-    owners, local, rows, cols = out_ref.shape
-    size = v_ref.shape[-1]
-    norb = owners * local
-    count = norb // size
-    vs = {}
-    for at, (j, i) in enumerate(block_list(count)):
-        vs[i, j] = split(v_ref[at])
+    _, local, rows, cols = out_ref.shape
+    count, size, _ = v_ref.shape
+    step = min(size, local)
     for i in range(count):
-        vh = jnp.concatenate([vs[i, j][0] for j in range(i + 1)], axis=1)
-        vl = jnp.concatenate([vs[i, j][1] for j in range(i + 1)], axis=1)
-        upto = pl.ds(0, (i + 1) * size)
-        total = mm(vh, low[upto, :]) + mm(vl, high[upto, :]) + mm(vh, high[upto, :])
-        step = min(size, local)
+        upto = (i + 1) * size
+        total = product(v_ref[i, :, :upto], high[pl.ds(0, upto), :], low[pl.ds(0, upto), :])
         for q in range(size // step):
-            row0 = i * size + q * step
-            own, off = row0 // local, row0 % local
-            for r in range(rows):
-                out_ref[own, pl.ds(off, step), r, :] = total[
-                    q * step : (q + 1) * step, r * cols : (r + 1) * cols
-                ]
+            own, off = divmod(i * size + q * step, local)
+            put_rows(out_ref.at[own, pl.ds(off, step)], total[q * step : (q + 1) * step], rows, cols)
 
 
 def rotate(v, high, low, owners, rows):
@@ -321,6 +328,103 @@
         compiler_params=big,
         name="rotate",
     )(v, high, low)
+
+
+def far_kernel(shape, layer_ref, v_ref, *refs):
+    owners, slabs, chunks = shape
+    below, above = refs[:chunks], refs[chunks : 2 * chunks]
+    outs, (high, low) = refs[2 * chunks : -2], refs[-2:]
+    _, rows, cols = outs[0].shape
+    layer = layer_ref[0]
+    for side, parts in ((1, below), (-1, above)):
+        gather_cells(parts, owners, slabs, high, low)
+        for hop in (2, 1):
+            to = jnp.clip(layer + side * hop, 0, owners - 1)
+            out = outs[(0 if side > 0 else 2) + hop - 1]
+            put_rows(out, product(v_ref[to], high[...], low[...]), rows, cols)
+
+
+def rotate_far(layer, v, below, above, owners, slabs):
+    _, rows, _, cols = below[0].shape
+    norb = v.shape[2]
+    wide = pltpu.VMEM((norb, rows * cols), bf16)
+    return pl.pallas_call(
+        functools.partial(far_kernel, (owners, slabs, len(below))),
+        out_shape=[jax.ShapeDtypeStruct((norb // owners, rows, cols), f32)] * 4,
+        in_specs=[smem] + [vmem] * (1 + 2 * len(below)),
+        out_specs=[vmem] * 4,
+        scratch_shapes=[wide, wide],
+        compiler_params=big,
+        name="rotate_far",
+    )(layer, v, *below, *above)
+
+
+def near_kernel(shape, layer_ref, v_ref, my_high, my_low, *refs):
+    owners, slabs, chunks = shape
+    below, above = refs[:chunks], refs[chunks : 2 * chunks]
+    out_ref, high, low = refs[2 * chunks :]
+    _, _, rows, cols = out_ref.shape
+    layer = layer_ref[0]
+
+    def put(plane, h, l):
+        value = product(v_ref[layer], h[...], l[...])
+        for r in range(rows):
+            out_ref[plane, :, r, :] = value[:, r * cols : (r + 1) * cols]
+
+    put(layer, my_high, my_low)
+
+    @pl.when(layer > 0)
+    def _():
+        gather_cells(below, owners, slabs, high, low)
+        put(jnp.maximum(layer - 1, 0), high, low)
+
+    @pl.when(layer < owners - 1)
+    def _():
+        gather_cells(above, owners, slabs, high, low)
+        put(jnp.minimum(layer + 1, owners - 1), high, low)
+
+
+def rotate_near(layer, v, high, low, below, above, owners, slabs):
+    _, rows, _, cols = below[0].shape
+    norb = v.shape[2]
+    wide = pltpu.VMEM((norb, rows * cols), bf16)
+    return pl.pallas_call(
+        functools.partial(near_kernel, (owners, slabs, len(below))),
+        out_shape=jax.ShapeDtypeStruct((owners, norb // owners, rows, cols), f32),
+        in_specs=[smem] + [vmem] * (3 + 2 * len(below)),
+        out_specs=vmem,
+        scratch_shapes=[wide, wide],
+        compiler_params=big,
+        name="rotate_near",
+    )(layer, v, high, low, *below, *above)
+
+
+def join_kernel(layer_ref, near_ref, up1, up2, down1, down2, out_ref):
+    owners = near_ref.shape[0]
+    for z in range(owners):
+
+        @pl.when(layer_ref[0] == z)
+        def _():
+            for p in range(owners):
+                source = {-3: up2, -2: up1, 2: down1, 3: down2}.get(p - z)
+                out_ref[:, p] = near_ref[p] if source is None else source[...]
+
+
+def join(layer, near, far):
+    owners, local, rows, cols = near.shape
+    return pl.pallas_call(
+        join_kernel,
+        out_shape=jax.ShapeDtypeStruct((local, owners, rows, cols), f32),
+        in_specs=[smem] + [vmem] * 5,
+        out_specs=vmem,
+        compiler_params=big,
+        name="join",
+    )(layer, near, *far)
+
+
+def shift(values, axis, by, count):
+    pairs = [(i, i + by) for i in range(count) if 0 <= i + by < count]
+    return [lax.ppermute(value, axis, pairs) for value in values]
 
 
 def swap_all(pieces, axis):
@@ -380,13 +484,27 @@
     size = 128
     total_cells = float(nx * rows * cols)
     *pieces, high, low = margin_blocks(place, cells, owners, slabs, size, slabs)
+    nearby = owners == 4 and planes == owners
+    if nearby:
+        below = shift(cells, "orb", 1, owners)
+        above = shift(cells, "orb", -1, owners)
     mine = tree_sum(swap_all(pieces, "grid"))
     mine = tree_sum(swap_all([mine] * owners, "orb"))
     margin = swap_all([mine] * slabs, "grid")
-    inverse = inverse_blocks(place, margin, 1.0 / total_cells)
-    rotated = rotate(inverse, high, low, owners, part_rows)
-    back = lax.all_to_all(rotated, "orb", split_axis=0, concat_axis=0, tiled=True)
-    return jnp.swapaxes(back, 0, 1).reshape(local, planes, rows, cols)
+    inverse = inverse_rows(place, margin, 1.0 / total_cells)
+    if not nearby:
+        rotated = rotate(inverse, high, low, owners, part_rows)
+        back = lax.all_to_all(rotated, "orb", split_axis=0, concat_axis=0, tiled=True)
+        return jnp.swapaxes(back, 0, 1).reshape(local, planes, rows, cols)
+    layer = lax.axis_index("orb").astype(jnp.int32).reshape(1)
+    up1, up2, down1, down2 = rotate_far(layer, inverse, below, above, owners, slabs)
+    inner = range(1, owners - 1)
+    up2 = lax.ppermute(up2, "orb", [(i, i + 2) for i in inner if i + 2 < owners])
+    down2 = lax.ppermute(down2, "orb", [(i, i - 2) for i in inner if i >= 2])
+    up1 = lax.ppermute(up1, "orb", [(i, i + 1) for i in inner])
+    down1 = lax.ppermute(down1, "orb", [(i, i - 1) for i in inner])
+    near = rotate_near(layer, inverse, high, low, below, above, owners, slabs)
+    return join(layer, near, (up1, up2, down1, down2))
 
 
 def solution(mesh):

time: 224 us -> 279 us (1.25)
  waiting for transfers between devices: 51.9 us -> 135 us
  blocking collectives: 82.2 us -> 29.9 us
  starting transfers between devices: 35 us -> 47.4 us
  Pallas kernels: 42.9 us -> 54.9 us
    ppermute x24, waiting for transfers between devices: 31.9 us -> 91.1 us  [swap_all(): lax.ppermute(pieces[s], axis, [(i, i ^ s) for i in range(count)])]
    all_to_all x1 -> x0, blocking collectives: 52.2 us -> none  [orthonormalized(): lax.all_to_all(rotated, 'orb', split_axis=0, concat_axis=0, tiled=True)]
    ppermute x0 -> x8, waiting for transfers between devices: none -> 24.1 us  [the longest x1 12.4 us: orthonormalized(): down2 = lax.ppermute(down2, 'orb', [(i, i - 2) for i in inner if i >= 2])]
    ppermute x0 -> x8, starting transfers between devices: none -> 16.7 us  [the longest x4 12.7 us: shift(): return [lax.ppermute(value, axis, pairs) for value in values]]
    pallas_call x2 -> x4, Pallas kernels: 25 us -> 37 us  [the longest x1 19.8 us: inverse_rows(): pl.pallas_call(functools.partial(inverse_kernel, factor), out_shape=jax.S...]
    ppermute x24, starting transfers between devices: 24.9 us -> 20.5 us  [swap_all(): lax.ppermute(pieces[s], axis, [(i, i ^ s) for i in range(count)])]
  transfers between devices with their start and end apart: 26 -> 34, of which waited for: 14 -> 19; matrix products, arithmetic and copies ran while one was open for 1% -> 1% of each run, Pallas kernels for 3% -> 12%
where the time goes in v1:
time: 279 us; the launch traced here: 278 us
  waiting for transfers between devices  135 us (48%)
  Pallas kernels  54.9 us (20%)
  starting transfers between devices  47.4 us (17%)
  blocking collectives  29.9 us (11%)
  local copies, waits for them, and re-layouts  6.37 us (2%)
  other arithmetic  4.44 us (2%)
    ppermute x24, waiting for transfers between devices, swap_all(): lax.ppermute(pieces[s], axis, [(i, i ^ s) for i in range(count)])  91.1 us
    all_to_all x1, blocking collectives, orthonormalized(): lax.all_to_all(filtered, everyone, split_axis=0, concat_axis=0, tiled=True)  29.9 us
    ppermute x24, starting transfers between devices, swap_all(): lax.ppermute(pieces[s], axis, [(i, i ^ s) for i in range(count)])  20.5 us
    all_to_all x1, waiting for transfers between devices, orthonormalized(): lax.all_to_all(filtered, everyone, split_axis=0, concat_axis=0, tiled=True)  20 us
    pallas_call x1, Pallas kernels, inverse_rows(): pl.pallas_call(functools.partial(inverse_kernel, factor), out_shape=jax.S...  19.8 us
    ppermute x4, starting transfers between devices, shift(): return [lax.ppermute(value, axis, pairs) for value in values]  12.7 us
    pallas_call x2, Pallas kernels, filter_orbitals(): pl.pallas_call(functools.partial(filter_kernel, orbs), out_shape=jax.Shap...  12.5 us
    ppermute x1, waiting for transfers between devices, orthonormalized(): down2 = lax.ppermute(down2, 'orb', [(i, i - 2) for i in inner if i >= 2])  12.4 us
  transfers between devices with their start and end apart: 34, of which 19 were waited for; matrix products, arithmetic and copies ran while one was open for 1% of the time, Pallas kernels for 12%

profile of v1, /device:TPU:0, one launch (start us, length us, event | category | flops | bytes accessed | tf_op | source)
XLA Modules:
  0.0 278.5 jit_solution(10876875158128458651)
XLA Ops:
  0.0 1.7 fusion.12
  1.8 1.1 pad_maximum_fusion
  2.9 5.2 %all-to-all-start = ((f32[8,9,4,8,128]{4,3,2,1,0:T(8,128)}), f32[8,9,4,8,128]{4,3,2,1,0:T(8,128)S(1)}, u32[]{:S(2)}, u32[]{:S(2)}) async-start(f32[8,9,4,8,128]{4,3,2,1,0:T(8,128)} %pad_maximum_fusion), calls=%async_computation | async-start | bytes 2359296 | tf_op jit(solution)/shard_map/all_to_all | solution.py:462
  8.8 2.6 collective-permute-start.6
  11.9 1.4 collective-permute-start.4
  13.5 1.5 collective-permute-start.2
  15.0 1.4 fusion.6.xy_ref
  16.4 10.8 %collective-permute-done.6.refs_7_ = f32[1,8,4,8,128]{4,3,2,1,0:T(8,128)S(1)} collective-permute-done((f32[1,8,4,8,128]{4,3,2,1,0:T(8,128)S(1)}, f32[1,8,4,8,128]{4,3,2,1,0:T(8,128)S(1)}, u32[]{:S(2)}, u32[]{:S(2)}) %collective-permute-start.6) | collective-permute-done | bytes 131104 | tf_op jit(solution)/shard_map/ppermute | solution.py:433
  27.8 3.3 %collective-permute-done.5.refs_6_ = f32[1,8,4,8,128]{4,3,2,1,0:T(8,128)S(1)} collective-permute-done((f32[1,8,4,8,128]{4,3,2,1,0:T(8,128)S(1)}, f32[1,8,4,8,128]{4,3,2,1,0:T(8,128)S(1)}, u32[]{:S(2)}, u32[]{:S(2)}) %collective-permute-start.5) | collective-permute-done | bytes 131104 | tf_op jit(solution)/shard_map/ppermute | solution.py:433
  31.1 0.9 select_convert_fusion.z_ref
  32.0 3.1 %collective-permute-done.3.refs_4_ = f32[1,8,4,8,128]{4,3,2,1,0:T(8,128)S(1)} collective-permute-done((f32[1,8,4,8,128]{4,3,2,1,0:T(8,128)S(1)}, f32[1,8,4,8,128]{4,3,2,1,0:T(8,128)S(1)}, u32[]{:S(2)}, u32[]{:S(2)}) %collective-permute-start.3) | collective-permute-done | bytes 131104 | tf_op jit(solution)/shard_map/ppermute | solution.py:433
  36.3 6.3 %filter.3 = f32[4,8,8,8,128]{4,3,2,1,0:T(8,128)} custom-call(s32[1]{0:T(128)} %bitcast.1.place_ref, bf16[256,256]{1,0:T(8,128)(2,1)} %fusion.6.xy_ref, bf16[256,256]{1,0:T(8,128)(2,1)} %select_convert_fusion.z_ref, f32[8,9,4,8,128]{4,3,2,1,0:T(8,128)} %copy-done, f32[1,8,4,8,128]{4,3,2,1,0:T(8,128)} %get-tuple-element.42.refs_0_, ...), custom_call_target="tpu_custom_call" | custom-call | tf_op jit(solution)/shard_map/filter/pallas_call | solution.py:96
  42.6 4.9 %all-to-all-start.2 = ((f32[32,8,8,128]{3,2,1,0:T(8,128)}), f32[32,8,8,128]{3,2,1,0:T(8,128)S(1)}, u32[]{:S(2)}, u32[]{:S(2)}) async-start(f32[32,8,8,128]{3,2,1,0:T(8,128)} %bitcast.7), calls=%async_computation.2 | async-start | bytes 2097152 | tf_op jit(solution)/shard_map/all_to_all | solution.py:482
  47.5 6.2 %filter.2 = f32[4,8,8,8,128]{4,3,2,1,0:T(8,128)} custom-call(s32[1]{0:T(128)} %bitcast.1.place_ref, bf16[256,256]{1,0:T(8,128)(2,1)} %fusion.6.xy_ref, bf16[256,256]{1,0:T(8,128)(2,1)} %select_convert_fusion.z_ref, f32[8,9,4,8,128]{4,3,2,1,0:T(8,128)} %copy-done, f32[8,9,4,8,128]{4,3,2,1,0:T(8,128)} %copy-done), custom_call_target="tpu_custom_call" | custom-call | tf_op jit(solution)/shard_map/filter/pallas_call | solution.py:96
  53.8 20.0 %all-to-all-done.2.refs_1_ = f32[32,8,8,128]{3,2,1,0:T(8,128)S(1)} async-done(((f32[32,8,8,128]{3,2,1,0:T(8,128)}), f32[32,8,8,128]{3,2,1,0:T(8,128)S(1)}, u32[]{:S(2)}, u32[]{:S(2)}) %all-to-all-start.2) | async-done | bytes 1048608 | tf_op jit(solution)/shard_map/all_to_all | solution.py:482
  73.7 29.9 %all_to_all.15.refs_0_ = f32[32,8,8,128]{3,2,1,0:T(8,128)} all-to-all(f32[32,8,8,128]{3,2,1,0:T(8,128)} %bitcast.8), channel_id=1, replica_groups=mesh['grid'=8,'orb'=4] {'orb','grid'}, dimensions={0} | all-to-all | bytes 2097152 | tf_op jit(solution)/shard_map/all_to_all | solution.py:482
  103.7 5.4 %margin.1 = (f32[10,16,128]{2,1,0:T(8,128)}, f32[10,16,128]{2,1,0:T(8,128)}, f32[10,16,128]{2,1,0:T(8,128)}, f32[10,16,128]{2,1,0:T(8,128)}, f32[10,16,128]{2,1,...) custom-call(s32[1]{0:T(128)} %bitcast.1.place_ref, ...), custom_call_target="tpu_custom_call" | custom-call | tf_op jit(solution)/shard_map/margin/pallas_call | solution.py:145
  109.1 1.5 collective-permute-start.8
  110.9 1.5 collective-permute-start.10
  112.7 2.4 collective-permute-start.12
  116.1 4.1 %collective-permute-done.11 = f32[10,16,128]{2,1,0:T(8,128)S(1)} collective-permute-done((f32[10,16,128]{2,1,0:T(8,128)}, f32[10,16,128]{2,1,0:T(8,128)S(1)}, u32[]{:S(2)}, u32[]{:S(2)}) %collective-permute-start.11) | collective-permute-done | bytes 81952 | tf_op jit(solution)/shard_map/ppermute | solution.py:433
  120.7 0.9 add_add_fusion.2
  121.6 1.5 collective-permute-start.16
  123.1 1.3 collective-permute-start.26
  124.4 4.6 %collective-permute-start.24 = (f32[32,8,8,128]{3,2,1,0:T(8,128)S(1)}, f32[32,8,8,128]{3,2,1,0:T(8,128)S(1)}, u32[]{:S(2)}, u32[]{:S(2)}) collective-permute-start(f32[32,8,8,128]{3,2,1,0:T(8,128)S(1)} %copy-done.2), channel_id=1, source_target_pairs={{0,1},{1,2},{2,3},{4,5},{5,6},{6,7},{8,9},{9,10},{10,11},{12,13},{... | collective-permute-start | bytes 3145736 | tf_op jit(solution)/shard_map/ppermute | solution.py:427
  129.0 1.3 collective-permute-start.27
  130.3 5.6 %collective-permute-start.25 = (f32[32,8,8,128]{3,2,1,0:T(8,128)}, f32[32,8,8,128]{3,2,1,0:T(8,128)}, u32[]{:S(2)}, u32[]{:S(2)}) collective-permute-start(f32[32,8,8,128]{3,2,1,0:T(8,128)} %copy-done.1), channel_id=1, source_target_pairs={{0,1},{1,2},{2,3},{4,5},{5,6},{6,7},{8,9},{9,10},{10,11},{12,13},{... | collective-permute-start | bytes 3145736 | tf_op jit(solution)/shard_map/ppermute | solution.py:427
  135.9 1.1 collective-permute-start.15
  137.0 39.9 %collective-permute-done.15 = f32[10,16,128]{2,1,0:T(8,128)S(1)} collective-permute-done((f32[10,16,128]{2,1,0:T(8,128)S(1)}, f32[10,16,128]{2,1,0:T(8,128)S(1)}, u32[]{:S(2)}, u32[]{:S(2)}) %collective-permute-start.15) | collective-permute-done | bytes 81952 | tf_op jit(solution)/shard_map/ppermute | solution.py:433
  176.8 1.0 collective-permute-start.14
  177.8 3.4 %collective-permute-done.14 = f32[10,16,128]{2,1,0:T(8,128)S(1)} collective-permute-done((f32[10,16,128]{2,1,0:T(8,128)S(1)}, f32[10,16,128]{2,1,0:T(8,128)S(1)}, u32[]{:S(2)}, u32[]{:S(2)}) %collective-permute-start.14) | collective-permute-done | bytes 81952 | tf_op jit(solution)/shard_map/ppermute | solution.py:433
  181.4 4.8 %collective-permute-done.23.refs_7_ = f32[10,16,128]{2,1,0:T(8,128)S(1)} collective-permute-done((f32[10,16,128]{2,1,0:T(8,128)S(1)}, f32[10,16,128]{2,1,0:T(8,128)S(1)}, u32[]{:S(2)}, u32[]{:S(2)}) %collective-permute-start.23) | collective-permute-done | bytes 81952 | tf_op jit(solution)/shard_map/ppermute | solution.py:433
  186.2 1.5 collective-permute-start.22
  187.7 3.9 %collective-permute-done.22.refs_6_ = f32[10,16,128]{2,1,0:T(8,128)S(1)} collective-permute-done((f32[10,16,128]{2,1,0:T(8,128)S(1)}, f32[10,16,128]{2,1,0:T(8,128)S(1)}, u32[]{:S(2)}, u32[]{:S(2)}) %collective-permute-start.22) | collective-permute-done | bytes 81952 | tf_op jit(solution)/shard_map/ppermute | solution.py:433
  191.6 4.7 %collective-permute-done.21.refs_5_ = f32[10,16,128]{2,1,0:T(8,128)S(1)} collective-permute-done((f32[10,16,128]{2,1,0:T(8,128)S(1)}, f32[10,16,128]{2,1,0:T(8,128)S(1)}, u32[]{:S(2)}, u32[]{:S(2)}) %collective-permute-start.21) | collective-permute-done | bytes 81952 | tf_op jit(solution)/shard_map/ppermute | solution.py:433
  196.9 3.8 %collective-permute-done.20.refs_4_ = f32[10,16,128]{2,1,0:T(8,128)S(1)} collective-permute-done((f32[10,16,128]{2,1,0:T(8,128)S(1)}, f32[10,16,128]{2,1,0:T(8,128)S(1)}, u32[]{:S(2)}, u32[]{:S(2)}) %collective-permute-start.20) | collective-permute-done | bytes 81952 | tf_op jit(solution)/shard_map/ppermute | solution.py:433
  200.7 3.9 %collective-permute-done.19.refs_3_ = f32[10,16,128]{2,1,0:T(8,128)S(1)} collective-permute-done((f32[10,16,128]{2,1,0:T(8,128)S(1)}, f32[10,16,128]{2,1,0:T(8,128)S(1)}, u32[]{:S(2)}, u32[]{:S(2)}) %collective-permute-start.19) | collective-permute-done | bytes 81952 | tf_op jit(solution)/shard_map/ppermute | solution.py:433
  204.6 1.4 collective-permute-start.18
  206.1 3.0 %collective-permute-done.18.refs_2_ = f32[10,16,128]{2,1,0:T(8,128)S(1)} collective-permute-done((f32[10,16,128]{2,1,0:T(8,128)S(1)}, f32[10,16,128]{2,1,0:T(8,128)S(1)}, u32[]{:S(2)}, u32[]{:S(2)}) %collective-permute-start.18) | collective-permute-done | bytes 81952 | tf_op jit(solution)/shard_map/ppermute | solution.py:433
  209.7 1.4 collective-permute-done.17.refs_1_
  211.2 19.8 %inverse.1.v_ref = f32[4,128,512]{2,1,0:T(8,128)} custom-call(s32[1]{0:T(128)} %bitcast.1.place_ref, f32[10,16,128]{2,1,0:T(8,128)} %copy-done.9, f32[10,16,128]{2,1,0:T(8,128)} %collective-permute-done.17.refs_1_, f32[10,16,128]{2,1,0:T(8,128)} %copy-done.22, f32[10,16,128]{2,1,0:T(8,128)} %copy-done.21, f32[10,16,128]{2,1,0:T(8,128)} %copy-done.20, ...), custom_call_target="tpu_custom_call" | custom-call | tf_op jit(solution)/shard_map/inverse/pallas_call | solution.py:276
  232.3 7.0 %rotate_far.1 = (f32[128,8,128]{2,1,0:T(8,128)}, f32[128,8,128]{2,1,0:T(8,128)}, f32[128,8,128]{2,1,0:T(8,128)}, f32[128,8,128]{2,1,0:T(8,128)}) custom-call(s32[1]{0:T(128)} %bitcast.layer_ref, f32[4,128,512]{2,1,0:T(8,128)} %inverse.1.v_ref, f32[32,8,8,128]{3,2,1,0:T(8,128)} %copy-done.4, f32[32,8,8,128]{3,2,1,0:T(8,128)} %collective-permute-done.25.refs_1_, ...), custom_call_target="tpu_custom_call" | custom-call | tf_op jit(solution)/shard_map/rotate_far/pallas_call | solution.py:351
  240.7 1.3 collective-permute-start.30
  242.0 1.3 collective-permute-start.31
  243.3 6.4 %rotate_near.1.near_ref = f32[4,128,8,128]{3,2,1,0:T(8,128)} custom-call(s32[1]{0:T(128)} %bitcast.layer_ref, f32[4,128,512]{2,1,0:T(8,128)} %inverse.1.v_ref, bf16[512,1024]{1,0:T(8,128)(2,1)} %get-tuple-element.27.my_high, bf16[512,1024]{1,0:T(8,128)(2,1)} %get-tuple-element.28.my_low, f32[32,8,8,128]{3,2,1,0:T(8,128)} %copy-done.4, ...), custom_call_target="tpu_custom_call" | custom-call | tf_op jit(solution)/shard_map/rotate_near/pallas_call | solution.py:391
  249.7 11.7 %collective-permute-done.30.down1 = f32[128,8,128]{2,1,0:T(8,128)S(1)} collective-permute-done((f32[128,8,128]{2,1,0:T(8,128)}, f32[128,8,128]{2,1,0:T(8,128)S(1)}, u32[]{:S(2)}, u32[]{:S(2)}) %collective-permute-start.30) | collective-permute-done | bytes 524320 | tf_op jit(solution)/shard_map/ppermute | solution.py:505
  261.5 12.4 %collective-permute-done.31.down2 = f32[128,8,128]{2,1,0:T(8,128)S(1)} collective-permute-done((f32[128,8,128]{2,1,0:T(8,128)}, f32[128,8,128]{2,1,0:T(8,128)S(1)}, u32[]{:S(2)}, u32[]{:S(2)}) %collective-permute-start.31) | collective-permute-done | bytes 524320 | tf_op jit(solution)/shard_map/ppermute | solution.py:503
  274.7 3.8 %join.1 = f32[128,4,8,128]{3,2,1,0:T(8,128)} custom-call(s32[1]{0:T(128)} %bitcast.layer_ref, f32[4,128,8,128]{3,2,1,0:T(8,128)} %rotate_near.1.near_ref, f32[128,8,128]{2,1,0:T(8,128)} %copy-done.5, f32[128,8,128]{2,1,0:T(8,128)} %copy-done.6, f32[128,8,128]{2,1,0:T(8,128)} %copy-done.7, f32[128,8,128]{2,1,0:T(8,128)} %copy-done.8), custom_call_target="tpu_custom_call" | custom-call | tf_op jit(solution)/shard_map/join/pallas_call | solution.py:415
  (89 shorter events, 10.2 us)
Async XLA Ops:
  2.9 32.4 %all-to-all-start = ((f32[8,9,4,8,128]{4,3,2,1,0:T(8,128)}), f32[8,9,4,8,128]{4,3,2,1,0:T(8,128)S(1)}, u32[]{:S(2)}, u32[]{:S(2)}) async-start(f32[8,9,4,8,128]{4,3,2,1,0:T(8,128)} %pad_maximum_fusion), calls=%async_computation | async-start | bytes 2359296 | tf_op jit(solution)/shard_map/all_to_all | solution.py:462
  8.8 18.4 %collective-permute-start.6 = (f32[1,8,4,8,128]{4,3,2,1,0:T(8,128)S(1)}, f32[1,8,4,8,128]{4,3,2,1,0:T(8,128)S(1)}, u32[]{:S(2)}, u32[]{:S(2)}) collective-permute-start(f32[1,8,4,8,128]{4,3,2,1,0:T(8,128)S(1)} %get-tuple-element.35), channel_id=1, source_target_pairs={{0,28},{4,24},{8,20},{12,16},{16,12},{20,8},{24,4},{28,0},{1,29},{... | collective-permute-start | bytes 393224 | tf_op jit(solution)/shard_map/ppermute | solution.py:433
  11.5 19.6 %collective-permute-start.5 = (f32[1,8,4,8,128]{4,3,2,1,0:T(8,128)S(1)}, f32[1,8,4,8,128]{4,3,2,1,0:T(8,128)S(1)}, u32[]{:S(2)}, u32[]{:S(2)}) collective-permute-start(f32[1,8,4,8,128]{4,3,2,1,0:T(8,128)S(1)} %get-tuple-element.36), channel_id=1, source_target_pairs={{0,24},{4,28},{8,16},{12,20},{16,8},{20,12},{24,0},{28,4},{1,25},{... | collective-permute-start | bytes 393224 | tf_op jit(solution)/shard_map/ppermute | solution.py:433
  11.9 20.2 %collective-permute-start.4 = (f32[1,8,4,8,128]{4,3,2,1,0:T(8,128)S(1)}, f32[1,8,4,8,128]{4,3,2,1,0:T(8,128)S(1)}, u32[]{:S(2)}, u32[]{:S(2)}) collective-permute-start(f32[1,8,4,8,128]{4,3,2,1,0:T(8,128)S(1)} %get-tuple-element.37), channel_id=1, source_target_pairs={{0,20},{4,16},{8,28},{12,24},{16,4},{20,0},{24,12},{28,8},{1,21},{... | collective-permute-start | bytes 393224 | tf_op jit(solution)/shard_map/ppermute | solution.py:433
  13.2 21.9 %collective-permute-start.3 = (f32[1,8,4,8,128]{4,3,2,1,0:T(8,128)S(1)}, f32[1,8,4,8,128]{4,3,2,1,0:T(8,128)S(1)}, u32[]{:S(2)}, u32[]{:S(2)}) collective-permute-start(f32[1,8,4,8,128]{4,3,2,1,0:T(8,128)S(1)} %get-tuple-element.38), channel_id=1, source_target_pairs={{0,16},{4,20},{8,24},{12,28},{16,0},{20,4},{24,8},{28,12},{1,17},{... | collective-permute-start | bytes 393224 | tf_op jit(solution)/shard_map/ppermute | solution.py:433
  13.5 21.6 %collective-permute-start.2 = (f32[1,8,4,8,128]{4,3,2,1,0:T(8,128)S(1)}, f32[1,8,4,8,128]{4,3,2,1,0:T(8,128)S(1)}, u32[]{:S(2)}, u32[]{:S(2)}) collective-permute-start(f32[1,8,4,8,128]{4,3,2,1,0:T(8,128)S(1)} %get-tuple-element.39), channel_id=1, source_target_pairs={{0,12},{4,8},{8,4},{12,0},{16,28},{20,24},{24,20},{28,16},{1,13},{... | collective-permute-start | bytes 393224 | tf_op jit(solution)/shard_map/ppermute | solution.py:433
  27.2 8.1 %copy-start.10 = (f32[1,8,4,8,128]{4,3,2,1,0:T(8,128)}, f32[1,8,4,8,128]{4,3,2,1,0:T(8,128)S(1)}, u32[]{:S(2)}) copy-start(f32[1,8,4,8,128]{4,3,2,1,0:T(8,128)S(1)} %collective-permute-done.6.refs_7_) | copy-start | bytes 393220
  27.2 8.0 %collective-permute-start.1 = (f32[1,8,4,8,128]{4,3,2,1,0:T(8,128)S(1)}, f32[1,8,4,8,128]{4,3,2,1,0:T(8,128)S(1)}, u32[]{:S(2)}, u32[]{:S(2)}) collective-permute-start(f32[1,8,4,8,128]{4,3,2,1,0:T(8,128)S(1)} %get-tuple-element.40), channel_id=1, source_target_pairs={{0,8},{4,12},{8,0},{12,4},{16,24},{20,28},{24,16},{28,20},{1,9},{5... | collective-permute-start | bytes 393224 | tf_op jit(solution)/shard_map/ppermute | solution.py:433
  31.1 4.2 %copy-start.11 = (f32[1,8,4,8,128]{4,3,2,1,0:T(8,128)}, f32[1,8,4,8,128]{4,3,2,1,0:T(8,128)S(1)}, u32[]{:S(2)}) copy-start(f32[1,8,4,8,128]{4,3,2,1,0:T(8,128)S(1)} %collective-permute-done.5.refs_6_) | copy-start | bytes 393220
  31.1 4.1 %collective-permute-start = (f32[1,8,4,8,128]{4,3,2,1,0:T(8,128)S(1)}, f32[1,8,4,8,128]{4,3,2,1,0:T(8,128)S(1)}, u32[]{:S(2)}, u32[]{:S(2)}) collective-permute-start(f32[1,8,4,8,128]{4,3,2,1,0:T(8,128)S(1)} %get-tuple-element.41), channel_id=1, source_target_pairs={{0,4},{4,0},{8,12},{12,8},{16,20},{20,16},{24,28},{28,24},{1,5},{5... | collective-permute-start | bytes 393224 | tf_op jit(solution)/shard_map/ppermute | solution.py:433
  32.0 3.2 %copy-start.12 = (f32[1,8,4,8,128]{4,3,2,1,0:T(8,128)}, f32[1,8,4,8,128]{4,3,2,1,0:T(8,128)S(1)}, u32[]{:S(2)}) copy-start(f32[1,8,4,8,128]{4,3,2,1,0:T(8,128)S(1)} %collective-permute-done.4.refs_5_) | copy-start | bytes 393220
  42.6 31.1 %all-to-all-start.2 = ((f32[32,8,8,128]{3,2,1,0:T(8,128)}), f32[32,8,8,128]{3,2,1,0:T(8,128)S(1)}, u32[]{:S(2)}, u32[]{:S(2)}) async-start(f32[32,8,8,128]{3,2,1,0:T(8,128)} %bitcast.7), calls=%async_computation.2 | async-start | bytes 2097152 | tf_op jit(solution)/shard_map/all_to_all | solution.py:482
  73.7 29.9 %copy-start.1 = (f32[32,8,8,128]{3,2,1,0:T(8,128)}, f32[32,8,8,128]{3,2,1,0:T(8,128)S(1)}, u32[]{:S(2)}) copy-start(f32[32,8,8,128]{3,2,1,0:T(8,128)S(1)} %all-to-all-done.2.refs_1_) | copy-start | bytes 3145732
  103.7 19.4 %copy-start.2 = (f32[32,8,8,128]{3,2,1,0:T(8,128)S(1)}, f32[32,8,8,128]{3,2,1,0:T(8,128)}, u32[]{:S(2)}) copy-start(f32[32,8,8,128]{3,2,1,0:T(8,128)} %all_to_all.15.refs_0_) | copy-start | bytes 3145732
  109.1 3.6 %collective-permute-start.7 = (f32[10,16,128]{2,1,0:T(8,128)}, f32[10,16,128]{2,1,0:T(8,128)S(1)}, u32[]{:S(2)}, u32[]{:S(2)}) collective-permute-start(f32[10,16,128]{2,1,0:T(8,128)} %get-tuple-element.20), channel_id=1, source_target_pairs={{0,4},{4,0},{8,12},{12,8},{16,20},{20,16},{24,28},{28,24},{1,5},{5... | collective-permute-start | bytes 245768 | tf_op jit(solution)/shard_map/ppermute | solution.py:433
  109.1 6.0 %collective-permute-start.8 = (f32[10,16,128]{2,1,0:T(8,128)}, f32[10,16,128]{2,1,0:T(8,128)S(1)}, u32[]{:S(2)}, u32[]{:S(2)}) collective-permute-start(f32[10,16,128]{2,1,0:T(8,128)} %get-tuple-element.21), channel_id=1, source_target_pairs={{0,8},{4,12},{8,0},{12,4},{16,24},{20,28},{24,16},{28,20},{1,9},{5... | collective-permute-start | bytes 245768 | tf_op jit(solution)/shard_map/ppermute | solution.py:433
  110.6 5.1 %collective-permute-start.9 = (f32[10,16,128]{2,1,0:T(8,128)}, f32[10,16,128]{2,1,0:T(8,128)S(1)}, u32[]{:S(2)}, u32[]{:S(2)}) collective-permute-start(f32[10,16,128]{2,1,0:T(8,128)} %get-tuple-element.22), channel_id=1, source_target_pairs={{0,12},{4,8},{8,4},{12,0},{16,28},{20,24},{24,20},{28,16},{1,13},{... | collective-permute-start | bytes 245768 | tf_op jit(solution)/shard_map/ppermute | solution.py:433
  110.9 5.2 %collective-permute-start.10 = (f32[10,16,128]{2,1,0:T(8,128)}, f32[10,16,128]{2,1,0:T(8,128)S(1)}, u32[]{:S(2)}, u32[]{:S(2)}) collective-permute-start(f32[10,16,128]{2,1,0:T(8,128)} %get-tuple-element.23), channel_id=1, source_target_pairs={{0,16},{4,20},{8,24},{12,28},{16,0},{20,4},{24,8},{28,12},{1,17},{... | collective-permute-start | bytes 245768 | tf_op jit(solution)/shard_map/ppermute | solution.py:433
  112.4 7.8 %collective-permute-start.11 = (f32[10,16,128]{2,1,0:T(8,128)}, f32[10,16,128]{2,1,0:T(8,128)S(1)}, u32[]{:S(2)}, u32[]{:S(2)}) collective-permute-start(f32[10,16,128]{2,1,0:T(8,128)} %get-tuple-element.24), channel_id=1, source_target_pairs={{0,20},{4,16},{8,28},{12,24},{16,4},{20,0},{24,12},{28,8},{1,21},{... | collective-permute-start | bytes 245768 | tf_op jit(solution)/shard_map/ppermute | solution.py:433
  112.7 7.6 %collective-permute-start.12 = (f32[10,16,128]{2,1,0:T(8,128)}, f32[10,16,128]{2,1,0:T(8,128)S(1)}, u32[]{:S(2)}, u32[]{:S(2)}) collective-permute-start(f32[10,16,128]{2,1,0:T(8,128)} %get-tuple-element.25), channel_id=1, source_target_pairs={{0,24},{4,28},{8,16},{12,20},{16,8},{20,12},{24,0},{28,4},{1,25},{... | collective-permute-start | bytes 245768 | tf_op jit(solution)/shard_map/ppermute | solution.py:433
  115.1 5.6 %collective-permute-start.13 = (f32[10,16,128]{2,1,0:T(8,128)}, f32[10,16,128]{2,1,0:T(8,128)S(1)}, u32[]{:S(2)}, u32[]{:S(2)}) collective-permute-start(f32[10,16,128]{2,1,0:T(8,128)} %get-tuple-element.26), channel_id=1, source_target_pairs={{0,28},{4,24},{8,20},{12,16},{16,12},{20,8},{24,4},{28,0},{1,29},{... | collective-permute-start | bytes 245768 | tf_op jit(solution)/shard_map/ppermute | solution.py:433
  121.6 14.3 %collective-permute-start.16 = (f32[10,16,128]{2,1,0:T(8,128)S(1)}, f32[10,16,128]{2,1,0:T(8,128)S(1)}, u32[]{:S(2)}, u32[]{:S(2)}) collective-permute-start(f32[10,16,128]{2,1,0:T(8,128)S(1)} %add_add_fusion.2), channel_id=1, source_target_pairs={{0,3},{1,2},{2,1},{3,0},{4,7},{5,6},{6,5},{7,4},{8,11},{9,10},{10,... | collective-permute-start | bytes 245768 | tf_op jit(solution)/shard_map/ppermute | solution.py:433
  123.1 107.8 %collective-permute-start.26 = (f32[32,8,8,128]{3,2,1,0:T(8,128)S(1)}, f32[32,8,8,128]{3,2,1,0:T(8,128)S(1)}, u32[]{:S(2)}, u32[]{:S(2)}) collective-permute-start(f32[32,8,8,128]{3,2,1,0:T(8,128)S(1)} %copy-done.2), channel_id=1, source_target_pairs={{1,0},{2,1},{3,2},{5,4},{6,5},{7,6},{9,8},{10,9},{11,10},{13,12},{... | collective-permute-start | bytes 3145736 | tf_op jit(solution)/shard_map/ppermute | solution.py:427
  124.4 106.6 %collective-permute-start.24 = (f32[32,8,8,128]{3,2,1,0:T(8,128)S(1)}, f32[32,8,8,128]{3,2,1,0:T(8,128)S(1)}, u32[]{:S(2)}, u32[]{:S(2)}) collective-permute-start(f32[32,8,8,128]{3,2,1,0:T(8,128)S(1)} %copy-done.2), channel_id=1, source_target_pairs={{0,1},{1,2},{2,3},{4,5},{5,6},{6,7},{8,9},{9,10},{10,11},{12,13},{... | collective-permute-start | bytes 3145736 | tf_op jit(solution)/shard_map/ppermute | solution.py:427
  129.0 101.9 %collective-permute-start.27 = (f32[32,8,8,128]{3,2,1,0:T(8,128)}, f32[32,8,8,128]{3,2,1,0:T(8,128)}, u32[]{:S(2)}, u32[]{:S(2)}) collective-permute-start(f32[32,8,8,128]{3,2,1,0:T(8,128)} %copy-done.1), channel_id=1, source_target_pairs={{1,0},{2,1},{3,2},{5,4},{6,5},{7,6},{9,8},{10,9},{11,10},{13,12},{... | collective-permute-start | bytes 3145736 | tf_op jit(solution)/shard_map/ppermute | solution.py:427
  130.3 100.7 %collective-permute-start.25 = (f32[32,8,8,128]{3,2,1,0:T(8,128)}, f32[32,8,8,128]{3,2,1,0:T(8,128)}, u32[]{:S(2)}, u32[]{:S(2)}) collective-permute-start(f32[32,8,8,128]{3,2,1,0:T(8,128)} %copy-done.1), channel_id=1, source_target_pairs={{0,1},{1,2},{2,3},{4,5},{5,6},{6,7},{8,9},{9,10},{10,11},{12,13},{... | collective-permute-start | bytes 3145736 | tf_op jit(solution)/shard_map/ppermute | solution.py:427
  135.9 41.0 %collective-permute-start.15 = (f32[10,16,128]{2,1,0:T(8,128)S(1)}, f32[10,16,128]{2,1,0:T(8,128)S(1)}, u32[]{:S(2)}, u32[]{:S(2)}) collective-permute-start(f32[10,16,128]{2,1,0:T(8,128)S(1)} %add_add_fusion.2), channel_id=1, source_target_pairs={{0,2},{1,3},{2,0},{3,1},{4,6},{5,7},{6,4},{7,5},{8,10},{9,11},{10,... | collective-permute-start | bytes 245768 | tf_op jit(solution)/shard_map/ppermute | solution.py:433
  176.8 4.4 %collective-permute-start.14 = (f32[10,16,128]{2,1,0:T(8,128)S(1)}, f32[10,16,128]{2,1,0:T(8,128)S(1)}, u32[]{:S(2)}, u32[]{:S(2)}) collective-permute-start(f32[10,16,128]{2,1,0:T(8,128)S(1)} %add_add_fusion.2), channel_id=1, source_target_pairs={{0,1},{1,0},{2,3},{3,2},{4,5},{5,4},{6,7},{7,6},{8,9},{9,8},{10,11... | collective-permute-start | bytes 245768 | tf_op jit(solution)/shard_map/ppermute | solution.py:433
  181.3 29.8 %copy-start.9 = (f32[10,16,128]{2,1,0:T(8,128)}, f32[10,16,128]{2,1,0:T(8,128)S(1)}, u32[]{:S(2)}) copy-start(f32[10,16,128]{2,1,0:T(8,128)S(1)} %add_add_fusion.1.refs_0_) | copy-start | bytes 245764
  181.3 4.9 %collective-permute-start.23 = (f32[10,16,128]{2,1,0:T(8,128)S(1)}, f32[10,16,128]{2,1,0:T(8,128)S(1)}, u32[]{:S(2)}, u32[]{:S(2)}) collective-permute-start(f32[10,16,128]{2,1,0:T(8,128)S(1)} %add_add_fusion.1.refs_0_), channel_id=1, source_target_pairs={{0,28},{4,24},{8,20},{12,16},{16,12},{20,8},{24,4},{28,0},{1,29},{... | collective-permute-start | bytes 245768 | tf_op jit(solution)/shard_map/ppermute | solution.py:433
  186.2 24.9 %copy-start.17 = (f32[10,16,128]{2,1,0:T(8,128)}, f32[10,16,128]{2,1,0:T(8,128)S(1)}, u32[]{:S(2)}) copy-start(f32[10,16,128]{2,1,0:T(8,128)S(1)} %collective-permute-done.23.refs_7_) | copy-start | bytes 245764
  186.2 5.3 %collective-permute-start.22 = (f32[10,16,128]{2,1,0:T(8,128)S(1)}, f32[10,16,128]{2,1,0:T(8,128)S(1)}, u32[]{:S(2)}, u32[]{:S(2)}) collective-permute-start(f32[10,16,128]{2,1,0:T(8,128)S(1)} %add_add_fusion.1.refs_0_), channel_id=1, source_target_pairs={{0,24},{4,28},{8,16},{12,20},{16,8},{20,12},{24,0},{28,4},{1,25},{... | collective-permute-start | bytes 245768 | tf_op jit(solution)/shard_map/ppermute | solution.py:433
  191.6 19.6 %copy-start.18 = (f32[10,16,128]{2,1,0:T(8,128)}, f32[10,16,128]{2,1,0:T(8,128)S(1)}, u32[]{:S(2)}) copy-start(f32[10,16,128]{2,1,0:T(8,128)S(1)} %collective-permute-done.22.refs_6_) | copy-start | bytes 245764
  191.6 4.7 %collective-permute-start.21 = (f32[10,16,128]{2,1,0:T(8,128)S(1)}, f32[10,16,128]{2,1,0:T(8,128)S(1)}, u32[]{:S(2)}, u32[]{:S(2)}) collective-permute-start(f32[10,16,128]{2,1,0:T(8,128)S(1)} %add_add_fusion.1.refs_0_), channel_id=1, source_target_pairs={{0,20},{4,16},{8,28},{12,24},{16,4},{20,0},{24,12},{28,8},{1,21},{... | collective-permute-start | bytes 245768 | tf_op jit(solution)/shard_map/ppermute | solution.py:433
  196.3 14.9 %copy-start.19 = (f32[10,16,128]{2,1,0:T(8,128)}, f32[10,16,128]{2,1,0:T(8,128)S(1)}, u32[]{:S(2)}) copy-start(f32[10,16,128]{2,1,0:T(8,128)S(1)} %collective-permute-done.21.refs_5_) | copy-start | bytes 245764
  196.3 4.4 %collective-permute-start.20 = (f32[10,16,128]{2,1,0:T(8,128)S(1)}, f32[10,16,128]{2,1,0:T(8,128)S(1)}, u32[]{:S(2)}, u32[]{:S(2)}) collective-permute-start(f32[10,16,128]{2,1,0:T(8,128)S(1)} %add_add_fusion.1.refs_0_), channel_id=1, source_target_pairs={{0,16},{4,20},{8,24},{12,28},{16,0},{20,4},{24,8},{28,12},{1,17},{... | collective-permute-start | bytes 245768 | tf_op jit(solution)/shard_map/ppermute | solution.py:433
  200.7 10.4 %copy-start.20 = (f32[10,16,128]{2,1,0:T(8,128)}, f32[10,16,128]{2,1,0:T(8,128)S(1)}, u32[]{:S(2)}) copy-start(f32[10,16,128]{2,1,0:T(8,128)S(1)} %collective-permute-done.20.refs_4_) | copy-start | bytes 245764
  200.7 3.9 %collective-permute-start.19 = (f32[10,16,128]{2,1,0:T(8,128)S(1)}, f32[10,16,128]{2,1,0:T(8,128)S(1)}, u32[]{:S(2)}, u32[]{:S(2)}) collective-permute-start(f32[10,16,128]{2,1,0:T(8,128)S(1)} %add_add_fusion.1.refs_0_), channel_id=1, source_target_pairs={{0,12},{4,8},{8,4},{12,0},{16,28},{20,24},{24,20},{28,16},{1,13},{... | collective-permute-start | bytes 245768 | tf_op jit(solution)/shard_map/ppermute | solution.py:433
  204.6 4.4 %copy-start.21 = (f32[10,16,128]{2,1,0:T(8,128)}, f32[10,16,128]{2,1,0:T(8,128)S(1)}, u32[]{:S(2)}) copy-start(f32[10,16,128]{2,1,0:T(8,128)S(1)} %collective-permute-done.19.refs_3_) | copy-start | bytes 245764
  204.6 4.4 %collective-permute-start.18 = (f32[10,16,128]{2,1,0:T(8,128)S(1)}, f32[10,16,128]{2,1,0:T(8,128)S(1)}, u32[]{:S(2)}, u32[]{:S(2)}) collective-permute-start(f32[10,16,128]{2,1,0:T(8,128)S(1)} %add_add_fusion.1.refs_0_), channel_id=1, source_target_pairs={{0,8},{4,12},{8,0},{12,4},{16,24},{20,28},{24,16},{28,20},{1,9},{5... | collective-permute-start | bytes 245768 | tf_op jit(solution)/shard_map/ppermute | solution.py:433
  209.7 1.4 collective-permute-start.17
  239.3 10.4 %collective-permute-start.28 = (f32[128,8,128]{2,1,0:T(8,128)}, f32[128,8,128]{2,1,0:T(8,128)S(1)}, u32[]{:S(2)}, u32[]{:S(2)}) collective-permute-start(f32[128,8,128]{2,1,0:T(8,128)} %get-tuple-element.29), channel_id=1, source_target_pairs={{1,2},{2,3},{5,6},{6,7},{9,10},{10,11},{13,14},{14,15},{17,18},{18... | collective-permute-start | bytes 1572872 | tf_op jit(solution)/shard_map/ppermute | solution.py:504
  240.0 9.8 %collective-permute-start.29 = (f32[128,8,128]{2,1,0:T(8,128)}, f32[128,8,128]{2,1,0:T(8,128)S(1)}, u32[]{:S(2)}, u32[]{:S(2)}) collective-permute-start(f32[128,8,128]{2,1,0:T(8,128)} %get-tuple-element.30), channel_id=1, source_target_pairs={{1,3},{5,7},{9,11},{13,15},{17,19},{21,23},{25,27},{29,31}} | collective-permute-start | bytes 1572872 | tf_op jit(solution)/shard_map/ppermute | solution.py:502
  240.7 20.8 %collective-permute-start.30 = (f32[128,8,128]{2,1,0:T(8,128)}, f32[128,8,128]{2,1,0:T(8,128)S(1)}, u32[]{:S(2)}, u32[]{:S(2)}) collective-permute-start(f32[128,8,128]{2,1,0:T(8,128)} %get-tuple-element.31), channel_id=1, source_target_pairs={{1,0},{2,1},{5,4},{6,5},{9,8},{10,9},{13,12},{14,13},{17,16},{18,1... | collective-permute-start | bytes 1572872 | tf_op jit(solution)/shard_map/ppermute | solution.py:505
  242.0 31.9 %collective-permute-start.31 = (f32[128,8,128]{2,1,0:T(8,128)}, f32[128,8,128]{2,1,0:T(8,128)S(1)}, u32[]{:S(2)}, u32[]{:S(2)}) collective-permute-start(f32[128,8,128]{2,1,0:T(8,128)} %get-tuple-element.32), channel_id=1, source_target_pairs={{2,0},{6,4},{10,8},{14,12},{18,16},{22,20},{26,24},{30,28}} | collective-permute-start | bytes 1572872 | tf_op jit(solution)/shard_map/ppermute | solution.py:503
  249.7 24.2 %copy-start.5 = (f32[128,8,128]{2,1,0:T(8,128)}, f32[128,8,128]{2,1,0:T(8,128)S(1)}, u32[]{:S(2)}) copy-start(f32[128,8,128]{2,1,0:T(8,128)S(1)} %collective-permute-done.28.up1) | copy-start | bytes 1572868
  249.7 24.2 %copy-start.6 = (f32[128,8,128]{2,1,0:T(8,128)}, f32[128,8,128]{2,1,0:T(8,128)S(1)}, u32[]{:S(2)}) copy-start(f32[128,8,128]{2,1,0:T(8,128)S(1)} %collective-permute-done.29.up2) | copy-start | bytes 1572868
  261.5 12.4 %copy-start.7 = (f32[128,8,128]{2,1,0:T(8,128)}, f32[128,8,128]{2,1,0:T(8,128)S(1)}, u32[]{:S(2)}) copy-start(f32[128,8,128]{2,1,0:T(8,128)S(1)} %collective-permute-done.30.down1) | copy-start | bytes 1572868
  (10 other events, 9.3 us)

commit v2 on v1

--- a/solution.py
+++ b/solution.py
@@ -22,6 +22,7 @@
 vmem = pl.BlockSpec(memory_space=pltpu.VMEM)
 smem = pl.BlockSpec(memory_space=pltpu.SMEM)
 big = pltpu.CompilerParams(vmem_limit_bytes=56 << 20)
+small = pltpu.CompilerParams(vmem_limit_bytes=12 << 20)
 
 
 def split(value):
@@ -99,7 +100,7 @@
         in_specs=[smem] + [vmem] * (3 + len(parts)),
         out_specs=vmem,
         scratch_shapes=[pltpu.VMEM((flat, z.shape[0]), f32), pltpu.VMEM((orbs, flat, cols), f32)],
-        compiler_params=big,
+        compiler_params=small if flat <= 256 else big,
         name="filter",
     )(place, xy, z, with_pot, *parts)
 
@@ -148,7 +149,7 @@
         in_specs=[smem] + [vmem] * len(parts),
         out_specs=[vmem] * len(outs),
         scratch_shapes=[pltpu.VMEM((blocks, size, size), f32)],
-        compiler_params=big,
+        compiler_params=small,
         name="margin",
     )(place, *parts)
 
@@ -279,7 +280,7 @@
         in_specs=[smem] + [vmem] * len(pieces),
         out_specs=vmem,
         scratch_shapes=[pltpu.VMEM((blocks, size, size), f32), pltpu.VMEM((size, 2 * size), f32)],
-        compiler_params=big,
+        compiler_params=small,
         name="inverse",
     )(place, *pieces)
 
@@ -325,7 +326,7 @@
         out_shape=jax.ShapeDtypeStruct((owners, norb // owners, rows, wide // rows), f32),
         in_specs=[vmem] * 3,
         out_specs=vmem,
-        compiler_params=big,
+        compiler_params=small,
         name="rotate",
     )(v, high, low)
 
@@ -354,7 +355,7 @@
         in_specs=[smem] + [vmem] * (1 + 2 * len(below)),
         out_specs=[vmem] * 4,
         scratch_shapes=[wide, wide],
-        compiler_params=big,
+        compiler_params=small,
         name="rotate_far",
     )(layer, v, *below, *above)
 
@@ -369,7 +370,7 @@
     def put(plane, h, l):
         value = product(v_ref[layer], h[...], l[...])
         for r in range(rows):
-            out_ref[plane, :, r, :] = value[:, r * cols : (r + 1) * cols]
+            out_ref[:, plane, r, :] = value[:, r * cols : (r + 1) * cols]
 
     put(layer, my_high, my_low)
 
@@ -390,36 +391,45 @@
     wide = pltpu.VMEM((norb, rows * cols), bf16)
     return pl.pallas_call(
         functools.partial(near_kernel, (owners, slabs, len(below))),
-        out_shape=jax.ShapeDtypeStruct((owners, norb // owners, rows, cols), f32),
+        out_shape=jax.ShapeDtypeStruct((norb // owners, owners, rows, cols), f32),
         in_specs=[smem] + [vmem] * (3 + 2 * len(below)),
         out_specs=vmem,
         scratch_shapes=[wide, wide],
-        compiler_params=big,
+        compiler_params=small,
         name="rotate_near",
     )(layer, v, high, low, *below, *above)
 
 
-def join_kernel(layer_ref, near_ref, up1, up2, down1, down2, out_ref):
-    owners = near_ref.shape[0]
+def join_kernel(layer_ref, up1, up2, down1, down2, near_ref, out_ref, sems):
+    owners = out_ref.shape[1]
     for z in range(owners):
+        sources = {z - 3: up2, z - 2: up1, z + 2: down1, z + 3: down2}
 
         @pl.when(layer_ref[0] == z)
         def _():
-            for p in range(owners):
-                source = {-3: up2, -2: up1, 2: down1, 3: down2}.get(p - z)
-                out_ref[:, p] = near_ref[p] if source is None else source[...]
+            copies = [
+                pltpu.make_async_copy(source, out_ref.at[:, p], sems.at[p])
+                for p, source in sources.items()
+                if 0 <= p < owners
+            ]
+            for copy in copies:
+                copy.start()
+            for copy in copies:
+                copy.wait()
 
 
 def join(layer, near, far):
-    owners, local, rows, cols = near.shape
+    anywhere = pl.BlockSpec(memory_space=pl.ANY)
     return pl.pallas_call(
         join_kernel,
-        out_shape=jax.ShapeDtypeStruct((local, owners, rows, cols), f32),
-        in_specs=[smem] + [vmem] * 5,
-        out_specs=vmem,
-        compiler_params=big,
+        out_shape=jax.ShapeDtypeStruct(near.shape, f32),
+        in_specs=[smem] + [vmem] * 4 + [anywhere],
+        out_specs=anywhere,
+        scratch_shapes=[pltpu.SemaphoreType.DMA((near.shape[1],))],
+        input_output_aliases={5: 0},
+        compiler_params=small,
         name="join",
-    )(layer, near, *far)
+    )(layer, *far, near)
 
 
 def shift(values, axis, by, count):
@@ -486,8 +496,10 @@
     *pieces, high, low = margin_blocks(place, cells, owners, slabs, size, slabs)
     nearby = owners == 4 and planes == owners
     if nearby:
-        below = shift(cells, "orb", 1, owners)
-        above = shift(cells, "orb", -1, owners)
+        below, above = [], []
+        for c in range(chunks):
+            below += shift(cells[c : c + 1], "orb", 1, owners)
+            above += shift(cells[c : c + 1], "orb", -1, owners)
     mine = tree_sum(swap_all(pieces, "grid"))
     mine = tree_sum(swap_all([mine] * owners, "orb"))
     margin = swap_all([mine] * slabs, "grid")

time: 279 us -> 270 us (0.968)
  Pallas kernels: 54.9 us -> 41 us
  waiting for transfers between devices: 135 us -> 141 us
    pallas_call x2, Pallas kernels: 12.5 us -> 7.99 us  [filter_orbitals(): pl.pallas_call(functools.partial(filter_kernel, orbs), out_shape=jax.Shap...]
    unnamed x48 -> x22, local copies, waits for them, and re-layouts: 3.87 us -> 6.49 us
  transfers between devices with their start and end apart: 34 -> 34, of which waited for: 19 -> 19; matrix products, arithmetic and copies ran while one was open for 1% -> 0% of each run, Pallas kernels for 12% -> 10%
where the time goes in v2:
time: 270 us
  waiting for transfers between devices  141 us (52%)
  starting transfers between devices  46.9 us (17%)
  Pallas kernels  41 us (15%)
  blocking collectives  29.6 us (11%)
  local copies, waits for them, and re-layouts  8.31 us (3%)
    ppermute x24, waiting for transfers between devices, swap_all(): lax.ppermute(pieces[s], axis, [(i, i ^ s) for i in range(count)])  93.6 us
    all_to_all x1, blocking collectives, orthonormalized(): lax.all_to_all(filtered, everyone, split_axis=0, concat_axis=0, tiled=True)  29.6 us
    all_to_all x1, waiting for transfers between devices, orthonormalized(): lax.all_to_all(filtered, everyone, split_axis=0, concat_axis=0, tiled=True)  22.7 us
    ppermute x24, starting transfers between devices, swap_all(): lax.ppermute(pieces[s], axis, [(i, i ^ s) for i in range(count)])  19.2 us
    pallas_call x1, Pallas kernels, inverse_rows(): pl.pallas_call(functools.partial(inverse_kernel, factor), out_shape=jax.S...  18.5 us
    ppermute x4, starting transfers between devices, shift(): return [lax.ppermute(value, axis, pairs) for value in values]  13.6 us
    ppermute x1, waiting for transfers between devices, orthonormalized(): down1 = lax.ppermute(down1, 'orb', [(i, i - 1) for i in inner])  12.5 us
    ppermute x1, waiting for transfers between devices, orthonormalized(): down2 = lax.ppermute(down2, 'orb', [(i, i - 2) for i in inner if i >= 2])  12.4 us
  transfers between devices with their start and end apart: 34, of which 19 were waited for; matrix products, arithmetic and copies ran while one was open for 0% of the time, Pallas kernels for 10%

profile of v2, /device:TPU:0, one launch (start us, length us, event | category | flops | bytes accessed | tf_op | source)
XLA Modules:
  0.0 269.8 jit_solution(2068377201814133849)
XLA Ops:
  0.0 1.7 fusion.12
  1.8 1.1 pad_maximum_fusion
  2.9 5.2 %all-to-all-start = ((f32[8,9,4,8,128]{4,3,2,1,0:T(8,128)}), f32[8,9,4,8,128]{4,3,2,1,0:T(8,128)S(1)}, u32[]{:S(2)}, u32[]{:S(2)}) async-start(f32[8,9,4,8,128]{4,3,2,1,0:T(8,128)} %pad_maximum_fusion), calls=%async_computation | async-start | bytes 2359296 | tf_op jit(solution)/shard_map/all_to_all | solution.py:472
  8.2 2.7 %collective-permute-start.6 = (f32[1,8,4,8,128]{4,3,2,1,0:T(8,128)S(1)}, f32[1,8,4,8,128]{4,3,2,1,0:T(8,128)S(1)}, u32[]{:S(2)}, u32[]{:S(2)}) collective-permute-start(f32[1,8,4,8,128]{4,3,2,1,0:T(8,128)S(1)} %get-tuple-element.35), channel_id=1, source_target_pairs={{0,28},{4,24},{8,20},{12,16},{16,12},{20,8},{24,4},{28,0},{1,29},{... | collective-permute-start | bytes 393224 | tf_op jit(solution)/shard_map/ppermute | solution.py:443
  11.3 1.4 collective-permute-start.4
  12.9 1.5 collective-permute-start.2
  15.2 12.0 %collective-permute-done.6.refs_7_ = f32[1,8,4,8,128]{4,3,2,1,0:T(8,128)S(1)} collective-permute-done((f32[1,8,4,8,128]{4,3,2,1,0:T(8,128)S(1)}, f32[1,8,4,8,128]{4,3,2,1,0:T(8,128)S(1)}, u32[]{:S(2)}, u32[]{:S(2)}) %collective-permute-start.6) | collective-permute-done | bytes 131104 | tf_op jit(solution)/shard_map/ppermute | solution.py:443
  27.8 3.3 %collective-permute-done.5.refs_6_ = f32[1,8,4,8,128]{4,3,2,1,0:T(8,128)S(1)} collective-permute-done((f32[1,8,4,8,128]{4,3,2,1,0:T(8,128)S(1)}, f32[1,8,4,8,128]{4,3,2,1,0:T(8,128)S(1)}, u32[]{:S(2)}, u32[]{:S(2)}) %collective-permute-start.5) | collective-permute-done | bytes 131104 | tf_op jit(solution)/shard_map/ppermute | solution.py:443
  31.8 3.4 %collective-permute-done.3.refs_4_ = f32[1,8,4,8,128]{4,3,2,1,0:T(8,128)S(1)} collective-permute-done((f32[1,8,4,8,128]{4,3,2,1,0:T(8,128)S(1)}, f32[1,8,4,8,128]{4,3,2,1,0:T(8,128)S(1)}, u32[]{:S(2)}, u32[]{:S(2)}) %collective-permute-start.3) | collective-permute-done | bytes 131104 | tf_op jit(solution)/shard_map/ppermute | solution.py:443
  35.2 4.5 %filter.3 = f32[4,8,8,8,128]{4,3,2,1,0:T(8,128)} custom-call(s32[1]{0:T(128)} %bitcast.1.place_ref, bf16[256,256]{1,0:T(8,128)(2,1)S(1)} %fusion.6.xy_ref, bf16[256,256]{1,0:T(8,128)(2,1)S(1)} %select_convert_fusion.z_ref, f32[8,9,4,8,128]{4,3,2,1,0:T(8,128)S(1)} %all-to-all-done.pot_ref.refs_0_, f32[1,8,4,8,128]{4,3,2,1,0:T(8,128)S(1)} %get-tuple-element.42.refs_0_, ...), custom_call_target="tpu_custom_call" | custom-call | tf_op jit(solution)/shard_map/filter/pallas_call | solution.py:97
  39.8 4.9 %all-to-all-start.2 = ((f32[32,8,8,128]{3,2,1,0:T(8,128)}), f32[32,8,8,128]{3,2,1,0:T(8,128)S(1)}, u32[]{:S(2)}, u32[]{:S(2)}) async-start(f32[32,8,8,128]{3,2,1,0:T(8,128)} %bitcast.5), calls=%async_computation.2 | async-start | bytes 2097152 | tf_op jit(solution)/shard_map/all_to_all | solution.py:492
  44.7 3.5 %filter.2 = f32[4,8,8,8,128]{4,3,2,1,0:T(8,128)S(1)} custom-call(s32[1]{0:T(128)} %bitcast.1.place_ref, bf16[256,256]{1,0:T(8,128)(2,1)S(1)} %fusion.6.xy_ref, bf16[256,256]{1,0:T(8,128)(2,1)S(1)} %select_convert_fusion.z_ref, f32[8,9,4,8,128]{4,3,2,1,0:T(8,128)S(1)} %all-to-all-done.pot_ref.refs_0_, f32[8,9,4,8,128]{4,3,2,1,0:T(8,128)S(1)} %all-to-all-done.pot_ref.refs_0_), custom_call_target="tpu_custom_call" | custom-call | tf_op jit(solution)/shard_map/filter/pallas_call | solution.py:97
  48.2 22.7 %all-to-all-done.2.refs_1_ = f32[32,8,8,128]{3,2,1,0:T(8,128)S(1)} async-done(((f32[32,8,8,128]{3,2,1,0:T(8,128)}), f32[32,8,8,128]{3,2,1,0:T(8,128)S(1)}, u32[]{:S(2)}, u32[]{:S(2)}) %all-to-all-start.2) | async-done | bytes 1048608 | tf_op jit(solution)/shard_map/all_to_all | solution.py:492
  70.9 29.6 %all_to_all.15.refs_0_ = f32[32,8,8,128]{3,2,1,0:T(8,128)S(1)} all-to-all(f32[32,8,8,128]{3,2,1,0:T(8,128)S(1)} %bitcast.6), channel_id=1, replica_groups=mesh['grid'=8,'orb'=4] {'orb','grid'}, dimensions={0} | all-to-all | bytes 2097152 | tf_op jit(solution)/shard_map/all_to_all | solution.py:492
  100.5 2.7 margin.1
  103.2 1.0 copy-done
  104.2 1.0 copy-done.2
  105.1 1.5 collective-permute-start.8
  107.0 1.5 collective-permute-start.10
  108.6 2.4 collective-permute-start.12
  111.8 5.0 %collective-permute-done.11 = f32[10,16,128]{2,1,0:T(8,128)S(1)} collective-permute-done((f32[10,16,128]{2,1,0:T(8,128)S(1)}, f32[10,16,128]{2,1,0:T(8,128)S(1)}, u32[]{:S(2)}, u32[]{:S(2)}) %collective-permute-start.11) | collective-permute-done | bytes 81952 | tf_op jit(solution)/shard_map/ppermute | solution.py:443
  116.8 1.1 collective-permute-start.16
  117.9 1.3 collective-permute-start.26
  119.2 5.5 %collective-permute-start.24 = (f32[32,8,8,128]{3,2,1,0:T(8,128)S(1)}, f32[32,8,8,128]{3,2,1,0:T(8,128)}, u32[]{:S(2)}, u32[]{:S(2)}) collective-permute-start(f32[32,8,8,128]{3,2,1,0:T(8,128)S(1)} %all_to_all.15.refs_0_), channel_id=1, source_target_pairs={{0,1},{1,2},{2,3},{4,5},{5,6},{6,7},{8,9},{9,10},{10,11},{12,13},{... | collective-permute-start | bytes 3145736 | tf_op jit(solution)/shard_map/ppermute | solution.py:437
  124.7 1.3 collective-permute-start.27
  126.0 5.5 %collective-permute-start.25 = (f32[32,8,8,128]{3,2,1,0:T(8,128)S(1)}, f32[32,8,8,128]{3,2,1,0:T(8,128)}, u32[]{:S(2)}, u32[]{:S(2)}) collective-permute-start(f32[32,8,8,128]{3,2,1,0:T(8,128)S(1)} %all-to-all-done.2.refs_1_), channel_id=1, source_target_pairs={{0,1},{1,2},{2,3},{4,5},{5,6},{6,7},{8,9},{9,10},{10,11},{12,13},{... | collective-permute-start | bytes 3145736 | tf_op jit(solution)/shard_map/ppermute | solution.py:437
  131.9 39.9 %collective-permute-done.15 = f32[10,16,128]{2,1,0:T(8,128)S(1)} collective-permute-done((f32[10,16,128]{2,1,0:T(8,128)S(1)}, f32[10,16,128]{2,1,0:T(8,128)S(1)}, u32[]{:S(2)}, u32[]{:S(2)}) %collective-permute-start.15) | collective-permute-done | bytes 81952 | tf_op jit(solution)/shard_map/ppermute | solution.py:443
  171.8 1.1 collective-permute-start.14
  172.9 3.4 %collective-permute-done.14 = f32[10,16,128]{2,1,0:T(8,128)S(1)} collective-permute-done((f32[10,16,128]{2,1,0:T(8,128)S(1)}, f32[10,16,128]{2,1,0:T(8,128)S(1)}, u32[]{:S(2)}, u32[]{:S(2)}) %collective-permute-start.14) | collective-permute-done | bytes 81952 | tf_op jit(solution)/shard_map/ppermute | solution.py:443
  176.3 4.8 %collective-permute-done.23.refs_7_ = f32[10,16,128]{2,1,0:T(8,128)S(1)} collective-permute-done((f32[10,16,128]{2,1,0:T(8,128)S(1)}, f32[10,16,128]{2,1,0:T(8,128)S(1)}, u32[]{:S(2)}, u32[]{:S(2)}) %collective-permute-start.23) | collective-permute-done | bytes 81952 | tf_op jit(solution)/shard_map/ppermute | solution.py:443
  181.2 1.5 collective-permute-start.22
  182.6 3.9 %collective-permute-done.22.refs_6_ = f32[10,16,128]{2,1,0:T(8,128)S(1)} collective-permute-done((f32[10,16,128]{2,1,0:T(8,128)S(1)}, f32[10,16,128]{2,1,0:T(8,128)S(1)}, u32[]{:S(2)}, u32[]{:S(2)}) %collective-permute-start.22) | collective-permute-done | bytes 81952 | tf_op jit(solution)/shard_map/ppermute | solution.py:443
  186.5 4.7 %collective-permute-done.21.refs_5_ = f32[10,16,128]{2,1,0:T(8,128)S(1)} collective-permute-done((f32[10,16,128]{2,1,0:T(8,128)S(1)}, f32[10,16,128]{2,1,0:T(8,128)S(1)}, u32[]{:S(2)}, u32[]{:S(2)}) %collective-permute-start.21) | collective-permute-done | bytes 81952 | tf_op jit(solution)/shard_map/ppermute | solution.py:443
  191.9 3.8 %collective-permute-done.20.refs_4_ = f32[10,16,128]{2,1,0:T(8,128)S(1)} collective-permute-done((f32[10,16,128]{2,1,0:T(8,128)S(1)}, f32[10,16,128]{2,1,0:T(8,128)S(1)}, u32[]{:S(2)}, u32[]{:S(2)}) %collective-permute-start.20) | collective-permute-done | bytes 81952 | tf_op jit(solution)/shard_map/ppermute | solution.py:443
  196.3 4.2 %collective-permute-done.19.refs_3_ = f32[10,16,128]{2,1,0:T(8,128)S(1)} collective-permute-done((f32[10,16,128]{2,1,0:T(8,128)S(1)}, f32[10,16,128]{2,1,0:T(8,128)S(1)}, u32[]{:S(2)}, u32[]{:S(2)}) %collective-permute-start.19) | collective-permute-done | bytes 81952 | tf_op jit(solution)/shard_map/ppermute | solution.py:443
  201.1 1.1 collective-permute-start.18
  202.2 3.3 %collective-permute-done.18.refs_2_ = f32[10,16,128]{2,1,0:T(8,128)S(1)} collective-permute-done((f32[10,16,128]{2,1,0:T(8,128)S(1)}, f32[10,16,128]{2,1,0:T(8,128)S(1)}, u32[]{:S(2)}, u32[]{:S(2)}) %collective-permute-start.18) | collective-permute-done | bytes 81952 | tf_op jit(solution)/shard_map/ppermute | solution.py:443
  206.1 1.4 collective-permute-done.17.refs_1_
  207.6 0.9 copy-done.5
  209.3 0.9 copy-done.9
  210.2 18.5 %inverse.1.v_ref = f32[4,128,512]{2,1,0:T(8,128)S(1)} custom-call(s32[1]{0:T(128)} %bitcast.1.place_ref, f32[10,16,128]{2,1,0:T(8,128)S(1)} %add_add_fusion.1.refs_0_, f32[10,16,128]{2,1,0:T(8,128)} %collective-permute-done.17.refs_1_, f32[10,16,128]{2,1,0:T(8,128)S(1)} %copy-done.9, f32[10,16,128]{2,1,0:T(8,128)S(1)} %copy-done.7, ...), custom_call_target="tpu_custom_call" | custom-call | tf_op jit(solution)/shard_map/inverse/pallas_call | solution.py:277
  228.8 5.7 %rotate_far.1 = (f32[128,8,128]{2,1,0:T(8,128)S(1)}, f32[128,8,128]{2,1,0:T(8,128)S(1)}, f32[128,8,128]{2,1,0:T(8,128)S(1)}, f32[128,8,128]{2,1,0:T(8,128)S(1)}) custom-call(s32[1]{0:T(128)} %bitcast.layer_ref, f32[4,128,512]{2,1,0:T(8,128)S(1)} %inverse.1.v_ref, f32[32,8,8,128]{3,2,1,0:T(8,128)} %collective-permute-done.24.refs_0_, ...), custom_call_target="tpu_custom_call" | custom-call | tf_op jit(solution)/shard_map/rotate_far/pallas_call | solution.py:352
  235.9 1.3 collective-permute-start.30
  237.2 1.3 collective-permute-start.31
  238.5 5.2 %rotate_near.1.near_ref = f32[128,4,8,128]{3,2,1,0:T(8,128)} custom-call(s32[1]{0:T(128)} %bitcast.layer_ref, f32[4,128,512]{2,1,0:T(8,128)S(1)} %inverse.1.v_ref, bf16[512,1024]{1,0:T(8,128)(2,1)S(1)} %copy-done.1, bf16[512,1024]{1,0:T(8,128)(2,1)S(1)} %copy-done.3, f32[32,8,8,128]{3,2,1,0:T(8,128)} %collective-permute-done.24.refs_0_, ...), custom_call_target="tpu_custom_call" | custom-call | tf_op jit(solution)/shard_map/rotate_near/pallas_call | solution.py:392
  243.7 12.5 %collective-permute-done.30.down1 = f32[128,8,128]{2,1,0:T(8,128)S(1)} collective-permute-done((f32[128,8,128]{2,1,0:T(8,128)S(1)}, f32[128,8,128]{2,1,0:T(8,128)S(1)}, u32[]{:S(2)}, u32[]{:S(2)}) %collective-permute-start.30) | collective-permute-done | bytes 524320 | tf_op jit(solution)/shard_map/ppermute | solution.py:517
  256.2 12.4 %collective-permute-done.31.down2 = f32[128,8,128]{2,1,0:T(8,128)S(1)} collective-permute-done((f32[128,8,128]{2,1,0:T(8,128)S(1)}, f32[128,8,128]{2,1,0:T(8,128)S(1)}, u32[]{:S(2)}, u32[]{:S(2)}) %collective-permute-start.31) | collective-permute-done | bytes 524320 | tf_op jit(solution)/shard_map/ppermute | solution.py:515
  268.6 1.0 join.1
  (63 shorter events, 9.6 us)
Async XLA Ops:
  0.0 1.7 copy-start.10
  2.9 32.4 %all-to-all-start = ((f32[8,9,4,8,128]{4,3,2,1,0:T(8,128)}), f32[8,9,4,8,128]{4,3,2,1,0:T(8,128)S(1)}, u32[]{:S(2)}, u32[]{:S(2)}) async-start(f32[8,9,4,8,128]{4,3,2,1,0:T(8,128)} %pad_maximum_fusion), calls=%async_computation | async-start | bytes 2359296 | tf_op jit(solution)/shard_map/all_to_all | solution.py:472
  8.2 19.0 %collective-permute-start.6 = (f32[1,8,4,8,128]{4,3,2,1,0:T(8,128)S(1)}, f32[1,8,4,8,128]{4,3,2,1,0:T(8,128)S(1)}, u32[]{:S(2)}, u32[]{:S(2)}) collective-permute-start(f32[1,8,4,8,128]{4,3,2,1,0:T(8,128)S(1)} %get-tuple-element.35), channel_id=1, source_target_pairs={{0,28},{4,24},{8,20},{12,16},{16,12},{20,8},{24,4},{28,0},{1,29},{... | collective-permute-start | bytes 393224 | tf_op jit(solution)/shard_map/ppermute | solution.py:443
  10.9 20.2 %collective-permute-start.5 = (f32[1,8,4,8,128]{4,3,2,1,0:T(8,128)S(1)}, f32[1,8,4,8,128]{4,3,2,1,0:T(8,128)S(1)}, u32[]{:S(2)}, u32[]{:S(2)}) collective-permute-start(f32[1,8,4,8,128]{4,3,2,1,0:T(8,128)S(1)} %get-tuple-element.36), channel_id=1, source_target_pairs={{0,24},{4,28},{8,16},{12,20},{16,8},{20,12},{24,0},{28,4},{1,25},{... | collective-permute-start | bytes 393224 | tf_op jit(solution)/shard_map/ppermute | solution.py:443
  11.3 20.5 %collective-permute-start.4 = (f32[1,8,4,8,128]{4,3,2,1,0:T(8,128)S(1)}, f32[1,8,4,8,128]{4,3,2,1,0:T(8,128)S(1)}, u32[]{:S(2)}, u32[]{:S(2)}) collective-permute-start(f32[1,8,4,8,128]{4,3,2,1,0:T(8,128)S(1)} %get-tuple-element.37), channel_id=1, source_target_pairs={{0,20},{4,16},{8,28},{12,24},{16,4},{20,0},{24,12},{28,8},{1,21},{... | collective-permute-start | bytes 393224 | tf_op jit(solution)/shard_map/ppermute | solution.py:443
  12.6 22.5 %collective-permute-start.3 = (f32[1,8,4,8,128]{4,3,2,1,0:T(8,128)S(1)}, f32[1,8,4,8,128]{4,3,2,1,0:T(8,128)S(1)}, u32[]{:S(2)}, u32[]{:S(2)}) collective-permute-start(f32[1,8,4,8,128]{4,3,2,1,0:T(8,128)S(1)} %get-tuple-element.38), channel_id=1, source_target_pairs={{0,16},{4,20},{8,24},{12,28},{16,0},{20,4},{24,8},{28,12},{1,17},{... | collective-permute-start | bytes 393224 | tf_op jit(solution)/shard_map/ppermute | solution.py:443
  12.9 22.2 %collective-permute-start.2 = (f32[1,8,4,8,128]{4,3,2,1,0:T(8,128)S(1)}, f32[1,8,4,8,128]{4,3,2,1,0:T(8,128)S(1)}, u32[]{:S(2)}, u32[]{:S(2)}) collective-permute-start(f32[1,8,4,8,128]{4,3,2,1,0:T(8,128)S(1)} %get-tuple-element.39), channel_id=1, source_target_pairs={{0,12},{4,8},{8,4},{12,0},{16,28},{20,24},{24,20},{28,16},{1,13},{... | collective-permute-start | bytes 393224 | tf_op jit(solution)/shard_map/ppermute | solution.py:443
  27.2 8.0 %collective-permute-start.1 = (f32[1,8,4,8,128]{4,3,2,1,0:T(8,128)S(1)}, f32[1,8,4,8,128]{4,3,2,1,0:T(8,128)S(1)}, u32[]{:S(2)}, u32[]{:S(2)}) collective-permute-start(f32[1,8,4,8,128]{4,3,2,1,0:T(8,128)S(1)} %get-tuple-element.40), channel_id=1, source_target_pairs={{0,8},{4,12},{8,0},{12,4},{16,24},{20,28},{24,16},{28,20},{1,9},{5... | collective-permute-start | bytes 393224 | tf_op jit(solution)/shard_map/ppermute | solution.py:443
  31.1 4.1 %collective-permute-start = (f32[1,8,4,8,128]{4,3,2,1,0:T(8,128)S(1)}, f32[1,8,4,8,128]{4,3,2,1,0:T(8,128)S(1)}, u32[]{:S(2)}, u32[]{:S(2)}) collective-permute-start(f32[1,8,4,8,128]{4,3,2,1,0:T(8,128)S(1)} %get-tuple-element.41), channel_id=1, source_target_pairs={{0,4},{4,0},{8,12},{12,8},{16,20},{20,16},{24,28},{28,24},{1,5},{5... | collective-permute-start | bytes 393224 | tf_op jit(solution)/shard_map/ppermute | solution.py:443
  39.8 31.1 %all-to-all-start.2 = ((f32[32,8,8,128]{3,2,1,0:T(8,128)}), f32[32,8,8,128]{3,2,1,0:T(8,128)S(1)}, u32[]{:S(2)}, u32[]{:S(2)}) async-start(f32[32,8,8,128]{3,2,1,0:T(8,128)} %bitcast.5), calls=%async_computation.2 | async-start | bytes 2097152 | tf_op jit(solution)/shard_map/all_to_all | solution.py:492
  103.2 1.0 copy-start
  104.2 1.0 copy-start.2
  105.1 3.5 %collective-permute-start.7 = (f32[10,16,128]{2,1,0:T(8,128)S(1)}, f32[10,16,128]{2,1,0:T(8,128)S(1)}, u32[]{:S(2)}, u32[]{:S(2)}) collective-permute-start(f32[10,16,128]{2,1,0:T(8,128)S(1)} %get-tuple-element.20), channel_id=1, source_target_pairs={{0,4},{4,0},{8,12},{12,8},{16,20},{20,16},{24,28},{28,24},{1,5},{5... | collective-permute-start | bytes 245768 | tf_op jit(solution)/shard_map/ppermute | solution.py:443
  105.1 5.9 %collective-permute-start.8 = (f32[10,16,128]{2,1,0:T(8,128)S(1)}, f32[10,16,128]{2,1,0:T(8,128)S(1)}, u32[]{:S(2)}, u32[]{:S(2)}) collective-permute-start(f32[10,16,128]{2,1,0:T(8,128)S(1)} %get-tuple-element.21), channel_id=1, source_target_pairs={{0,8},{4,12},{8,0},{12,4},{16,24},{20,28},{24,16},{28,20},{1,9},{5... | collective-permute-start | bytes 245768 | tf_op jit(solution)/shard_map/ppermute | solution.py:443
  106.6 5.1 %collective-permute-start.9 = (f32[10,16,128]{2,1,0:T(8,128)S(1)}, f32[10,16,128]{2,1,0:T(8,128)S(1)}, u32[]{:S(2)}, u32[]{:S(2)}) collective-permute-start(f32[10,16,128]{2,1,0:T(8,128)S(1)} %get-tuple-element.22), channel_id=1, source_target_pairs={{0,12},{4,8},{8,4},{12,0},{16,28},{20,24},{24,20},{28,16},{1,13},{... | collective-permute-start | bytes 245768 | tf_op jit(solution)/shard_map/ppermute | solution.py:443
  107.0 4.8 %collective-permute-start.10 = (f32[10,16,128]{2,1,0:T(8,128)S(1)}, f32[10,16,128]{2,1,0:T(8,128)S(1)}, u32[]{:S(2)}, u32[]{:S(2)}) collective-permute-start(f32[10,16,128]{2,1,0:T(8,128)S(1)} %get-tuple-element.23), channel_id=1, source_target_pairs={{0,16},{4,20},{8,24},{12,28},{16,0},{20,4},{24,8},{28,12},{1,17},{... | collective-permute-start | bytes 245768 | tf_op jit(solution)/shard_map/ppermute | solution.py:443
  108.5 8.3 %collective-permute-start.11 = (f32[10,16,128]{2,1,0:T(8,128)S(1)}, f32[10,16,128]{2,1,0:T(8,128)S(1)}, u32[]{:S(2)}, u32[]{:S(2)}) collective-permute-start(f32[10,16,128]{2,1,0:T(8,128)S(1)} %get-tuple-element.24), channel_id=1, source_target_pairs={{0,20},{4,16},{8,28},{12,24},{16,4},{20,0},{24,12},{28,8},{1,21},{... | collective-permute-start | bytes 245768 | tf_op jit(solution)/shard_map/ppermute | solution.py:443
  108.6 8.1 %collective-permute-start.12 = (f32[10,16,128]{2,1,0:T(8,128)S(1)}, f32[10,16,128]{2,1,0:T(8,128)S(1)}, u32[]{:S(2)}, u32[]{:S(2)}) collective-permute-start(f32[10,16,128]{2,1,0:T(8,128)S(1)} %get-tuple-element.25), channel_id=1, source_target_pairs={{0,24},{4,28},{8,16},{12,20},{16,8},{20,12},{24,0},{28,4},{1,25},{... | collective-permute-start | bytes 245768 | tf_op jit(solution)/shard_map/ppermute | solution.py:443
  111.0 5.7 %collective-permute-start.13 = (f32[10,16,128]{2,1,0:T(8,128)S(1)}, f32[10,16,128]{2,1,0:T(8,128)S(1)}, u32[]{:S(2)}, u32[]{:S(2)}) collective-permute-start(f32[10,16,128]{2,1,0:T(8,128)S(1)} %get-tuple-element.26), channel_id=1, source_target_pairs={{0,28},{4,24},{8,20},{12,16},{16,12},{20,8},{24,4},{28,0},{1,29},{... | collective-permute-start | bytes 245768 | tf_op jit(solution)/shard_map/ppermute | solution.py:443
  116.8 14.8 %collective-permute-start.16 = (f32[10,16,128]{2,1,0:T(8,128)S(1)}, f32[10,16,128]{2,1,0:T(8,128)S(1)}, u32[]{:S(2)}, u32[]{:S(2)}) collective-permute-start(f32[10,16,128]{2,1,0:T(8,128)S(1)} %add_add_fusion.2), channel_id=1, source_target_pairs={{0,3},{1,2},{2,1},{3,0},{4,7},{5,6},{6,5},{7,4},{8,11},{9,10},{10,... | collective-permute-start | bytes 245768 | tf_op jit(solution)/shard_map/ppermute | solution.py:443
  117.9 110.8 %collective-permute-start.26 = (f32[32,8,8,128]{3,2,1,0:T(8,128)S(1)}, f32[32,8,8,128]{3,2,1,0:T(8,128)S(1)}, u32[]{:S(2)}, u32[]{:S(2)}) collective-permute-start(f32[32,8,8,128]{3,2,1,0:T(8,128)S(1)} %all_to_all.15.refs_0_), channel_id=1, source_target_pairs={{1,0},{2,1},{3,2},{5,4},{6,5},{7,6},{9,8},{10,9},{11,10},{13,12},{... | collective-permute-start | bytes 3145736 | tf_op jit(solution)/shard_map/ppermute | solution.py:437
  119.2 109.5 %collective-permute-start.24 = (f32[32,8,8,128]{3,2,1,0:T(8,128)S(1)}, f32[32,8,8,128]{3,2,1,0:T(8,128)}, u32[]{:S(2)}, u32[]{:S(2)}) collective-permute-start(f32[32,8,8,128]{3,2,1,0:T(8,128)S(1)} %all_to_all.15.refs_0_), channel_id=1, source_target_pairs={{0,1},{1,2},{2,3},{4,5},{5,6},{6,7},{8,9},{9,10},{10,11},{12,13},{... | collective-permute-start | bytes 3145736 | tf_op jit(solution)/shard_map/ppermute | solution.py:437
  124.7 104.0 %collective-permute-start.27 = (f32[32,8,8,128]{3,2,1,0:T(8,128)S(1)}, f32[32,8,8,128]{3,2,1,0:T(8,128)}, u32[]{:S(2)}, u32[]{:S(2)}) collective-permute-start(f32[32,8,8,128]{3,2,1,0:T(8,128)S(1)} %all-to-all-done.2.refs_1_), channel_id=1, source_target_pairs={{1,0},{2,1},{3,2},{5,4},{6,5},{7,6},{9,8},{10,9},{11,10},{13,12},{... | collective-permute-start | bytes 3145736 | tf_op jit(solution)/shard_map/ppermute | solution.py:437
  126.0 102.7 %collective-permute-start.25 = (f32[32,8,8,128]{3,2,1,0:T(8,128)S(1)}, f32[32,8,8,128]{3,2,1,0:T(8,128)}, u32[]{:S(2)}, u32[]{:S(2)}) collective-permute-start(f32[32,8,8,128]{3,2,1,0:T(8,128)S(1)} %all-to-all-done.2.refs_1_), channel_id=1, source_target_pairs={{0,1},{1,2},{2,3},{4,5},{5,6},{6,7},{8,9},{9,10},{10,11},{12,13},{... | collective-permute-start | bytes 3145736 | tf_op jit(solution)/shard_map/ppermute | solution.py:437
  131.6 40.2 %collective-permute-start.15 = (f32[10,16,128]{2,1,0:T(8,128)S(1)}, f32[10,16,128]{2,1,0:T(8,128)S(1)}, u32[]{:S(2)}, u32[]{:S(2)}) collective-permute-start(f32[10,16,128]{2,1,0:T(8,128)S(1)} %add_add_fusion.2), channel_id=1, source_target_pairs={{0,2},{1,3},{2,0},{3,1},{4,6},{5,7},{6,4},{7,5},{8,10},{9,11},{10,... | collective-permute-start | bytes 245768 | tf_op jit(solution)/shard_map/ppermute | solution.py:443
  171.8 4.4 %collective-permute-start.14 = (f32[10,16,128]{2,1,0:T(8,128)S(1)}, f32[10,16,128]{2,1,0:T(8,128)S(1)}, u32[]{:S(2)}, u32[]{:S(2)}) collective-permute-start(f32[10,16,128]{2,1,0:T(8,128)S(1)} %add_add_fusion.2), channel_id=1, source_target_pairs={{0,1},{1,0},{2,3},{3,2},{4,5},{5,4},{6,7},{7,6},{8,9},{9,8},{10,11... | collective-permute-start | bytes 245768 | tf_op jit(solution)/shard_map/ppermute | solution.py:443
  176.3 4.9 %collective-permute-start.23 = (f32[10,16,128]{2,1,0:T(8,128)S(1)}, f32[10,16,128]{2,1,0:T(8,128)S(1)}, u32[]{:S(2)}, u32[]{:S(2)}) collective-permute-start(f32[10,16,128]{2,1,0:T(8,128)S(1)} %add_add_fusion.1.refs_0_), channel_id=1, source_target_pairs={{0,28},{4,24},{8,20},{12,16},{16,12},{20,8},{24,4},{28,0},{1,29},{... | collective-permute-start | bytes 245768 | tf_op jit(solution)/shard_map/ppermute | solution.py:443
  181.2 5.3 %collective-permute-start.22 = (f32[10,16,128]{2,1,0:T(8,128)S(1)}, f32[10,16,128]{2,1,0:T(8,128)S(1)}, u32[]{:S(2)}, u32[]{:S(2)}) collective-permute-start(f32[10,16,128]{2,1,0:T(8,128)S(1)} %add_add_fusion.1.refs_0_), channel_id=1, source_target_pairs={{0,24},{4,28},{8,16},{12,20},{16,8},{20,12},{24,0},{28,4},{1,25},{... | collective-permute-start | bytes 245768 | tf_op jit(solution)/shard_map/ppermute | solution.py:443
  186.5 4.7 %collective-permute-start.21 = (f32[10,16,128]{2,1,0:T(8,128)S(1)}, f32[10,16,128]{2,1,0:T(8,128)S(1)}, u32[]{:S(2)}, u32[]{:S(2)}) collective-permute-start(f32[10,16,128]{2,1,0:T(8,128)S(1)} %add_add_fusion.1.refs_0_), channel_id=1, source_target_pairs={{0,20},{4,16},{8,28},{12,24},{16,4},{20,0},{24,12},{28,8},{1,21},{... | collective-permute-start | bytes 245768 | tf_op jit(solution)/shard_map/ppermute | solution.py:443
  191.2 4.5 %collective-permute-start.20 = (f32[10,16,128]{2,1,0:T(8,128)S(1)}, f32[10,16,128]{2,1,0:T(8,128)S(1)}, u32[]{:S(2)}, u32[]{:S(2)}) collective-permute-start(f32[10,16,128]{2,1,0:T(8,128)S(1)} %add_add_fusion.1.refs_0_), channel_id=1, source_target_pairs={{0,16},{4,20},{8,24},{12,28},{16,0},{20,4},{24,8},{28,12},{1,17},{... | collective-permute-start | bytes 245768 | tf_op jit(solution)/shard_map/ppermute | solution.py:443
  195.6 0.6 copy-start.4
  196.3 4.2 %collective-permute-start.19 = (f32[10,16,128]{2,1,0:T(8,128)S(1)}, f32[10,16,128]{2,1,0:T(8,128)S(1)}, u32[]{:S(2)}, u32[]{:S(2)}) collective-permute-start(f32[10,16,128]{2,1,0:T(8,128)S(1)} %add_add_fusion.1.refs_0_), channel_id=1, source_target_pairs={{0,12},{4,8},{8,4},{12,0},{16,28},{20,24},{24,20},{28,16},{1,13},{... | collective-permute-start | bytes 245768 | tf_op jit(solution)/shard_map/ppermute | solution.py:443
  200.4 0.6 copy-start.6
  201.1 4.4 %collective-permute-start.18 = (f32[10,16,128]{2,1,0:T(8,128)S(1)}, f32[10,16,128]{2,1,0:T(8,128)S(1)}, u32[]{:S(2)}, u32[]{:S(2)}) collective-permute-start(f32[10,16,128]{2,1,0:T(8,128)S(1)} %add_add_fusion.1.refs_0_), channel_id=1, source_target_pairs={{0,8},{4,12},{8,0},{12,4},{16,24},{20,28},{24,16},{28,20},{1,9},{5... | collective-permute-start | bytes 245768 | tf_op jit(solution)/shard_map/ppermute | solution.py:443
  205.5 0.6 copy-start.8
  206.1 1.4 collective-permute-start.17
  207.6 0.9 copy-start.5
  208.4 0.9 copy-start.7
  209.3 0.9 copy-start.9
  228.8 9.7 %copy-start.1 = (bf16[512,1024]{1,0:T(8,128)(2,1)S(1)}, bf16[512,1024]{1,0:T(8,128)(2,1)}, u32[]{:S(2)}) copy-start(bf16[512,1024]{1,0:T(8,128)(2,1)} %copy-done) | copy-start | bytes 3145732
  228.8 9.7 %copy-start.3 = (bf16[512,1024]{1,0:T(8,128)(2,1)S(1)}, bf16[512,1024]{1,0:T(8,128)(2,1)}, u32[]{:S(2)}) copy-start(bf16[512,1024]{1,0:T(8,128)(2,1)} %copy-done.2) | copy-start | bytes 3145732
  234.5 9.2 %collective-permute-start.28 = (f32[128,8,128]{2,1,0:T(8,128)S(1)}, f32[128,8,128]{2,1,0:T(8,128)S(1)}, u32[]{:S(2)}, u32[]{:S(2)}) collective-permute-start(f32[128,8,128]{2,1,0:T(8,128)S(1)} %get-tuple-element.27), channel_id=1, source_target_pairs={{1,2},{2,3},{5,6},{6,7},{9,10},{10,11},{13,14},{14,15},{17,18},{18... | collective-permute-start | bytes 1572872 | tf_op jit(solution)/shard_map/ppermute | solution.py:516
  235.2 8.5 %collective-permute-start.29 = (f32[128,8,128]{2,1,0:T(8,128)S(1)}, f32[128,8,128]{2,1,0:T(8,128)S(1)}, u32[]{:S(2)}, u32[]{:S(2)}) collective-permute-start(f32[128,8,128]{2,1,0:T(8,128)S(1)} %get-tuple-element.28), channel_id=1, source_target_pairs={{1,3},{5,7},{9,11},{13,15},{17,19},{21,23},{25,27},{29,31}} | collective-permute-start | bytes 1572872 | tf_op jit(solution)/shard_map/ppermute | solution.py:514
  235.9 20.3 %collective-permute-start.30 = (f32[128,8,128]{2,1,0:T(8,128)S(1)}, f32[128,8,128]{2,1,0:T(8,128)S(1)}, u32[]{:S(2)}, u32[]{:S(2)}) collective-permute-start(f32[128,8,128]{2,1,0:T(8,128)S(1)} %get-tuple-element.29), channel_id=1, source_target_pairs={{1,0},{2,1},{5,4},{6,5},{9,8},{10,9},{13,12},{14,13},{17,16},{18,1... | collective-permute-start | bytes 1572872 | tf_op jit(solution)/shard_map/ppermute | solution.py:517
  237.2 31.4 %collective-permute-start.31 = (f32[128,8,128]{2,1,0:T(8,128)S(1)}, f32[128,8,128]{2,1,0:T(8,128)S(1)}, u32[]{:S(2)}, u32[]{:S(2)}) collective-permute-start(f32[128,8,128]{2,1,0:T(8,128)S(1)} %get-tuple-element.30), channel_id=1, source_target_pairs={{2,0},{6,4},{10,8},{14,12},{18,16},{22,20},{26,24},{30,28}} | collective-permute-start | bytes 1572872 | tf_op jit(solution)/shard_map/ppermute | solution.py:515

commit v3 on v2

--- a/solution.py
+++ b/solution.py
@@ -23,6 +23,7 @@
 smem = pl.BlockSpec(memory_space=pltpu.SMEM)
 big = pltpu.CompilerParams(vmem_limit_bytes=56 << 20)
 small = pltpu.CompilerParams(vmem_limit_bytes=12 << 20)
+middle = pltpu.CompilerParams(vmem_limit_bytes=20 << 20)
 
 
 def split(value):
@@ -60,7 +61,7 @@
 
 def filter_kernel(orbs, place_ref, xy_ref, z_ref, pot_ref, *refs):
     *parts, out_ref, diag, level = refs
-    planes, slabs, rows, _, cols = out_ref.shape
+    planes, slabs, _, rows, cols = out_ref.shape
     pair = z_ref.shape[0] // cols
     flat = slabs * planes * rows
     pot = pot_ref[:, pot_ref.shape[1] - 1].reshape(flat, cols)
@@ -88,7 +89,7 @@
         for e in range(pair):
             value = level3[:, e * cols : (e + 1) * cols].reshape(slabs, planes, rows, cols)
             for g in range(slabs):
-                out_ref[:, g, :, q + e, :] = value[g]
+                out_ref[:, g, q + e] = value[g]
 
 
 def filter_orbitals(place, parts, with_pot, orbs, xy, z):
@@ -96,7 +97,7 @@
     flat = slabs * planes * rows
     return pl.pallas_call(
         functools.partial(filter_kernel, orbs),
-        out_shape=jax.ShapeDtypeStruct((planes, slabs, rows, orbs, cols), f32),
+        out_shape=jax.ShapeDtypeStruct((planes, slabs, orbs, rows, cols), f32),
         in_specs=[smem] + [vmem] * (3 + len(parts)),
         out_specs=vmem,
         scratch_shapes=[pltpu.VMEM((flat, z.shape[0]), f32), pltpu.VMEM((orbs, flat, cols), f32)],
@@ -109,13 +110,36 @@
     return [(i, j) for i in range(count) for j in range(i, count)]
 
 
-def margin_kernel(shape, place_ref, *refs):
-    owners, slabs, chunks, pieces = shape
+def cells_spec(parts, owners, slabs):
+    return owners, slabs, parts[0].shape[2], tuple(part.shape[1] for part in parts)
+
+
+def flat_cells(parts):
+    return [part.reshape(-1, part.shape[-1]) for part in parts]
+
+
+def gather_cells(spec, parts, high, low):
+    owners, slabs, rows, orbs = spec
+    cols = parts[0].shape[-1]
+    base = 0
+    for z in range(owners):
+        for part, count in zip(parts, orbs):
+            span = slabs * count
+            for r in range(rows):
+                value = part[pl.ds(z * span * rows + r, span, stride=rows), :]
+                h, l = split(value)
+                high[pl.ds(base, span), r * cols : (r + 1) * cols] = h
+                low[pl.ds(base, span), r * cols : (r + 1) * cols] = l
+            base += span
+
+
+def margin_kernel(spec, pieces, place_ref, *refs):
+    chunks = len(spec[3])
     parts = refs[:chunks]
     outs = refs[chunks : chunks + pieces]
     high, low, acc = refs[chunks + pieces :]
-    norb = chunks * parts[0].shape[0] * parts[0].shape[2]
-    gather_cells(parts, owners, slabs, high, low)
+    norb = high.shape[0]
+    gather_cells(spec, parts, high, low)
     size = acc.shape[-1]
     contract = (((1,), (1,)), ((), ()))
     at = 0
@@ -136,19 +160,22 @@
         outs[s][...] = acc[:, pl.ds(first, part), :]
 
 
-def margin_blocks(place, parts, owners, slabs, size, pieces):
-    _, rows, orbs, cols = parts[0].shape
-    norb = len(parts) * parts[0].shape[0] * orbs
-    count = norb // size
+def wide_scratch(spec, cols):
+    owners, slabs, rows, orbs = spec
+    return [pltpu.VMEM((owners * slabs * sum(orbs), rows * cols), bf16)] * 2
+
+
+def margin_blocks(place, spec, parts, size, pieces):
+    owners, slabs, _, orbs = spec
+    count = owners * slabs * sum(orbs) // size
     blocks = count * (count + 1) // 2
-    wide = jax.ShapeDtypeStruct((norb, rows * cols), bf16)
-    outs = [jax.ShapeDtypeStruct((blocks, size // pieces, size), f32)] * pieces + [wide, wide]
-    return pl.pallas_call(
-        functools.partial(margin_kernel, (owners, slabs, len(parts), pieces)),
+    outs = [jax.ShapeDtypeStruct((blocks, size // pieces, size), f32)] * pieces
+    return pl.pallas_call(
+        functools.partial(margin_kernel, spec, pieces),
         out_shape=outs,
         in_specs=[smem] + [vmem] * len(parts),
         out_specs=[vmem] * len(outs),
-        scratch_shapes=[pltpu.VMEM((blocks, size, size), f32)],
+        scratch_shapes=wide_scratch(spec, parts[0].shape[1]) + [pltpu.VMEM((blocks, size, size), f32)],
         compiler_params=small,
         name="margin",
     )(place, *parts)
@@ -285,18 +312,6 @@
     )(place, *pieces)
 
 
-def gather_cells(parts, owners, slabs, high, low):
-    _, rows, orbs, cols = parts[0].shape
-    span = slabs * orbs
-    for z in range(owners):
-        for c in range(len(parts)):
-            at = pl.ds((z * len(parts) + c) * span, span)
-            for r in range(rows):
-                h, l = split(parts[c][z * slabs : (z + 1) * slabs, r].reshape(span, cols))
-                high[at, r * cols : (r + 1) * cols] = h
-                low[at, r * cols : (r + 1) * cols] = l
-
-
 def product(weights, high, low):
     h, l = split(weights)
     return mm(h, low) + mm(l, high) + mm(h, high)
@@ -307,7 +322,9 @@
         out[:, r, :] = value[:, r * cols : (r + 1) * cols]
 
 
-def rotate_kernel(v_ref, high, low, out_ref):
+def rotate_kernel(spec, v_ref, *refs):
+    *parts, out_ref, high, low = refs
+    gather_cells(spec, parts, high, low)
     _, local, rows, cols = out_ref.shape
     count, size, _ = v_ref.shape
     step = min(size, local)
@@ -319,98 +336,100 @@
             put_rows(out_ref.at[own, pl.ds(off, step)], total[q * step : (q + 1) * step], rows, cols)
 
 
-def rotate(v, high, low, owners, rows):
-    norb, wide = high.shape
-    return pl.pallas_call(
-        rotate_kernel,
-        out_shape=jax.ShapeDtypeStruct((owners, norb // owners, rows, wide // rows), f32),
-        in_specs=[vmem] * 3,
+def rotate(v, spec, parts):
+    owners, slabs, rows, orbs = spec
+    cols = parts[0].shape[1]
+    return pl.pallas_call(
+        functools.partial(rotate_kernel, spec),
+        out_shape=jax.ShapeDtypeStruct((owners, slabs * sum(orbs), rows, cols), f32),
+        in_specs=[vmem] * (1 + len(parts)),
         out_specs=vmem,
-        compiler_params=small,
+        scratch_shapes=wide_scratch(spec, cols),
+        compiler_params=middle,
         name="rotate",
-    )(v, high, low)
-
-
-def far_kernel(shape, layer_ref, v_ref, *refs):
-    owners, slabs, chunks = shape
-    below, above = refs[:chunks], refs[chunks : 2 * chunks]
-    outs, (high, low) = refs[2 * chunks : -2], refs[-2:]
-    _, rows, cols = outs[0].shape
+    )(v, *parts)
+
+
+def twin_side(layer):
+    return jnp.where(lax.rem(layer, 2) == 1, 1, -1)
+
+
+def far_kernel(spec, layer_ref, v_ref, *refs):
+    chunks = len(spec[3])
+    twin, facing = refs[:chunks], refs[chunks : 2 * chunks]
+    skip, step, back, high, low = refs[2 * chunks :]
+    _, rows, cols = step.shape
     layer = layer_ref[0]
-    for side, parts in ((1, below), (-1, above)):
-        gather_cells(parts, owners, slabs, high, low)
-        for hop in (2, 1):
-            to = jnp.clip(layer + side * hop, 0, owners - 1)
-            out = outs[(0 if side > 0 else 2) + hop - 1]
-            put_rows(out, product(v_ref[to], high[...], low[...]), rows, cols)
-
-
-def rotate_far(layer, v, below, above, owners, slabs):
-    _, rows, _, cols = below[0].shape
-    norb = v.shape[2]
-    wide = pltpu.VMEM((norb, rows * cols), bf16)
-    return pl.pallas_call(
-        functools.partial(far_kernel, (owners, slabs, len(below))),
-        out_shape=[jax.ShapeDtypeStruct((norb // owners, rows, cols), f32)] * 4,
-        in_specs=[smem] + [vmem] * (1 + 2 * len(below)),
-        out_specs=[vmem] * 4,
-        scratch_shapes=[wide, wide],
-        compiler_params=small,
+    side = twin_side(layer)
+
+    def put(out, to):
+        to = jnp.clip(to, 0, v_ref.shape[0] - 1)
+        put_rows(out, product(v_ref[to], high[...], low[...]), rows, cols)
+
+    gather_cells(spec, twin, high, low)
+    put(skip, layer + 2 * side)
+    put(step, layer + side)
+    gather_cells(spec, facing, high, low)
+    put(back, layer - side)
+
+
+def rotate_far(layer, v, spec, twin, facing):
+    _, slabs, rows, orbs = spec
+    cols = twin[0].shape[1]
+    return pl.pallas_call(
+        functools.partial(far_kernel, spec),
+        out_shape=[jax.ShapeDtypeStruct((slabs * sum(orbs), rows, cols), f32)] * 3,
+        in_specs=[smem] + [vmem] * (1 + 2 * len(twin)),
+        out_specs=[vmem] * 3,
+        scratch_shapes=wide_scratch(spec, cols),
+        compiler_params=middle,
         name="rotate_far",
-    )(layer, v, *below, *above)
-
-
-def near_kernel(shape, layer_ref, v_ref, my_high, my_low, *refs):
-    owners, slabs, chunks = shape
-    below, above = refs[:chunks], refs[chunks : 2 * chunks]
-    out_ref, high, low = refs[2 * chunks :]
-    _, _, rows, cols = out_ref.shape
+    )(layer, v, *twin, *facing)
+
+
+def near_kernel(spec, layer_ref, v_ref, *refs):
+    chunks = len(spec[3])
+    mine, twin, facing = (refs[k * chunks : (k + 1) * chunks] for k in range(3))
+    out_ref, high, low = refs[3 * chunks :]
+    owners, rows, cols = out_ref.shape[1:]
     layer = layer_ref[0]
-
-    def put(plane, h, l):
-        value = product(v_ref[layer], h[...], l[...])
+    side = twin_side(layer)
+
+    def put(plane, parts):
+        gather_cells(spec, parts, high, low)
+        value = product(v_ref[layer], high[...], low[...])
         for r in range(rows):
             out_ref[:, plane, r, :] = value[:, r * cols : (r + 1) * cols]
 
-    put(layer, my_high, my_low)
-
-    @pl.when(layer > 0)
+    put(layer, mine)
+    put(layer - side, twin)
+
+    @pl.when((layer > 0) & (layer < owners - 1))
     def _():
-        gather_cells(below, owners, slabs, high, low)
-        put(jnp.maximum(layer - 1, 0), high, low)
-
-    @pl.when(layer < owners - 1)
-    def _():
-        gather_cells(above, owners, slabs, high, low)
-        put(jnp.minimum(layer + 1, owners - 1), high, low)
-
-
-def rotate_near(layer, v, high, low, below, above, owners, slabs):
-    _, rows, _, cols = below[0].shape
-    norb = v.shape[2]
-    wide = pltpu.VMEM((norb, rows * cols), bf16)
-    return pl.pallas_call(
-        functools.partial(near_kernel, (owners, slabs, len(below))),
-        out_shape=jax.ShapeDtypeStruct((norb // owners, owners, rows, cols), f32),
-        in_specs=[smem] + [vmem] * (3 + 2 * len(below)),
+        put(jnp.clip(layer + side, 0, owners - 1), facing)
+
+
+def rotate_near(layer, v, spec, mine, twin, facing):
+    owners, slabs, rows, orbs = spec
+    cols = mine[0].shape[1]
+    return pl.pallas_call(
+        functools.partial(near_kernel, spec),
+        out_shape=jax.ShapeDtypeStruct((slabs * sum(orbs), owners, rows, cols), f32),
+        in_specs=[smem] + [vmem] * (1 + 3 * len(mine)),
         out_specs=vmem,
-        scratch_shapes=[wide, wide],
-        compiler_params=small,
+        scratch_shapes=wide_scratch(spec, cols),
+        compiler_params=middle,
         name="rotate_near",
-    )(layer, v, high, low, *below, *above)
-
-
-def join_kernel(layer_ref, up1, up2, down1, down2, near_ref, out_ref, sems):
-    owners = out_ref.shape[1]
-    for z in range(owners):
-        sources = {z - 3: up2, z - 2: up1, z + 2: down1, z + 3: down2}
+    )(layer, v, *mine, *twin, *facing)
+
+
+def join_kernel(layer_ref, skip, step, back, near_ref, out_ref, sems):
+    for z, planes in enumerate((((skip, 3), (back, 2)), ((step, 3),), ((step, 0),), ((skip, 0), (back, 1)))):
 
         @pl.when(layer_ref[0] == z)
         def _():
             copies = [
-                pltpu.make_async_copy(source, out_ref.at[:, p], sems.at[p])
-                for p, source in sources.items()
-                if 0 <= p < owners
+                pltpu.make_async_copy(source, out_ref.at[:, p], sems.at[n]) for n, (source, p) in enumerate(planes)
             ]
             for copy in copies:
                 copy.start()
@@ -423,18 +442,13 @@
     return pl.pallas_call(
         join_kernel,
         out_shape=jax.ShapeDtypeStruct(near.shape, f32),
-        in_specs=[smem] + [vmem] * 4 + [anywhere],
+        in_specs=[smem] + [vmem] * 3 + [anywhere],
         out_specs=anywhere,
-        scratch_shapes=[pltpu.SemaphoreType.DMA((near.shape[1],))],
-        input_output_aliases={5: 0},
+        scratch_shapes=[pltpu.SemaphoreType.DMA((2,))],
+        input_output_aliases={4: 0},
         compiler_params=small,
         name="join",
     )(layer, *far, near)
-
-
-def shift(values, axis, by, count):
-    pairs = [(i, i + by) for i in range(count) if 0 <= i + by < count]
-    return [lax.ppermute(value, axis, pairs) for value in values]
 
 
 def swap_all(pieces, axis):
@@ -454,69 +468,67 @@
     local, planes, rows, cols = orbitals.shape
     slabs = lax.axis_size("grid")
     owners = lax.axis_size("orb")
-    chunks = 2 if local % (16 * slabs) == 0 else 1
-    orbs = local // slabs // chunks
+    orbs = local // slabs
+    dealt = (orbs // 4, orbs - orbs // 4) if orbs % 16 == 0 else (orbs,)
     everyone = ("orb", "grid")
     nx = slabs * planes
     place = lax.axis_index("grid").astype(jnp.int32).reshape(1)
 
     xy = plane_matrix(nx, rows)
-    z = line_matrix(cols, 2 if orbs % 2 == 0 else 1)
-
+    z = line_matrix(cols, 2 if all(count % 2 == 0 for count in dealt) else 1)
+
+    first = orbitals[: slabs * dealt[0]].reshape(slabs, dealt[0], planes, rows, cols)
     spread = jnp.broadcast_to(potential, (slabs, 1, planes, rows, cols))
-    parts = [
-        orbitals[c * slabs * orbs : (c + 1) * slabs * orbs].reshape(slabs, orbs, planes, rows, cols)
-        for c in range(chunks)
-    ]
-    first = jnp.concatenate([parts[0], spread], axis=1)
+    first = jnp.concatenate([first, spread], axis=1)
     with_pot = lax.all_to_all(first, "grid", split_axis=0, concat_axis=0, tiled=True)
     arrived = [[with_pot]]
-    for part in parts[1:]:
+    for count in dealt[1:]:
         pieces = [
-            lax.dynamic_slice_in_dim(part, place[0] ^ s, 1, axis=0) for s in range(slabs)
+            lax.dynamic_slice_in_dim(orbitals, slabs * dealt[0] + (place[0] ^ s) * count, count, axis=0)[None]
+            for s in range(slabs)
         ]
         arrived.append(swap_all(pieces, "grid"))
 
     cells = []
-    for c in range(chunks):
-        filtered = filter_orbitals(place, arrived[c], with_pot, orbs, xy, z)
+    for c, count in enumerate(dealt):
+        filtered = filter_orbitals(place, arrived[c], with_pot, count, xy, z)
         if planes >= owners:
             each = planes // owners
-            part_rows = each * rows
-            filtered = filtered.reshape(owners, each, slabs, rows, orbs, cols)
+            filtered = filtered.reshape(owners, each, slabs, count, rows, cols)
+            filtered = jnp.transpose(filtered, (0, 2, 3, 1, 4, 5))
         else:
             each = owners // planes
-            part_rows = rows // each
-            filtered = filtered.reshape(planes, slabs, each, part_rows, orbs, cols)
-        filtered = jnp.swapaxes(filtered, 1, 2).reshape(owners * slabs, part_rows, orbs, cols)
+            filtered = filtered.reshape(planes, slabs, count, each, rows // each, cols)
+            filtered = jnp.transpose(filtered, (0, 3, 1, 2, 4, 5))
+        filtered = filtered.reshape(owners * slabs, count, planes * rows // owners, cols)
         cells.append(lax.all_to_all(filtered, everyone, split_axis=0, concat_axis=0, tiled=True))
 
     size = 128
     total_cells = float(nx * rows * cols)
-    *pieces, high, low = margin_blocks(place, cells, owners, slabs, size, slabs)
-    nearby = owners == 4 and planes == owners
-    if nearby:
-        below, above = [], []
-        for c in range(chunks):
-            below += shift(cells[c : c + 1], "orb", 1, owners)
-            above += shift(cells[c : c + 1], "orb", -1, owners)
+    spec = cells_spec(cells, owners, slabs)
+    cells = flat_cells(cells)
+    pieces = margin_blocks(place, spec, cells, size, slabs)
+    four = owners == 4 and planes == owners
+    if four:
+        twin, facing = [], []
+        for part in cells:
+            twin.append(lax.ppermute(part, "orb", [(0, 1), (1, 0), (2, 3), (3, 2)]))
+            facing.append(lax.ppermute(part, "orb", [(0, 0), (1, 2), (2, 1), (3, 3)]))
     mine = tree_sum(swap_all(pieces, "grid"))
     mine = tree_sum(swap_all([mine] * owners, "orb"))
     margin = swap_all([mine] * slabs, "grid")
     inverse = inverse_rows(place, margin, 1.0 / total_cells)
-    if not nearby:
-        rotated = rotate(inverse, high, low, owners, part_rows)
+    if not four:
+        rotated = rotate(inverse, spec, cells)
         back = lax.all_to_all(rotated, "orb", split_axis=0, concat_axis=0, tiled=True)
         return jnp.swapaxes(back, 0, 1).reshape(local, planes, rows, cols)
     layer = lax.axis_index("orb").astype(jnp.int32).reshape(1)
-    up1, up2, down1, down2 = rotate_far(layer, inverse, below, above, owners, slabs)
-    inner = range(1, owners - 1)
-    up2 = lax.ppermute(up2, "orb", [(i, i + 2) for i in inner if i + 2 < owners])
-    down2 = lax.ppermute(down2, "orb", [(i, i - 2) for i in inner if i >= 2])
-    up1 = lax.ppermute(up1, "orb", [(i, i + 1) for i in inner])
-    down1 = lax.ppermute(down1, "orb", [(i, i - 1) for i in inner])
-    near = rotate_near(layer, inverse, high, low, below, above, owners, slabs)
-    return join(layer, near, (up1, up2, down1, down2))
+    skip, step, back = rotate_far(layer, inverse, spec, twin, facing)
+    skip = lax.ppermute(skip, "orb", [(0, 1), (1, 3), (2, 0), (3, 2)])
+    step = lax.ppermute(step, "orb", [(0, 0), (1, 2), (2, 1), (3, 3)])
+    back = lax.ppermute(back, "orb", [(0, 1), (1, 0), (2, 3), (3, 2)])
+    near = rotate_near(layer, inverse, spec, cells, twin, facing)
+    return join(layer, near, (skip, step, back))
 
 
 def solution(mesh):

time: 270 us -> 231 us (0.86)
  blocking collectives: 29.6 us -> 0 us
  waiting for transfers between devices: 141 us -> 125 us
  starting transfers between devices: 46.9 us -> 53 us
    all_to_all x1 -> x0, blocking collectives: 29.6 us -> none  [orthonormalized(): lax.all_to_all(filtered, everyone, split_axis=0, concat_axis=0, tiled=True)]
    ppermute x24, waiting for transfers between devices: 93.6 us -> 65 us  [swap_all(): lax.ppermute(pieces[s], axis, [(i, i ^ s) for i in range(count)])]
    all_to_all x1 -> x2, waiting for transfers between devices: 22.7 us -> 45.4 us  [orthonormalized(): lax.all_to_all(filtered, everyone, split_axis=0, concat_axis=0, tiled=True)]
    ppermute x8 -> x7, waiting for transfers between devices: 24.9 us -> 14.5 us  [the longest x1 10.4 us: orthonormalized(): back = lax.ppermute(back, 'orb', [(0, 1), (1, 0), (2, 3), (3, 2)])]
    ppermute x24, starting transfers between devices: 19.2 us -> 23.9 us  [swap_all(): lax.ppermute(pieces[s], axis, [(i, i ^ s) for i in range(count)])]
    all_to_all x1 -> x2, starting transfers between devices: 4.91 us -> 7.9 us  [orthonormalized(): lax.all_to_all(filtered, everyone, split_axis=0, concat_axis=0, tiled=True)]
    unnamed x22 -> x10, local copies, waits for them, and re-layouts: 6.49 us -> 4.19 us
    ppermute x8 -> x7, starting transfers between devices: 17.6 us -> 16 us  [the longest x2 6.12 us: orthonormalized(): facing.append(lax.ppermute(part, 'orb', [(0, 0), (1, 2), (2, 1), (3, 3)]))]
  transfers between devices with their start and end apart: 34 -> 34, of which waited for: 19 -> 22; matrix products, arithmetic and copies ran while one was open for 0% -> 1% of each run, Pallas kernels for 10% -> 14%
where the time goes in v3:
time: 231 us; the launch traced here: 230 us
  waiting for transfers between devices  125 us (54%)
  starting transfers between devices  53 us (23%)
  Pallas kernels  42.1 us (18%)
  local copies, waits for them, and re-layouts  7.63 us (3%)
    ppermute x24, waiting for transfers between devices, swap_all(): lax.ppermute(pieces[s], axis, [(i, i ^ s) for i in range(count)])  65 us
    all_to_all x2, waiting for transfers between devices, orthonormalized(): lax.all_to_all(filtered, everyone, split_axis=0, concat_axis=0, tiled=True)  45.4 us
    ppermute x24, starting transfers between devices, swap_all(): lax.ppermute(pieces[s], axis, [(i, i ^ s) for i in range(count)])  23.9 us
    pallas_call x1, Pallas kernels, inverse_rows(): pl.pallas_call(functools.partial(inverse_kernel, factor), out_shape=jax.S...  18.5 us
    ppermute x1, waiting for transfers between devices, orthonormalized(): back = lax.ppermute(back, 'orb', [(0, 1), (1, 0), (2, 3), (3, 2)])  10.4 us
    all_to_all x2, starting transfers between devices, orthonormalized(): lax.all_to_all(filtered, everyone, split_axis=0, concat_axis=0, tiled=True)  7.9 us
    pallas_call x2, Pallas kernels, filter_orbitals(): pl.pallas_call(functools.partial(filter_kernel, orbs), out_shape=jax.Shap...  7.36 us
    pallas_call x1, Pallas kernels, rotate_near(): pl.pallas_call(functools.partial(near_kernel, spec), out_shape=jax.ShapeD...  6.15 us
  transfers between devices with their start and end apart: 34, of which 22 were waited for; matrix products, arithmetic and copies ran while one was open for 1% of the time, Pallas kernels for 14%

profile of v3, /device:TPU:0, one launch (start us, length us, event | category | flops | bytes accessed | tf_op | source)
XLA Modules:
  0.0 230.0 jit_solution(14427658957663223744)
XLA Ops:
  0.0 1.1 slice.3
  2.7 5.2 %all-to-all-start = ((f32[8,5,4,8,128]{4,3,2,1,0:T(8,128)}), f32[8,5,4,8,128]{4,3,2,1,0:T(8,128)S(1)}, u32[]{:S(2)}, u32[]{:S(2)}) async-start(f32[8,5,4,8,128]{4,3,2,1,0:T(8,128)} %pad_maximum_fusion), calls=%async_computation | async-start | bytes 1310720 | tf_op jit(solution)/shard_map/all_to_all | solution.py:483
  7.9 1.6 dynamic-slice_bitcast_fusion
  9.6 2.7 %collective-permute-start.6 = (f32[1,12,4,8,128]{4,3,2,1,0:T(8,128)S(1)}, f32[1,12,4,8,128]{4,3,2,1,0:T(8,128)S(1)}, u32[]{:S(2)}, u32[]{:S(2)}) collective-permute-start(f32[1,12,4,8,128]{4,3,2,1,0:T(8,128)S(1)} %get-tuple-element.27), channel_id=1, source_target_pairs={{0,28},{4,24},{8,20},{12,16},{16,12},{20,8},{24,4},{28,0},{1,29},{... | collective-permute-start | bytes 589832 | tf_op jit(solution)/shard_map/ppermute | solution.py:457
  12.8 1.5 collective-permute-start.3
  14.3 1.5 collective-permute-start.1
  16.6 6.2 %collective-permute-done.6.refs_7_ = f32[1,12,4,8,128]{4,3,2,1,0:T(8,128)S(1)} collective-permute-done((f32[1,12,4,8,128]{4,3,2,1,0:T(8,128)S(1)}, f32[1,12,4,8,128]{4,3,2,1,0:T(8,128)S(1)}, u32[]{:S(2)}, u32[]{:S(2)}) %collective-permute-start.6) | collective-permute-done | bytes 196640 | tf_op jit(solution)/shard_map/ppermute | solution.py:457
  23.7 2.3 collective-permute-done.4.refs_5_
  26.0 1.8 collective-permute-start.5
  28.1 2.7 %collective-permute-done.3.refs_4_ = f32[1,12,4,8,128]{4,3,2,1,0:T(8,128)S(1)} collective-permute-done((f32[1,12,4,8,128]{4,3,2,1,0:T(8,128)S(1)}, f32[1,12,4,8,128]{4,3,2,1,0:T(8,128)S(1)}, u32[]{:S(2)}, u32[]{:S(2)}) %collective-permute-start.3) | collective-permute-done | bytes 196640 | tf_op jit(solution)/shard_map/ppermute | solution.py:457
  31.4 4.5 %collective-permute-done.5.refs_6_ = f32[1,12,4,8,128]{4,3,2,1,0:T(8,128)S(1)} collective-permute-done((f32[1,12,4,8,128]{4,3,2,1,0:T(8,128)S(1)}, f32[1,12,4,8,128]{4,3,2,1,0:T(8,128)S(1)}, u32[]{:S(2)}, u32[]{:S(2)}) %collective-permute-start.5) | collective-permute-done | bytes 196640 | tf_op jit(solution)/shard_map/ppermute | solution.py:457
  35.9 4.7 %filter.3 = f32[4,8,12,8,128]{4,3,2,1,0:T(8,128)S(1)} custom-call(s32[1]{0:T(128)} %bitcast.1.place_ref, bf16[256,256]{1,0:T(8,128)(2,1)S(1)} %fusion.6.xy_ref, bf16[256,256]{1,0:T(8,128)(2,1)S(1)} %select_convert_fusion.z_ref, f32[8,5,4,8,128]{4,3,2,1,0:T(8,128)S(1)} %all-to-all-done.pot_ref.refs_0_, f32[1,12,4,8,128]{4,3,2,1,0:T(8,128)S(1)} %get-tuple-element.33.refs_0_, ...), custom_call_target="tpu_custom_call" | custom-call | tf_op jit(solution)/shard_map/filter/pallas_call | solution.py:98
  40.6 1.1 copy-done
  41.7 4.0 %all-to-all-start.2 = ((f32[32,12,8,128]{3,2,1,0:T(8,128)}), f32[32,12,8,128]{3,2,1,0:T(8,128)S(1)}, u32[]{:S(2)}, u32[]{:S(2)}) async-start(f32[32,12,8,128]{3,2,1,0:T(8,128)} %bitcast.27), calls=%async_computation.2 | async-start | bytes 3145728 | tf_op jit(solution)/shard_map/all_to_all | solution.py:504
  45.7 2.7 %filter.2 = f32[4,8,4,8,128]{4,3,2,1,0:T(8,128)} custom-call(s32[1]{0:T(128)} %bitcast.1.place_ref, bf16[256,256]{1,0:T(8,128)(2,1)S(1)} %fusion.6.xy_ref, bf16[256,256]{1,0:T(8,128)(2,1)S(1)} %select_convert_fusion.z_ref, f32[8,5,4,8,128]{4,3,2,1,0:T(8,128)S(1)} %all-to-all-done.pot_ref.refs_0_, f32[8,5,4,8,128]{4,3,2,1,0:T(8,128)S(1)} %all-to-all-done.pot_ref.refs_0_), custom_call_target="tpu_custom_call" | custom-call | tf_op jit(solution)/shard_map/filter/pallas_call | solution.py:98
  48.4 34.9 %all-to-all-done.2 = f32[32,12,8,128]{3,2,1,0:T(8,128)S(1)} async-done(((f32[32,12,8,128]{3,2,1,0:T(8,128)}), f32[32,12,8,128]{3,2,1,0:T(8,128)S(1)}, u32[]{:S(2)}, u32[]{:S(2)}) %all-to-all-start.2) | async-done | bytes 1572896 | tf_op jit(solution)/shard_map/all_to_all | solution.py:504
  83.4 3.9 %all-to-all-start.1 = ((f32[32,4,8,128]{3,2,1,0:T(8,128)}), f32[32,4,8,128]{3,2,1,0:T(8,128)}, u32[]{:S(2)}, u32[]{:S(2)}) async-start(f32[32,4,8,128]{3,2,1,0:T(8,128)} %bitcast.3), calls=%async_computation.1 | async-start | bytes 1048576 | tf_op jit(solution)/shard_map/all_to_all | solution.py:504
  88.1 4.4 %collective-permute-start.25 = (f32[3072,128]{1,0:T(8,128)S(1)}, f32[3072,128]{1,0:T(8,128)}, u32[]{:S(2)}, u32[]{:S(2)}) collective-permute-start(f32[3072,128]{1,0:T(8,128)S(1)} %bitcast.24), channel_id=1, source_target_pairs={{0,1},{1,0},{2,3},{3,2},{4,5},{5,4},{6,7},{7,6},{8,9},{9,8},{10,11... | collective-permute-start | bytes 4718600 | tf_op jit(solution)/shard_map/ppermute | solution.py:515
  92.4 10.4 %all-to-all-done.1 = f32[32,4,8,128]{3,2,1,0:T(8,128)} async-done(((f32[32,4,8,128]{3,2,1,0:T(8,128)}), f32[32,4,8,128]{3,2,1,0:T(8,128)}, u32[]{:S(2)}, u32[]{:S(2)}) %all-to-all-start.1) | async-done | bytes 524320 | tf_op jit(solution)/shard_map/all_to_all | solution.py:504
  102.9 3.9 %margin.1 = (f32[10,16,128]{2,1,0:T(8,128)S(1)}, f32[10,16,128]{2,1,0:T(8,128)S(1)}, f32[10,16,128]{2,1,0:T(8,128)S(1)}, f32[10,16,128]{2,1,0:T(8,128)S(1)}, f32...) custom-call(s32[1]{0:T(128)} %bitcast.1.place_ref, ...), custom_call_target="tpu_custom_call" | custom-call | tf_op jit(solution)/shard_map/margin/pallas_call | solution.py:173
  106.9 1.5 collective-permute-start.8
  108.8 1.4 collective-permute-start.10
  110.2 2.0 collective-permute-done.8
  113.1 2.2 collective-permute-start.12
  116.7 2.2 collective-permute-done.12
  119.0 1.3 collective-permute-done.13
  120.3 1.1 collective-permute-start.16
  121.4 2.0 collective-permute-start.15
  123.3 1.4 collective-permute-start.14
  124.8 11.7 %collective-permute-done.16 = f32[10,16,128]{2,1,0:T(8,128)S(1)} collective-permute-done((f32[10,16,128]{2,1,0:T(8,128)S(1)}, f32[10,16,128]{2,1,0:T(8,128)S(1)}, u32[]{:S(2)}, u32[]{:S(2)}) %collective-permute-start.16) | collective-permute-done | bytes 81952 | tf_op jit(solution)/shard_map/ppermute | solution.py:457
  136.4 6.5 %collective-permute-done.15 = f32[10,16,128]{2,1,0:T(8,128)S(1)} collective-permute-done((f32[10,16,128]{2,1,0:T(8,128)S(1)}, f32[10,16,128]{2,1,0:T(8,128)S(1)}, u32[]{:S(2)}, u32[]{:S(2)}) %collective-permute-start.15) | collective-permute-done | bytes 81952 | tf_op jit(solution)/shard_map/ppermute | solution.py:457
  142.9 1.6 collective-permute-start.23
  144.5 5.4 %collective-permute-start.26 = (f32[1024,128]{1,0:T(8,128)}, f32[1024,128]{1,0:T(8,128)}, u32[]{:S(2)}, u32[]{:S(2)}) collective-permute-start(f32[1024,128]{1,0:T(8,128)} %bitcast.4.refs_0_), channel_id=1, source_target_pairs={{0,0},{1,2},{2,1},{3,3},{4,4},{5,6},{6,5},{7,7},{8,8},{9,10},{10,9... | collective-permute-start | bytes 1572872 | tf_op jit(solution)/shard_map/ppermute | solution.py:516
  149.9 0.9 collective-permute-start.22
  150.8 5.3 %collective-permute-done.22.refs_6_ = f32[10,16,128]{2,1,0:T(8,128)S(1)} collective-permute-done((f32[10,16,128]{2,1,0:T(8,128)S(1)}, f32[10,16,128]{2,1,0:T(8,128)S(1)}, u32[]{:S(2)}, u32[]{:S(2)}) %collective-permute-start.22) | collective-permute-done | bytes 81952 | tf_op jit(solution)/shard_map/ppermute | solution.py:457
  156.4 4.2 %collective-permute-done.21.refs_5_ = f32[10,16,128]{2,1,0:T(8,128)S(1)} collective-permute-done((f32[10,16,128]{2,1,0:T(8,128)S(1)}, f32[10,16,128]{2,1,0:T(8,128)S(1)}, u32[]{:S(2)}, u32[]{:S(2)}) %collective-permute-start.21) | collective-permute-done | bytes 81952 | tf_op jit(solution)/shard_map/ppermute | solution.py:457
  161.1 4.3 %collective-permute-done.20.refs_4_ = f32[10,16,128]{2,1,0:T(8,128)S(1)} collective-permute-done((f32[10,16,128]{2,1,0:T(8,128)S(1)}, f32[10,16,128]{2,1,0:T(8,128)S(1)}, u32[]{:S(2)}, u32[]{:S(2)}) %collective-permute-start.20) | collective-permute-done | bytes 81952 | tf_op jit(solution)/shard_map/ppermute | solution.py:457
  165.5 4.6 %collective-permute-done.19.refs_3_ = f32[10,16,128]{2,1,0:T(8,128)S(1)} collective-permute-done((f32[10,16,128]{2,1,0:T(8,128)S(1)}, f32[10,16,128]{2,1,0:T(8,128)S(1)}, u32[]{:S(2)}, u32[]{:S(2)}) %collective-permute-start.19) | collective-permute-done | bytes 81952 | tf_op jit(solution)/shard_map/ppermute | solution.py:457
  171.4 3.8 %collective-permute-done.18.refs_2_ = f32[10,16,128]{2,1,0:T(8,128)S(1)} collective-permute-done((f32[10,16,128]{2,1,0:T(8,128)S(1)}, f32[10,16,128]{2,1,0:T(8,128)S(1)}, u32[]{:S(2)}, u32[]{:S(2)}) %collective-permute-start.18) | collective-permute-done | bytes 81952 | tf_op jit(solution)/shard_map/ppermute | solution.py:457
  175.8 1.4 collective-permute-done.17.refs_1_
  179.0 18.5 %inverse.1.v_ref = f32[4,128,512]{2,1,0:T(8,128)S(1)} custom-call(s32[1]{0:T(128)} %bitcast.1.place_ref, f32[10,16,128]{2,1,0:T(8,128)S(1)} %add_add_fusion.1.refs_0_, f32[10,16,128]{2,1,0:T(8,128)} %collective-permute-done.17.refs_1_, f32[10,16,128]{2,1,0:T(8,128)S(1)} %copy-done.4, f32[10,16,128]{2,1,0:T(8,128)S(1)} %copy-done.2, ...), custom_call_target="tpu_custom_call" | custom-call | tf_op jit(solution)/shard_map/inverse/pallas_call | solution.py:304
  197.5 5.2 %rotate_far.1 = (f32[128,8,128]{2,1,0:T(8,128)S(1)}, f32[128,8,128]{2,1,0:T(8,128)S(1)}, f32[128,8,128]{2,1,0:T(8,128)S(1)}) custom-call(s32[1]{0:T(128)} %bitcast.layer_ref, f32[4,128,512]{2,1,0:T(8,128)S(1)} %inverse.1.v_ref, f32[1024,128]{1,0:T(8,128)} %collective-permute-done.24.refs_0_.refs_2_, f32[3072,128]{1,0:T(8,128)} %collective-permute-done.25.refs_1_.refs_3_, ...), custom_call_target="tpu_custom_call" | custom-call | tf_op jit(solution)/shard_map/rotate_far/pallas_call | solution.py:379
  202.7 1.5 collective-permute-start.28
  204.9 3.4 %collective-permute-start.30 = (f32[128,8,128]{2,1,0:T(8,128)S(1)}, f32[128,8,128]{2,1,0:T(8,128)S(1)}, u32[]{:S(2)}, u32[]{:S(2)}) collective-permute-start(f32[128,8,128]{2,1,0:T(8,128)S(1)} %get-tuple-element.26), channel_id=1, source_target_pairs={{0,1},{1,0},{2,3},{3,2},{4,5},{5,4},{6,7},{7,6},{8,9},{9,8},{10,11... | collective-permute-start | bytes 1572872 | tf_op jit(solution)/shard_map/ppermute | solution.py:529
  208.2 6.1 %rotate_near.1.near_ref = f32[128,4,8,128]{3,2,1,0:T(8,128)} custom-call(s32[1]{0:T(128)} %bitcast.layer_ref, f32[4,128,512]{2,1,0:T(8,128)S(1)} %inverse.1.v_ref, f32[1024,128]{1,0:T(8,128)} %bitcast.4.refs_0_, f32[3072,128]{1,0:T(8,128)S(1)} %bitcast.26, f32[1024,128]{1,0:T(8,128)} %collective-permute-done.24.refs_0_.refs_2_, ...), custom_call_target="tpu_custom_call" | custom-call | tf_op jit(solution)/shard_map/rotate_near/pallas_call | solution.py:415
  214.4 4.1 %collective-permute-done.28.skip = f32[128,8,128]{2,1,0:T(8,128)S(1)} collective-permute-done((f32[128,8,128]{2,1,0:T(8,128)S(1)}, f32[128,8,128]{2,1,0:T(8,128)S(1)}, u32[]{:S(2)}, u32[]{:S(2)}) %collective-permute-start.28) | collective-permute-done | bytes 524320 | tf_op jit(solution)/shard_map/ppermute | solution.py:527
  218.5 10.4 %collective-permute-done.30.back = f32[128,8,128]{2,1,0:T(8,128)S(1)} collective-permute-done((f32[128,8,128]{2,1,0:T(8,128)S(1)}, f32[128,8,128]{2,1,0:T(8,128)S(1)}, u32[]{:S(2)}, u32[]{:S(2)}) %collective-permute-start.30) | collective-permute-done | bytes 524320 | tf_op jit(solution)/shard_map/ppermute | solution.py:529
  228.9 1.0 join.1
  (50 shorter events, 13.7 us)
Async XLA Ops:
  2.7 33.2 %all-to-all-start = ((f32[8,5,4,8,128]{4,3,2,1,0:T(8,128)}), f32[8,5,4,8,128]{4,3,2,1,0:T(8,128)S(1)}, u32[]{:S(2)}, u32[]{:S(2)}) async-start(f32[8,5,4,8,128]{4,3,2,1,0:T(8,128)} %pad_maximum_fusion), calls=%async_computation | async-start | bytes 1310720 | tf_op jit(solution)/shard_map/all_to_all | solution.py:483
  9.6 13.2 %collective-permute-start.6 = (f32[1,12,4,8,128]{4,3,2,1,0:T(8,128)S(1)}, f32[1,12,4,8,128]{4,3,2,1,0:T(8,128)S(1)}, u32[]{:S(2)}, u32[]{:S(2)}) collective-permute-start(f32[1,12,4,8,128]{4,3,2,1,0:T(8,128)S(1)} %get-tuple-element.27), channel_id=1, source_target_pairs={{0,28},{4,24},{8,20},{12,16},{16,12},{20,8},{24,4},{28,0},{1,29},{... | collective-permute-start | bytes 589832 | tf_op jit(solution)/shard_map/ppermute | solution.py:457
  12.3 13.7 %collective-permute-start.4 = (f32[1,12,4,8,128]{4,3,2,1,0:T(8,128)S(1)}, f32[1,12,4,8,128]{4,3,2,1,0:T(8,128)S(1)}, u32[]{:S(2)}, u32[]{:S(2)}) collective-permute-start(f32[1,12,4,8,128]{4,3,2,1,0:T(8,128)S(1)} %get-tuple-element.28), channel_id=1, source_target_pairs={{0,20},{4,16},{8,28},{12,24},{16,4},{20,0},{24,12},{28,8},{1,21},{... | collective-permute-start | bytes 589832 | tf_op jit(solution)/shard_map/ppermute | solution.py:457
  12.8 17.9 %collective-permute-start.3 = (f32[1,12,4,8,128]{4,3,2,1,0:T(8,128)S(1)}, f32[1,12,4,8,128]{4,3,2,1,0:T(8,128)S(1)}, u32[]{:S(2)}, u32[]{:S(2)}) collective-permute-start(f32[1,12,4,8,128]{4,3,2,1,0:T(8,128)S(1)} %get-tuple-element.29), channel_id=1, source_target_pairs={{0,16},{4,20},{8,24},{12,28},{16,0},{20,4},{24,8},{28,12},{1,17},{... | collective-permute-start | bytes 589832 | tf_op jit(solution)/shard_map/ppermute | solution.py:457
  14.3 16.5 %collective-permute-start.2 = (f32[1,12,4,8,128]{4,3,2,1,0:T(8,128)S(1)}, f32[1,12,4,8,128]{4,3,2,1,0:T(8,128)S(1)}, u32[]{:S(2)}, u32[]{:S(2)}) collective-permute-start(f32[1,12,4,8,128]{4,3,2,1,0:T(8,128)S(1)} %get-tuple-element.30), channel_id=1, source_target_pairs={{0,12},{4,8},{8,4},{12,0},{16,28},{20,24},{24,20},{28,16},{1,13},{... | collective-permute-start | bytes 589832 | tf_op jit(solution)/shard_map/ppermute | solution.py:457
  14.3 17.1 %collective-permute-start.1 = (f32[1,12,4,8,128]{4,3,2,1,0:T(8,128)S(1)}, f32[1,12,4,8,128]{4,3,2,1,0:T(8,128)S(1)}, u32[]{:S(2)}, u32[]{:S(2)}) collective-permute-start(f32[1,12,4,8,128]{4,3,2,1,0:T(8,128)S(1)} %get-tuple-element.31), channel_id=1, source_target_pairs={{0,8},{4,12},{8,0},{12,4},{16,24},{20,28},{24,16},{28,20},{1,9},{5... | collective-permute-start | bytes 589832 | tf_op jit(solution)/shard_map/ppermute | solution.py:457
  22.8 8.6 %collective-permute-start = (f32[1,12,4,8,128]{4,3,2,1,0:T(8,128)S(1)}, f32[1,12,4,8,128]{4,3,2,1,0:T(8,128)S(1)}, u32[]{:S(2)}, u32[]{:S(2)}) collective-permute-start(f32[1,12,4,8,128]{4,3,2,1,0:T(8,128)S(1)} %get-tuple-element.32), channel_id=1, source_target_pairs={{0,4},{4,0},{8,12},{12,8},{16,20},{20,16},{24,28},{28,24},{1,5},{5... | collective-permute-start | bytes 589832 | tf_op jit(solution)/shard_map/ppermute | solution.py:457
  26.0 10.0 %collective-permute-start.5 = (f32[1,12,4,8,128]{4,3,2,1,0:T(8,128)S(1)}, f32[1,12,4,8,128]{4,3,2,1,0:T(8,128)S(1)}, u32[]{:S(2)}, u32[]{:S(2)}) collective-permute-start(f32[1,12,4,8,128]{4,3,2,1,0:T(8,128)S(1)} %get-tuple-element.34), channel_id=1, source_target_pairs={{0,24},{4,28},{8,16},{12,20},{16,8},{20,12},{24,0},{28,4},{1,25},{... | collective-permute-start | bytes 589832 | tf_op jit(solution)/shard_map/ppermute | solution.py:457
  40.6 1.1 copy-start
  41.7 41.6 %all-to-all-start.2 = ((f32[32,12,8,128]{3,2,1,0:T(8,128)}), f32[32,12,8,128]{3,2,1,0:T(8,128)S(1)}, u32[]{:S(2)}, u32[]{:S(2)}) async-start(f32[32,12,8,128]{3,2,1,0:T(8,128)} %bitcast.27), calls=%async_computation.2 | async-start | bytes 3145728 | tf_op jit(solution)/shard_map/all_to_all | solution.py:504
  83.4 19.5 %all-to-all-start.1 = ((f32[32,4,8,128]{3,2,1,0:T(8,128)}), f32[32,4,8,128]{3,2,1,0:T(8,128)}, u32[]{:S(2)}, u32[]{:S(2)}) async-start(f32[32,4,8,128]{3,2,1,0:T(8,128)} %bitcast.3), calls=%async_computation.1 | async-start | bytes 1048576 | tf_op jit(solution)/shard_map/all_to_all | solution.py:504
  87.3 110.2 %collective-permute-start.27 = (f32[3072,128]{1,0:T(8,128)S(1)}, f32[3072,128]{1,0:T(8,128)S(1)}, u32[]{:S(2)}, u32[]{:S(2)}) collective-permute-start(f32[3072,128]{1,0:T(8,128)S(1)} %bitcast.23), channel_id=1, source_target_pairs={{0,0},{1,2},{2,1},{3,3},{4,4},{5,6},{6,5},{7,7},{8,8},{9,10},{10,9... | collective-permute-start | bytes 4718600 | tf_op jit(solution)/shard_map/ppermute | solution.py:516
  88.1 109.4 %collective-permute-start.25 = (f32[3072,128]{1,0:T(8,128)S(1)}, f32[3072,128]{1,0:T(8,128)}, u32[]{:S(2)}, u32[]{:S(2)}) collective-permute-start(f32[3072,128]{1,0:T(8,128)S(1)} %bitcast.24), channel_id=1, source_target_pairs={{0,1},{1,0},{2,3},{3,2},{4,5},{5,4},{6,7},{7,6},{8,9},{9,8},{10,11... | collective-permute-start | bytes 4718600 | tf_op jit(solution)/shard_map/ppermute | solution.py:515
  106.8 1.9 collective-permute-start.7
  106.9 5.2 %collective-permute-start.8 = (f32[10,16,128]{2,1,0:T(8,128)S(1)}, f32[10,16,128]{2,1,0:T(8,128)S(1)}, u32[]{:S(2)}, u32[]{:S(2)}) collective-permute-start(f32[10,16,128]{2,1,0:T(8,128)S(1)} %get-tuple-element.18), channel_id=1, source_target_pairs={{0,8},{4,12},{8,0},{12,4},{16,24},{20,28},{24,16},{28,20},{1,9},{5... | collective-permute-start | bytes 245768 | tf_op jit(solution)/shard_map/ppermute | solution.py:457
  108.4 4.7 %collective-permute-start.9 = (f32[10,16,128]{2,1,0:T(8,128)S(1)}, f32[10,16,128]{2,1,0:T(8,128)S(1)}, u32[]{:S(2)}, u32[]{:S(2)}) collective-permute-start(f32[10,16,128]{2,1,0:T(8,128)S(1)} %get-tuple-element.19), channel_id=1, source_target_pairs={{0,12},{4,8},{8,4},{12,0},{16,28},{20,24},{24,20},{28,16},{1,13},{... | collective-permute-start | bytes 245768 | tf_op jit(solution)/shard_map/ppermute | solution.py:457
  108.8 6.5 %collective-permute-start.10 = (f32[10,16,128]{2,1,0:T(8,128)S(1)}, f32[10,16,128]{2,1,0:T(8,128)S(1)}, u32[]{:S(2)}, u32[]{:S(2)}) collective-permute-start(f32[10,16,128]{2,1,0:T(8,128)S(1)} %get-tuple-element.20), channel_id=1, source_target_pairs={{0,16},{4,20},{8,24},{12,28},{16,0},{20,4},{24,8},{28,12},{1,17},{... | collective-permute-start | bytes 245768 | tf_op jit(solution)/shard_map/ppermute | solution.py:457
  112.1 4.6 %collective-permute-start.11 = (f32[10,16,128]{2,1,0:T(8,128)S(1)}, f32[10,16,128]{2,1,0:T(8,128)S(1)}, u32[]{:S(2)}, u32[]{:S(2)}) collective-permute-start(f32[10,16,128]{2,1,0:T(8,128)S(1)} %get-tuple-element.21), channel_id=1, source_target_pairs={{0,20},{4,16},{8,28},{12,24},{16,4},{20,0},{24,12},{28,8},{1,21},{... | collective-permute-start | bytes 245768 | tf_op jit(solution)/shard_map/ppermute | solution.py:457
  113.1 5.9 %collective-permute-start.12 = (f32[10,16,128]{2,1,0:T(8,128)S(1)}, f32[10,16,128]{2,1,0:T(8,128)S(1)}, u32[]{:S(2)}, u32[]{:S(2)}) collective-permute-start(f32[10,16,128]{2,1,0:T(8,128)S(1)} %get-tuple-element.22), channel_id=1, source_target_pairs={{0,24},{4,28},{8,16},{12,20},{16,8},{20,12},{24,0},{28,4},{1,25},{... | collective-permute-start | bytes 245768 | tf_op jit(solution)/shard_map/ppermute | solution.py:457
  115.3 5.0 %collective-permute-start.13 = (f32[10,16,128]{2,1,0:T(8,128)S(1)}, f32[10,16,128]{2,1,0:T(8,128)S(1)}, u32[]{:S(2)}, u32[]{:S(2)}) collective-permute-start(f32[10,16,128]{2,1,0:T(8,128)S(1)} %get-tuple-element.23), channel_id=1, source_target_pairs={{0,28},{4,24},{8,20},{12,16},{16,12},{20,8},{24,4},{28,0},{1,29},{... | collective-permute-start | bytes 245768 | tf_op jit(solution)/shard_map/ppermute | solution.py:457
  120.3 16.1 %collective-permute-start.16 = (f32[10,16,128]{2,1,0:T(8,128)S(1)}, f32[10,16,128]{2,1,0:T(8,128)S(1)}, u32[]{:S(2)}, u32[]{:S(2)}) collective-permute-start(f32[10,16,128]{2,1,0:T(8,128)S(1)} %add_add_fusion.2), channel_id=1, source_target_pairs={{0,3},{1,2},{2,1},{3,0},{4,7},{5,6},{6,5},{7,4},{8,11},{9,10},{10,... | collective-permute-start | bytes 245768 | tf_op jit(solution)/shard_map/ppermute | solution.py:457
  121.4 21.5 %collective-permute-start.15 = (f32[10,16,128]{2,1,0:T(8,128)S(1)}, f32[10,16,128]{2,1,0:T(8,128)S(1)}, u32[]{:S(2)}, u32[]{:S(2)}) collective-permute-start(f32[10,16,128]{2,1,0:T(8,128)S(1)} %add_add_fusion.2), channel_id=1, source_target_pairs={{0,2},{1,3},{2,0},{3,1},{4,6},{5,7},{6,4},{7,5},{8,10},{9,11},{10,... | collective-permute-start | bytes 245768 | tf_op jit(solution)/shard_map/ppermute | solution.py:457
  123.3 19.5 %collective-permute-start.14 = (f32[10,16,128]{2,1,0:T(8,128)S(1)}, f32[10,16,128]{2,1,0:T(8,128)S(1)}, u32[]{:S(2)}, u32[]{:S(2)}) collective-permute-start(f32[10,16,128]{2,1,0:T(8,128)S(1)} %add_add_fusion.2), channel_id=1, source_target_pairs={{0,1},{1,0},{2,3},{3,2},{4,5},{5,4},{6,7},{7,6},{8,9},{9,8},{10,11... | collective-permute-start | bytes 245768 | tf_op jit(solution)/shard_map/ppermute | solution.py:457
  142.9 7.0 %collective-permute-start.23 = (f32[10,16,128]{2,1,0:T(8,128)S(1)}, f32[10,16,128]{2,1,0:T(8,128)S(1)}, u32[]{:S(2)}, u32[]{:S(2)}) collective-permute-start(f32[10,16,128]{2,1,0:T(8,128)S(1)} %add_add_fusion.1.refs_0_), channel_id=1, source_target_pairs={{0,28},{4,24},{8,20},{12,16},{16,12},{20,8},{24,4},{28,0},{1,29},{... | collective-permute-start | bytes 245768 | tf_op jit(solution)/shard_map/ppermute | solution.py:457
  144.5 52.9 %collective-permute-start.26 = (f32[1024,128]{1,0:T(8,128)}, f32[1024,128]{1,0:T(8,128)}, u32[]{:S(2)}, u32[]{:S(2)}) collective-permute-start(f32[1024,128]{1,0:T(8,128)} %bitcast.4.refs_0_), channel_id=1, source_target_pairs={{0,0},{1,2},{2,1},{3,3},{4,4},{5,6},{6,5},{7,7},{8,8},{9,10},{10,9... | collective-permute-start | bytes 1572872 | tf_op jit(solution)/shard_map/ppermute | solution.py:516
  149.9 47.6 %collective-permute-start.24 = (f32[1024,128]{1,0:T(8,128)}, f32[1024,128]{1,0:T(8,128)}, u32[]{:S(2)}, u32[]{:S(2)}) collective-permute-start(f32[1024,128]{1,0:T(8,128)} %bitcast.4.refs_0_), channel_id=1, source_target_pairs={{0,1},{1,0},{2,3},{3,2},{4,5},{5,4},{6,7},{7,6},{8,9},{9,8},{10,11... | collective-permute-start | bytes 1572872 | tf_op jit(solution)/shard_map/ppermute | solution.py:515
  149.9 6.3 %collective-permute-start.22 = (f32[10,16,128]{2,1,0:T(8,128)S(1)}, f32[10,16,128]{2,1,0:T(8,128)S(1)}, u32[]{:S(2)}, u32[]{:S(2)}) collective-permute-start(f32[10,16,128]{2,1,0:T(8,128)S(1)} %add_add_fusion.1.refs_0_), channel_id=1, source_target_pairs={{0,24},{4,28},{8,16},{12,20},{16,8},{20,12},{24,0},{28,4},{1,25},{... | collective-permute-start | bytes 245768 | tf_op jit(solution)/shard_map/ppermute | solution.py:457
  156.2 4.5 %collective-permute-start.21 = (f32[10,16,128]{2,1,0:T(8,128)S(1)}, f32[10,16,128]{2,1,0:T(8,128)S(1)}, u32[]{:S(2)}, u32[]{:S(2)}) collective-permute-start(f32[10,16,128]{2,1,0:T(8,128)S(1)} %add_add_fusion.1.refs_0_), channel_id=1, source_target_pairs={{0,20},{4,16},{8,28},{12,24},{16,4},{20,0},{24,12},{28,8},{1,21},{... | collective-permute-start | bytes 245768 | tf_op jit(solution)/shard_map/ppermute | solution.py:457
  160.6 4.9 %collective-permute-start.20 = (f32[10,16,128]{2,1,0:T(8,128)S(1)}, f32[10,16,128]{2,1,0:T(8,128)S(1)}, u32[]{:S(2)}, u32[]{:S(2)}) collective-permute-start(f32[10,16,128]{2,1,0:T(8,128)S(1)} %add_add_fusion.1.refs_0_), channel_id=1, source_target_pairs={{0,16},{4,20},{8,24},{12,28},{16,0},{20,4},{24,8},{28,12},{1,17},{... | collective-permute-start | bytes 245768 | tf_op jit(solution)/shard_map/ppermute | solution.py:457
  165.5 4.6 %collective-permute-start.19 = (f32[10,16,128]{2,1,0:T(8,128)S(1)}, f32[10,16,128]{2,1,0:T(8,128)S(1)}, u32[]{:S(2)}, u32[]{:S(2)}) collective-permute-start(f32[10,16,128]{2,1,0:T(8,128)S(1)} %add_add_fusion.1.refs_0_), channel_id=1, source_target_pairs={{0,12},{4,8},{8,4},{12,0},{16,28},{20,24},{24,20},{28,16},{1,13},{... | collective-permute-start | bytes 245768 | tf_op jit(solution)/shard_map/ppermute | solution.py:457
  170.1 0.6 copy-start.1
  170.7 4.4 %collective-permute-start.18 = (f32[10,16,128]{2,1,0:T(8,128)S(1)}, f32[10,16,128]{2,1,0:T(8,128)S(1)}, u32[]{:S(2)}, u32[]{:S(2)}) collective-permute-start(f32[10,16,128]{2,1,0:T(8,128)S(1)} %add_add_fusion.1.refs_0_), channel_id=1, source_target_pairs={{0,8},{4,12},{8,0},{12,4},{16,24},{20,28},{24,16},{28,20},{1,9},{5... | collective-permute-start | bytes 245768 | tf_op jit(solution)/shard_map/ppermute | solution.py:457
  175.1 0.6 copy-start.3
  175.8 1.4 collective-permute-start.17
  177.2 0.9 copy-start.2
  178.1 0.9 copy-start.4
  202.7 15.8 %collective-permute-start.28 = (f32[128,8,128]{2,1,0:T(8,128)S(1)}, f32[128,8,128]{2,1,0:T(8,128)S(1)}, u32[]{:S(2)}, u32[]{:S(2)}) collective-permute-start(f32[128,8,128]{2,1,0:T(8,128)S(1)} %get-tuple-element.24), channel_id=1, source_target_pairs={{0,1},{1,3},{2,0},{3,2},{4,5},{5,7},{6,4},{7,6},{8,9},{9,11},{10,8... | collective-permute-start | bytes 1572872 | tf_op jit(solution)/shard_map/ppermute | solution.py:527
  204.2 14.3 %collective-permute-start.29 = (f32[128,8,128]{2,1,0:T(8,128)S(1)}, f32[128,8,128]{2,1,0:T(8,128)S(1)}, u32[]{:S(2)}, u32[]{:S(2)}) collective-permute-start(f32[128,8,128]{2,1,0:T(8,128)S(1)} %get-tuple-element.25), channel_id=1, source_target_pairs={{0,0},{1,2},{2,1},{3,3},{4,4},{5,6},{6,5},{7,7},{8,8},{9,10},{10,9... | collective-permute-start | bytes 1572872 | tf_op jit(solution)/shard_map/ppermute | solution.py:528
  204.9 24.0 %collective-permute-start.30 = (f32[128,8,128]{2,1,0:T(8,128)S(1)}, f32[128,8,128]{2,1,0:T(8,128)S(1)}, u32[]{:S(2)}, u32[]{:S(2)}) collective-permute-start(f32[128,8,128]{2,1,0:T(8,128)S(1)} %get-tuple-element.26), channel_id=1, source_target_pairs={{0,1},{1,0},{2,3},{3,2},{4,5},{5,4},{6,7},{7,6},{8,9},{9,8},{10,11... | collective-permute-start | bytes 1572872 | tf_op jit(solution)/shard_map/ppermute | solution.py:529

commit v4 on v3

--- a/solution.py
+++ b/solution.py
@@ -92,6 +92,10 @@
                 out_ref[:, g, q + e] = value[g]
 
 
+def in_vmem(value):
+    return pltpu.with_memory_space_constraint(value, pltpu.VMEM)
+
+
 def filter_orbitals(place, parts, with_pot, orbs, xy, z):
     slabs, _, planes, rows, cols = with_pot.shape
     flat = slabs * planes * rows
@@ -103,7 +107,7 @@
         scratch_shapes=[pltpu.VMEM((flat, z.shape[0]), f32), pltpu.VMEM((orbs, flat, cols), f32)],
         compiler_params=small if flat <= 256 else big,
         name="filter",
-    )(place, xy, z, with_pot, *parts)
+    )(place, xy, z, with_pot, *(in_vmem(part) for part in parts))
 
 
 def block_list(count):
@@ -207,21 +211,21 @@
             pivot = spread(cols[j][0], j)
             diag = jnp.where(row == j, pivot, diag)
             inv = pl.reciprocal(pivot, approx=True)
-            inv = inv * (2.0 - pivot * inv)
+            better = 2.0 - pivot * inv
             below = jnp.where(row > j, cols[j][0], 0.0)
             for k in range(j + 1, 8):
                 over = spread(cols[j][0], k)
-                cols[k][0] = cols[k][0] - (below * over) * inv
+                cols[k][0] = cols[k][0] - ((below * over) * inv) * better
                 if t + 1 < groups:
-                    over = over * inv
+                    over = (over * inv) * better
                     for v in range(1, groups - t):
                         cols[k][v] = cols[k][v] - cols[j][v] * over
             for p in (pd, pi):
                 over = spread(p[t], j)
                 if j < 7:
-                    p[t] = p[t] - (below * over) * inv
+                    p[t] = p[t] - ((below * over) * inv) * better
                 if t + 1 < groups:
-                    over = over * inv
+                    over = (over * inv) * better
                     for v in range(1, groups - t):
                         p[t + v] = p[t + v] - cols[j][v] * over
         scale = lax.rsqrt(diag)
@@ -354,37 +358,40 @@
     return jnp.where(lax.rem(layer, 2) == 1, 1, -1)
 
 
-def far_kernel(spec, layer_ref, v_ref, *refs):
+def skip_kernel(spec, layer_ref, v_ref, *refs):
+    *twin, skip, high, low = refs
+    gather_cells(spec, twin, high, low)
+    _, rows, cols = skip.shape
+    layer = layer_ref[0]
+    to = jnp.clip(layer + 2 * twin_side(layer), 0, v_ref.shape[0] - 1)
+    put_rows(skip, product(v_ref[to], high[...], low[...]), rows, cols)
+
+
+def step_kernel(spec, layer_ref, v_ref, *refs):
     chunks = len(spec[3])
     twin, facing = refs[:chunks], refs[chunks : 2 * chunks]
-    skip, step, back, high, low = refs[2 * chunks :]
+    step, back, high, low = refs[2 * chunks :]
     _, rows, cols = step.shape
     layer = layer_ref[0]
     side = twin_side(layer)
-
-    def put(out, to):
+    for out, parts, to in ((step, twin, layer + side), (back, facing, layer - side)):
+        gather_cells(spec, parts, high, low)
         to = jnp.clip(to, 0, v_ref.shape[0] - 1)
         put_rows(out, product(v_ref[to], high[...], low[...]), rows, cols)
 
-    gather_cells(spec, twin, high, low)
-    put(skip, layer + 2 * side)
-    put(step, layer + side)
-    gather_cells(spec, facing, high, low)
-    put(back, layer - side)
-
-
-def rotate_far(layer, v, spec, twin, facing):
+
+def rotate_for_others(kernel, outs, layer, v, spec, parts):
     _, slabs, rows, orbs = spec
-    cols = twin[0].shape[1]
-    return pl.pallas_call(
-        functools.partial(far_kernel, spec),
-        out_shape=[jax.ShapeDtypeStruct((slabs * sum(orbs), rows, cols), f32)] * 3,
-        in_specs=[smem] + [vmem] * (1 + 2 * len(twin)),
-        out_specs=[vmem] * 3,
+    cols = parts[0].shape[1]
+    return pl.pallas_call(
+        functools.partial(kernel, spec),
+        out_shape=[jax.ShapeDtypeStruct((slabs * sum(orbs), rows, cols), f32)] * outs,
+        in_specs=[smem] + [vmem] * (1 + len(parts)),
+        out_specs=[vmem] * outs,
         scratch_shapes=wide_scratch(spec, cols),
         compiler_params=middle,
         name="rotate_far",
-    )(layer, v, *twin, *facing)
+    )(layer, v, *parts)
 
 
 def near_kernel(spec, layer_ref, v_ref, *refs):
@@ -469,7 +476,8 @@
     slabs = lax.axis_size("grid")
     owners = lax.axis_size("orb")
     orbs = local // slabs
-    dealt = (orbs // 4, orbs - orbs // 4) if orbs % 16 == 0 else (orbs,)
+    few = orbs // 16 * 6
+    dealt = (few, orbs - few) if orbs % 16 == 0 else (orbs,)
     everyone = ("orb", "grid")
     nx = slabs * planes
     place = lax.axis_index("grid").astype(jnp.int32).reshape(1)
@@ -523,7 +531,8 @@
         back = lax.all_to_all(rotated, "orb", split_axis=0, concat_axis=0, tiled=True)
         return jnp.swapaxes(back, 0, 1).reshape(local, planes, rows, cols)
     layer = lax.axis_index("orb").astype(jnp.int32).reshape(1)
-    skip, step, back = rotate_far(layer, inverse, spec, twin, facing)
+    (skip,) = rotate_for_others(skip_kernel, 1, layer, inverse, spec, twin)
+    step, back = rotate_for_others(step_kernel, 2, layer, inverse, spec, twin + facing)
     skip = lax.ppermute(skip, "orb", [(0, 1), (1, 3), (2, 0), (3, 2)])
     step = lax.ppermute(step, "orb", [(0, 0), (1, 2), (2, 1), (3, 3)])
     back = lax.ppermute(back, "orb", [(0, 1), (1, 0), (2, 3), (3, 2)])

time: 231 us -> 231 us (level)
  blocking collectives: 0 us -> 37 us
  waiting for transfers between devices: 125 us -> 95.9 us
  starting transfers between devices: 53 us -> 40.7 us
  local copies, waits for them, and re-layouts: 7.63 us -> 11.8 us
    all_to_all x2 -> x1, waiting for transfers between devices: 45.4 us -> 0.01 us  [orthonormalized(): lax.all_to_all(filtered, everyone, split_axis=0, concat_axis=0, tiled=True)]
    all_to_all x0 -> x1, blocking collectives: none -> 37 us  [orthonormalized(): lax.all_to_all(filtered, everyone, split_axis=0, concat_axis=0, tiled=True)]
    all_to_all x1, waiting for transfers between devices: 0.01 us -> 12.9 us  [orthonormalized(): lax.all_to_all(first, 'grid', split_axis=0, concat_axis=0, tiled=True)]
    ppermute x1, waiting for transfers between devices: 4.13 us -> 11.1 us  [orthonormalized(): skip = lax.ppermute(skip, 'orb', [(0, 1), (1, 3), (2, 0), (3, 2)])]
    ppermute x1, waiting for transfers between devices: 10.4 us -> 3.6 us  [orthonormalized(): back = lax.ppermute(back, 'orb', [(0, 1), (1, 0), (2, 3), (3, 2)])]
    unnamed x10 -> x24, local copies, waits for them, and re-layouts: 4.19 us -> 9.1 us
    all_to_all x2 -> x1, starting transfers between devices: 7.9 us -> 4.01 us  [orthonormalized(): lax.all_to_all(filtered, everyone, split_axis=0, concat_axis=0, tiled=True)]
    ppermute x24, waiting for transfers between devices: 65 us -> 68.3 us  [swap_all(): lax.ppermute(pieces[s], axis, [(i, i ^ s) for i in range(count)])]
  transfers between devices with their start and end apart: 34 -> 33, of which waited for: 22 -> 21; matrix products, arithmetic and copies ran while one was open for 1% -> 1% of each run, Pallas kernels for 14% -> 13%
where the time goes in v4:
time: 231 us
  waiting for transfers between devices  95.9 us (42%)
  Pallas kernels  42.8 us (19%)
  starting transfers between devices  40.7 us (18%)
  blocking collectives  37 us (16%)
  local copies, waits for them, and re-layouts  11.8 us (5%)
    ppermute x24, waiting for transfers between devices, swap_all(): lax.ppermute(pieces[s], axis, [(i, i ^ s) for i in range(count)])  68.3 us
    all_to_all x1, blocking collectives, orthonormalized(): lax.all_to_all(filtered, everyone, split_axis=0, concat_axis=0, tiled=True)  37 us
    ppermute x24, starting transfers between devices, swap_all(): lax.ppermute(pieces[s], axis, [(i, i ^ s) for i in range(count)])  21.6 us
    pallas_call x1, Pallas kernels, inverse_rows(): pl.pallas_call(functools.partial(inverse_kernel, factor), out_shape=jax.S...  18.1 us
    all_to_all x1, waiting for transfers between devices, orthonormalized(): lax.all_to_all(first, 'grid', split_axis=0, concat_axis=0, tiled=True)  12.9 us
    ppermute x1, waiting for transfers between devices, orthonormalized(): skip = lax.ppermute(skip, 'orb', [(0, 1), (1, 3), (2, 0), (3, 2)])  11.1 us
    unnamed x24, local copies, waits for them, and re-layouts  9.1 us
    pallas_call x2, Pallas kernels, rotate_for_others(): pl.pallas_call(functools.partial(kernel, spec), out_shape=[jax.ShapeDtype...  7.46 us
  transfers between devices with their start and end apart: 33, of which 21 were waited for; matrix products, arithmetic and copies ran while one was open for 1% of the time, Pallas kernels for 13%

profile of v4, /device:TPU:0, one launch (start us, length us, event | category | flops | bytes accessed | tf_op | source)
XLA Modules:
  0.0 230.7 jit_solution(8972976318594150210)
XLA Ops:
  1.1 1.0 pad_maximum_fusion
  2.2 5.2 %all-to-all-start = ((f32[8,7,4,8,128]{4,3,2,1,0:T(8,128)}), f32[8,7,4,8,128]{4,3,2,1,0:T(8,128)S(1)}, u32[]{:S(2)}, u32[]{:S(2)}) async-start(f32[8,7,4,8,128]{4,3,2,1,0:T(8,128)} %pad_maximum_fusion), calls=%async_computation | async-start | bytes 1835008 | tf_op jit(solution)/shard_map/all_to_all | solution.py:491
  8.5 12.9 %all-to-all-done.pot_ref.refs_0_ = f32[8,7,4,8,128]{4,3,2,1,0:T(8,128)S(1)} async-done(((f32[8,7,4,8,128]{4,3,2,1,0:T(8,128)}), f32[8,7,4,8,128]{4,3,2,1,0:T(8,128)S(1)}, u32[]{:S(2)}, u32[]{:S(2)}) %all-to-all-start) | async-done | bytes 917536 | tf_op jit(solution)/shard_map/all_to_all | solution.py:491
  21.3 3.3 %filter.2 = f32[4,8,6,8,128]{4,3,2,1,0:T(8,128)} custom-call(s32[1]{0:T(128)} %bitcast.1.place_ref, bf16[256,256]{1,0:T(8,128)(2,1)S(1)} %fusion.6.xy_ref, bf16[256,256]{1,0:T(8,128)(2,1)S(1)} %select_convert_fusion.z_ref, f32[8,7,4,8,128]{4,3,2,1,0:T(8,128)S(1)} %all-to-all-done.pot_ref.refs_0_, f32[8,7,4,8,128]{4,3,2,1,0:T(8,128)S(1)} %all-to-all-done.pot_ref.refs_0_), custom_call_target="tpu_custom_call" | custom-call | tf_op jit(solution)/shard_map/filter/pallas_call | solution.py:102
  24.7 4.0 %all-to-all-start.1 = ((f32[32,6,8,128]{3,2,1,0:T(8,128)}), f32[32,6,8,128]{3,2,1,0:T(8,128)S(1)}, u32[]{:S(2)}, u32[]{:S(2)}) async-start(f32[32,6,8,128]{3,2,1,0:T(8,128)} %bitcast.3), calls=%async_computation.1 | async-start | bytes 1572864 | tf_op jit(solution)/shard_map/all_to_all | solution.py:512
  28.7 1.6 dynamic-slice_bitcast_fusion
  30.3 2.5 %collective-permute-start.6 = (f32[1,10,4,8,128]{4,3,2,1,0:T(8,128)S(1)}, f32[1,10,4,8,128]{4,3,2,1,0:T(8,128)S(1)}, u32[]{:S(2)}, u32[]{:S(2)}) collective-permute-start(f32[1,10,4,8,128]{4,3,2,1,0:T(8,128)S(1)} %get-tuple-element.25), channel_id=1, source_target_pairs={{0,28},{4,24},{8,20},{12,16},{16,12},{20,8},{24,4},{28,0},{1,29},{... | collective-permute-start | bytes 491528 | tf_op jit(solution)/shard_map/ppermute | solution.py:464
  33.3 1.5 collective-permute-start.3
  34.8 1.5 collective-permute-start.1
  36.2 6.1 %collective-permute-done.6.refs_7_ = f32[1,10,4,8,128]{4,3,2,1,0:T(8,128)S(1)} collective-permute-done((f32[1,10,4,8,128]{4,3,2,1,0:T(8,128)S(1)}, f32[1,10,4,8,128]{4,3,2,1,0:T(8,128)S(1)}, u32[]{:S(2)}, u32[]{:S(2)}) %collective-permute-start.6) | collective-permute-done | bytes 163872 | tf_op jit(solution)/shard_map/ppermute | solution.py:464
  42.3 1.4 collective-permute-start
  43.7 2.4 %collective-permute-done.4.refs_5_ = f32[1,10,4,8,128]{4,3,2,1,0:T(8,128)S(1)} collective-permute-done((f32[1,10,4,8,128]{4,3,2,1,0:T(8,128)S(1)}, f32[1,10,4,8,128]{4,3,2,1,0:T(8,128)S(1)}, u32[]{:S(2)}, u32[]{:S(2)}) %collective-permute-start.4) | collective-permute-done | bytes 163872 | tf_op jit(solution)/shard_map/ppermute | solution.py:464
  46.9 4.1 %collective-permute-done.3.refs_4_ = f32[1,10,4,8,128]{4,3,2,1,0:T(8,128)S(1)} collective-permute-done((f32[1,10,4,8,128]{4,3,2,1,0:T(8,128)S(1)}, f32[1,10,4,8,128]{4,3,2,1,0:T(8,128)S(1)}, u32[]{:S(2)}, u32[]{:S(2)}) %collective-permute-start.3) | collective-permute-done | bytes 163872 | tf_op jit(solution)/shard_map/ppermute | solution.py:464
  51.0 4.1 %collective-permute-done.5.refs_6_ = f32[1,10,4,8,128]{4,3,2,1,0:T(8,128)S(1)} collective-permute-done((f32[1,10,4,8,128]{4,3,2,1,0:T(8,128)S(1)}, f32[1,10,4,8,128]{4,3,2,1,0:T(8,128)S(1)}, u32[]{:S(2)}, u32[]{:S(2)}) %collective-permute-start.5) | collective-permute-done | bytes 163872 | tf_op jit(solution)/shard_map/ppermute | solution.py:464
  55.2 3.9 %filter.3 = f32[4,8,10,8,128]{4,3,2,1,0:T(8,128)S(1)} custom-call(s32[1]{0:T(128)} %bitcast.1.place_ref, bf16[256,256]{1,0:T(8,128)(2,1)S(1)} %fusion.6.xy_ref, bf16[256,256]{1,0:T(8,128)(2,1)S(1)} %select_convert_fusion.z_ref, f32[8,7,4,8,128]{4,3,2,1,0:T(8,128)S(1)} %all-to-all-done.pot_ref.refs_0_, f32[1,10,4,8,128]{4,3,2,1,0:T(8,128)S(1)} %get-tuple-element.31.refs_0_, ...), custom_call_target="tpu_custom_call" | custom-call | tf_op jit(solution)/shard_map/filter/pallas_call | solution.py:102
  59.0 37.0 %all_to_all.15 = f32[32,10,8,128]{3,2,1,0:T(8,128)S(1)} all-to-all(f32[32,10,8,128]{3,2,1,0:T(8,128)S(1)} %bitcast.31), channel_id=1, replica_groups=mesh['grid'=8,'orb'=4] {'orb','grid'}, dimensions={0} | all-to-all | bytes 2621440 | tf_op jit(solution)/shard_map/all_to_all | solution.py:512
  96.1 2.9 %margin.1 = (f32[10,16,128]{2,1,0:T(8,128)S(1)}, f32[10,16,128]{2,1,0:T(8,128)S(1)}, f32[10,16,128]{2,1,0:T(8,128)S(1)}, f32[10,16,128]{2,1,0:T(8,128)S(1)}, f32...) custom-call(s32[1]{0:T(128)} %bitcast.1.place_ref, ...), custom_call_target="tpu_custom_call" | custom-call | tf_op jit(solution)/shard_map/margin/pallas_call | solution.py:177
  99.0 1.8 collective-permute-start.28
  100.8 1.4 collective-permute-start.25
  103.9 3.5 %collective-permute-done.8 = f32[10,16,128]{2,1,0:T(8,128)S(1)} collective-permute-done((f32[10,16,128]{2,1,0:T(8,128)S(1)}, f32[10,16,128]{2,1,0:T(8,128)S(1)}, u32[]{:S(2)}, u32[]{:S(2)}) %collective-permute-start.8) | collective-permute-done | bytes 81952 | tf_op jit(solution)/shard_map/ppermute | solution.py:464
  107.6 1.3 collective-permute-start.12
  108.9 1.9 collective-permute-start.13
  111.3 2.5 %collective-permute-done.12 = f32[10,16,128]{2,1,0:T(8,128)S(1)} collective-permute-done((f32[10,16,128]{2,1,0:T(8,128)S(1)}, f32[10,16,128]{2,1,0:T(8,128)S(1)}, u32[]{:S(2)}, u32[]{:S(2)}) %collective-permute-start.12) | collective-permute-done | bytes 81952 | tf_op jit(solution)/shard_map/ppermute | solution.py:464
  113.8 1.6 collective-permute-done.13
  115.5 2.6 %collective-permute-start.16 = (f32[10,16,128]{2,1,0:T(8,128)S(1)}, f32[10,16,128]{2,1,0:T(8,128)S(1)}, u32[]{:S(2)}, u32[]{:S(2)}) collective-permute-start(f32[10,16,128]{2,1,0:T(8,128)S(1)} %add_add_fusion.2), channel_id=1, source_target_pairs={{0,3},{1,2},{2,1},{3,0},{4,7},{5,6},{6,5},{7,4},{8,11},{9,10},{10,... | collective-permute-start | bytes 245768 | tf_op jit(solution)/shard_map/ppermute | solution.py:464
  118.1 1.9 collective-permute-start.14
  120.0 16.2 %collective-permute-done.16 = f32[10,16,128]{2,1,0:T(8,128)S(1)} collective-permute-done((f32[10,16,128]{2,1,0:T(8,128)S(1)}, f32[10,16,128]{2,1,0:T(8,128)S(1)}, u32[]{:S(2)}, u32[]{:S(2)}) %collective-permute-start.16) | collective-permute-done | bytes 81952 | tf_op jit(solution)/shard_map/ppermute | solution.py:464
  136.2 1.5 collective-permute-start.27
  137.7 2.0 collective-permute-done.15
  139.7 1.5 collective-permute-start.24
  141.3 4.8 %collective-permute-done.23.refs_7_ = f32[10,16,128]{2,1,0:T(8,128)S(1)} collective-permute-done((f32[10,16,128]{2,1,0:T(8,128)S(1)}, f32[10,16,128]{2,1,0:T(8,128)S(1)}, u32[]{:S(2)}, u32[]{:S(2)}) %collective-permute-start.23) | collective-permute-done | bytes 81952 | tf_op jit(solution)/shard_map/ppermute | solution.py:464
  146.7 1.5 collective-permute-start.22
  148.2 3.9 %collective-permute-done.22.refs_6_ = f32[10,16,128]{2,1,0:T(8,128)S(1)} collective-permute-done((f32[10,16,128]{2,1,0:T(8,128)S(1)}, f32[10,16,128]{2,1,0:T(8,128)S(1)}, u32[]{:S(2)}, u32[]{:S(2)}) %collective-permute-start.22) | collective-permute-done | bytes 81952 | tf_op jit(solution)/shard_map/ppermute | solution.py:464
  152.7 4.0 %collective-permute-done.21.refs_5_ = f32[10,16,128]{2,1,0:T(8,128)S(1)} collective-permute-done((f32[10,16,128]{2,1,0:T(8,128)S(1)}, f32[10,16,128]{2,1,0:T(8,128)S(1)}, u32[]{:S(2)}, u32[]{:S(2)}) %collective-permute-start.21) | collective-permute-done | bytes 81952 | tf_op jit(solution)/shard_map/ppermute | solution.py:464
  157.2 1.4 collective-permute-start.20
  158.6 3.1 %collective-permute-done.20.refs_4_ = f32[10,16,128]{2,1,0:T(8,128)S(1)} collective-permute-done((f32[10,16,128]{2,1,0:T(8,128)S(1)}, f32[10,16,128]{2,1,0:T(8,128)S(1)}, u32[]{:S(2)}, u32[]{:S(2)}) %collective-permute-start.20) | collective-permute-done | bytes 81952 | tf_op jit(solution)/shard_map/ppermute | solution.py:464
  162.6 4.4 %collective-permute-done.19.refs_3_ = f32[10,16,128]{2,1,0:T(8,128)S(1)} collective-permute-done((f32[10,16,128]{2,1,0:T(8,128)S(1)}, f32[10,16,128]{2,1,0:T(8,128)S(1)}, u32[]{:S(2)}, u32[]{:S(2)}) %collective-permute-start.19) | collective-permute-done | bytes 81952 | tf_op jit(solution)/shard_map/ppermute | solution.py:464
  167.7 0.9 collective-permute-start.18
  168.6 3.5 %collective-permute-done.18.refs_2_ = f32[10,16,128]{2,1,0:T(8,128)S(1)} collective-permute-done((f32[10,16,128]{2,1,0:T(8,128)S(1)}, f32[10,16,128]{2,1,0:T(8,128)S(1)}, u32[]{:S(2)}, u32[]{:S(2)}) %collective-permute-start.18) | collective-permute-done | bytes 81952 | tf_op jit(solution)/shard_map/ppermute | solution.py:464
  172.7 1.4 collective-permute-done.17.refs_1_
  179.5 18.1 %inverse.1.v_ref = f32[4,128,512]{2,1,0:T(8,128)S(1)} custom-call(s32[1]{0:T(128)} %bitcast.1.place_ref, f32[10,16,128]{2,1,0:T(8,128)S(1)} %add_add_fusion.1.refs_0_, f32[10,16,128]{2,1,0:T(8,128)} %collective-permute-done.17.refs_1_, f32[10,16,128]{2,1,0:T(8,128)S(1)} %copy-done.11, f32[10,16,128]{2,1,0:T(8,128)S(1)} %copy-done.9, ...), custom_call_target="tpu_custom_call" | custom-call | tf_op jit(solution)/shard_map/inverse/pallas_call | solution.py:308
  197.7 4.8 %rotate_far.3 = (f32[128,8,128]{2,1,0:T(8,128)S(1)}, f32[128,8,128]{2,1,0:T(8,128)S(1)}) custom-call(s32[1]{0:T(128)} %bitcast.layer_ref, f32[4,128,512]{2,1,0:T(8,128)S(1)} %inverse.1.v_ref, f32[1536,128]{1,0:T(8,128)} %collective-permute-done.24.refs_0_.refs_2_, f32[2560,128]{1,0:T(8,128)S(1)} %collective-permute-done.25.refs_1_.refs_3_, ...), custom_call_target="tpu_custom_call" | custom-call | tf_op jit(solution)/shard_map/rotate_far/pallas_call | solution.py:386
  203.2 2.9 %collective-permute-start.30 = (f32[128,8,128]{2,1,0:T(8,128)S(1)}, f32[128,8,128]{2,1,0:T(8,128)S(1)}, u32[]{:S(2)}, u32[]{:S(2)}) collective-permute-start(f32[128,8,128]{2,1,0:T(8,128)S(1)} %get-tuple-element.24), channel_id=1, source_target_pairs={{0,1},{1,0},{2,3},{3,2},{4,5},{5,4},{6,7},{7,6},{8,9},{9,8},{10,11... | collective-permute-start | bytes 1572872 | tf_op jit(solution)/shard_map/ppermute | solution.py:538
  206.0 2.6 %rotate_far.2 = f32[128,8,128]{2,1,0:T(8,128)S(1)} custom-call(s32[1]{0:T(128)} %bitcast.layer_ref, f32[4,128,512]{2,1,0:T(8,128)S(1)} %inverse.1.v_ref, f32[1536,128]{1,0:T(8,128)} %collective-permute-done.24.refs_0_.refs_2_, f32[2560,128]{1,0:T(8,128)S(1)} %collective-permute-done.25.refs_1_.refs_3_), custom_call_target="tpu_custom_call" | custom-call | tf_op jit(solution)/shard_map/rotate_far/pallas_call | solution.py:386
  208.8 6.1 %rotate_near.1.near_ref = f32[128,4,8,128]{3,2,1,0:T(8,128)} custom-call(s32[1]{0:T(128)} %bitcast.layer_ref, f32[4,128,512]{2,1,0:T(8,128)S(1)} %inverse.1.v_ref, f32[1536,128]{1,0:T(8,128)S(1)} %bitcast.30, f32[2560,128]{1,0:T(8,128)S(1)} %bitcast.26, f32[1536,128]{1,0:T(8,128)} %collective-permute-done.24.refs_0_.refs_2_, ...), custom_call_target="tpu_custom_call" | custom-call | tf_op jit(solution)/shard_map/rotate_near/pallas_call | solution.py:422
  214.9 3.6 %collective-permute-done.30.back = f32[128,8,128]{2,1,0:T(8,128)S(1)} collective-permute-done((f32[128,8,128]{2,1,0:T(8,128)S(1)}, f32[128,8,128]{2,1,0:T(8,128)S(1)}, u32[]{:S(2)}, u32[]{:S(2)}) %collective-permute-start.30) | collective-permute-done | bytes 524320 | tf_op jit(solution)/shard_map/ppermute | solution.py:538
  218.5 11.1 %collective-permute-done.26.skip = f32[128,8,128]{2,1,0:T(8,128)S(1)} collective-permute-done((f32[128,8,128]{2,1,0:T(8,128)S(1)}, f32[128,8,128]{2,1,0:T(8,128)S(1)}, u32[]{:S(2)}, u32[]{:S(2)}) %collective-permute-start.26) | collective-permute-done | bytes 524320 | tf_op jit(solution)/shard_map/ppermute | solution.py:536
  229.6 1.0 join.1
  (65 shorter events, 16.4 us)
Async XLA Ops:
  0.0 1.1 slice-start
  2.2 19.2 %all-to-all-start = ((f32[8,7,4,8,128]{4,3,2,1,0:T(8,128)}), f32[8,7,4,8,128]{4,3,2,1,0:T(8,128)S(1)}, u32[]{:S(2)}, u32[]{:S(2)}) async-start(f32[8,7,4,8,128]{4,3,2,1,0:T(8,128)} %pad_maximum_fusion), calls=%async_computation | async-start | bytes 1835008 | tf_op jit(solution)/shard_map/all_to_all | solution.py:491
  24.7 34.4 %all-to-all-start.1 = ((f32[32,6,8,128]{3,2,1,0:T(8,128)}), f32[32,6,8,128]{3,2,1,0:T(8,128)S(1)}, u32[]{:S(2)}, u32[]{:S(2)}) async-start(f32[32,6,8,128]{3,2,1,0:T(8,128)} %bitcast.3), calls=%async_computation.1 | async-start | bytes 1572864 | tf_op jit(solution)/shard_map/all_to_all | solution.py:512
  30.3 12.0 %collective-permute-start.6 = (f32[1,10,4,8,128]{4,3,2,1,0:T(8,128)S(1)}, f32[1,10,4,8,128]{4,3,2,1,0:T(8,128)S(1)}, u32[]{:S(2)}, u32[]{:S(2)}) collective-permute-start(f32[1,10,4,8,128]{4,3,2,1,0:T(8,128)S(1)} %get-tuple-element.25), channel_id=1, source_target_pairs={{0,28},{4,24},{8,20},{12,16},{16,12},{20,8},{24,4},{28,0},{1,29},{... | collective-permute-start | bytes 491528 | tf_op jit(solution)/shard_map/ppermute | solution.py:464
  32.7 13.4 %collective-permute-start.4 = (f32[1,10,4,8,128]{4,3,2,1,0:T(8,128)S(1)}, f32[1,10,4,8,128]{4,3,2,1,0:T(8,128)S(1)}, u32[]{:S(2)}, u32[]{:S(2)}) collective-permute-start(f32[1,10,4,8,128]{4,3,2,1,0:T(8,128)S(1)} %get-tuple-element.26), channel_id=1, source_target_pairs={{0,20},{4,16},{8,28},{12,24},{16,4},{20,0},{24,12},{28,8},{1,21},{... | collective-permute-start | bytes 491528 | tf_op jit(solution)/shard_map/ppermute | solution.py:464
  33.3 17.7 %collective-permute-start.3 = (f32[1,10,4,8,128]{4,3,2,1,0:T(8,128)S(1)}, f32[1,10,4,8,128]{4,3,2,1,0:T(8,128)S(1)}, u32[]{:S(2)}, u32[]{:S(2)}) collective-permute-start(f32[1,10,4,8,128]{4,3,2,1,0:T(8,128)S(1)} %get-tuple-element.27), channel_id=1, source_target_pairs={{0,16},{4,20},{8,24},{12,28},{16,0},{20,4},{24,8},{28,12},{1,17},{... | collective-permute-start | bytes 491528 | tf_op jit(solution)/shard_map/ppermute | solution.py:464
  34.8 16.3 %collective-permute-start.2 = (f32[1,10,4,8,128]{4,3,2,1,0:T(8,128)S(1)}, f32[1,10,4,8,128]{4,3,2,1,0:T(8,128)S(1)}, u32[]{:S(2)}, u32[]{:S(2)}) collective-permute-start(f32[1,10,4,8,128]{4,3,2,1,0:T(8,128)S(1)} %get-tuple-element.28), channel_id=1, source_target_pairs={{0,12},{4,8},{8,4},{12,0},{16,28},{20,24},{24,20},{28,16},{1,13},{... | collective-permute-start | bytes 491528 | tf_op jit(solution)/shard_map/ppermute | solution.py:464
  34.8 16.3 %collective-permute-start.1 = (f32[1,10,4,8,128]{4,3,2,1,0:T(8,128)S(1)}, f32[1,10,4,8,128]{4,3,2,1,0:T(8,128)S(1)}, u32[]{:S(2)}, u32[]{:S(2)}) collective-permute-start(f32[1,10,4,8,128]{4,3,2,1,0:T(8,128)S(1)} %get-tuple-element.29), channel_id=1, source_target_pairs={{0,8},{4,12},{8,0},{12,4},{16,24},{20,28},{24,16},{28,20},{1,9},{5... | collective-permute-start | bytes 491528 | tf_op jit(solution)/shard_map/ppermute | solution.py:464
  42.3 8.7 %collective-permute-start = (f32[1,10,4,8,128]{4,3,2,1,0:T(8,128)S(1)}, f32[1,10,4,8,128]{4,3,2,1,0:T(8,128)S(1)}, u32[]{:S(2)}, u32[]{:S(2)}) collective-permute-start(f32[1,10,4,8,128]{4,3,2,1,0:T(8,128)S(1)} %get-tuple-element.30), channel_id=1, source_target_pairs={{0,4},{4,0},{8,12},{12,8},{16,20},{20,16},{24,28},{28,24},{1,5},{5... | collective-permute-start | bytes 491528 | tf_op jit(solution)/shard_map/ppermute | solution.py:464
  46.1 9.1 %collective-permute-start.5 = (f32[1,10,4,8,128]{4,3,2,1,0:T(8,128)S(1)}, f32[1,10,4,8,128]{4,3,2,1,0:T(8,128)S(1)}, u32[]{:S(2)}, u32[]{:S(2)}) collective-permute-start(f32[1,10,4,8,128]{4,3,2,1,0:T(8,128)S(1)} %get-tuple-element.32), channel_id=1, source_target_pairs={{0,24},{4,28},{8,16},{12,20},{16,8},{20,12},{24,0},{28,4},{1,25},{... | collective-permute-start | bytes 491528 | tf_op jit(solution)/shard_map/ppermute | solution.py:464
  99.0 4.4 %collective-permute-start.7 = (f32[10,16,128]{2,1,0:T(8,128)S(1)}, f32[10,16,128]{2,1,0:T(8,128)S(1)}, u32[]{:S(2)}, u32[]{:S(2)}) collective-permute-start(f32[10,16,128]{2,1,0:T(8,128)S(1)} %get-tuple-element.16), channel_id=1, source_target_pairs={{0,4},{4,0},{8,12},{12,8},{16,20},{20,16},{24,28},{28,24},{1,5},{5... | collective-permute-start | bytes 245768 | tf_op jit(solution)/shard_map/ppermute | solution.py:464
  99.0 98.6 %collective-permute-start.28 = (f32[2560,128]{1,0:T(8,128)S(1)}, f32[2560,128]{1,0:T(8,128)}, u32[]{:S(2)}, u32[]{:S(2)}) collective-permute-start(f32[2560,128]{1,0:T(8,128)S(1)} %bitcast.24), channel_id=1, source_target_pairs={{0,0},{1,2},{2,1},{3,3},{4,4},{5,6},{6,5},{7,7},{8,8},{9,10},{10,9... | collective-permute-start | bytes 3932168 | tf_op jit(solution)/shard_map/ppermute | solution.py:524
  100.8 96.8 %collective-permute-start.25 = (f32[2560,128]{1,0:T(8,128)S(1)}, f32[2560,128]{1,0:T(8,128)S(1)}, u32[]{:S(2)}, u32[]{:S(2)}) collective-permute-start(f32[2560,128]{1,0:T(8,128)S(1)} %bitcast.25), channel_id=1, source_target_pairs={{0,1},{1,0},{2,3},{3,2},{4,5},{5,4},{6,7},{7,6},{8,9},{9,8},{10,11... | collective-permute-start | bytes 3932168 | tf_op jit(solution)/shard_map/ppermute | solution.py:523
  102.2 5.2 %collective-permute-start.8 = (f32[10,16,128]{2,1,0:T(8,128)S(1)}, f32[10,16,128]{2,1,0:T(8,128)S(1)}, u32[]{:S(2)}, u32[]{:S(2)}) collective-permute-start(f32[10,16,128]{2,1,0:T(8,128)S(1)} %get-tuple-element.17), channel_id=1, source_target_pairs={{0,8},{4,12},{8,0},{12,4},{16,24},{20,28},{24,16},{28,20},{1,9},{5... | collective-permute-start | bytes 245768 | tf_op jit(solution)/shard_map/ppermute | solution.py:464
  102.9 4.7 %collective-permute-start.9 = (f32[10,16,128]{2,1,0:T(8,128)S(1)}, f32[10,16,128]{2,1,0:T(8,128)S(1)}, u32[]{:S(2)}, u32[]{:S(2)}) collective-permute-start(f32[10,16,128]{2,1,0:T(8,128)S(1)} %get-tuple-element.18), channel_id=1, source_target_pairs={{0,12},{4,8},{8,4},{12,0},{16,28},{20,24},{24,20},{28,16},{1,13},{... | collective-permute-start | bytes 245768 | tf_op jit(solution)/shard_map/ppermute | solution.py:464
  103.3 5.5 %collective-permute-start.10 = (f32[10,16,128]{2,1,0:T(8,128)S(1)}, f32[10,16,128]{2,1,0:T(8,128)S(1)}, u32[]{:S(2)}, u32[]{:S(2)}) collective-permute-start(f32[10,16,128]{2,1,0:T(8,128)S(1)} %get-tuple-element.19), channel_id=1, source_target_pairs={{0,16},{4,20},{8,24},{12,28},{16,0},{20,4},{24,8},{28,12},{1,17},{... | collective-permute-start | bytes 245768 | tf_op jit(solution)/shard_map/ppermute | solution.py:464
  107.4 3.9 %collective-permute-start.11 = (f32[10,16,128]{2,1,0:T(8,128)S(1)}, f32[10,16,128]{2,1,0:T(8,128)S(1)}, u32[]{:S(2)}, u32[]{:S(2)}) collective-permute-start(f32[10,16,128]{2,1,0:T(8,128)S(1)} %get-tuple-element.20), channel_id=1, source_target_pairs={{0,20},{4,16},{8,28},{12,24},{16,4},{20,0},{24,12},{28,8},{1,21},{... | collective-permute-start | bytes 245768 | tf_op jit(solution)/shard_map/ppermute | solution.py:464
  107.6 6.2 %collective-permute-start.12 = (f32[10,16,128]{2,1,0:T(8,128)S(1)}, f32[10,16,128]{2,1,0:T(8,128)S(1)}, u32[]{:S(2)}, u32[]{:S(2)}) collective-permute-start(f32[10,16,128]{2,1,0:T(8,128)S(1)} %get-tuple-element.21), channel_id=1, source_target_pairs={{0,24},{4,28},{8,16},{12,20},{16,8},{20,12},{24,0},{28,4},{1,25},{... | collective-permute-start | bytes 245768 | tf_op jit(solution)/shard_map/ppermute | solution.py:464
  108.9 6.6 %collective-permute-start.13 = (f32[10,16,128]{2,1,0:T(8,128)S(1)}, f32[10,16,128]{2,1,0:T(8,128)S(1)}, u32[]{:S(2)}, u32[]{:S(2)}) collective-permute-start(f32[10,16,128]{2,1,0:T(8,128)S(1)} %get-tuple-element.22), channel_id=1, source_target_pairs={{0,28},{4,24},{8,20},{12,16},{16,12},{20,8},{24,4},{28,0},{1,29},{... | collective-permute-start | bytes 245768 | tf_op jit(solution)/shard_map/ppermute | solution.py:464
  115.5 20.7 %collective-permute-start.16 = (f32[10,16,128]{2,1,0:T(8,128)S(1)}, f32[10,16,128]{2,1,0:T(8,128)S(1)}, u32[]{:S(2)}, u32[]{:S(2)}) collective-permute-start(f32[10,16,128]{2,1,0:T(8,128)S(1)} %add_add_fusion.2), channel_id=1, source_target_pairs={{0,3},{1,2},{2,1},{3,0},{4,7},{5,6},{6,5},{7,4},{8,11},{9,10},{10,... | collective-permute-start | bytes 245768 | tf_op jit(solution)/shard_map/ppermute | solution.py:464
  118.1 21.6 %collective-permute-start.15 = (f32[10,16,128]{2,1,0:T(8,128)S(1)}, f32[10,16,128]{2,1,0:T(8,128)S(1)}, u32[]{:S(2)}, u32[]{:S(2)}) collective-permute-start(f32[10,16,128]{2,1,0:T(8,128)S(1)} %add_add_fusion.2), channel_id=1, source_target_pairs={{0,2},{1,3},{2,0},{3,1},{4,6},{5,7},{6,4},{7,5},{8,10},{9,11},{10,... | collective-permute-start | bytes 245768 | tf_op jit(solution)/shard_map/ppermute | solution.py:464
  118.1 23.1 %collective-permute-start.14 = (f32[10,16,128]{2,1,0:T(8,128)S(1)}, f32[10,16,128]{2,1,0:T(8,128)S(1)}, u32[]{:S(2)}, u32[]{:S(2)}) collective-permute-start(f32[10,16,128]{2,1,0:T(8,128)S(1)} %add_add_fusion.2), channel_id=1, source_target_pairs={{0,1},{1,0},{2,3},{3,2},{4,5},{5,4},{6,7},{7,6},{8,9},{9,8},{10,11... | collective-permute-start | bytes 245768 | tf_op jit(solution)/shard_map/ppermute | solution.py:464
  136.2 61.5 %collective-permute-start.27 = (f32[1536,128]{1,0:T(8,128)S(1)}, f32[1536,128]{1,0:T(8,128)}, u32[]{:S(2)}, u32[]{:S(2)}) collective-permute-start(f32[1536,128]{1,0:T(8,128)S(1)} %bitcast.28), channel_id=1, source_target_pairs={{0,0},{1,2},{2,1},{3,3},{4,4},{5,6},{6,5},{7,7},{8,8},{9,10},{10,9... | collective-permute-start | bytes 2359304 | tf_op jit(solution)/shard_map/ppermute | solution.py:524
  139.7 57.9 %collective-permute-start.24 = (f32[1536,128]{1,0:T(8,128)S(1)}, f32[1536,128]{1,0:T(8,128)}, u32[]{:S(2)}, u32[]{:S(2)}) collective-permute-start(f32[1536,128]{1,0:T(8,128)S(1)} %bitcast.29), channel_id=1, source_target_pairs={{0,1},{1,0},{2,3},{3,2},{4,5},{5,4},{6,7},{7,6},{8,9},{9,8},{10,11... | collective-permute-start | bytes 2359304 | tf_op jit(solution)/shard_map/ppermute | solution.py:523
  141.2 4.8 %collective-permute-start.23 = (f32[10,16,128]{2,1,0:T(8,128)S(1)}, f32[10,16,128]{2,1,0:T(8,128)S(1)}, u32[]{:S(2)}, u32[]{:S(2)}) collective-permute-start(f32[10,16,128]{2,1,0:T(8,128)S(1)} %add_add_fusion.1.refs_0_), channel_id=1, source_target_pairs={{0,28},{4,24},{8,20},{12,16},{16,12},{20,8},{24,4},{28,0},{1,29},{... | collective-permute-start | bytes 245768 | tf_op jit(solution)/shard_map/ppermute | solution.py:464
  146.1 0.6 copy-start
  146.7 5.3 %collective-permute-start.22 = (f32[10,16,128]{2,1,0:T(8,128)S(1)}, f32[10,16,128]{2,1,0:T(8,128)S(1)}, u32[]{:S(2)}, u32[]{:S(2)}) collective-permute-start(f32[10,16,128]{2,1,0:T(8,128)S(1)} %add_add_fusion.1.refs_0_), channel_id=1, source_target_pairs={{0,24},{4,28},{8,16},{12,20},{16,8},{20,12},{24,0},{28,4},{1,25},{... | collective-permute-start | bytes 245768 | tf_op jit(solution)/shard_map/ppermute | solution.py:464
  152.0 0.6 copy-start.2
  152.7 4.0 %collective-permute-start.21 = (f32[10,16,128]{2,1,0:T(8,128)S(1)}, f32[10,16,128]{2,1,0:T(8,128)S(1)}, u32[]{:S(2)}, u32[]{:S(2)}) collective-permute-start(f32[10,16,128]{2,1,0:T(8,128)S(1)} %add_add_fusion.1.refs_0_), channel_id=1, source_target_pairs={{0,20},{4,16},{8,28},{12,24},{16,4},{20,0},{24,12},{28,8},{1,21},{... | collective-permute-start | bytes 245768 | tf_op jit(solution)/shard_map/ppermute | solution.py:464
  156.6 0.6 copy-start.4
  157.2 4.4 %collective-permute-start.20 = (f32[10,16,128]{2,1,0:T(8,128)S(1)}, f32[10,16,128]{2,1,0:T(8,128)S(1)}, u32[]{:S(2)}, u32[]{:S(2)}) collective-permute-start(f32[10,16,128]{2,1,0:T(8,128)S(1)} %add_add_fusion.1.refs_0_), channel_id=1, source_target_pairs={{0,16},{4,20},{8,24},{12,28},{16,0},{20,4},{24,8},{28,12},{1,17},{... | collective-permute-start | bytes 245768 | tf_op jit(solution)/shard_map/ppermute | solution.py:464
  161.7 0.6 copy-start.6
  162.3 4.7 %collective-permute-start.19 = (f32[10,16,128]{2,1,0:T(8,128)S(1)}, f32[10,16,128]{2,1,0:T(8,128)S(1)}, u32[]{:S(2)}, u32[]{:S(2)}) collective-permute-start(f32[10,16,128]{2,1,0:T(8,128)S(1)} %add_add_fusion.1.refs_0_), channel_id=1, source_target_pairs={{0,12},{4,8},{8,4},{12,0},{16,28},{20,24},{24,20},{28,16},{1,13},{... | collective-permute-start | bytes 245768 | tf_op jit(solution)/shard_map/ppermute | solution.py:464
  167.0 0.6 copy-start.8
  167.7 4.4 %collective-permute-start.18 = (f32[10,16,128]{2,1,0:T(8,128)S(1)}, f32[10,16,128]{2,1,0:T(8,128)S(1)}, u32[]{:S(2)}, u32[]{:S(2)}) collective-permute-start(f32[10,16,128]{2,1,0:T(8,128)S(1)} %add_add_fusion.1.refs_0_), channel_id=1, source_target_pairs={{0,8},{4,12},{8,0},{12,4},{16,24},{20,28},{24,16},{28,20},{1,9},{5... | collective-permute-start | bytes 245768 | tf_op jit(solution)/shard_map/ppermute | solution.py:464
  172.1 0.6 copy-start.10
  172.7 1.4 collective-permute-start.17
  174.1 0.9 copy-start.1
  175.0 0.9 copy-start.3
  175.9 0.9 copy-start.5
  176.8 0.9 copy-start.7
  177.7 0.9 copy-start.9
  178.6 0.9 copy-start.11
  202.5 12.4 %collective-permute-start.29 = (f32[128,8,128]{2,1,0:T(8,128)S(1)}, f32[128,8,128]{2,1,0:T(8,128)S(1)}, u32[]{:S(2)}, u32[]{:S(2)}) collective-permute-start(f32[128,8,128]{2,1,0:T(8,128)S(1)} %get-tuple-element.23), channel_id=1, source_target_pairs={{0,0},{1,2},{2,1},{3,3},{4,4},{5,6},{6,5},{7,7},{8,8},{9,10},{10,9... | collective-permute-start | bytes 1572872 | tf_op jit(solution)/shard_map/ppermute | solution.py:537
  203.2 15.3 %collective-permute-start.30 = (f32[128,8,128]{2,1,0:T(8,128)S(1)}, f32[128,8,128]{2,1,0:T(8,128)S(1)}, u32[]{:S(2)}, u32[]{:S(2)}) collective-permute-start(f32[128,8,128]{2,1,0:T(8,128)S(1)} %get-tuple-element.24), channel_id=1, source_target_pairs={{0,1},{1,0},{2,3},{3,2},{4,5},{5,4},{6,7},{7,6},{8,9},{9,8},{10,11... | collective-permute-start | bytes 1572872 | tf_op jit(solution)/shard_map/ppermute | solution.py:538
  208.7 20.9 %collective-permute-start.26 = (f32[128,8,128]{2,1,0:T(8,128)S(1)}, f32[128,8,128]{2,1,0:T(8,128)S(1)}, u32[]{:S(2)}, u32[]{:S(2)}) collective-permute-start(f32[128,8,128]{2,1,0:T(8,128)S(1)} %rotate_far.2), channel_id=1, source_target_pairs={{0,1},{1,3},{2,0},{3,2},{4,5},{5,7},{6,4},{7,6},{8,9},{9,11},{10,8... | collective-permute-start | bytes 1572872 | tf_op jit(solution)/shard_map/ppermute | solution.py:536

commit v5 on v4

--- a/solution.py
+++ b/solution.py
@@ -244,33 +244,35 @@
     for s in range(pieces):
         first = pl.multiple_of((place_ref[0] ^ s) * part, part)
         work[:, pl.ds(first, part), :] = refs[s][...] * factor
-    tall = min(32, size)
+    tall = min(64, size)
     row = lax.broadcasted_iota(jnp.int32, (8, size), 0)
-    lane = lax.broadcasted_iota(jnp.int32, (tall, size), 1)
 
     def cut(j):
         return slice(j * size, (j + 1) * size)
 
-    def panel(s, carry):
-        base = pl.multiple_of(s * tall, tall)
-        pd = [w[pl.ds(base + 8 * t, 8), :size] for t in range(tall // 8)]
-        pi = [w[pl.ds(base + 8 * t, 8), size:] for t in range(tall // 8)]
+    def panel(s):
+        base = s * tall
+        pd = [w[base + 8 * t : base + 8 * t + 8, :size] for t in range(tall // 8)]
+        pi = [w[base + 8 * t : base + 8 * t + 8, size:] for t in range(tall // 8)]
         pd, pi = eliminate(pd, pi, base, row)
-        w[pl.ds(base, tall), size:] = pi
-        left = jnp.where(lane >= base + tall, pd, 0.0)
-        lh, lm, ll = split3(left)
+        w[base : base + tall, size:] = pi
+        after = base + tall
+        if after == size:
+            return
+        lh, lm, ll = split3(pd)
         rh, rm, rl = split3(jnp.concatenate([pd, pi], axis=1))
         a = jnp.concatenate([lh, lh, lm, lm, lh, ll], axis=0).astype(bf16)
         b = jnp.concatenate([rh, rm, rh, rm, rl, rh], axis=0).astype(bf16)
-        w[...] = w[...] - tdot(a, b)
-        return carry
+        full = tdot(a, b)
+        w[after:, :] = w[after:, :] - full[after:, :]
 
     r0 = lax.broadcasted_iota(jnp.int32, (size, size), 0)
     c0 = lax.broadcasted_iota(jnp.int32, (size, size), 1)
     for k in range(count):
         w[:, :size] = work[blocks[k, k]]
         w[:, size:] = jnp.where(r0 == c0, 1.0, 0.0)
-        lax.fori_loop(0, size // tall, panel, 0)
+        for s in range(size // tall):
+            panel(s)
         inv = w[:, size:]
         ih, il = split(inv)
         if k + 1 < count:
@@ -486,8 +488,9 @@
     z = line_matrix(cols, 2 if all(count % 2 == 0 for count in dealt) else 1)
 
     first = orbitals[: slabs * dealt[0]].reshape(slabs, dealt[0], planes, rows, cols)
-    spread = jnp.broadcast_to(potential, (slabs, 1, planes, rows, cols))
-    first = jnp.concatenate([first, spread], axis=1)
+    first = jnp.pad(first, ((0, 0), (0, 1), (0, 0), (0, 0), (0, 0)))
+    last = lax.broadcasted_iota(jnp.int32, first.shape, 1) == dealt[0]
+    first = jnp.where(last, potential[None, None], first)
     with_pot = lax.all_to_all(first, "grid", split_axis=0, concat_axis=0, tiled=True)
     arrived = [[with_pot]]
     for count in dealt[1:]:

time: 231 us -> 230 us (level)
  transfers between devices with their start and end apart: 33 -> 33, of which waited for: 21 -> 21; matrix products, arithmetic and copies ran while one was open for 1% -> 1% of each run, Pallas kernels for 13% -> 12%
where the time goes in v5:
time: 230 us; the launch traced here: 229 us
  waiting for transfers between devices  95.9 us (42%)
  Pallas kernels  40.7 us (18%)
  starting transfers between devices  40.6 us (18%)
  blocking collectives  37 us (16%)
  local copies, waits for them, and re-layouts  11.8 us (5%)
  other arithmetic  2.97 us (1%)
    ppermute x24, waiting for transfers between devices, swap_all(): lax.ppermute(pieces[s], axis, [(i, i ^ s) for i in range(count)])  68.4 us
    all_to_all x1, blocking collectives, orthonormalized(): lax.all_to_all(filtered, everyone, split_axis=0, concat_axis=0, tiled=True)  37 us
    ppermute x24, starting transfers between devices, swap_all(): lax.ppermute(pieces[s], axis, [(i, i ^ s) for i in range(count)])  21.6 us
    pallas_call x1, Pallas kernels, inverse_rows(): pl.pallas_call(functools.partial(inverse_kernel, factor), out_shape=jax.S...  15.9 us
    all_to_all x1, waiting for transfers between devices, orthonormalized(): lax.all_to_all(first, 'grid', split_axis=0, concat_axis=0, tiled=True)  12.9 us
    ppermute x1, waiting for transfers between devices, orthonormalized(): skip = lax.ppermute(skip, 'orb', [(0, 1), (1, 3), (2, 0), (3, 2)])  11 us
    unnamed x24, local copies, waits for them, and re-layouts  9.1 us
    pallas_call x2, Pallas kernels, rotate_for_others(): pl.pallas_call(functools.partial(kernel, spec), out_shape=[jax.ShapeDtype...  7.68 us
  transfers between devices with their start and end apart: 33, of which 21 were waited for; matrix products, arithmetic and copies ran while one was open for 1% of the time, Pallas kernels for 12%

profile of v5, /device:TPU:0, one launch (start us, length us, event | category | flops | bytes accessed | tf_op | source)
XLA Modules:
  0.0 229.5 jit_solution(5196107073902834797)
XLA Ops:
  0.0 1.1 slice-done
  1.1 1.8 pad_select_fusion
  3.0 5.2 %all-to-all-start = ((f32[8,7,4,8,128]{4,3,2,1,0:T(8,128)}), f32[8,7,4,8,128]{4,3,2,1,0:T(8,128)S(1)}, u32[]{:S(2)}, u32[]{:S(2)}) async-start(f32[8,7,4,8,128]{4,3,2,1,0:T(8,128)} %pad_select_fusion), calls=%async_computation | async-start | bytes 1835008 | tf_op jit(solution)/shard_map/all_to_all | solution.py:494
  9.3 12.9 %all-to-all-done.pot_ref.refs_0_ = f32[8,7,4,8,128]{4,3,2,1,0:T(8,128)S(1)} async-done(((f32[8,7,4,8,128]{4,3,2,1,0:T(8,128)}), f32[8,7,4,8,128]{4,3,2,1,0:T(8,128)S(1)}, u32[]{:S(2)}, u32[]{:S(2)}) %all-to-all-start) | async-done | bytes 917536 | tf_op jit(solution)/shard_map/all_to_all | solution.py:494
  22.1 3.3 %filter.2 = f32[4,8,6,8,128]{4,3,2,1,0:T(8,128)} custom-call(s32[1]{0:T(128)} %bitcast.1.place_ref, bf16[256,256]{1,0:T(8,128)(2,1)S(1)} %fusion.6.xy_ref, bf16[256,256]{1,0:T(8,128)(2,1)S(1)} %select_convert_fusion.z_ref, f32[8,7,4,8,128]{4,3,2,1,0:T(8,128)S(1)} %all-to-all-done.pot_ref.refs_0_, f32[8,7,4,8,128]{4,3,2,1,0:T(8,128)S(1)} %all-to-all-done.pot_ref.refs_0_), custom_call_target="tpu_custom_call" | custom-call | tf_op jit(solution)/shard_map/filter/pallas_call | solution.py:102
  25.5 4.0 %all-to-all-start.1 = ((f32[32,6,8,128]{3,2,1,0:T(8,128)}), f32[32,6,8,128]{3,2,1,0:T(8,128)S(1)}, u32[]{:S(2)}, u32[]{:S(2)}) async-start(f32[32,6,8,128]{3,2,1,0:T(8,128)} %bitcast.3), calls=%async_computation.1 | async-start | bytes 1572864 | tf_op jit(solution)/shard_map/all_to_all | solution.py:515
  29.5 1.5 dynamic-slice_bitcast_fusion
  31.1 2.5 %collective-permute-start.6 = (f32[1,10,4,8,128]{4,3,2,1,0:T(8,128)S(1)}, f32[1,10,4,8,128]{4,3,2,1,0:T(8,128)S(1)}, u32[]{:S(2)}, u32[]{:S(2)}) collective-permute-start(f32[1,10,4,8,128]{4,3,2,1,0:T(8,128)S(1)} %get-tuple-element.25), channel_id=1, source_target_pairs={{0,28},{4,24},{8,20},{12,16},{16,12},{20,8},{24,4},{28,0},{1,29},{... | collective-permute-start | bytes 491528 | tf_op jit(solution)/shard_map/ppermute | solution.py:466
  34.1 1.5 collective-permute-start.3
  35.6 1.5 collective-permute-start.1
  37.0 6.1 %collective-permute-done.6.refs_7_ = f32[1,10,4,8,128]{4,3,2,1,0:T(8,128)S(1)} collective-permute-done((f32[1,10,4,8,128]{4,3,2,1,0:T(8,128)S(1)}, f32[1,10,4,8,128]{4,3,2,1,0:T(8,128)S(1)}, u32[]{:S(2)}, u32[]{:S(2)}) %collective-permute-start.6) | collective-permute-done | bytes 163872 | tf_op jit(solution)/shard_map/ppermute | solution.py:466
  43.1 1.4 collective-permute-start
  44.5 2.4 %collective-permute-done.4.refs_5_ = f32[1,10,4,8,128]{4,3,2,1,0:T(8,128)S(1)} collective-permute-done((f32[1,10,4,8,128]{4,3,2,1,0:T(8,128)S(1)}, f32[1,10,4,8,128]{4,3,2,1,0:T(8,128)S(1)}, u32[]{:S(2)}, u32[]{:S(2)}) %collective-permute-start.4) | collective-permute-done | bytes 163872 | tf_op jit(solution)/shard_map/ppermute | solution.py:466
  47.7 4.1 %collective-permute-done.3.refs_4_ = f32[1,10,4,8,128]{4,3,2,1,0:T(8,128)S(1)} collective-permute-done((f32[1,10,4,8,128]{4,3,2,1,0:T(8,128)S(1)}, f32[1,10,4,8,128]{4,3,2,1,0:T(8,128)S(1)}, u32[]{:S(2)}, u32[]{:S(2)}) %collective-permute-start.3) | collective-permute-done | bytes 163872 | tf_op jit(solution)/shard_map/ppermute | solution.py:466
  51.8 4.1 %collective-permute-done.5.refs_6_ = f32[1,10,4,8,128]{4,3,2,1,0:T(8,128)S(1)} collective-permute-done((f32[1,10,4,8,128]{4,3,2,1,0:T(8,128)S(1)}, f32[1,10,4,8,128]{4,3,2,1,0:T(8,128)S(1)}, u32[]{:S(2)}, u32[]{:S(2)}) %collective-permute-start.5) | collective-permute-done | bytes 163872 | tf_op jit(solution)/shard_map/ppermute | solution.py:466
  56.0 3.9 %filter.3 = f32[4,8,10,8,128]{4,3,2,1,0:T(8,128)S(1)} custom-call(s32[1]{0:T(128)} %bitcast.1.place_ref, bf16[256,256]{1,0:T(8,128)(2,1)S(1)} %fusion.6.xy_ref, bf16[256,256]{1,0:T(8,128)(2,1)S(1)} %select_convert_fusion.z_ref, f32[8,7,4,8,128]{4,3,2,1,0:T(8,128)S(1)} %all-to-all-done.pot_ref.refs_0_, f32[1,10,4,8,128]{4,3,2,1,0:T(8,128)S(1)} %get-tuple-element.31.refs_0_, ...), custom_call_target="tpu_custom_call" | custom-call | tf_op jit(solution)/shard_map/filter/pallas_call | solution.py:102
  59.8 37.0 %all_to_all.15 = f32[32,10,8,128]{3,2,1,0:T(8,128)S(1)} all-to-all(f32[32,10,8,128]{3,2,1,0:T(8,128)S(1)} %bitcast.31), channel_id=1, replica_groups=mesh['grid'=8,'orb'=4] {'orb','grid'}, dimensions={0} | all-to-all | bytes 2621440 | tf_op jit(solution)/shard_map/all_to_all | solution.py:515
  96.9 2.9 %margin.1 = (f32[10,16,128]{2,1,0:T(8,128)S(1)}, f32[10,16,128]{2,1,0:T(8,128)S(1)}, f32[10,16,128]{2,1,0:T(8,128)S(1)}, f32[10,16,128]{2,1,0:T(8,128)S(1)}, f32...) custom-call(s32[1]{0:T(128)} %bitcast.1.place_ref, ...), custom_call_target="tpu_custom_call" | custom-call | tf_op jit(solution)/shard_map/margin/pallas_call | solution.py:177
  99.8 1.8 collective-permute-start.28
  101.6 1.4 collective-permute-start.25
  104.7 3.5 %collective-permute-done.8 = f32[10,16,128]{2,1,0:T(8,128)S(1)} collective-permute-done((f32[10,16,128]{2,1,0:T(8,128)S(1)}, f32[10,16,128]{2,1,0:T(8,128)S(1)}, u32[]{:S(2)}, u32[]{:S(2)}) %collective-permute-start.8) | collective-permute-done | bytes 81952 | tf_op jit(solution)/shard_map/ppermute | solution.py:466
  108.4 1.3 collective-permute-start.12
  109.7 1.9 collective-permute-start.13
  112.1 2.5 %collective-permute-done.12 = f32[10,16,128]{2,1,0:T(8,128)S(1)} collective-permute-done((f32[10,16,128]{2,1,0:T(8,128)S(1)}, f32[10,16,128]{2,1,0:T(8,128)S(1)}, u32[]{:S(2)}, u32[]{:S(2)}) %collective-permute-start.12) | collective-permute-done | bytes 81952 | tf_op jit(solution)/shard_map/ppermute | solution.py:466
  114.6 1.6 collective-permute-done.13
  116.3 2.5 %collective-permute-start.16 = (f32[10,16,128]{2,1,0:T(8,128)S(1)}, f32[10,16,128]{2,1,0:T(8,128)S(1)}, u32[]{:S(2)}, u32[]{:S(2)}) collective-permute-start(f32[10,16,128]{2,1,0:T(8,128)S(1)} %add_add_fusion.2), channel_id=1, source_target_pairs={{0,3},{1,2},{2,1},{3,0},{4,7},{5,6},{6,5},{7,4},{8,11},{9,10},{10,... | collective-permute-start | bytes 245768 | tf_op jit(solution)/shard_map/ppermute | solution.py:466
  118.9 1.9 collective-permute-start.14
  120.8 16.2 %collective-permute-done.16 = f32[10,16,128]{2,1,0:T(8,128)S(1)} collective-permute-done((f32[10,16,128]{2,1,0:T(8,128)S(1)}, f32[10,16,128]{2,1,0:T(8,128)S(1)}, u32[]{:S(2)}, u32[]{:S(2)}) %collective-permute-start.16) | collective-permute-done | bytes 81952 | tf_op jit(solution)/shard_map/ppermute | solution.py:466
  137.0 1.5 collective-permute-start.27
  138.5 2.0 collective-permute-done.15
  140.5 1.5 collective-permute-start.24
  142.1 4.8 %collective-permute-done.23.refs_7_ = f32[10,16,128]{2,1,0:T(8,128)S(1)} collective-permute-done((f32[10,16,128]{2,1,0:T(8,128)S(1)}, f32[10,16,128]{2,1,0:T(8,128)S(1)}, u32[]{:S(2)}, u32[]{:S(2)}) %collective-permute-start.23) | collective-permute-done | bytes 81952 | tf_op jit(solution)/shard_map/ppermute | solution.py:466
  147.5 1.5 collective-permute-start.22
  149.0 3.9 %collective-permute-done.22.refs_6_ = f32[10,16,128]{2,1,0:T(8,128)S(1)} collective-permute-done((f32[10,16,128]{2,1,0:T(8,128)S(1)}, f32[10,16,128]{2,1,0:T(8,128)S(1)}, u32[]{:S(2)}, u32[]{:S(2)}) %collective-permute-start.22) | collective-permute-done | bytes 81952 | tf_op jit(solution)/shard_map/ppermute | solution.py:466
  153.5 4.0 %collective-permute-done.21.refs_5_ = f32[10,16,128]{2,1,0:T(8,128)S(1)} collective-permute-done((f32[10,16,128]{2,1,0:T(8,128)S(1)}, f32[10,16,128]{2,1,0:T(8,128)S(1)}, u32[]{:S(2)}, u32[]{:S(2)}) %collective-permute-start.21) | collective-permute-done | bytes 81952 | tf_op jit(solution)/shard_map/ppermute | solution.py:466
  158.0 1.4 collective-permute-start.20
  159.4 3.1 %collective-permute-done.20.refs_4_ = f32[10,16,128]{2,1,0:T(8,128)S(1)} collective-permute-done((f32[10,16,128]{2,1,0:T(8,128)S(1)}, f32[10,16,128]{2,1,0:T(8,128)S(1)}, u32[]{:S(2)}, u32[]{:S(2)}) %collective-permute-start.20) | collective-permute-done | bytes 81952 | tf_op jit(solution)/shard_map/ppermute | solution.py:466
  163.4 4.4 %collective-permute-done.19.refs_3_ = f32[10,16,128]{2,1,0:T(8,128)S(1)} collective-permute-done((f32[10,16,128]{2,1,0:T(8,128)S(1)}, f32[10,16,128]{2,1,0:T(8,128)S(1)}, u32[]{:S(2)}, u32[]{:S(2)}) %collective-permute-start.19) | collective-permute-done | bytes 81952 | tf_op jit(solution)/shard_map/ppermute | solution.py:466
  169.3 3.5 %collective-permute-done.18.refs_2_ = f32[10,16,128]{2,1,0:T(8,128)S(1)} collective-permute-done((f32[10,16,128]{2,1,0:T(8,128)S(1)}, f32[10,16,128]{2,1,0:T(8,128)S(1)}, u32[]{:S(2)}, u32[]{:S(2)}) %collective-permute-start.18) | collective-permute-done | bytes 81952 | tf_op jit(solution)/shard_map/ppermute | solution.py:466
  173.5 1.4 collective-permute-done.17.refs_1_
  180.3 15.9 %inverse.1.v_ref = f32[4,128,512]{2,1,0:T(8,128)S(1)} custom-call(s32[1]{0:T(128)} %bitcast.1.place_ref, f32[10,16,128]{2,1,0:T(8,128)S(1)} %add_add_fusion.1.refs_0_, f32[10,16,128]{2,1,0:T(8,128)} %collective-permute-done.17.refs_1_, f32[10,16,128]{2,1,0:T(8,128)S(1)} %copy-done.11, f32[10,16,128]{2,1,0:T(8,128)S(1)} %copy-done.9, ...), custom_call_target="tpu_custom_call" | custom-call | tf_op jit(solution)/shard_map/inverse/pallas_call | solution.py:310
  196.2 5.0 %rotate_far.3 = (f32[128,8,128]{2,1,0:T(8,128)S(1)}, f32[128,8,128]{2,1,0:T(8,128)S(1)}) custom-call(s32[1]{0:T(128)} %bitcast.layer_ref, f32[4,128,512]{2,1,0:T(8,128)S(1)} %inverse.1.v_ref, f32[1536,128]{1,0:T(8,128)} %collective-permute-done.24.refs_0_.refs_2_, f32[2560,128]{1,0:T(8,128)S(1)} %collective-permute-done.25.refs_1_.refs_3_, ...), custom_call_target="tpu_custom_call" | custom-call | tf_op jit(solution)/shard_map/rotate_far/pallas_call | solution.py:388
  201.9 2.9 %collective-permute-start.30 = (f32[128,8,128]{2,1,0:T(8,128)S(1)}, f32[128,8,128]{2,1,0:T(8,128)S(1)}, u32[]{:S(2)}, u32[]{:S(2)}) collective-permute-start(f32[128,8,128]{2,1,0:T(8,128)S(1)} %get-tuple-element.24), channel_id=1, source_target_pairs={{0,1},{1,0},{2,3},{3,2},{4,5},{5,4},{6,7},{7,6},{8,9},{9,8},{10,11... | collective-permute-start | bytes 1572872 | tf_op jit(solution)/shard_map/ppermute | solution.py:541
  204.8 2.6 %rotate_far.2 = f32[128,8,128]{2,1,0:T(8,128)S(1)} custom-call(s32[1]{0:T(128)} %bitcast.layer_ref, f32[4,128,512]{2,1,0:T(8,128)S(1)} %inverse.1.v_ref, f32[1536,128]{1,0:T(8,128)} %collective-permute-done.24.refs_0_.refs_2_, f32[2560,128]{1,0:T(8,128)S(1)} %collective-permute-done.25.refs_1_.refs_3_), custom_call_target="tpu_custom_call" | custom-call | tf_op jit(solution)/shard_map/rotate_far/pallas_call | solution.py:388
  207.5 6.1 %rotate_near.1.near_ref = f32[128,4,8,128]{3,2,1,0:T(8,128)} custom-call(s32[1]{0:T(128)} %bitcast.layer_ref, f32[4,128,512]{2,1,0:T(8,128)S(1)} %inverse.1.v_ref, f32[1536,128]{1,0:T(8,128)S(1)} %bitcast.30, f32[2560,128]{1,0:T(8,128)S(1)} %bitcast.26, f32[1536,128]{1,0:T(8,128)} %collective-permute-done.24.refs_0_.refs_2_, ...), custom_call_target="tpu_custom_call" | custom-call | tf_op jit(solution)/shard_map/rotate_near/pallas_call | solution.py:424
  213.6 3.6 %collective-permute-done.30.back = f32[128,8,128]{2,1,0:T(8,128)S(1)} collective-permute-done((f32[128,8,128]{2,1,0:T(8,128)S(1)}, f32[128,8,128]{2,1,0:T(8,128)S(1)}, u32[]{:S(2)}, u32[]{:S(2)}) %collective-permute-start.30) | collective-permute-done | bytes 524320 | tf_op jit(solution)/shard_map/ppermute | solution.py:541
  217.3 11.0 %collective-permute-done.26.skip = f32[128,8,128]{2,1,0:T(8,128)S(1)} collective-permute-done((f32[128,8,128]{2,1,0:T(8,128)S(1)}, f32[128,8,128]{2,1,0:T(8,128)S(1)}, u32[]{:S(2)}, u32[]{:S(2)}) %collective-permute-start.26) | collective-permute-done | bytes 524320 | tf_op jit(solution)/shard_map/ppermute | solution.py:539
  228.3 1.0 join.1
  (65 shorter events, 16.2 us)
Async XLA Ops:
  0.0 1.1 slice-start
  3.0 19.2 %all-to-all-start = ((f32[8,7,4,8,128]{4,3,2,1,0:T(8,128)}), f32[8,7,4,8,128]{4,3,2,1,0:T(8,128)S(1)}, u32[]{:S(2)}, u32[]{:S(2)}) async-start(f32[8,7,4,8,128]{4,3,2,1,0:T(8,128)} %pad_select_fusion), calls=%async_computation | async-start | bytes 1835008 | tf_op jit(solution)/shard_map/all_to_all | solution.py:494
  25.5 34.4 %all-to-all-start.1 = ((f32[32,6,8,128]{3,2,1,0:T(8,128)}), f32[32,6,8,128]{3,2,1,0:T(8,128)S(1)}, u32[]{:S(2)}, u32[]{:S(2)}) async-start(f32[32,6,8,128]{3,2,1,0:T(8,128)} %bitcast.3), calls=%async_computation.1 | async-start | bytes 1572864 | tf_op jit(solution)/shard_map/all_to_all | solution.py:515
  31.1 12.0 %collective-permute-start.6 = (f32[1,10,4,8,128]{4,3,2,1,0:T(8,128)S(1)}, f32[1,10,4,8,128]{4,3,2,1,0:T(8,128)S(1)}, u32[]{:S(2)}, u32[]{:S(2)}) collective-permute-start(f32[1,10,4,8,128]{4,3,2,1,0:T(8,128)S(1)} %get-tuple-element.25), channel_id=1, source_target_pairs={{0,28},{4,24},{8,20},{12,16},{16,12},{20,8},{24,4},{28,0},{1,29},{... | collective-permute-start | bytes 491528 | tf_op jit(solution)/shard_map/ppermute | solution.py:466
  33.5 13.4 %collective-permute-start.4 = (f32[1,10,4,8,128]{4,3,2,1,0:T(8,128)S(1)}, f32[1,10,4,8,128]{4,3,2,1,0:T(8,128)S(1)}, u32[]{:S(2)}, u32[]{:S(2)}) collective-permute-start(f32[1,10,4,8,128]{4,3,2,1,0:T(8,128)S(1)} %get-tuple-element.26), channel_id=1, source_target_pairs={{0,20},{4,16},{8,28},{12,24},{16,4},{20,0},{24,12},{28,8},{1,21},{... | collective-permute-start | bytes 491528 | tf_op jit(solution)/shard_map/ppermute | solution.py:466
  34.1 17.7 %collective-permute-start.3 = (f32[1,10,4,8,128]{4,3,2,1,0:T(8,128)S(1)}, f32[1,10,4,8,128]{4,3,2,1,0:T(8,128)S(1)}, u32[]{:S(2)}, u32[]{:S(2)}) collective-permute-start(f32[1,10,4,8,128]{4,3,2,1,0:T(8,128)S(1)} %get-tuple-element.27), channel_id=1, source_target_pairs={{0,16},{4,20},{8,24},{12,28},{16,0},{20,4},{24,8},{28,12},{1,17},{... | collective-permute-start | bytes 491528 | tf_op jit(solution)/shard_map/ppermute | solution.py:466
  35.5 16.3 %collective-permute-start.2 = (f32[1,10,4,8,128]{4,3,2,1,0:T(8,128)S(1)}, f32[1,10,4,8,128]{4,3,2,1,0:T(8,128)S(1)}, u32[]{:S(2)}, u32[]{:S(2)}) collective-permute-start(f32[1,10,4,8,128]{4,3,2,1,0:T(8,128)S(1)} %get-tuple-element.28), channel_id=1, source_target_pairs={{0,12},{4,8},{8,4},{12,0},{16,28},{20,24},{24,20},{28,16},{1,13},{... | collective-permute-start | bytes 491528 | tf_op jit(solution)/shard_map/ppermute | solution.py:466
  35.6 16.3 %collective-permute-start.1 = (f32[1,10,4,8,128]{4,3,2,1,0:T(8,128)S(1)}, f32[1,10,4,8,128]{4,3,2,1,0:T(8,128)S(1)}, u32[]{:S(2)}, u32[]{:S(2)}) collective-permute-start(f32[1,10,4,8,128]{4,3,2,1,0:T(8,128)S(1)} %get-tuple-element.29), channel_id=1, source_target_pairs={{0,8},{4,12},{8,0},{12,4},{16,24},{20,28},{24,16},{28,20},{1,9},{5... | collective-permute-start | bytes 491528 | tf_op jit(solution)/shard_map/ppermute | solution.py:466
  43.1 8.7 %collective-permute-start = (f32[1,10,4,8,128]{4,3,2,1,0:T(8,128)S(1)}, f32[1,10,4,8,128]{4,3,2,1,0:T(8,128)S(1)}, u32[]{:S(2)}, u32[]{:S(2)}) collective-permute-start(f32[1,10,4,8,128]{4,3,2,1,0:T(8,128)S(1)} %get-tuple-element.30), channel_id=1, source_target_pairs={{0,4},{4,0},{8,12},{12,8},{16,20},{20,16},{24,28},{28,24},{1,5},{5... | collective-permute-start | bytes 491528 | tf_op jit(solution)/shard_map/ppermute | solution.py:466
  46.9 9.1 %collective-permute-start.5 = (f32[1,10,4,8,128]{4,3,2,1,0:T(8,128)S(1)}, f32[1,10,4,8,128]{4,3,2,1,0:T(8,128)S(1)}, u32[]{:S(2)}, u32[]{:S(2)}) collective-permute-start(f32[1,10,4,8,128]{4,3,2,1,0:T(8,128)S(1)} %get-tuple-element.32), channel_id=1, source_target_pairs={{0,24},{4,28},{8,16},{12,20},{16,8},{20,12},{24,0},{28,4},{1,25},{... | collective-permute-start | bytes 491528 | tf_op jit(solution)/shard_map/ppermute | solution.py:466
  99.8 4.4 %collective-permute-start.7 = (f32[10,16,128]{2,1,0:T(8,128)S(1)}, f32[10,16,128]{2,1,0:T(8,128)S(1)}, u32[]{:S(2)}, u32[]{:S(2)}) collective-permute-start(f32[10,16,128]{2,1,0:T(8,128)S(1)} %get-tuple-element.16), channel_id=1, source_target_pairs={{0,4},{4,0},{8,12},{12,8},{16,20},{20,16},{24,28},{28,24},{1,5},{5... | collective-permute-start | bytes 245768 | tf_op jit(solution)/shard_map/ppermute | solution.py:466
  99.8 96.3 %collective-permute-start.28 = (f32[2560,128]{1,0:T(8,128)S(1)}, f32[2560,128]{1,0:T(8,128)}, u32[]{:S(2)}, u32[]{:S(2)}) collective-permute-start(f32[2560,128]{1,0:T(8,128)S(1)} %bitcast.24), channel_id=1, source_target_pairs={{0,0},{1,2},{2,1},{3,3},{4,4},{5,6},{6,5},{7,7},{8,8},{9,10},{10,9... | collective-permute-start | bytes 3932168 | tf_op jit(solution)/shard_map/ppermute | solution.py:527
  101.6 94.6 %collective-permute-start.25 = (f32[2560,128]{1,0:T(8,128)S(1)}, f32[2560,128]{1,0:T(8,128)S(1)}, u32[]{:S(2)}, u32[]{:S(2)}) collective-permute-start(f32[2560,128]{1,0:T(8,128)S(1)} %bitcast.25), channel_id=1, source_target_pairs={{0,1},{1,0},{2,3},{3,2},{4,5},{5,4},{6,7},{7,6},{8,9},{9,8},{10,11... | collective-permute-start | bytes 3932168 | tf_op jit(solution)/shard_map/ppermute | solution.py:526
  103.0 5.2 %collective-permute-start.8 = (f32[10,16,128]{2,1,0:T(8,128)S(1)}, f32[10,16,128]{2,1,0:T(8,128)S(1)}, u32[]{:S(2)}, u32[]{:S(2)}) collective-permute-start(f32[10,16,128]{2,1,0:T(8,128)S(1)} %get-tuple-element.17), channel_id=1, source_target_pairs={{0,8},{4,12},{8,0},{12,4},{16,24},{20,28},{24,16},{28,20},{1,9},{5... | collective-permute-start | bytes 245768 | tf_op jit(solution)/shard_map/ppermute | solution.py:466
  103.7 4.7 %collective-permute-start.9 = (f32[10,16,128]{2,1,0:T(8,128)S(1)}, f32[10,16,128]{2,1,0:T(8,128)S(1)}, u32[]{:S(2)}, u32[]{:S(2)}) collective-permute-start(f32[10,16,128]{2,1,0:T(8,128)S(1)} %get-tuple-element.18), channel_id=1, source_target_pairs={{0,12},{4,8},{8,4},{12,0},{16,28},{20,24},{24,20},{28,16},{1,13},{... | collective-permute-start | bytes 245768 | tf_op jit(solution)/shard_map/ppermute | solution.py:466
  104.1 5.6 %collective-permute-start.10 = (f32[10,16,128]{2,1,0:T(8,128)S(1)}, f32[10,16,128]{2,1,0:T(8,128)S(1)}, u32[]{:S(2)}, u32[]{:S(2)}) collective-permute-start(f32[10,16,128]{2,1,0:T(8,128)S(1)} %get-tuple-element.19), channel_id=1, source_target_pairs={{0,16},{4,20},{8,24},{12,28},{16,0},{20,4},{24,8},{28,12},{1,17},{... | collective-permute-start | bytes 245768 | tf_op jit(solution)/shard_map/ppermute | solution.py:466
  108.2 3.9 %collective-permute-start.11 = (f32[10,16,128]{2,1,0:T(8,128)S(1)}, f32[10,16,128]{2,1,0:T(8,128)S(1)}, u32[]{:S(2)}, u32[]{:S(2)}) collective-permute-start(f32[10,16,128]{2,1,0:T(8,128)S(1)} %get-tuple-element.20), channel_id=1, source_target_pairs={{0,20},{4,16},{8,28},{12,24},{16,4},{20,0},{24,12},{28,8},{1,21},{... | collective-permute-start | bytes 245768 | tf_op jit(solution)/shard_map/ppermute | solution.py:466
  108.4 6.2 %collective-permute-start.12 = (f32[10,16,128]{2,1,0:T(8,128)S(1)}, f32[10,16,128]{2,1,0:T(8,128)S(1)}, u32[]{:S(2)}, u32[]{:S(2)}) collective-permute-start(f32[10,16,128]{2,1,0:T(8,128)S(1)} %get-tuple-element.21), channel_id=1, source_target_pairs={{0,24},{4,28},{8,16},{12,20},{16,8},{20,12},{24,0},{28,4},{1,25},{... | collective-permute-start | bytes 245768 | tf_op jit(solution)/shard_map/ppermute | solution.py:466
  109.7 6.6 %collective-permute-start.13 = (f32[10,16,128]{2,1,0:T(8,128)S(1)}, f32[10,16,128]{2,1,0:T(8,128)S(1)}, u32[]{:S(2)}, u32[]{:S(2)}) collective-permute-start(f32[10,16,128]{2,1,0:T(8,128)S(1)} %get-tuple-element.22), channel_id=1, source_target_pairs={{0,28},{4,24},{8,20},{12,16},{16,12},{20,8},{24,4},{28,0},{1,29},{... | collective-permute-start | bytes 245768 | tf_op jit(solution)/shard_map/ppermute | solution.py:466
  116.3 20.7 %collective-permute-start.16 = (f32[10,16,128]{2,1,0:T(8,128)S(1)}, f32[10,16,128]{2,1,0:T(8,128)S(1)}, u32[]{:S(2)}, u32[]{:S(2)}) collective-permute-start(f32[10,16,128]{2,1,0:T(8,128)S(1)} %add_add_fusion.2), channel_id=1, source_target_pairs={{0,3},{1,2},{2,1},{3,0},{4,7},{5,6},{6,5},{7,4},{8,11},{9,10},{10,... | collective-permute-start | bytes 245768 | tf_op jit(solution)/shard_map/ppermute | solution.py:466
  118.8 21.6 %collective-permute-start.15 = (f32[10,16,128]{2,1,0:T(8,128)S(1)}, f32[10,16,128]{2,1,0:T(8,128)S(1)}, u32[]{:S(2)}, u32[]{:S(2)}) collective-permute-start(f32[10,16,128]{2,1,0:T(8,128)S(1)} %add_add_fusion.2), channel_id=1, source_target_pairs={{0,2},{1,3},{2,0},{3,1},{4,6},{5,7},{6,4},{7,5},{8,10},{9,11},{10,... | collective-permute-start | bytes 245768 | tf_op jit(solution)/shard_map/ppermute | solution.py:466
  118.9 23.1 %collective-permute-start.14 = (f32[10,16,128]{2,1,0:T(8,128)S(1)}, f32[10,16,128]{2,1,0:T(8,128)S(1)}, u32[]{:S(2)}, u32[]{:S(2)}) collective-permute-start(f32[10,16,128]{2,1,0:T(8,128)S(1)} %add_add_fusion.2), channel_id=1, source_target_pairs={{0,1},{1,0},{2,3},{3,2},{4,5},{5,4},{6,7},{7,6},{8,9},{9,8},{10,11... | collective-permute-start | bytes 245768 | tf_op jit(solution)/shard_map/ppermute | solution.py:466
  137.0 59.2 %collective-permute-start.27 = (f32[1536,128]{1,0:T(8,128)S(1)}, f32[1536,128]{1,0:T(8,128)}, u32[]{:S(2)}, u32[]{:S(2)}) collective-permute-start(f32[1536,128]{1,0:T(8,128)S(1)} %bitcast.28), channel_id=1, source_target_pairs={{0,0},{1,2},{2,1},{3,3},{4,4},{5,6},{6,5},{7,7},{8,8},{9,10},{10,9... | collective-permute-start | bytes 2359304 | tf_op jit(solution)/shard_map/ppermute | solution.py:527
  140.5 55.7 %collective-permute-start.24 = (f32[1536,128]{1,0:T(8,128)S(1)}, f32[1536,128]{1,0:T(8,128)}, u32[]{:S(2)}, u32[]{:S(2)}) collective-permute-start(f32[1536,128]{1,0:T(8,128)S(1)} %bitcast.29), channel_id=1, source_target_pairs={{0,1},{1,0},{2,3},{3,2},{4,5},{5,4},{6,7},{7,6},{8,9},{9,8},{10,11... | collective-permute-start | bytes 2359304 | tf_op jit(solution)/shard_map/ppermute | solution.py:526
  142.0 4.8 %collective-permute-start.23 = (f32[10,16,128]{2,1,0:T(8,128)S(1)}, f32[10,16,128]{2,1,0:T(8,128)S(1)}, u32[]{:S(2)}, u32[]{:S(2)}) collective-permute-start(f32[10,16,128]{2,1,0:T(8,128)S(1)} %add_add_fusion.1.refs_0_), channel_id=1, source_target_pairs={{0,28},{4,24},{8,20},{12,16},{16,12},{20,8},{24,4},{28,0},{1,29},{... | collective-permute-start | bytes 245768 | tf_op jit(solution)/shard_map/ppermute | solution.py:466
  146.9 0.6 copy-start
  147.5 5.3 %collective-permute-start.22 = (f32[10,16,128]{2,1,0:T(8,128)S(1)}, f32[10,16,128]{2,1,0:T(8,128)S(1)}, u32[]{:S(2)}, u32[]{:S(2)}) collective-permute-start(f32[10,16,128]{2,1,0:T(8,128)S(1)} %add_add_fusion.1.refs_0_), channel_id=1, source_target_pairs={{0,24},{4,28},{8,16},{12,20},{16,8},{20,12},{24,0},{28,4},{1,25},{... | collective-permute-start | bytes 245768 | tf_op jit(solution)/shard_map/ppermute | solution.py:466
  152.8 0.6 copy-start.2
  153.5 4.0 %collective-permute-start.21 = (f32[10,16,128]{2,1,0:T(8,128)S(1)}, f32[10,16,128]{2,1,0:T(8,128)S(1)}, u32[]{:S(2)}, u32[]{:S(2)}) collective-permute-start(f32[10,16,128]{2,1,0:T(8,128)S(1)} %add_add_fusion.1.refs_0_), channel_id=1, source_target_pairs={{0,20},{4,16},{8,28},{12,24},{16,4},{20,0},{24,12},{28,8},{1,21},{... | collective-permute-start | bytes 245768 | tf_op jit(solution)/shard_map/ppermute | solution.py:466
  157.4 0.6 copy-start.4
  158.0 4.4 %collective-permute-start.20 = (f32[10,16,128]{2,1,0:T(8,128)S(1)}, f32[10,16,128]{2,1,0:T(8,128)S(1)}, u32[]{:S(2)}, u32[]{:S(2)}) collective-permute-start(f32[10,16,128]{2,1,0:T(8,128)S(1)} %add_add_fusion.1.refs_0_), channel_id=1, source_target_pairs={{0,16},{4,20},{8,24},{12,28},{16,0},{20,4},{24,8},{28,12},{1,17},{... | collective-permute-start | bytes 245768 | tf_op jit(solution)/shard_map/ppermute | solution.py:466
  162.5 0.6 copy-start.6
  163.1 4.7 %collective-permute-start.19 = (f32[10,16,128]{2,1,0:T(8,128)S(1)}, f32[10,16,128]{2,1,0:T(8,128)S(1)}, u32[]{:S(2)}, u32[]{:S(2)}) collective-permute-start(f32[10,16,128]{2,1,0:T(8,128)S(1)} %add_add_fusion.1.refs_0_), channel_id=1, source_target_pairs={{0,12},{4,8},{8,4},{12,0},{16,28},{20,24},{24,20},{28,16},{1,13},{... | collective-permute-start | bytes 245768 | tf_op jit(solution)/shard_map/ppermute | solution.py:466
  167.8 0.6 copy-start.8
  168.4 4.4 %collective-permute-start.18 = (f32[10,16,128]{2,1,0:T(8,128)S(1)}, f32[10,16,128]{2,1,0:T(8,128)S(1)}, u32[]{:S(2)}, u32[]{:S(2)}) collective-permute-start(f32[10,16,128]{2,1,0:T(8,128)S(1)} %add_add_fusion.1.refs_0_), channel_id=1, source_target_pairs={{0,8},{4,12},{8,0},{12,4},{16,24},{20,28},{24,16},{28,20},{1,9},{5... | collective-permute-start | bytes 245768 | tf_op jit(solution)/shard_map/ppermute | solution.py:466
  172.9 0.6 copy-start.10
  173.5 1.4 collective-permute-start.17
  174.9 0.9 copy-start.1
  175.8 0.9 copy-start.3
  176.7 0.9 copy-start.5
  177.6 0.9 copy-start.7
  178.5 0.9 copy-start.9
  179.4 0.9 copy-start.11
  201.2 12.4 %collective-permute-start.29 = (f32[128,8,128]{2,1,0:T(8,128)S(1)}, f32[128,8,128]{2,1,0:T(8,128)S(1)}, u32[]{:S(2)}, u32[]{:S(2)}) collective-permute-start(f32[128,8,128]{2,1,0:T(8,128)S(1)} %get-tuple-element.23), channel_id=1, source_target_pairs={{0,0},{1,2},{2,1},{3,3},{4,4},{5,6},{6,5},{7,7},{8,8},{9,10},{10,9... | collective-permute-start | bytes 1572872 | tf_op jit(solution)/shard_map/ppermute | solution.py:540
  201.9 15.3 %collective-permute-start.30 = (f32[128,8,128]{2,1,0:T(8,128)S(1)}, f32[128,8,128]{2,1,0:T(8,128)S(1)}, u32[]{:S(2)}, u32[]{:S(2)}) collective-permute-start(f32[128,8,128]{2,1,0:T(8,128)S(1)} %get-tuple-element.24), channel_id=1, source_target_pairs={{0,1},{1,0},{2,3},{3,2},{4,5},{5,4},{6,7},{7,6},{8,9},{9,8},{10,11... | collective-permute-start | bytes 1572872 | tf_op jit(solution)/shard_map/ppermute | solution.py:541
  207.4 20.8 %collective-permute-start.26 = (f32[128,8,128]{2,1,0:T(8,128)S(1)}, f32[128,8,128]{2,1,0:T(8,128)S(1)}, u32[]{:S(2)}, u32[]{:S(2)}) collective-permute-start(f32[128,8,128]{2,1,0:T(8,128)S(1)} %rotate_far.2), channel_id=1, source_target_pairs={{0,1},{1,3},{2,0},{3,2},{4,5},{5,7},{6,4},{7,6},{8,9},{9,11},{10,8... | collective-permute-start | bytes 1572872 | tf_op jit(solution)/shard_map/ppermute | solution.py:539

commit v6 on v5

--- a/solution.py
+++ b/solution.py
@@ -393,7 +393,7 @@
         scratch_shapes=wide_scratch(spec, cols),
         compiler_params=middle,
         name="rotate_far",
-    )(layer, v, *parts)
+    )(layer, in_vmem(v), *(in_vmem(part) for part in parts))
 
 
 def near_kernel(spec, layer_ref, v_ref, *refs):
@@ -488,9 +488,8 @@
     z = line_matrix(cols, 2 if all(count % 2 == 0 for count in dealt) else 1)
 
     first = orbitals[: slabs * dealt[0]].reshape(slabs, dealt[0], planes, rows, cols)
-    first = jnp.pad(first, ((0, 0), (0, 1), (0, 0), (0, 0), (0, 0)))
-    last = lax.broadcasted_iota(jnp.int32, first.shape, 1) == dealt[0]
-    first = jnp.where(last, potential[None, None], first)
+    spread = jnp.broadcast_to(potential, (slabs, 1, planes, rows, cols))
+    first = jnp.concatenate([first, spread], axis=1)
     with_pot = lax.all_to_all(first, "grid", split_axis=0, concat_axis=0, tiled=True)
     arrived = [[with_pot]]
     for count in dealt[1:]:

time: 230 us -> 229 us (level)
  no operation moved by 1% of the time
where the time goes in v6:
time: 229 us
  waiting for transfers between devices  95.9 us (42%)
  starting transfers between devices  40.7 us (18%)
  Pallas kernels  40.7 us (18%)
  blocking collectives  37 us (16%)
  local copies, waits for them, and re-layouts  11.8 us (5%)
    ppermute x24, waiting for transfers between devices, swap_all(): lax.ppermute(pieces[s], axis, [(i, i ^ s) for i in range(count)])  68.3 us
    all_to_all x1, blocking collectives, orthonormalized(): lax.all_to_all(filtered, everyone, split_axis=0, concat_axis=0, tiled=True)  37 us
    ppermute x24, starting transfers between devices, swap_all(): lax.ppermute(pieces[s], axis, [(i, i ^ s) for i in range(count)])  21.6 us
    pallas_call x1, Pallas kernels, inverse_rows(): pl.pallas_call(functools.partial(inverse_kernel, factor), out_shape=jax.S...  15.9 us
    all_to_all x1, waiting for transfers between devices, orthonormalized(): lax.all_to_all(first, 'grid', split_axis=0, concat_axis=0, tiled=True)  12.9 us
    ppermute x1, waiting for transfers between devices, orthonormalized(): skip = lax.ppermute(skip, 'orb', [(0, 1), (1, 3), (2, 0), (3, 2)])  11.1 us
    unnamed x24, local copies, waits for them, and re-layouts  9.1 us
    pallas_call x2, Pallas kernels, rotate_for_others(): pl.pallas_call(functools.partial(kernel, spec), out_shape=[jax.ShapeDtype...  7.68 us
  transfers between devices with their start and end apart: 33, of which 21 were waited for; matrix products, arithmetic and copies ran while one was open for 1% of the time, Pallas kernels for 12%

profile of v6, /device:TPU:0, one launch (start us, length us, event | category | flops | bytes accessed | tf_op | source)
XLA Modules:
  0.0 228.7 jit_solution(3458742720566254830)
XLA Ops:
  1.1 1.0 pad_maximum_fusion
  2.2 5.2 %all-to-all-start = ((f32[8,7,4,8,128]{4,3,2,1,0:T(8,128)}), f32[8,7,4,8,128]{4,3,2,1,0:T(8,128)S(1)}, u32[]{:S(2)}, u32[]{:S(2)}) async-start(f32[8,7,4,8,128]{4,3,2,1,0:T(8,128)} %pad_maximum_fusion), calls=%async_computation | async-start | bytes 1835008 | tf_op jit(solution)/shard_map/all_to_all | solution.py:493
  8.5 12.9 %all-to-all-done.pot_ref.refs_0_ = f32[8,7,4,8,128]{4,3,2,1,0:T(8,128)S(1)} async-done(((f32[8,7,4,8,128]{4,3,2,1,0:T(8,128)}), f32[8,7,4,8,128]{4,3,2,1,0:T(8,128)S(1)}, u32[]{:S(2)}, u32[]{:S(2)}) %all-to-all-start) | async-done | bytes 917536 | tf_op jit(solution)/shard_map/all_to_all | solution.py:493
  21.3 3.3 %filter.2 = f32[4,8,6,8,128]{4,3,2,1,0:T(8,128)} custom-call(s32[1]{0:T(128)} %bitcast.1.place_ref, bf16[256,256]{1,0:T(8,128)(2,1)S(1)} %fusion.6.xy_ref, bf16[256,256]{1,0:T(8,128)(2,1)S(1)} %select_convert_fusion.z_ref, f32[8,7,4,8,128]{4,3,2,1,0:T(8,128)S(1)} %all-to-all-done.pot_ref.refs_0_, f32[8,7,4,8,128]{4,3,2,1,0:T(8,128)S(1)} %all-to-all-done.pot_ref.refs_0_), custom_call_target="tpu_custom_call" | custom-call | tf_op jit(solution)/shard_map/filter/pallas_call | solution.py:102
  24.7 4.0 %all-to-all-start.1 = ((f32[32,6,8,128]{3,2,1,0:T(8,128)}), f32[32,6,8,128]{3,2,1,0:T(8,128)S(1)}, u32[]{:S(2)}, u32[]{:S(2)}) async-start(f32[32,6,8,128]{3,2,1,0:T(8,128)} %bitcast.3), calls=%async_computation.1 | async-start | bytes 1572864 | tf_op jit(solution)/shard_map/all_to_all | solution.py:514
  28.7 1.6 dynamic-slice_bitcast_fusion
  30.3 2.5 %collective-permute-start.6 = (f32[1,10,4,8,128]{4,3,2,1,0:T(8,128)S(1)}, f32[1,10,4,8,128]{4,3,2,1,0:T(8,128)S(1)}, u32[]{:S(2)}, u32[]{:S(2)}) collective-permute-start(f32[1,10,4,8,128]{4,3,2,1,0:T(8,128)S(1)} %get-tuple-element.25), channel_id=1, source_target_pairs={{0,28},{4,24},{8,20},{12,16},{16,12},{20,8},{24,4},{28,0},{1,29},{... | collective-permute-start | bytes 491528 | tf_op jit(solution)/shard_map/ppermute | solution.py:466
  33.3 1.5 collective-permute-start.3
  34.8 1.5 collective-permute-start.1
  36.2 6.1 %collective-permute-done.6.refs_7_ = f32[1,10,4,8,128]{4,3,2,1,0:T(8,128)S(1)} collective-permute-done((f32[1,10,4,8,128]{4,3,2,1,0:T(8,128)S(1)}, f32[1,10,4,8,128]{4,3,2,1,0:T(8,128)S(1)}, u32[]{:S(2)}, u32[]{:S(2)}) %collective-permute-start.6) | collective-permute-done | bytes 163872 | tf_op jit(solution)/shard_map/ppermute | solution.py:466
  42.3 1.4 collective-permute-start
  43.7 2.4 %collective-permute-done.4.refs_5_ = f32[1,10,4,8,128]{4,3,2,1,0:T(8,128)S(1)} collective-permute-done((f32[1,10,4,8,128]{4,3,2,1,0:T(8,128)S(1)}, f32[1,10,4,8,128]{4,3,2,1,0:T(8,128)S(1)}, u32[]{:S(2)}, u32[]{:S(2)}) %collective-permute-start.4) | collective-permute-done | bytes 163872 | tf_op jit(solution)/shard_map/ppermute | solution.py:466
  46.9 4.1 %collective-permute-done.3.refs_4_ = f32[1,10,4,8,128]{4,3,2,1,0:T(8,128)S(1)} collective-permute-done((f32[1,10,4,8,128]{4,3,2,1,0:T(8,128)S(1)}, f32[1,10,4,8,128]{4,3,2,1,0:T(8,128)S(1)}, u32[]{:S(2)}, u32[]{:S(2)}) %collective-permute-start.3) | collective-permute-done | bytes 163872 | tf_op jit(solution)/shard_map/ppermute | solution.py:466
  51.0 4.1 %collective-permute-done.5.refs_6_ = f32[1,10,4,8,128]{4,3,2,1,0:T(8,128)S(1)} collective-permute-done((f32[1,10,4,8,128]{4,3,2,1,0:T(8,128)S(1)}, f32[1,10,4,8,128]{4,3,2,1,0:T(8,128)S(1)}, u32[]{:S(2)}, u32[]{:S(2)}) %collective-permute-start.5) | collective-permute-done | bytes 163872 | tf_op jit(solution)/shard_map/ppermute | solution.py:466
  55.2 3.9 %filter.3 = f32[4,8,10,8,128]{4,3,2,1,0:T(8,128)S(1)} custom-call(s32[1]{0:T(128)} %bitcast.1.place_ref, bf16[256,256]{1,0:T(8,128)(2,1)S(1)} %fusion.6.xy_ref, bf16[256,256]{1,0:T(8,128)(2,1)S(1)} %select_convert_fusion.z_ref, f32[8,7,4,8,128]{4,3,2,1,0:T(8,128)S(1)} %all-to-all-done.pot_ref.refs_0_, f32[1,10,4,8,128]{4,3,2,1,0:T(8,128)S(1)} %get-tuple-element.31.refs_0_, ...), custom_call_target="tpu_custom_call" | custom-call | tf_op jit(solution)/shard_map/filter/pallas_call | solution.py:102
  59.0 37.0 %all_to_all.15 = f32[32,10,8,128]{3,2,1,0:T(8,128)S(1)} all-to-all(f32[32,10,8,128]{3,2,1,0:T(8,128)S(1)} %bitcast.31), channel_id=1, replica_groups=mesh['grid'=8,'orb'=4] {'orb','grid'}, dimensions={0} | all-to-all | bytes 2621440 | tf_op jit(solution)/shard_map/all_to_all | solution.py:514
  96.1 2.9 %margin.1 = (f32[10,16,128]{2,1,0:T(8,128)S(1)}, f32[10,16,128]{2,1,0:T(8,128)S(1)}, f32[10,16,128]{2,1,0:T(8,128)S(1)}, f32[10,16,128]{2,1,0:T(8,128)S(1)}, f32...) custom-call(s32[1]{0:T(128)} %bitcast.1.place_ref, ...), custom_call_target="tpu_custom_call" | custom-call | tf_op jit(solution)/shard_map/margin/pallas_call | solution.py:177
  99.0 1.8 collective-permute-start.28
  100.8 1.4 collective-permute-start.25
  103.9 3.5 %collective-permute-done.8 = f32[10,16,128]{2,1,0:T(8,128)S(1)} collective-permute-done((f32[10,16,128]{2,1,0:T(8,128)S(1)}, f32[10,16,128]{2,1,0:T(8,128)S(1)}, u32[]{:S(2)}, u32[]{:S(2)}) %collective-permute-start.8) | collective-permute-done | bytes 81952 | tf_op jit(solution)/shard_map/ppermute | solution.py:466
  107.6 1.3 collective-permute-start.12
  108.9 1.9 collective-permute-start.13
  111.3 2.5 %collective-permute-done.12 = f32[10,16,128]{2,1,0:T(8,128)S(1)} collective-permute-done((f32[10,16,128]{2,1,0:T(8,128)S(1)}, f32[10,16,128]{2,1,0:T(8,128)S(1)}, u32[]{:S(2)}, u32[]{:S(2)}) %collective-permute-start.12) | collective-permute-done | bytes 81952 | tf_op jit(solution)/shard_map/ppermute | solution.py:466
  113.8 1.6 collective-permute-done.13
  115.5 2.6 %collective-permute-start.16 = (f32[10,16,128]{2,1,0:T(8,128)S(1)}, f32[10,16,128]{2,1,0:T(8,128)S(1)}, u32[]{:S(2)}, u32[]{:S(2)}) collective-permute-start(f32[10,16,128]{2,1,0:T(8,128)S(1)} %add_add_fusion.2), channel_id=1, source_target_pairs={{0,3},{1,2},{2,1},{3,0},{4,7},{5,6},{6,5},{7,4},{8,11},{9,10},{10,... | collective-permute-start | bytes 245768 | tf_op jit(solution)/shard_map/ppermute | solution.py:466
  118.1 1.9 collective-permute-start.14
  120.0 16.2 %collective-permute-done.16 = f32[10,16,128]{2,1,0:T(8,128)S(1)} collective-permute-done((f32[10,16,128]{2,1,0:T(8,128)S(1)}, f32[10,16,128]{2,1,0:T(8,128)S(1)}, u32[]{:S(2)}, u32[]{:S(2)}) %collective-permute-start.16) | collective-permute-done | bytes 81952 | tf_op jit(solution)/shard_map/ppermute | solution.py:466
  136.2 1.5 collective-permute-start.27
  137.7 2.0 collective-permute-done.15
  139.7 1.5 collective-permute-start.24
  141.3 4.8 %collective-permute-done.23.refs_7_ = f32[10,16,128]{2,1,0:T(8,128)S(1)} collective-permute-done((f32[10,16,128]{2,1,0:T(8,128)S(1)}, f32[10,16,128]{2,1,0:T(8,128)S(1)}, u32[]{:S(2)}, u32[]{:S(2)}) %collective-permute-start.23) | collective-permute-done | bytes 81952 | tf_op jit(solution)/shard_map/ppermute | solution.py:466
  146.7 1.5 collective-permute-start.22
  148.2 3.9 %collective-permute-done.22.refs_6_ = f32[10,16,128]{2,1,0:T(8,128)S(1)} collective-permute-done((f32[10,16,128]{2,1,0:T(8,128)S(1)}, f32[10,16,128]{2,1,0:T(8,128)S(1)}, u32[]{:S(2)}, u32[]{:S(2)}) %collective-permute-start.22) | collective-permute-done | bytes 81952 | tf_op jit(solution)/shard_map/ppermute | solution.py:466
  152.7 4.0 %collective-permute-done.21.refs_5_ = f32[10,16,128]{2,1,0:T(8,128)S(1)} collective-permute-done((f32[10,16,128]{2,1,0:T(8,128)S(1)}, f32[10,16,128]{2,1,0:T(8,128)S(1)}, u32[]{:S(2)}, u32[]{:S(2)}) %collective-permute-start.21) | collective-permute-done | bytes 81952 | tf_op jit(solution)/shard_map/ppermute | solution.py:466
  157.2 1.4 collective-permute-start.20
  158.6 3.1 %collective-permute-done.20.refs_4_ = f32[10,16,128]{2,1,0:T(8,128)S(1)} collective-permute-done((f32[10,16,128]{2,1,0:T(8,128)S(1)}, f32[10,16,128]{2,1,0:T(8,128)S(1)}, u32[]{:S(2)}, u32[]{:S(2)}) %collective-permute-start.20) | collective-permute-done | bytes 81952 | tf_op jit(solution)/shard_map/ppermute | solution.py:466
  162.6 4.4 %collective-permute-done.19.refs_3_ = f32[10,16,128]{2,1,0:T(8,128)S(1)} collective-permute-done((f32[10,16,128]{2,1,0:T(8,128)S(1)}, f32[10,16,128]{2,1,0:T(8,128)S(1)}, u32[]{:S(2)}, u32[]{:S(2)}) %collective-permute-start.19) | collective-permute-done | bytes 81952 | tf_op jit(solution)/shard_map/ppermute | solution.py:466
  167.7 0.9 collective-permute-start.18
  168.6 3.5 %collective-permute-done.18.refs_2_ = f32[10,16,128]{2,1,0:T(8,128)S(1)} collective-permute-done((f32[10,16,128]{2,1,0:T(8,128)S(1)}, f32[10,16,128]{2,1,0:T(8,128)S(1)}, u32[]{:S(2)}, u32[]{:S(2)}) %collective-permute-start.18) | collective-permute-done | bytes 81952 | tf_op jit(solution)/shard_map/ppermute | solution.py:466
  172.7 1.4 collective-permute-done.17.refs_1_
  179.5 15.9 %inverse.1.v_ref = f32[4,128,512]{2,1,0:T(8,128)S(1)} custom-call(s32[1]{0:T(128)} %bitcast.1.place_ref, f32[10,16,128]{2,1,0:T(8,128)S(1)} %add_add_fusion.1.refs_0_, f32[10,16,128]{2,1,0:T(8,128)} %collective-permute-done.17.refs_1_, f32[10,16,128]{2,1,0:T(8,128)S(1)} %copy-done.11, f32[10,16,128]{2,1,0:T(8,128)S(1)} %copy-done.9, ...), custom_call_target="tpu_custom_call" | custom-call | tf_op jit(solution)/shard_map/inverse/pallas_call | solution.py:310
  195.4 5.0 %rotate_far.3 = (f32[128,8,128]{2,1,0:T(8,128)S(1)}, f32[128,8,128]{2,1,0:T(8,128)S(1)}) custom-call(s32[1]{0:T(128)} %bitcast.layer_ref, f32[4,128,512]{2,1,0:T(8,128)S(1)} %inverse.1.v_ref, f32[1536,128]{1,0:T(8,128)} %collective-permute-done.24.refs_0_.refs_2_, f32[2560,128]{1,0:T(8,128)S(1)} %collective-permute-done.25.refs_1_.refs_3_, ...), custom_call_target="tpu_custom_call" | custom-call | tf_op jit(solution)/shard_map/rotate_far/pallas_call | solution.py:388
  201.1 2.9 %collective-permute-start.30 = (f32[128,8,128]{2,1,0:T(8,128)S(1)}, f32[128,8,128]{2,1,0:T(8,128)S(1)}, u32[]{:S(2)}, u32[]{:S(2)}) collective-permute-start(f32[128,8,128]{2,1,0:T(8,128)S(1)} %get-tuple-element.24), channel_id=1, source_target_pairs={{0,1},{1,0},{2,3},{3,2},{4,5},{5,4},{6,7},{7,6},{8,9},{9,8},{10,11... | collective-permute-start | bytes 1572872 | tf_op jit(solution)/shard_map/ppermute | solution.py:540
  204.0 2.6 %rotate_far.2 = f32[128,8,128]{2,1,0:T(8,128)S(1)} custom-call(s32[1]{0:T(128)} %bitcast.layer_ref, f32[4,128,512]{2,1,0:T(8,128)S(1)} %inverse.1.v_ref, f32[1536,128]{1,0:T(8,128)} %collective-permute-done.24.refs_0_.refs_2_, f32[2560,128]{1,0:T(8,128)S(1)} %collective-permute-done.25.refs_1_.refs_3_), custom_call_target="tpu_custom_call" | custom-call | tf_op jit(solution)/shard_map/rotate_far/pallas_call | solution.py:388
  206.7 6.1 %rotate_near.1.near_ref = f32[128,4,8,128]{3,2,1,0:T(8,128)} custom-call(s32[1]{0:T(128)} %bitcast.layer_ref, f32[4,128,512]{2,1,0:T(8,128)S(1)} %inverse.1.v_ref, f32[1536,128]{1,0:T(8,128)S(1)} %bitcast.30, f32[2560,128]{1,0:T(8,128)S(1)} %bitcast.26, f32[1536,128]{1,0:T(8,128)} %collective-permute-done.24.refs_0_.refs_2_, ...), custom_call_target="tpu_custom_call" | custom-call | tf_op jit(solution)/shard_map/rotate_near/pallas_call | solution.py:424
  212.9 3.6 %collective-permute-done.30.back = f32[128,8,128]{2,1,0:T(8,128)S(1)} collective-permute-done((f32[128,8,128]{2,1,0:T(8,128)S(1)}, f32[128,8,128]{2,1,0:T(8,128)S(1)}, u32[]{:S(2)}, u32[]{:S(2)}) %collective-permute-start.30) | collective-permute-done | bytes 524320 | tf_op jit(solution)/shard_map/ppermute | solution.py:540
  216.5 11.1 %collective-permute-done.26.skip = f32[128,8,128]{2,1,0:T(8,128)S(1)} collective-permute-done((f32[128,8,128]{2,1,0:T(8,128)S(1)}, f32[128,8,128]{2,1,0:T(8,128)S(1)}, u32[]{:S(2)}, u32[]{:S(2)}) %collective-permute-start.26) | collective-permute-done | bytes 524320 | tf_op jit(solution)/shard_map/ppermute | solution.py:538
  227.5 1.0 join.1
  (65 shorter events, 16.4 us)
Async XLA Ops:
  0.0 1.1 slice-start
  2.2 19.2 %all-to-all-start = ((f32[8,7,4,8,128]{4,3,2,1,0:T(8,128)}), f32[8,7,4,8,128]{4,3,2,1,0:T(8,128)S(1)}, u32[]{:S(2)}, u32[]{:S(2)}) async-start(f32[8,7,4,8,128]{4,3,2,1,0:T(8,128)} %pad_maximum_fusion), calls=%async_computation | async-start | bytes 1835008 | tf_op jit(solution)/shard_map/all_to_all | solution.py:493
  24.7 34.4 %all-to-all-start.1 = ((f32[32,6,8,128]{3,2,1,0:T(8,128)}), f32[32,6,8,128]{3,2,1,0:T(8,128)S(1)}, u32[]{:S(2)}, u32[]{:S(2)}) async-start(f32[32,6,8,128]{3,2,1,0:T(8,128)} %bitcast.3), calls=%async_computation.1 | async-start | bytes 1572864 | tf_op jit(solution)/shard_map/all_to_all | solution.py:514
  30.3 12.0 %collective-permute-start.6 = (f32[1,10,4,8,128]{4,3,2,1,0:T(8,128)S(1)}, f32[1,10,4,8,128]{4,3,2,1,0:T(8,128)S(1)}, u32[]{:S(2)}, u32[]{:S(2)}) collective-permute-start(f32[1,10,4,8,128]{4,3,2,1,0:T(8,128)S(1)} %get-tuple-element.25), channel_id=1, source_target_pairs={{0,28},{4,24},{8,20},{12,16},{16,12},{20,8},{24,4},{28,0},{1,29},{... | collective-permute-start | bytes 491528 | tf_op jit(solution)/shard_map/ppermute | solution.py:466
  32.7 13.4 %collective-permute-start.4 = (f32[1,10,4,8,128]{4,3,2,1,0:T(8,128)S(1)}, f32[1,10,4,8,128]{4,3,2,1,0:T(8,128)S(1)}, u32[]{:S(2)}, u32[]{:S(2)}) collective-permute-start(f32[1,10,4,8,128]{4,3,2,1,0:T(8,128)S(1)} %get-tuple-element.26), channel_id=1, source_target_pairs={{0,20},{4,16},{8,28},{12,24},{16,4},{20,0},{24,12},{28,8},{1,21},{... | collective-permute-start | bytes 491528 | tf_op jit(solution)/shard_map/ppermute | solution.py:466
  33.3 17.7 %collective-permute-start.3 = (f32[1,10,4,8,128]{4,3,2,1,0:T(8,128)S(1)}, f32[1,10,4,8,128]{4,3,2,1,0:T(8,128)S(1)}, u32[]{:S(2)}, u32[]{:S(2)}) collective-permute-start(f32[1,10,4,8,128]{4,3,2,1,0:T(8,128)S(1)} %get-tuple-element.27), channel_id=1, source_target_pairs={{0,16},{4,20},{8,24},{12,28},{16,0},{20,4},{24,8},{28,12},{1,17},{... | collective-permute-start | bytes 491528 | tf_op jit(solution)/shard_map/ppermute | solution.py:466
  34.8 16.3 %collective-permute-start.2 = (f32[1,10,4,8,128]{4,3,2,1,0:T(8,128)S(1)}, f32[1,10,4,8,128]{4,3,2,1,0:T(8,128)S(1)}, u32[]{:S(2)}, u32[]{:S(2)}) collective-permute-start(f32[1,10,4,8,128]{4,3,2,1,0:T(8,128)S(1)} %get-tuple-element.28), channel_id=1, source_target_pairs={{0,12},{4,8},{8,4},{12,0},{16,28},{20,24},{24,20},{28,16},{1,13},{... | collective-permute-start | bytes 491528 | tf_op jit(solution)/shard_map/ppermute | solution.py:466
  34.8 16.3 %collective-permute-start.1 = (f32[1,10,4,8,128]{4,3,2,1,0:T(8,128)S(1)}, f32[1,10,4,8,128]{4,3,2,1,0:T(8,128)S(1)}, u32[]{:S(2)}, u32[]{:S(2)}) collective-permute-start(f32[1,10,4,8,128]{4,3,2,1,0:T(8,128)S(1)} %get-tuple-element.29), channel_id=1, source_target_pairs={{0,8},{4,12},{8,0},{12,4},{16,24},{20,28},{24,16},{28,20},{1,9},{5... | collective-permute-start | bytes 491528 | tf_op jit(solution)/shard_map/ppermute | solution.py:466
  42.3 8.7 %collective-permute-start = (f32[1,10,4,8,128]{4,3,2,1,0:T(8,128)S(1)}, f32[1,10,4,8,128]{4,3,2,1,0:T(8,128)S(1)}, u32[]{:S(2)}, u32[]{:S(2)}) collective-permute-start(f32[1,10,4,8,128]{4,3,2,1,0:T(8,128)S(1)} %get-tuple-element.30), channel_id=1, source_target_pairs={{0,4},{4,0},{8,12},{12,8},{16,20},{20,16},{24,28},{28,24},{1,5},{5... | collective-permute-start | bytes 491528 | tf_op jit(solution)/shard_map/ppermute | solution.py:466
  46.1 9.1 %collective-permute-start.5 = (f32[1,10,4,8,128]{4,3,2,1,0:T(8,128)S(1)}, f32[1,10,4,8,128]{4,3,2,1,0:T(8,128)S(1)}, u32[]{:S(2)}, u32[]{:S(2)}) collective-permute-start(f32[1,10,4,8,128]{4,3,2,1,0:T(8,128)S(1)} %get-tuple-element.32), channel_id=1, source_target_pairs={{0,24},{4,28},{8,16},{12,20},{16,8},{20,12},{24,0},{28,4},{1,25},{... | collective-permute-start | bytes 491528 | tf_op jit(solution)/shard_map/ppermute | solution.py:466
  99.0 4.4 %collective-permute-start.7 = (f32[10,16,128]{2,1,0:T(8,128)S(1)}, f32[10,16,128]{2,1,0:T(8,128)S(1)}, u32[]{:S(2)}, u32[]{:S(2)}) collective-permute-start(f32[10,16,128]{2,1,0:T(8,128)S(1)} %get-tuple-element.16), channel_id=1, source_target_pairs={{0,4},{4,0},{8,12},{12,8},{16,20},{20,16},{24,28},{28,24},{1,5},{5... | collective-permute-start | bytes 245768 | tf_op jit(solution)/shard_map/ppermute | solution.py:466
  99.0 96.3 %collective-permute-start.28 = (f32[2560,128]{1,0:T(8,128)S(1)}, f32[2560,128]{1,0:T(8,128)}, u32[]{:S(2)}, u32[]{:S(2)}) collective-permute-start(f32[2560,128]{1,0:T(8,128)S(1)} %bitcast.24), channel_id=1, source_target_pairs={{0,0},{1,2},{2,1},{3,3},{4,4},{5,6},{6,5},{7,7},{8,8},{9,10},{10,9... | collective-permute-start | bytes 3932168 | tf_op jit(solution)/shard_map/ppermute | solution.py:526
  100.8 94.6 %collective-permute-start.25 = (f32[2560,128]{1,0:T(8,128)S(1)}, f32[2560,128]{1,0:T(8,128)S(1)}, u32[]{:S(2)}, u32[]{:S(2)}) collective-permute-start(f32[2560,128]{1,0:T(8,128)S(1)} %bitcast.25), channel_id=1, source_target_pairs={{0,1},{1,0},{2,3},{3,2},{4,5},{5,4},{6,7},{7,6},{8,9},{9,8},{10,11... | collective-permute-start | bytes 3932168 | tf_op jit(solution)/shard_map/ppermute | solution.py:525
  102.2 5.2 %collective-permute-start.8 = (f32[10,16,128]{2,1,0:T(8,128)S(1)}, f32[10,16,128]{2,1,0:T(8,128)S(1)}, u32[]{:S(2)}, u32[]{:S(2)}) collective-permute-start(f32[10,16,128]{2,1,0:T(8,128)S(1)} %get-tuple-element.17), channel_id=1, source_target_pairs={{0,8},{4,12},{8,0},{12,4},{16,24},{20,28},{24,16},{28,20},{1,9},{5... | collective-permute-start | bytes 245768 | tf_op jit(solution)/shard_map/ppermute | solution.py:466
  102.9 4.7 %collective-permute-start.9 = (f32[10,16,128]{2,1,0:T(8,128)S(1)}, f32[10,16,128]{2,1,0:T(8,128)S(1)}, u32[]{:S(2)}, u32[]{:S(2)}) collective-permute-start(f32[10,16,128]{2,1,0:T(8,128)S(1)} %get-tuple-element.18), channel_id=1, source_target_pairs={{0,12},{4,8},{8,4},{12,0},{16,28},{20,24},{24,20},{28,16},{1,13},{... | collective-permute-start | bytes 245768 | tf_op jit(solution)/shard_map/ppermute | solution.py:466
  103.3 5.5 %collective-permute-start.10 = (f32[10,16,128]{2,1,0:T(8,128)S(1)}, f32[10,16,128]{2,1,0:T(8,128)S(1)}, u32[]{:S(2)}, u32[]{:S(2)}) collective-permute-start(f32[10,16,128]{2,1,0:T(8,128)S(1)} %get-tuple-element.19), channel_id=1, source_target_pairs={{0,16},{4,20},{8,24},{12,28},{16,0},{20,4},{24,8},{28,12},{1,17},{... | collective-permute-start | bytes 245768 | tf_op jit(solution)/shard_map/ppermute | solution.py:466
  107.4 3.9 %collective-permute-start.11 = (f32[10,16,128]{2,1,0:T(8,128)S(1)}, f32[10,16,128]{2,1,0:T(8,128)S(1)}, u32[]{:S(2)}, u32[]{:S(2)}) collective-permute-start(f32[10,16,128]{2,1,0:T(8,128)S(1)} %get-tuple-element.20), channel_id=1, source_target_pairs={{0,20},{4,16},{8,28},{12,24},{16,4},{20,0},{24,12},{28,8},{1,21},{... | collective-permute-start | bytes 245768 | tf_op jit(solution)/shard_map/ppermute | solution.py:466
  107.6 6.2 %collective-permute-start.12 = (f32[10,16,128]{2,1,0:T(8,128)S(1)}, f32[10,16,128]{2,1,0:T(8,128)S(1)}, u32[]{:S(2)}, u32[]{:S(2)}) collective-permute-start(f32[10,16,128]{2,1,0:T(8,128)S(1)} %get-tuple-element.21), channel_id=1, source_target_pairs={{0,24},{4,28},{8,16},{12,20},{16,8},{20,12},{24,0},{28,4},{1,25},{... | collective-permute-start | bytes 245768 | tf_op jit(solution)/shard_map/ppermute | solution.py:466
  108.9 6.6 %collective-permute-start.13 = (f32[10,16,128]{2,1,0:T(8,128)S(1)}, f32[10,16,128]{2,1,0:T(8,128)S(1)}, u32[]{:S(2)}, u32[]{:S(2)}) collective-permute-start(f32[10,16,128]{2,1,0:T(8,128)S(1)} %get-tuple-element.22), channel_id=1, source_target_pairs={{0,28},{4,24},{8,20},{12,16},{16,12},{20,8},{24,4},{28,0},{1,29},{... | collective-permute-start | bytes 245768 | tf_op jit(solution)/shard_map/ppermute | solution.py:466
  115.5 20.7 %collective-permute-start.16 = (f32[10,16,128]{2,1,0:T(8,128)S(1)}, f32[10,16,128]{2,1,0:T(8,128)S(1)}, u32[]{:S(2)}, u32[]{:S(2)}) collective-permute-start(f32[10,16,128]{2,1,0:T(8,128)S(1)} %add_add_fusion.2), channel_id=1, source_target_pairs={{0,3},{1,2},{2,1},{3,0},{4,7},{5,6},{6,5},{7,4},{8,11},{9,10},{10,... | collective-permute-start | bytes 245768 | tf_op jit(solution)/shard_map/ppermute | solution.py:466
  118.1 21.6 %collective-permute-start.15 = (f32[10,16,128]{2,1,0:T(8,128)S(1)}, f32[10,16,128]{2,1,0:T(8,128)S(1)}, u32[]{:S(2)}, u32[]{:S(2)}) collective-permute-start(f32[10,16,128]{2,1,0:T(8,128)S(1)} %add_add_fusion.2), channel_id=1, source_target_pairs={{0,2},{1,3},{2,0},{3,1},{4,6},{5,7},{6,4},{7,5},{8,10},{9,11},{10,... | collective-permute-start | bytes 245768 | tf_op jit(solution)/shard_map/ppermute | solution.py:466
  118.1 23.1 %collective-permute-start.14 = (f32[10,16,128]{2,1,0:T(8,128)S(1)}, f32[10,16,128]{2,1,0:T(8,128)S(1)}, u32[]{:S(2)}, u32[]{:S(2)}) collective-permute-start(f32[10,16,128]{2,1,0:T(8,128)S(1)} %add_add_fusion.2), channel_id=1, source_target_pairs={{0,1},{1,0},{2,3},{3,2},{4,5},{5,4},{6,7},{7,6},{8,9},{9,8},{10,11... | collective-permute-start | bytes 245768 | tf_op jit(solution)/shard_map/ppermute | solution.py:466
  136.2 59.2 %collective-permute-start.27 = (f32[1536,128]{1,0:T(8,128)S(1)}, f32[1536,128]{1,0:T(8,128)}, u32[]{:S(2)}, u32[]{:S(2)}) collective-permute-start(f32[1536,128]{1,0:T(8,128)S(1)} %bitcast.28), channel_id=1, source_target_pairs={{0,0},{1,2},{2,1},{3,3},{4,4},{5,6},{6,5},{7,7},{8,8},{9,10},{10,9... | collective-permute-start | bytes 2359304 | tf_op jit(solution)/shard_map/ppermute | solution.py:526
  139.7 55.7 %collective-permute-start.24 = (f32[1536,128]{1,0:T(8,128)S(1)}, f32[1536,128]{1,0:T(8,128)}, u32[]{:S(2)}, u32[]{:S(2)}) collective-permute-start(f32[1536,128]{1,0:T(8,128)S(1)} %bitcast.29), channel_id=1, source_target_pairs={{0,1},{1,0},{2,3},{3,2},{4,5},{5,4},{6,7},{7,6},{8,9},{9,8},{10,11... | collective-permute-start | bytes 2359304 | tf_op jit(solution)/shard_map/ppermute | solution.py:525
  141.2 4.8 %collective-permute-start.23 = (f32[10,16,128]{2,1,0:T(8,128)S(1)}, f32[10,16,128]{2,1,0:T(8,128)S(1)}, u32[]{:S(2)}, u32[]{:S(2)}) collective-permute-start(f32[10,16,128]{2,1,0:T(8,128)S(1)} %add_add_fusion.1.refs_0_), channel_id=1, source_target_pairs={{0,28},{4,24},{8,20},{12,16},{16,12},{20,8},{24,4},{28,0},{1,29},{... | collective-permute-start | bytes 245768 | tf_op jit(solution)/shard_map/ppermute | solution.py:466
  146.1 0.6 copy-start
  146.7 5.3 %collective-permute-start.22 = (f32[10,16,128]{2,1,0:T(8,128)S(1)}, f32[10,16,128]{2,1,0:T(8,128)S(1)}, u32[]{:S(2)}, u32[]{:S(2)}) collective-permute-start(f32[10,16,128]{2,1,0:T(8,128)S(1)} %add_add_fusion.1.refs_0_), channel_id=1, source_target_pairs={{0,24},{4,28},{8,16},{12,20},{16,8},{20,12},{24,0},{28,4},{1,25},{... | collective-permute-start | bytes 245768 | tf_op jit(solution)/shard_map/ppermute | solution.py:466
  152.0 0.6 copy-start.2
  152.7 4.0 %collective-permute-start.21 = (f32[10,16,128]{2,1,0:T(8,128)S(1)}, f32[10,16,128]{2,1,0:T(8,128)S(1)}, u32[]{:S(2)}, u32[]{:S(2)}) collective-permute-start(f32[10,16,128]{2,1,0:T(8,128)S(1)} %add_add_fusion.1.refs_0_), channel_id=1, source_target_pairs={{0,20},{4,16},{8,28},{12,24},{16,4},{20,0},{24,12},{28,8},{1,21},{... | collective-permute-start | bytes 245768 | tf_op jit(solution)/shard_map/ppermute | solution.py:466
  156.6 0.6 copy-start.4
  157.2 4.4 %collective-permute-start.20 = (f32[10,16,128]{2,1,0:T(8,128)S(1)}, f32[10,16,128]{2,1,0:T(8,128)S(1)}, u32[]{:S(2)}, u32[]{:S(2)}) collective-permute-start(f32[10,16,128]{2,1,0:T(8,128)S(1)} %add_add_fusion.1.refs_0_), channel_id=1, source_target_pairs={{0,16},{4,20},{8,24},{12,28},{16,0},{20,4},{24,8},{28,12},{1,17},{... | collective-permute-start | bytes 245768 | tf_op jit(solution)/shard_map/ppermute | solution.py:466
  161.7 0.6 copy-start.6
  162.3 4.7 %collective-permute-start.19 = (f32[10,16,128]{2,1,0:T(8,128)S(1)}, f32[10,16,128]{2,1,0:T(8,128)S(1)}, u32[]{:S(2)}, u32[]{:S(2)}) collective-permute-start(f32[10,16,128]{2,1,0:T(8,128)S(1)} %add_add_fusion.1.refs_0_), channel_id=1, source_target_pairs={{0,12},{4,8},{8,4},{12,0},{16,28},{20,24},{24,20},{28,16},{1,13},{... | collective-permute-start | bytes 245768 | tf_op jit(solution)/shard_map/ppermute | solution.py:466
  167.0 0.6 copy-start.8
  167.7 4.4 %collective-permute-start.18 = (f32[10,16,128]{2,1,0:T(8,128)S(1)}, f32[10,16,128]{2,1,0:T(8,128)S(1)}, u32[]{:S(2)}, u32[]{:S(2)}) collective-permute-start(f32[10,16,128]{2,1,0:T(8,128)S(1)} %add_add_fusion.1.refs_0_), channel_id=1, source_target_pairs={{0,8},{4,12},{8,0},{12,4},{16,24},{20,28},{24,16},{28,20},{1,9},{5... | collective-permute-start | bytes 245768 | tf_op jit(solution)/shard_map/ppermute | solution.py:466
  172.1 0.6 copy-start.10
  172.7 1.4 collective-permute-start.17
  174.1 0.9 copy-start.1
  175.0 0.9 copy-start.3
  175.9 0.9 copy-start.5
  176.8 0.9 copy-start.7
  177.7 0.9 copy-start.9
  178.6 0.9 copy-start.11
  200.4 12.4 %collective-permute-start.29 = (f32[128,8,128]{2,1,0:T(8,128)S(1)}, f32[128,8,128]{2,1,0:T(8,128)S(1)}, u32[]{:S(2)}, u32[]{:S(2)}) collective-permute-start(f32[128,8,128]{2,1,0:T(8,128)S(1)} %get-tuple-element.23), channel_id=1, source_target_pairs={{0,0},{1,2},{2,1},{3,3},{4,4},{5,6},{6,5},{7,7},{8,8},{9,10},{10,9... | collective-permute-start | bytes 1572872 | tf_op jit(solution)/shard_map/ppermute | solution.py:539
  201.1 15.3 %collective-permute-start.30 = (f32[128,8,128]{2,1,0:T(8,128)S(1)}, f32[128,8,128]{2,1,0:T(8,128)S(1)}, u32[]{:S(2)}, u32[]{:S(2)}) collective-permute-start(f32[128,8,128]{2,1,0:T(8,128)S(1)} %get-tuple-element.24), channel_id=1, source_target_pairs={{0,1},{1,0},{2,3},{3,2},{4,5},{5,4},{6,7},{7,6},{8,9},{9,8},{10,11... | collective-permute-start | bytes 1572872 | tf_op jit(solution)/shard_map/ppermute | solution.py:540
  206.6 20.9 %collective-permute-start.26 = (f32[128,8,128]{2,1,0:T(8,128)S(1)}, f32[128,8,128]{2,1,0:T(8,128)S(1)}, u32[]{:S(2)}, u32[]{:S(2)}) collective-permute-start(f32[128,8,128]{2,1,0:T(8,128)S(1)} %rotate_far.2), channel_id=1, source_target_pairs={{0,1},{1,3},{2,0},{3,2},{4,5},{5,7},{6,4},{7,6},{8,9},{9,11},{10,8... | collective-permute-start | bytes 1572872 | tf_op jit(solution)/shard_map/ppermute | solution.py:538

commit v7 on v6

--- a/solution.py
+++ b/solution.py
@@ -152,9 +152,10 @@
         rest = pl.ds(i * size, norb - i * size)
         h, l = high[mine, :], low[mine, :]
         hr, lr = high[rest, :], low[rest, :]
+        both = jnp.concatenate([h, l], axis=0)
+        both = lax.dot_general(both, hr, contract, preferred_element_type=f32)
         total = lax.dot_general(h, lr, contract, preferred_element_type=f32)
-        total = total + lax.dot_general(l, hr, contract, preferred_element_type=f32)
-        total = total + lax.dot_general(h, hr, contract, preferred_element_type=f32)
+        total = both[:size] + (both[size:] + total)
         for j in range(norb // size - i):
             acc[at] = total[:, j * size : (j + 1) * size]
             at += 1
@@ -320,7 +321,9 @@
 
 def product(weights, high, low):
     h, l = split(weights)
-    return mm(h, low) + mm(l, high) + mm(h, high)
+    count = h.shape[0]
+    both = mm(jnp.concatenate([h, l], axis=0), high)
+    return both[:count] + (both[count:] + mm(h, low))
 
 
 def put_rows(out, value, rows, cols):

time: 229 us -> 228 us (level)
  no operation moved by 1% of the time
where the time goes in v7:
time: 228 us
  waiting for transfers between devices  96.3 us (42%)
  starting transfers between devices  40.7 us (18%)
  Pallas kernels  39.3 us (17%)
  blocking collectives  37 us (16%)
  local copies, waits for them, and re-layouts  11.8 us (5%)
    ppermute x24, waiting for transfers between devices, swap_all(): lax.ppermute(pieces[s], axis, [(i, i ^ s) for i in range(count)])  68.3 us
    all_to_all x1, blocking collectives, orthonormalized(): lax.all_to_all(filtered, everyone, split_axis=0, concat_axis=0, tiled=True)  37 us
    ppermute x24, starting transfers between devices, swap_all(): lax.ppermute(pieces[s], axis, [(i, i ^ s) for i in range(count)])  21.6 us
    pallas_call x1, Pallas kernels, inverse_rows(): pl.pallas_call(functools.partial(inverse_kernel, factor), out_shape=jax.S...  15.9 us
    all_to_all x1, waiting for transfers between devices, orthonormalized(): lax.all_to_all(first, 'grid', split_axis=0, concat_axis=0, tiled=True)  12.9 us
    ppermute x1, waiting for transfers between devices, orthonormalized(): skip = lax.ppermute(skip, 'orb', [(0, 1), (1, 3), (2, 0), (3, 2)])  11.1 us
    unnamed x24, local copies, waits for them, and re-layouts  9.1 us
    pallas_call x2, Pallas kernels, rotate_for_others(): pl.pallas_call(functools.partial(kernel, spec), out_shape=[jax.ShapeDtype...  7.26 us
  transfers between devices with their start and end apart: 33, of which 21 were waited for; matrix products, arithmetic and copies ran while one was open for 1% of the time, Pallas kernels for 12%

profile of v7, /device:TPU:0, one launch (start us, length us, event | category | flops | bytes accessed | tf_op | source)
XLA Modules:
  0.0 227.7 jit_solution(1594421692208344778)
XLA Ops:
  1.1 1.0 pad_maximum_fusion
  2.2 5.2 %all-to-all-start = ((f32[8,7,4,8,128]{4,3,2,1,0:T(8,128)}), f32[8,7,4,8,128]{4,3,2,1,0:T(8,128)S(1)}, u32[]{:S(2)}, u32[]{:S(2)}) async-start(f32[8,7,4,8,128]{4,3,2,1,0:T(8,128)} %pad_maximum_fusion), calls=%async_computation | async-start | bytes 1835008 | tf_op jit(solution)/shard_map/all_to_all | solution.py:496
  8.5 12.9 %all-to-all-done.pot_ref.refs_0_ = f32[8,7,4,8,128]{4,3,2,1,0:T(8,128)S(1)} async-done(((f32[8,7,4,8,128]{4,3,2,1,0:T(8,128)}), f32[8,7,4,8,128]{4,3,2,1,0:T(8,128)S(1)}, u32[]{:S(2)}, u32[]{:S(2)}) %all-to-all-start) | async-done | bytes 917536 | tf_op jit(solution)/shard_map/all_to_all | solution.py:496
  21.3 3.3 %filter.2 = f32[4,8,6,8,128]{4,3,2,1,0:T(8,128)} custom-call(s32[1]{0:T(128)} %bitcast.1.place_ref, bf16[256,256]{1,0:T(8,128)(2,1)S(1)} %fusion.6.xy_ref, bf16[256,256]{1,0:T(8,128)(2,1)S(1)} %select_convert_fusion.z_ref, f32[8,7,4,8,128]{4,3,2,1,0:T(8,128)S(1)} %all-to-all-done.pot_ref.refs_0_, f32[8,7,4,8,128]{4,3,2,1,0:T(8,128)S(1)} %all-to-all-done.pot_ref.refs_0_), custom_call_target="tpu_custom_call" | custom-call | tf_op jit(solution)/shard_map/filter/pallas_call | solution.py:102
  24.7 4.0 %all-to-all-start.1 = ((f32[32,6,8,128]{3,2,1,0:T(8,128)}), f32[32,6,8,128]{3,2,1,0:T(8,128)S(1)}, u32[]{:S(2)}, u32[]{:S(2)}) async-start(f32[32,6,8,128]{3,2,1,0:T(8,128)} %bitcast.3), calls=%async_computation.1 | async-start | bytes 1572864 | tf_op jit(solution)/shard_map/all_to_all | solution.py:517
  28.7 1.6 dynamic-slice_bitcast_fusion
  30.3 2.5 %collective-permute-start.6 = (f32[1,10,4,8,128]{4,3,2,1,0:T(8,128)S(1)}, f32[1,10,4,8,128]{4,3,2,1,0:T(8,128)S(1)}, u32[]{:S(2)}, u32[]{:S(2)}) collective-permute-start(f32[1,10,4,8,128]{4,3,2,1,0:T(8,128)S(1)} %get-tuple-element.25), channel_id=1, source_target_pairs={{0,28},{4,24},{8,20},{12,16},{16,12},{20,8},{24,4},{28,0},{1,29},{... | collective-permute-start | bytes 491528 | tf_op jit(solution)/shard_map/ppermute | solution.py:469
  33.3 1.5 collective-permute-start.3
  34.8 1.5 collective-permute-start.1
  36.2 6.1 %collective-permute-done.6.refs_7_ = f32[1,10,4,8,128]{4,3,2,1,0:T(8,128)S(1)} collective-permute-done((f32[1,10,4,8,128]{4,3,2,1,0:T(8,128)S(1)}, f32[1,10,4,8,128]{4,3,2,1,0:T(8,128)S(1)}, u32[]{:S(2)}, u32[]{:S(2)}) %collective-permute-start.6) | collective-permute-done | bytes 163872 | tf_op jit(solution)/shard_map/ppermute | solution.py:469
  42.3 1.4 collective-permute-start
  43.7 2.4 %collective-permute-done.4.refs_5_ = f32[1,10,4,8,128]{4,3,2,1,0:T(8,128)S(1)} collective-permute-done((f32[1,10,4,8,128]{4,3,2,1,0:T(8,128)S(1)}, f32[1,10,4,8,128]{4,3,2,1,0:T(8,128)S(1)}, u32[]{:S(2)}, u32[]{:S(2)}) %collective-permute-start.4) | collective-permute-done | bytes 163872 | tf_op jit(solution)/shard_map/ppermute | solution.py:469
  46.9 4.1 %collective-permute-done.3.refs_4_ = f32[1,10,4,8,128]{4,3,2,1,0:T(8,128)S(1)} collective-permute-done((f32[1,10,4,8,128]{4,3,2,1,0:T(8,128)S(1)}, f32[1,10,4,8,128]{4,3,2,1,0:T(8,128)S(1)}, u32[]{:S(2)}, u32[]{:S(2)}) %collective-permute-start.3) | collective-permute-done | bytes 163872 | tf_op jit(solution)/shard_map/ppermute | solution.py:469
  51.0 4.1 %collective-permute-done.5.refs_6_ = f32[1,10,4,8,128]{4,3,2,1,0:T(8,128)S(1)} collective-permute-done((f32[1,10,4,8,128]{4,3,2,1,0:T(8,128)S(1)}, f32[1,10,4,8,128]{4,3,2,1,0:T(8,128)S(1)}, u32[]{:S(2)}, u32[]{:S(2)}) %collective-permute-start.5) | collective-permute-done | bytes 163872 | tf_op jit(solution)/shard_map/ppermute | solution.py:469
  55.2 3.9 %filter.3 = f32[4,8,10,8,128]{4,3,2,1,0:T(8,128)S(1)} custom-call(s32[1]{0:T(128)} %bitcast.1.place_ref, bf16[256,256]{1,0:T(8,128)(2,1)S(1)} %fusion.6.xy_ref, bf16[256,256]{1,0:T(8,128)(2,1)S(1)} %select_convert_fusion.z_ref, f32[8,7,4,8,128]{4,3,2,1,0:T(8,128)S(1)} %all-to-all-done.pot_ref.refs_0_, f32[1,10,4,8,128]{4,3,2,1,0:T(8,128)S(1)} %get-tuple-element.31.refs_0_, ...), custom_call_target="tpu_custom_call" | custom-call | tf_op jit(solution)/shard_map/filter/pallas_call | solution.py:102
  59.0 37.0 %all_to_all.15 = f32[32,10,8,128]{3,2,1,0:T(8,128)S(1)} all-to-all(f32[32,10,8,128]{3,2,1,0:T(8,128)S(1)} %bitcast.31), channel_id=1, replica_groups=mesh['grid'=8,'orb'=4] {'orb','grid'}, dimensions={0} | all-to-all | bytes 2621440 | tf_op jit(solution)/shard_map/all_to_all | solution.py:517
  96.1 2.1 margin.1
  98.3 1.8 collective-permute-start.28
  100.1 1.4 collective-permute-start.25
  103.2 3.5 %collective-permute-done.8 = f32[10,16,128]{2,1,0:T(8,128)S(1)} collective-permute-done((f32[10,16,128]{2,1,0:T(8,128)S(1)}, f32[10,16,128]{2,1,0:T(8,128)S(1)}, u32[]{:S(2)}, u32[]{:S(2)}) %collective-permute-start.8) | collective-permute-done | bytes 81952 | tf_op jit(solution)/shard_map/ppermute | solution.py:469
  106.9 1.3 collective-permute-start.12
  108.1 1.9 collective-permute-start.13
  110.6 2.5 %collective-permute-done.12 = f32[10,16,128]{2,1,0:T(8,128)S(1)} collective-permute-done((f32[10,16,128]{2,1,0:T(8,128)S(1)}, f32[10,16,128]{2,1,0:T(8,128)S(1)}, u32[]{:S(2)}, u32[]{:S(2)}) %collective-permute-start.12) | collective-permute-done | bytes 81952 | tf_op jit(solution)/shard_map/ppermute | solution.py:469
  113.1 1.6 collective-permute-done.13
  114.8 2.6 %collective-permute-start.16 = (f32[10,16,128]{2,1,0:T(8,128)S(1)}, f32[10,16,128]{2,1,0:T(8,128)S(1)}, u32[]{:S(2)}, u32[]{:S(2)}) collective-permute-start(f32[10,16,128]{2,1,0:T(8,128)S(1)} %add_add_fusion.2), channel_id=1, source_target_pairs={{0,3},{1,2},{2,1},{3,0},{4,7},{5,6},{6,5},{7,4},{8,11},{9,10},{10,... | collective-permute-start | bytes 245768 | tf_op jit(solution)/shard_map/ppermute | solution.py:469
  117.3 1.9 collective-permute-start.14
  119.2 16.2 %collective-permute-done.16 = f32[10,16,128]{2,1,0:T(8,128)S(1)} collective-permute-done((f32[10,16,128]{2,1,0:T(8,128)S(1)}, f32[10,16,128]{2,1,0:T(8,128)S(1)}, u32[]{:S(2)}, u32[]{:S(2)}) %collective-permute-start.16) | collective-permute-done | bytes 81952 | tf_op jit(solution)/shard_map/ppermute | solution.py:469
  135.4 1.5 collective-permute-start.27
  137.0 2.0 collective-permute-done.15
  139.0 1.5 collective-permute-start.24
  140.6 4.8 %collective-permute-done.23.refs_7_ = f32[10,16,128]{2,1,0:T(8,128)S(1)} collective-permute-done((f32[10,16,128]{2,1,0:T(8,128)S(1)}, f32[10,16,128]{2,1,0:T(8,128)S(1)}, u32[]{:S(2)}, u32[]{:S(2)}) %collective-permute-start.23) | collective-permute-done | bytes 81952 | tf_op jit(solution)/shard_map/ppermute | solution.py:469
  146.0 1.5 collective-permute-start.22
  147.4 3.9 %collective-permute-done.22.refs_6_ = f32[10,16,128]{2,1,0:T(8,128)S(1)} collective-permute-done((f32[10,16,128]{2,1,0:T(8,128)S(1)}, f32[10,16,128]{2,1,0:T(8,128)S(1)}, u32[]{:S(2)}, u32[]{:S(2)}) %collective-permute-start.22) | collective-permute-done | bytes 81952 | tf_op jit(solution)/shard_map/ppermute | solution.py:469
  151.9 4.0 %collective-permute-done.21.refs_5_ = f32[10,16,128]{2,1,0:T(8,128)S(1)} collective-permute-done((f32[10,16,128]{2,1,0:T(8,128)S(1)}, f32[10,16,128]{2,1,0:T(8,128)S(1)}, u32[]{:S(2)}, u32[]{:S(2)}) %collective-permute-start.21) | collective-permute-done | bytes 81952 | tf_op jit(solution)/shard_map/ppermute | solution.py:469
  156.5 1.4 collective-permute-start.20
  157.9 3.1 %collective-permute-done.20.refs_4_ = f32[10,16,128]{2,1,0:T(8,128)S(1)} collective-permute-done((f32[10,16,128]{2,1,0:T(8,128)S(1)}, f32[10,16,128]{2,1,0:T(8,128)S(1)}, u32[]{:S(2)}, u32[]{:S(2)}) %collective-permute-start.20) | collective-permute-done | bytes 81952 | tf_op jit(solution)/shard_map/ppermute | solution.py:469
  161.9 4.4 %collective-permute-done.19.refs_3_ = f32[10,16,128]{2,1,0:T(8,128)S(1)} collective-permute-done((f32[10,16,128]{2,1,0:T(8,128)S(1)}, f32[10,16,128]{2,1,0:T(8,128)S(1)}, u32[]{:S(2)}, u32[]{:S(2)}) %collective-permute-start.19) | collective-permute-done | bytes 81952 | tf_op jit(solution)/shard_map/ppermute | solution.py:469
  166.9 0.9 collective-permute-start.18
  167.8 3.5 %collective-permute-done.18.refs_2_ = f32[10,16,128]{2,1,0:T(8,128)S(1)} collective-permute-done((f32[10,16,128]{2,1,0:T(8,128)S(1)}, f32[10,16,128]{2,1,0:T(8,128)S(1)}, u32[]{:S(2)}, u32[]{:S(2)}) %collective-permute-start.18) | collective-permute-done | bytes 81952 | tf_op jit(solution)/shard_map/ppermute | solution.py:469
  172.0 1.4 collective-permute-done.17.refs_1_
  178.7 15.9 %inverse.1.v_ref = f32[4,128,512]{2,1,0:T(8,128)S(1)} custom-call(s32[1]{0:T(128)} %bitcast.1.place_ref, f32[10,16,128]{2,1,0:T(8,128)S(1)} %add_add_fusion.1.refs_0_, f32[10,16,128]{2,1,0:T(8,128)} %collective-permute-done.17.refs_1_, f32[10,16,128]{2,1,0:T(8,128)S(1)} %copy-done.11, f32[10,16,128]{2,1,0:T(8,128)S(1)} %copy-done.9, ...), custom_call_target="tpu_custom_call" | custom-call | tf_op jit(solution)/shard_map/inverse/pallas_call | solution.py:311
  194.7 4.8 %rotate_far.3 = (f32[128,8,128]{2,1,0:T(8,128)S(1)}, f32[128,8,128]{2,1,0:T(8,128)S(1)}) custom-call(s32[1]{0:T(128)} %bitcast.layer_ref, f32[4,128,512]{2,1,0:T(8,128)S(1)} %inverse.1.v_ref, f32[1536,128]{1,0:T(8,128)} %collective-permute-done.24.refs_0_.refs_2_, f32[2560,128]{1,0:T(8,128)S(1)} %collective-permute-done.25.refs_1_.refs_3_, ...), custom_call_target="tpu_custom_call" | custom-call | tf_op jit(solution)/shard_map/rotate_far/pallas_call | solution.py:391
  200.2 2.9 %collective-permute-start.30 = (f32[128,8,128]{2,1,0:T(8,128)S(1)}, f32[128,8,128]{2,1,0:T(8,128)S(1)}, u32[]{:S(2)}, u32[]{:S(2)}) collective-permute-start(f32[128,8,128]{2,1,0:T(8,128)S(1)} %get-tuple-element.24), channel_id=1, source_target_pairs={{0,1},{1,0},{2,3},{3,2},{4,5},{5,4},{6,7},{7,6},{8,9},{9,8},{10,11... | collective-permute-start | bytes 1572872 | tf_op jit(solution)/shard_map/ppermute | solution.py:543
  203.0 2.4 %rotate_far.2 = f32[128,8,128]{2,1,0:T(8,128)S(1)} custom-call(s32[1]{0:T(128)} %bitcast.layer_ref, f32[4,128,512]{2,1,0:T(8,128)S(1)} %inverse.1.v_ref, f32[1536,128]{1,0:T(8,128)} %collective-permute-done.24.refs_0_.refs_2_, f32[2560,128]{1,0:T(8,128)S(1)} %collective-permute-done.25.refs_1_.refs_3_), custom_call_target="tpu_custom_call" | custom-call | tf_op jit(solution)/shard_map/rotate_far/pallas_call | solution.py:391
  205.6 5.9 %rotate_near.1.near_ref = f32[128,4,8,128]{3,2,1,0:T(8,128)} custom-call(s32[1]{0:T(128)} %bitcast.layer_ref, f32[4,128,512]{2,1,0:T(8,128)S(1)} %inverse.1.v_ref, f32[1536,128]{1,0:T(8,128)S(1)} %bitcast.30, f32[2560,128]{1,0:T(8,128)S(1)} %bitcast.26, f32[1536,128]{1,0:T(8,128)} %collective-permute-done.24.refs_0_.refs_2_, ...), custom_call_target="tpu_custom_call" | custom-call | tf_op jit(solution)/shard_map/rotate_near/pallas_call | solution.py:427
  211.5 4.1 %collective-permute-done.30.back = f32[128,8,128]{2,1,0:T(8,128)S(1)} collective-permute-done((f32[128,8,128]{2,1,0:T(8,128)S(1)}, f32[128,8,128]{2,1,0:T(8,128)S(1)}, u32[]{:S(2)}, u32[]{:S(2)}) %collective-permute-start.30) | collective-permute-done | bytes 524320 | tf_op jit(solution)/shard_map/ppermute | solution.py:543
  215.5 11.1 %collective-permute-done.26.skip = f32[128,8,128]{2,1,0:T(8,128)S(1)} collective-permute-done((f32[128,8,128]{2,1,0:T(8,128)S(1)}, f32[128,8,128]{2,1,0:T(8,128)S(1)}, u32[]{:S(2)}, u32[]{:S(2)}) %collective-permute-start.26) | collective-permute-done | bytes 524320 | tf_op jit(solution)/shard_map/ppermute | solution.py:541
  226.6 1.0 join.1
  (65 shorter events, 16.4 us)
Async XLA Ops:
  0.0 1.1 slice-start
  2.2 19.2 %all-to-all-start = ((f32[8,7,4,8,128]{4,3,2,1,0:T(8,128)}), f32[8,7,4,8,128]{4,3,2,1,0:T(8,128)S(1)}, u32[]{:S(2)}, u32[]{:S(2)}) async-start(f32[8,7,4,8,128]{4,3,2,1,0:T(8,128)} %pad_maximum_fusion), calls=%async_computation | async-start | bytes 1835008 | tf_op jit(solution)/shard_map/all_to_all | solution.py:496
  24.7 34.4 %all-to-all-start.1 = ((f32[32,6,8,128]{3,2,1,0:T(8,128)}), f32[32,6,8,128]{3,2,1,0:T(8,128)S(1)}, u32[]{:S(2)}, u32[]{:S(2)}) async-start(f32[32,6,8,128]{3,2,1,0:T(8,128)} %bitcast.3), calls=%async_computation.1 | async-start | bytes 1572864 | tf_op jit(solution)/shard_map/all_to_all | solution.py:517
  30.3 12.0 %collective-permute-start.6 = (f32[1,10,4,8,128]{4,3,2,1,0:T(8,128)S(1)}, f32[1,10,4,8,128]{4,3,2,1,0:T(8,128)S(1)}, u32[]{:S(2)}, u32[]{:S(2)}) collective-permute-start(f32[1,10,4,8,128]{4,3,2,1,0:T(8,128)S(1)} %get-tuple-element.25), channel_id=1, source_target_pairs={{0,28},{4,24},{8,20},{12,16},{16,12},{20,8},{24,4},{28,0},{1,29},{... | collective-permute-start | bytes 491528 | tf_op jit(solution)/shard_map/ppermute | solution.py:469
  32.7 13.4 %collective-permute-start.4 = (f32[1,10,4,8,128]{4,3,2,1,0:T(8,128)S(1)}, f32[1,10,4,8,128]{4,3,2,1,0:T(8,128)S(1)}, u32[]{:S(2)}, u32[]{:S(2)}) collective-permute-start(f32[1,10,4,8,128]{4,3,2,1,0:T(8,128)S(1)} %get-tuple-element.26), channel_id=1, source_target_pairs={{0,20},{4,16},{8,28},{12,24},{16,4},{20,0},{24,12},{28,8},{1,21},{... | collective-permute-start | bytes 491528 | tf_op jit(solution)/shard_map/ppermute | solution.py:469
  33.3 17.7 %collective-permute-start.3 = (f32[1,10,4,8,128]{4,3,2,1,0:T(8,128)S(1)}, f32[1,10,4,8,128]{4,3,2,1,0:T(8,128)S(1)}, u32[]{:S(2)}, u32[]{:S(2)}) collective-permute-start(f32[1,10,4,8,128]{4,3,2,1,0:T(8,128)S(1)} %get-tuple-element.27), channel_id=1, source_target_pairs={{0,16},{4,20},{8,24},{12,28},{16,0},{20,4},{24,8},{28,12},{1,17},{... | collective-permute-start | bytes 491528 | tf_op jit(solution)/shard_map/ppermute | solution.py:469
  34.8 16.3 %collective-permute-start.2 = (f32[1,10,4,8,128]{4,3,2,1,0:T(8,128)S(1)}, f32[1,10,4,8,128]{4,3,2,1,0:T(8,128)S(1)}, u32[]{:S(2)}, u32[]{:S(2)}) collective-permute-start(f32[1,10,4,8,128]{4,3,2,1,0:T(8,128)S(1)} %get-tuple-element.28), channel_id=1, source_target_pairs={{0,12},{4,8},{8,4},{12,0},{16,28},{20,24},{24,20},{28,16},{1,13},{... | collective-permute-start | bytes 491528 | tf_op jit(solution)/shard_map/ppermute | solution.py:469
  34.8 16.3 %collective-permute-start.1 = (f32[1,10,4,8,128]{4,3,2,1,0:T(8,128)S(1)}, f32[1,10,4,8,128]{4,3,2,1,0:T(8,128)S(1)}, u32[]{:S(2)}, u32[]{:S(2)}) collective-permute-start(f32[1,10,4,8,128]{4,3,2,1,0:T(8,128)S(1)} %get-tuple-element.29), channel_id=1, source_target_pairs={{0,8},{4,12},{8,0},{12,4},{16,24},{20,28},{24,16},{28,20},{1,9},{5... | collective-permute-start | bytes 491528 | tf_op jit(solution)/shard_map/ppermute | solution.py:469
  42.3 8.7 %collective-permute-start = (f32[1,10,4,8,128]{4,3,2,1,0:T(8,128)S(1)}, f32[1,10,4,8,128]{4,3,2,1,0:T(8,128)S(1)}, u32[]{:S(2)}, u32[]{:S(2)}) collective-permute-start(f32[1,10,4,8,128]{4,3,2,1,0:T(8,128)S(1)} %get-tuple-element.30), channel_id=1, source_target_pairs={{0,4},{4,0},{8,12},{12,8},{16,20},{20,16},{24,28},{28,24},{1,5},{5... | collective-permute-start | bytes 491528 | tf_op jit(solution)/shard_map/ppermute | solution.py:469
  46.1 9.1 %collective-permute-start.5 = (f32[1,10,4,8,128]{4,3,2,1,0:T(8,128)S(1)}, f32[1,10,4,8,128]{4,3,2,1,0:T(8,128)S(1)}, u32[]{:S(2)}, u32[]{:S(2)}) collective-permute-start(f32[1,10,4,8,128]{4,3,2,1,0:T(8,128)S(1)} %get-tuple-element.32), channel_id=1, source_target_pairs={{0,24},{4,28},{8,16},{12,20},{16,8},{20,12},{24,0},{28,4},{1,25},{... | collective-permute-start | bytes 491528 | tf_op jit(solution)/shard_map/ppermute | solution.py:469
  98.2 4.4 %collective-permute-start.7 = (f32[10,16,128]{2,1,0:T(8,128)S(1)}, f32[10,16,128]{2,1,0:T(8,128)S(1)}, u32[]{:S(2)}, u32[]{:S(2)}) collective-permute-start(f32[10,16,128]{2,1,0:T(8,128)S(1)} %get-tuple-element.16), channel_id=1, source_target_pairs={{0,4},{4,0},{8,12},{12,8},{16,20},{20,16},{24,28},{28,24},{1,5},{5... | collective-permute-start | bytes 245768 | tf_op jit(solution)/shard_map/ppermute | solution.py:469
  98.3 96.3 %collective-permute-start.28 = (f32[2560,128]{1,0:T(8,128)S(1)}, f32[2560,128]{1,0:T(8,128)}, u32[]{:S(2)}, u32[]{:S(2)}) collective-permute-start(f32[2560,128]{1,0:T(8,128)S(1)} %bitcast.24), channel_id=1, source_target_pairs={{0,0},{1,2},{2,1},{3,3},{4,4},{5,6},{6,5},{7,7},{8,8},{9,10},{10,9... | collective-permute-start | bytes 3932168 | tf_op jit(solution)/shard_map/ppermute | solution.py:529
  100.1 94.6 %collective-permute-start.25 = (f32[2560,128]{1,0:T(8,128)S(1)}, f32[2560,128]{1,0:T(8,128)S(1)}, u32[]{:S(2)}, u32[]{:S(2)}) collective-permute-start(f32[2560,128]{1,0:T(8,128)S(1)} %bitcast.25), channel_id=1, source_target_pairs={{0,1},{1,0},{2,3},{3,2},{4,5},{5,4},{6,7},{7,6},{8,9},{9,8},{10,11... | collective-permute-start | bytes 3932168 | tf_op jit(solution)/shard_map/ppermute | solution.py:528
  101.5 5.2 %collective-permute-start.8 = (f32[10,16,128]{2,1,0:T(8,128)S(1)}, f32[10,16,128]{2,1,0:T(8,128)S(1)}, u32[]{:S(2)}, u32[]{:S(2)}) collective-permute-start(f32[10,16,128]{2,1,0:T(8,128)S(1)} %get-tuple-element.17), channel_id=1, source_target_pairs={{0,8},{4,12},{8,0},{12,4},{16,24},{20,28},{24,16},{28,20},{1,9},{5... | collective-permute-start | bytes 245768 | tf_op jit(solution)/shard_map/ppermute | solution.py:469
  102.1 4.7 %collective-permute-start.9 = (f32[10,16,128]{2,1,0:T(8,128)S(1)}, f32[10,16,128]{2,1,0:T(8,128)S(1)}, u32[]{:S(2)}, u32[]{:S(2)}) collective-permute-start(f32[10,16,128]{2,1,0:T(8,128)S(1)} %get-tuple-element.18), channel_id=1, source_target_pairs={{0,12},{4,8},{8,4},{12,0},{16,28},{20,24},{24,20},{28,16},{1,13},{... | collective-permute-start | bytes 245768 | tf_op jit(solution)/shard_map/ppermute | solution.py:469
  102.6 5.5 %collective-permute-start.10 = (f32[10,16,128]{2,1,0:T(8,128)S(1)}, f32[10,16,128]{2,1,0:T(8,128)S(1)}, u32[]{:S(2)}, u32[]{:S(2)}) collective-permute-start(f32[10,16,128]{2,1,0:T(8,128)S(1)} %get-tuple-element.19), channel_id=1, source_target_pairs={{0,16},{4,20},{8,24},{12,28},{16,0},{20,4},{24,8},{28,12},{1,17},{... | collective-permute-start | bytes 245768 | tf_op jit(solution)/shard_map/ppermute | solution.py:469
  106.7 3.9 %collective-permute-start.11 = (f32[10,16,128]{2,1,0:T(8,128)S(1)}, f32[10,16,128]{2,1,0:T(8,128)S(1)}, u32[]{:S(2)}, u32[]{:S(2)}) collective-permute-start(f32[10,16,128]{2,1,0:T(8,128)S(1)} %get-tuple-element.20), channel_id=1, source_target_pairs={{0,20},{4,16},{8,28},{12,24},{16,4},{20,0},{24,12},{28,8},{1,21},{... | collective-permute-start | bytes 245768 | tf_op jit(solution)/shard_map/ppermute | solution.py:469
  106.9 6.2 %collective-permute-start.12 = (f32[10,16,128]{2,1,0:T(8,128)S(1)}, f32[10,16,128]{2,1,0:T(8,128)S(1)}, u32[]{:S(2)}, u32[]{:S(2)}) collective-permute-start(f32[10,16,128]{2,1,0:T(8,128)S(1)} %get-tuple-element.21), channel_id=1, source_target_pairs={{0,24},{4,28},{8,16},{12,20},{16,8},{20,12},{24,0},{28,4},{1,25},{... | collective-permute-start | bytes 245768 | tf_op jit(solution)/shard_map/ppermute | solution.py:469
  108.1 6.6 %collective-permute-start.13 = (f32[10,16,128]{2,1,0:T(8,128)S(1)}, f32[10,16,128]{2,1,0:T(8,128)S(1)}, u32[]{:S(2)}, u32[]{:S(2)}) collective-permute-start(f32[10,16,128]{2,1,0:T(8,128)S(1)} %get-tuple-element.22), channel_id=1, source_target_pairs={{0,28},{4,24},{8,20},{12,16},{16,12},{20,8},{24,4},{28,0},{1,29},{... | collective-permute-start | bytes 245768 | tf_op jit(solution)/shard_map/ppermute | solution.py:469
  114.8 20.7 %collective-permute-start.16 = (f32[10,16,128]{2,1,0:T(8,128)S(1)}, f32[10,16,128]{2,1,0:T(8,128)S(1)}, u32[]{:S(2)}, u32[]{:S(2)}) collective-permute-start(f32[10,16,128]{2,1,0:T(8,128)S(1)} %add_add_fusion.2), channel_id=1, source_target_pairs={{0,3},{1,2},{2,1},{3,0},{4,7},{5,6},{6,5},{7,4},{8,11},{9,10},{10,... | collective-permute-start | bytes 245768 | tf_op jit(solution)/shard_map/ppermute | solution.py:469
  117.3 21.6 %collective-permute-start.15 = (f32[10,16,128]{2,1,0:T(8,128)S(1)}, f32[10,16,128]{2,1,0:T(8,128)S(1)}, u32[]{:S(2)}, u32[]{:S(2)}) collective-permute-start(f32[10,16,128]{2,1,0:T(8,128)S(1)} %add_add_fusion.2), channel_id=1, source_target_pairs={{0,2},{1,3},{2,0},{3,1},{4,6},{5,7},{6,4},{7,5},{8,10},{9,11},{10,... | collective-permute-start | bytes 245768 | tf_op jit(solution)/shard_map/ppermute | solution.py:469
  117.3 23.1 %collective-permute-start.14 = (f32[10,16,128]{2,1,0:T(8,128)S(1)}, f32[10,16,128]{2,1,0:T(8,128)S(1)}, u32[]{:S(2)}, u32[]{:S(2)}) collective-permute-start(f32[10,16,128]{2,1,0:T(8,128)S(1)} %add_add_fusion.2), channel_id=1, source_target_pairs={{0,1},{1,0},{2,3},{3,2},{4,5},{5,4},{6,7},{7,6},{8,9},{9,8},{10,11... | collective-permute-start | bytes 245768 | tf_op jit(solution)/shard_map/ppermute | solution.py:469
  135.4 59.2 %collective-permute-start.27 = (f32[1536,128]{1,0:T(8,128)S(1)}, f32[1536,128]{1,0:T(8,128)}, u32[]{:S(2)}, u32[]{:S(2)}) collective-permute-start(f32[1536,128]{1,0:T(8,128)S(1)} %bitcast.28), channel_id=1, source_target_pairs={{0,0},{1,2},{2,1},{3,3},{4,4},{5,6},{6,5},{7,7},{8,8},{9,10},{10,9... | collective-permute-start | bytes 2359304 | tf_op jit(solution)/shard_map/ppermute | solution.py:529
  139.0 55.7 %collective-permute-start.24 = (f32[1536,128]{1,0:T(8,128)S(1)}, f32[1536,128]{1,0:T(8,128)}, u32[]{:S(2)}, u32[]{:S(2)}) collective-permute-start(f32[1536,128]{1,0:T(8,128)S(1)} %bitcast.29), channel_id=1, source_target_pairs={{0,1},{1,0},{2,3},{3,2},{4,5},{5,4},{6,7},{7,6},{8,9},{9,8},{10,11... | collective-permute-start | bytes 2359304 | tf_op jit(solution)/shard_map/ppermute | solution.py:528
  140.5 4.8 %collective-permute-start.23 = (f32[10,16,128]{2,1,0:T(8,128)S(1)}, f32[10,16,128]{2,1,0:T(8,128)S(1)}, u32[]{:S(2)}, u32[]{:S(2)}) collective-permute-start(f32[10,16,128]{2,1,0:T(8,128)S(1)} %add_add_fusion.1.refs_0_), channel_id=1, source_target_pairs={{0,28},{4,24},{8,20},{12,16},{16,12},{20,8},{24,4},{28,0},{1,29},{... | collective-permute-start | bytes 245768 | tf_op jit(solution)/shard_map/ppermute | solution.py:469
  145.3 0.6 copy-start
  146.0 5.3 %collective-permute-start.22 = (f32[10,16,128]{2,1,0:T(8,128)S(1)}, f32[10,16,128]{2,1,0:T(8,128)S(1)}, u32[]{:S(2)}, u32[]{:S(2)}) collective-permute-start(f32[10,16,128]{2,1,0:T(8,128)S(1)} %add_add_fusion.1.refs_0_), channel_id=1, source_target_pairs={{0,24},{4,28},{8,16},{12,20},{16,8},{20,12},{24,0},{28,4},{1,25},{... | collective-permute-start | bytes 245768 | tf_op jit(solution)/shard_map/ppermute | solution.py:469
  151.3 0.6 copy-start.2
  151.9 4.0 %collective-permute-start.21 = (f32[10,16,128]{2,1,0:T(8,128)S(1)}, f32[10,16,128]{2,1,0:T(8,128)S(1)}, u32[]{:S(2)}, u32[]{:S(2)}) collective-permute-start(f32[10,16,128]{2,1,0:T(8,128)S(1)} %add_add_fusion.1.refs_0_), channel_id=1, source_target_pairs={{0,20},{4,16},{8,28},{12,24},{16,4},{20,0},{24,12},{28,8},{1,21},{... | collective-permute-start | bytes 245768 | tf_op jit(solution)/shard_map/ppermute | solution.py:469
  155.9 0.6 copy-start.4
  156.5 4.4 %collective-permute-start.20 = (f32[10,16,128]{2,1,0:T(8,128)S(1)}, f32[10,16,128]{2,1,0:T(8,128)S(1)}, u32[]{:S(2)}, u32[]{:S(2)}) collective-permute-start(f32[10,16,128]{2,1,0:T(8,128)S(1)} %add_add_fusion.1.refs_0_), channel_id=1, source_target_pairs={{0,16},{4,20},{8,24},{12,28},{16,0},{20,4},{24,8},{28,12},{1,17},{... | collective-permute-start | bytes 245768 | tf_op jit(solution)/shard_map/ppermute | solution.py:469
  161.0 0.6 copy-start.6
  161.6 4.7 %collective-permute-start.19 = (f32[10,16,128]{2,1,0:T(8,128)S(1)}, f32[10,16,128]{2,1,0:T(8,128)S(1)}, u32[]{:S(2)}, u32[]{:S(2)}) collective-permute-start(f32[10,16,128]{2,1,0:T(8,128)S(1)} %add_add_fusion.1.refs_0_), channel_id=1, source_target_pairs={{0,12},{4,8},{8,4},{12,0},{16,28},{20,24},{24,20},{28,16},{1,13},{... | collective-permute-start | bytes 245768 | tf_op jit(solution)/shard_map/ppermute | solution.py:469
  166.3 0.6 copy-start.8
  166.9 4.4 %collective-permute-start.18 = (f32[10,16,128]{2,1,0:T(8,128)S(1)}, f32[10,16,128]{2,1,0:T(8,128)S(1)}, u32[]{:S(2)}, u32[]{:S(2)}) collective-permute-start(f32[10,16,128]{2,1,0:T(8,128)S(1)} %add_add_fusion.1.refs_0_), channel_id=1, source_target_pairs={{0,8},{4,12},{8,0},{12,4},{16,24},{20,28},{24,16},{28,20},{1,9},{5... | collective-permute-start | bytes 245768 | tf_op jit(solution)/shard_map/ppermute | solution.py:469
  171.4 0.6 copy-start.10
  172.0 1.4 collective-permute-start.17
  173.4 0.9 copy-start.1
  174.3 0.9 copy-start.3
  175.2 0.9 copy-start.5
  176.1 0.9 copy-start.7
  177.0 0.9 copy-start.9
  177.8 0.9 copy-start.11
  199.5 12.0 %collective-permute-start.29 = (f32[128,8,128]{2,1,0:T(8,128)S(1)}, f32[128,8,128]{2,1,0:T(8,128)S(1)}, u32[]{:S(2)}, u32[]{:S(2)}) collective-permute-start(f32[128,8,128]{2,1,0:T(8,128)S(1)} %get-tuple-element.23), channel_id=1, source_target_pairs={{0,0},{1,2},{2,1},{3,3},{4,4},{5,6},{6,5},{7,7},{8,8},{9,10},{10,9... | collective-permute-start | bytes 1572872 | tf_op jit(solution)/shard_map/ppermute | solution.py:542
  200.2 15.3 %collective-permute-start.30 = (f32[128,8,128]{2,1,0:T(8,128)S(1)}, f32[128,8,128]{2,1,0:T(8,128)S(1)}, u32[]{:S(2)}, u32[]{:S(2)}) collective-permute-start(f32[128,8,128]{2,1,0:T(8,128)S(1)} %get-tuple-element.24), channel_id=1, source_target_pairs={{0,1},{1,0},{2,3},{3,2},{4,5},{5,4},{6,7},{7,6},{8,9},{9,8},{10,11... | collective-permute-start | bytes 1572872 | tf_op jit(solution)/shard_map/ppermute | solution.py:543
  205.5 21.1 %collective-permute-start.26 = (f32[128,8,128]{2,1,0:T(8,128)S(1)}, f32[128,8,128]{2,1,0:T(8,128)S(1)}, u32[]{:S(2)}, u32[]{:S(2)}) collective-permute-start(f32[128,8,128]{2,1,0:T(8,128)S(1)} %rotate_far.2), channel_id=1, source_target_pairs={{0,1},{1,3},{2,0},{3,2},{4,5},{5,7},{6,4},{7,6},{8,9},{9,11},{10,8... | collective-permute-start | bytes 1572872 | tf_op jit(solution)/shard_map/ppermute | solution.py:541

commit v8 on v7

--- a/solution.py
+++ b/solution.py
@@ -528,7 +528,10 @@
             twin.append(lax.ppermute(part, "orb", [(0, 1), (1, 0), (2, 3), (3, 2)]))
             facing.append(lax.ppermute(part, "orb", [(0, 0), (1, 2), (2, 1), (3, 3)]))
     mine = tree_sum(swap_all(pieces, "grid"))
-    mine = tree_sum(swap_all([mine] * owners, "orb"))
+    apart = 1
+    while apart < owners:
+        mine = mine + lax.ppermute(mine, "orb", [(i, i ^ apart) for i in range(owners)])
+        apart *= 2
     margin = swap_all([mine] * slabs, "grid")
     inverse = inverse_rows(place, margin, 1.0 / total_cells)
     if not four:

time: 228 us -> 238 us (1.044)
  blocking collectives: 37 us -> 0 us
  waiting for transfers between devices: 96.3 us -> 132 us
  starting transfers between devices: 40.7 us -> 50.3 us
    all_to_all x1 -> x2, waiting for transfers between devices: 0.01 us -> 44.6 us  [orthonormalized(): lax.all_to_all(filtered, everyone, split_axis=0, concat_axis=0, tiled=True)]
    all_to_all x1 -> x0, blocking collectives: 37 us -> none  [orthonormalized(): lax.all_to_all(filtered, everyone, split_axis=0, concat_axis=0, tiled=True)]
    ppermute x0 -> x2, waiting for transfers between devices: none -> 28.7 us  [orthonormalized(): lax.ppermute(mine, 'orb', [(i, i ^ apart) for i in range(owners)])]
    ppermute x24 -> x21, waiting for transfers between devices: 68.3 us -> 43.7 us  [swap_all(): lax.ppermute(pieces[s], axis, [(i, i ^ s) for i in range(count)])]
    all_to_all x1, waiting for transfers between devices: 12.9 us -> 0.01 us  [orthonormalized(): lax.all_to_all(first, 'grid', split_axis=0, concat_axis=0, tiled=True)]
    ppermute x1, waiting for transfers between devices: 11.1 us -> 0.01 us  [orthonormalized(): skip = lax.ppermute(skip, 'orb', [(0, 1), (1, 3), (2, 0), (3, 2)])]
    ppermute x1, waiting for transfers between devices: 4.06 us -> 14.8 us  [orthonormalized(): back = lax.ppermute(back, 'orb', [(0, 1), (1, 0), (2, 3), (3, 2)])]
    all_to_all x1 -> x2, starting transfers between devices: 4.01 us -> 7.62 us  [orthonormalized(): lax.all_to_all(filtered, everyone, split_axis=0, concat_axis=0, tiled=True)]
  transfers between devices with their start and end apart: 33 -> 33, of which waited for: 21 -> 22; matrix products, arithmetic and copies ran while one was open for 1% -> 1% of each run, Pallas kernels for 12% -> 13%
where the time goes in v8:
time: 238 us; the launch traced here: 237 us
  waiting for transfers between devices  132 us (55%)
  starting transfers between devices  50.3 us (21%)
  Pallas kernels  40.4 us (17%)
  local copies, waits for them, and re-layouts  11.8 us (5%)
    all_to_all x2, waiting for transfers between devices, orthonormalized(): lax.all_to_all(filtered, everyone, split_axis=0, concat_axis=0, tiled=True)  44.6 us
    ppermute x21, waiting for transfers between devices, swap_all(): lax.ppermute(pieces[s], axis, [(i, i ^ s) for i in range(count)])  43.7 us
    ppermute x2, waiting for transfers between devices, orthonormalized(): lax.ppermute(mine, 'orb', [(i, i ^ apart) for i in range(owners)])  28.7 us
    ppermute x21, starting transfers between devices, swap_all(): lax.ppermute(pieces[s], axis, [(i, i ^ s) for i in range(count)])  23.2 us
    pallas_call x1, Pallas kernels, inverse_rows(): pl.pallas_call(functools.partial(inverse_kernel, factor), out_shape=jax.S...  15.9 us
    ppermute x1, waiting for transfers between devices, orthonormalized(): back = lax.ppermute(back, 'orb', [(0, 1), (1, 0), (2, 3), (3, 2)])  14.8 us
    unnamed x24, local copies, waits for them, and re-layouts  9.1 us
    pallas_call x2, Pallas kernels, filter_orbitals(): pl.pallas_call(functools.partial(filter_kernel, orbs), out_shape=jax.Shap...  8.24 us
  transfers between devices with their start and end apart: 33, of which 22 were waited for; matrix products, arithmetic and copies ran while one was open for 1% of the time, Pallas kernels for 13%

profile of v8, /device:TPU:0, one launch (start us, length us, event | category | flops | bytes accessed | tf_op | source)
XLA Modules:
  0.0 236.8 jit_solution(17174878773102386669)
XLA Ops:
  1.1 1.0 pad_maximum_fusion
  2.2 5.2 %all-to-all-start = ((f32[8,7,4,8,128]{4,3,2,1,0:T(8,128)}), f32[8,7,4,8,128]{4,3,2,1,0:T(8,128)S(1)}, u32[]{:S(2)}, u32[]{:S(2)}) async-start(f32[8,7,4,8,128]{4,3,2,1,0:T(8,128)} %pad_maximum_fusion), calls=%async_computation | async-start | bytes 1835008 | tf_op jit(solution)/shard_map/all_to_all | solution.py:496
  7.4 1.5 dynamic-slice_bitcast_fusion
  8.9 2.7 %collective-permute-start.6 = (f32[1,10,4,8,128]{4,3,2,1,0:T(8,128)S(1)}, f32[1,10,4,8,128]{4,3,2,1,0:T(8,128)S(1)}, u32[]{:S(2)}, u32[]{:S(2)}) collective-permute-start(f32[1,10,4,8,128]{4,3,2,1,0:T(8,128)S(1)} %get-tuple-element.25), channel_id=1, source_target_pairs={{0,28},{4,24},{8,20},{12,16},{16,12},{20,8},{24,4},{28,0},{1,29},{... | collective-permute-start | bytes 491528 | tf_op jit(solution)/shard_map/ppermute | solution.py:469
  12.2 1.5 collective-permute-start.3
  13.6 1.5 collective-permute-start.1
  15.9 8.5 %collective-permute-done.6.refs_7_ = f32[1,10,4,8,128]{4,3,2,1,0:T(8,128)S(1)} collective-permute-done((f32[1,10,4,8,128]{4,3,2,1,0:T(8,128)S(1)}, f32[1,10,4,8,128]{4,3,2,1,0:T(8,128)S(1)}, u32[]{:S(2)}, u32[]{:S(2)}) %collective-permute-start.6) | collective-permute-done | bytes 163872 | tf_op jit(solution)/shard_map/ppermute | solution.py:469
  24.4 0.9 collective-permute-start
  25.3 1.6 collective-permute-done.4.refs_5_
  26.8 1.8 collective-permute-start.5
  28.9 2.0 collective-permute-done.3.refs_4_
  31.6 3.8 %collective-permute-done.5.refs_6_ = f32[1,10,4,8,128]{4,3,2,1,0:T(8,128)S(1)} collective-permute-done((f32[1,10,4,8,128]{4,3,2,1,0:T(8,128)S(1)}, f32[1,10,4,8,128]{4,3,2,1,0:T(8,128)S(1)}, u32[]{:S(2)}, u32[]{:S(2)}) %collective-permute-start.5) | collective-permute-done | bytes 163872 | tf_op jit(solution)/shard_map/ppermute | solution.py:469
  35.4 4.9 %filter.3 = f32[4,8,10,8,128]{4,3,2,1,0:T(8,128)} custom-call(s32[1]{0:T(128)} %bitcast.1.place_ref, bf16[256,256]{1,0:T(8,128)(2,1)S(1)} %fusion.6.xy_ref, bf16[256,256]{1,0:T(8,128)(2,1)S(1)} %select_convert_fusion.z_ref, f32[8,7,4,8,128]{4,3,2,1,0:T(8,128)S(1)} %all-to-all-done.pot_ref.refs_0_, f32[1,10,4,8,128]{4,3,2,1,0:T(8,128)S(1)} %get-tuple-element.31.refs_0_, ...), custom_call_target="tpu_custom_call" | custom-call | tf_op jit(solution)/shard_map/filter/pallas_call | solution.py:102
  40.3 4.0 %all-to-all-start.2 = ((f32[32,10,8,128]{3,2,1,0:T(8,128)}), f32[32,10,8,128]{3,2,1,0:T(8,128)S(1)}, u32[]{:S(2)}, u32[]{:S(2)}) async-start(f32[32,10,8,128]{3,2,1,0:T(8,128)} %bitcast.13), calls=%async_computation.2 | async-start | bytes 2621440 | tf_op jit(solution)/shard_map/all_to_all | solution.py:517
  44.4 3.3 %filter.2 = f32[4,8,6,8,128]{4,3,2,1,0:T(8,128)} custom-call(s32[1]{0:T(128)} %bitcast.1.place_ref, bf16[256,256]{1,0:T(8,128)(2,1)S(1)} %fusion.6.xy_ref, bf16[256,256]{1,0:T(8,128)(2,1)S(1)} %select_convert_fusion.z_ref, f32[8,7,4,8,128]{4,3,2,1,0:T(8,128)S(1)} %all-to-all-done.pot_ref.refs_0_, f32[8,7,4,8,128]{4,3,2,1,0:T(8,128)S(1)} %all-to-all-done.pot_ref.refs_0_), custom_call_target="tpu_custom_call" | custom-call | tf_op jit(solution)/shard_map/filter/pallas_call | solution.py:102
  47.7 28.6 %all-to-all-done.2 = f32[32,10,8,128]{3,2,1,0:T(8,128)S(1)} async-done(((f32[32,10,8,128]{3,2,1,0:T(8,128)}), f32[32,10,8,128]{3,2,1,0:T(8,128)S(1)}, u32[]{:S(2)}, u32[]{:S(2)}) %all-to-all-start.2) | async-done | bytes 1310752 | tf_op jit(solution)/shard_map/all_to_all | solution.py:517
  76.3 3.6 %all-to-all-start.1 = ((f32[32,6,8,128]{3,2,1,0:T(8,128)}), f32[32,6,8,128]{3,2,1,0:T(8,128)S(1)}, u32[]{:S(2)}, u32[]{:S(2)}) async-start(f32[32,6,8,128]{3,2,1,0:T(8,128)} %bitcast.3), calls=%async_computation.1 | async-start | bytes 1572864 | tf_op jit(solution)/shard_map/all_to_all | solution.py:517
  79.9 1.8 collective-permute-start.27
  81.7 3.4 %collective-permute-start.24 = (f32[2560,128]{1,0:T(8,128)S(1)}, f32[2560,128]{1,0:T(8,128)S(1)}, u32[]{:S(2)}, u32[]{:S(2)}) collective-permute-start(f32[2560,128]{1,0:T(8,128)S(1)} %bitcast.24), channel_id=1, source_target_pairs={{0,1},{1,0},{2,3},{3,2},{4,5},{5,4},{6,7},{7,6},{8,9},{9,8},{10,11... | collective-permute-start | bytes 3932168 | tf_op jit(solution)/shard_map/ppermute | solution.py:528
  85.1 15.9 %all-to-all-done.1 = f32[32,6,8,128]{3,2,1,0:T(8,128)S(1)} async-done(((f32[32,6,8,128]{3,2,1,0:T(8,128)}), f32[32,6,8,128]{3,2,1,0:T(8,128)S(1)}, u32[]{:S(2)}, u32[]{:S(2)}) %all-to-all-start.1) | async-done | bytes 786464 | tf_op jit(solution)/shard_map/all_to_all | solution.py:517
  101.1 2.1 margin.1
  103.3 1.5 collective-permute-start.8
  105.2 1.5 collective-permute-start.10
  106.7 1.8 collective-permute-done.8
  109.6 2.2 collective-permute-start.12
  113.2 1.5 collective-permute-start.26
  115.4 1.1 collective-permute-start.23
  117.7 24.3 %collective-permute-done.14 = f32[10,16,128]{2,1,0:T(8,128)S(1)} collective-permute-done((f32[10,16,128]{2,1,0:T(8,128)S(1)}, f32[10,16,128]{2,1,0:T(8,128)S(1)}, u32[]{:S(2)}, u32[]{:S(2)}) %collective-permute-start.14) | collective-permute-done | bytes 81952 | tf_op jit(solution)/shard_map/ppermute | solution.py:533
  142.1 2.5 %collective-permute-start.15 = (f32[10,16,128]{2,1,0:T(8,128)S(1)}, f32[10,16,128]{2,1,0:T(8,128)S(1)}, u32[]{:S(2)}, u32[]{:S(2)}) collective-permute-start(f32[10,16,128]{2,1,0:T(8,128)S(1)} %add.315), channel_id=1, source_target_pairs={{0,2},{1,3},{2,0},{3,1},{4,6},{5,7},{6,4},{7,5},{8,10},{9,11},{10,... | collective-permute-start | bytes 245768 | tf_op jit(solution)/shard_map/ppermute | solution.py:533
  144.6 4.4 %collective-permute-done.15 = f32[10,16,128]{2,1,0:T(8,128)S(1)} collective-permute-done((f32[10,16,128]{2,1,0:T(8,128)S(1)}, f32[10,16,128]{2,1,0:T(8,128)S(1)}, u32[]{:S(2)}, u32[]{:S(2)}) %collective-permute-start.15) | collective-permute-done | bytes 81952 | tf_op jit(solution)/shard_map/ppermute | solution.py:533
  149.0 1.9 collective-permute-start.22
  150.9 3.7 %collective-permute-done.22.refs_7_ = f32[10,16,128]{2,1,0:T(8,128)S(1)} collective-permute-done((f32[10,16,128]{2,1,0:T(8,128)S(1)}, f32[10,16,128]{2,1,0:T(8,128)S(1)}, u32[]{:S(2)}, u32[]{:S(2)}) %collective-permute-start.22) | collective-permute-done | bytes 81952 | tf_op jit(solution)/shard_map/ppermute | solution.py:469
  155.3 2.4 %collective-permute-start.21 = (f32[10,16,128]{2,1,0:T(8,128)S(1)}, f32[10,16,128]{2,1,0:T(8,128)S(1)}, u32[]{:S(2)}, u32[]{:S(2)}) collective-permute-start(f32[10,16,128]{2,1,0:T(8,128)S(1)} %add.316.refs_0_), channel_id=1, source_target_pairs={{0,24},{4,28},{8,16},{12,20},{16,8},{20,12},{24,0},{28,4},{1,25},{... | collective-permute-start | bytes 245768 | tf_op jit(solution)/shard_map/ppermute | solution.py:469
  157.7 2.9 %collective-permute-done.21.refs_6_ = f32[10,16,128]{2,1,0:T(8,128)S(1)} collective-permute-done((f32[10,16,128]{2,1,0:T(8,128)S(1)}, f32[10,16,128]{2,1,0:T(8,128)S(1)}, u32[]{:S(2)}, u32[]{:S(2)}) %collective-permute-start.21) | collective-permute-done | bytes 81952 | tf_op jit(solution)/shard_map/ppermute | solution.py:469
  161.7 4.2 %collective-permute-done.20.refs_5_ = f32[10,16,128]{2,1,0:T(8,128)S(1)} collective-permute-done((f32[10,16,128]{2,1,0:T(8,128)S(1)}, f32[10,16,128]{2,1,0:T(8,128)S(1)}, u32[]{:S(2)}, u32[]{:S(2)}) %collective-permute-start.20) | collective-permute-done | bytes 81952 | tf_op jit(solution)/shard_map/ppermute | solution.py:469
  166.5 1.2 collective-permute-start.19
  167.6 3.3 %collective-permute-done.19.refs_4_ = f32[10,16,128]{2,1,0:T(8,128)S(1)} collective-permute-done((f32[10,16,128]{2,1,0:T(8,128)S(1)}, f32[10,16,128]{2,1,0:T(8,128)S(1)}, u32[]{:S(2)}, u32[]{:S(2)}) %collective-permute-start.19) | collective-permute-done | bytes 81952 | tf_op jit(solution)/shard_map/ppermute | solution.py:469
  172.1 4.1 %collective-permute-done.18.refs_3_ = f32[10,16,128]{2,1,0:T(8,128)S(1)} collective-permute-done((f32[10,16,128]{2,1,0:T(8,128)S(1)}, f32[10,16,128]{2,1,0:T(8,128)S(1)}, u32[]{:S(2)}, u32[]{:S(2)}) %collective-permute-start.18) | collective-permute-done | bytes 81952 | tf_op jit(solution)/shard_map/ppermute | solution.py:469
  176.8 1.2 collective-permute-start.17
  178.0 3.2 %collective-permute-done.17.refs_2_ = f32[10,16,128]{2,1,0:T(8,128)S(1)} collective-permute-done((f32[10,16,128]{2,1,0:T(8,128)S(1)}, f32[10,16,128]{2,1,0:T(8,128)S(1)}, u32[]{:S(2)}, u32[]{:S(2)}) %collective-permute-start.17) | collective-permute-done | bytes 81952 | tf_op jit(solution)/shard_map/ppermute | solution.py:469
  181.9 1.4 collective-permute-done.16.refs_1_
  188.6 15.9 %inverse.1.v_ref = f32[4,128,512]{2,1,0:T(8,128)S(1)} custom-call(s32[1]{0:T(128)} %bitcast.1.place_ref, f32[10,16,128]{2,1,0:T(8,128)S(1)} %add.316.refs_0_, f32[10,16,128]{2,1,0:T(8,128)} %collective-permute-done.16.refs_1_, f32[10,16,128]{2,1,0:T(8,128)S(1)} %copy-done.11, f32[10,16,128]{2,1,0:T(8,128)S(1)} %copy-done.9, f32[10,16,128]{2,1,0:T(8,128)S(1)} %copy-done.7, ...), custom_call_target="tpu_custom_call" | custom-call | tf_op jit(solution)/shard_map/inverse/pallas_call | solution.py:311
  204.6 4.8 %rotate_far.3 = (f32[128,8,128]{2,1,0:T(8,128)S(1)}, f32[128,8,128]{2,1,0:T(8,128)S(1)}) custom-call(s32[1]{0:T(128)} %bitcast.layer_ref, f32[4,128,512]{2,1,0:T(8,128)S(1)} %inverse.1.v_ref, f32[1536,128]{1,0:T(8,128)} %collective-permute-done.23.refs_0_.refs_2_, f32[2560,128]{1,0:T(8,128)S(1)} %collective-permute-done.24.refs_1_.refs_3_, ...), custom_call_target="tpu_custom_call" | custom-call | tf_op jit(solution)/shard_map/rotate_far/pallas_call | solution.py:391
  210.1 2.3 collective-permute-start.29
  212.4 2.4 %rotate_far.2 = f32[128,8,128]{2,1,0:T(8,128)S(1)} custom-call(s32[1]{0:T(128)} %bitcast.layer_ref, f32[4,128,512]{2,1,0:T(8,128)S(1)} %inverse.1.v_ref, f32[1536,128]{1,0:T(8,128)} %collective-permute-done.23.refs_0_.refs_2_, f32[2560,128]{1,0:T(8,128)S(1)} %collective-permute-done.24.refs_1_.refs_3_), custom_call_target="tpu_custom_call" | custom-call | tf_op jit(solution)/shard_map/rotate_far/pallas_call | solution.py:391
  214.9 5.9 %rotate_near.1.near_ref = f32[128,4,8,128]{3,2,1,0:T(8,128)} custom-call(s32[1]{0:T(128)} %bitcast.layer_ref, f32[4,128,512]{2,1,0:T(8,128)S(1)} %inverse.1.v_ref, f32[1536,128]{1,0:T(8,128)S(1)} %bitcast.30, f32[2560,128]{1,0:T(8,128)S(1)} %bitcast.26, f32[1536,128]{1,0:T(8,128)} %collective-permute-done.23.refs_0_.refs_2_, ...), custom_call_target="tpu_custom_call" | custom-call | tf_op jit(solution)/shard_map/rotate_near/pallas_call | solution.py:427
  220.8 14.8 %collective-permute-done.29.back = f32[128,8,128]{2,1,0:T(8,128)S(1)} collective-permute-done((f32[128,8,128]{2,1,0:T(8,128)S(1)}, f32[128,8,128]{2,1,0:T(8,128)S(1)}, u32[]{:S(2)}, u32[]{:S(2)}) %collective-permute-start.29) | collective-permute-done | bytes 524320 | tf_op jit(solution)/shard_map/ppermute | solution.py:546
  235.6 1.0 join.1
  (65 shorter events, 19.1 us)
Async XLA Ops:
  0.0 1.1 slice-start
  2.2 33.3 %all-to-all-start = ((f32[8,7,4,8,128]{4,3,2,1,0:T(8,128)}), f32[8,7,4,8,128]{4,3,2,1,0:T(8,128)S(1)}, u32[]{:S(2)}, u32[]{:S(2)}) async-start(f32[8,7,4,8,128]{4,3,2,1,0:T(8,128)} %pad_maximum_fusion), calls=%async_computation | async-start | bytes 1835008 | tf_op jit(solution)/shard_map/all_to_all | solution.py:496
  8.9 15.5 %collective-permute-start.6 = (f32[1,10,4,8,128]{4,3,2,1,0:T(8,128)S(1)}, f32[1,10,4,8,128]{4,3,2,1,0:T(8,128)S(1)}, u32[]{:S(2)}, u32[]{:S(2)}) collective-permute-start(f32[1,10,4,8,128]{4,3,2,1,0:T(8,128)S(1)} %get-tuple-element.25), channel_id=1, source_target_pairs={{0,28},{4,24},{8,20},{12,16},{16,12},{20,8},{24,4},{28,0},{1,29},{... | collective-permute-start | bytes 491528 | tf_op jit(solution)/shard_map/ppermute | solution.py:469
  11.6 15.2 %collective-permute-start.4 = (f32[1,10,4,8,128]{4,3,2,1,0:T(8,128)S(1)}, f32[1,10,4,8,128]{4,3,2,1,0:T(8,128)S(1)}, u32[]{:S(2)}, u32[]{:S(2)}) collective-permute-start(f32[1,10,4,8,128]{4,3,2,1,0:T(8,128)S(1)} %get-tuple-element.26), channel_id=1, source_target_pairs={{0,20},{4,16},{8,28},{12,24},{16,4},{20,0},{24,12},{28,8},{1,21},{... | collective-permute-start | bytes 491528 | tf_op jit(solution)/shard_map/ppermute | solution.py:469
  12.2 18.7 %collective-permute-start.3 = (f32[1,10,4,8,128]{4,3,2,1,0:T(8,128)S(1)}, f32[1,10,4,8,128]{4,3,2,1,0:T(8,128)S(1)}, u32[]{:S(2)}, u32[]{:S(2)}) collective-permute-start(f32[1,10,4,8,128]{4,3,2,1,0:T(8,128)S(1)} %get-tuple-element.27), channel_id=1, source_target_pairs={{0,16},{4,20},{8,24},{12,28},{16,0},{20,4},{24,8},{28,12},{1,17},{... | collective-permute-start | bytes 491528 | tf_op jit(solution)/shard_map/ppermute | solution.py:469
  13.6 17.3 %collective-permute-start.2 = (f32[1,10,4,8,128]{4,3,2,1,0:T(8,128)S(1)}, f32[1,10,4,8,128]{4,3,2,1,0:T(8,128)S(1)}, u32[]{:S(2)}, u32[]{:S(2)}) collective-permute-start(f32[1,10,4,8,128]{4,3,2,1,0:T(8,128)S(1)} %get-tuple-element.28), channel_id=1, source_target_pairs={{0,12},{4,8},{8,4},{12,0},{16,28},{20,24},{24,20},{28,16},{1,13},{... | collective-permute-start | bytes 491528 | tf_op jit(solution)/shard_map/ppermute | solution.py:469
  13.6 17.9 %collective-permute-start.1 = (f32[1,10,4,8,128]{4,3,2,1,0:T(8,128)S(1)}, f32[1,10,4,8,128]{4,3,2,1,0:T(8,128)S(1)}, u32[]{:S(2)}, u32[]{:S(2)}) collective-permute-start(f32[1,10,4,8,128]{4,3,2,1,0:T(8,128)S(1)} %get-tuple-element.29), channel_id=1, source_target_pairs={{0,8},{4,12},{8,0},{12,4},{16,24},{20,28},{24,16},{28,20},{1,9},{5... | collective-permute-start | bytes 491528 | tf_op jit(solution)/shard_map/ppermute | solution.py:469
  24.4 7.2 %collective-permute-start = (f32[1,10,4,8,128]{4,3,2,1,0:T(8,128)S(1)}, f32[1,10,4,8,128]{4,3,2,1,0:T(8,128)S(1)}, u32[]{:S(2)}, u32[]{:S(2)}) collective-permute-start(f32[1,10,4,8,128]{4,3,2,1,0:T(8,128)S(1)} %get-tuple-element.30), channel_id=1, source_target_pairs={{0,4},{4,0},{8,12},{12,8},{16,20},{20,16},{24,28},{28,24},{1,5},{5... | collective-permute-start | bytes 491528 | tf_op jit(solution)/shard_map/ppermute | solution.py:469
  26.8 8.6 %collective-permute-start.5 = (f32[1,10,4,8,128]{4,3,2,1,0:T(8,128)S(1)}, f32[1,10,4,8,128]{4,3,2,1,0:T(8,128)S(1)}, u32[]{:S(2)}, u32[]{:S(2)}) collective-permute-start(f32[1,10,4,8,128]{4,3,2,1,0:T(8,128)S(1)} %get-tuple-element.32), channel_id=1, source_target_pairs={{0,24},{4,28},{8,16},{12,20},{16,8},{20,12},{24,0},{28,4},{1,25},{... | collective-permute-start | bytes 491528 | tf_op jit(solution)/shard_map/ppermute | solution.py:469
  40.3 36.0 %all-to-all-start.2 = ((f32[32,10,8,128]{3,2,1,0:T(8,128)}), f32[32,10,8,128]{3,2,1,0:T(8,128)S(1)}, u32[]{:S(2)}, u32[]{:S(2)}) async-start(f32[32,10,8,128]{3,2,1,0:T(8,128)} %bitcast.13), calls=%async_computation.2 | async-start | bytes 2621440 | tf_op jit(solution)/shard_map/all_to_all | solution.py:517
  76.3 24.8 %all-to-all-start.1 = ((f32[32,6,8,128]{3,2,1,0:T(8,128)}), f32[32,6,8,128]{3,2,1,0:T(8,128)S(1)}, u32[]{:S(2)}, u32[]{:S(2)}) async-start(f32[32,6,8,128]{3,2,1,0:T(8,128)} %bitcast.3), calls=%async_computation.1 | async-start | bytes 1572864 | tf_op jit(solution)/shard_map/all_to_all | solution.py:517
  79.9 124.6 %collective-permute-start.27 = (f32[2560,128]{1,0:T(8,128)S(1)}, f32[2560,128]{1,0:T(8,128)}, u32[]{:S(2)}, u32[]{:S(2)}) collective-permute-start(f32[2560,128]{1,0:T(8,128)S(1)} %bitcast.23), channel_id=1, source_target_pairs={{0,0},{1,2},{2,1},{3,3},{4,4},{5,6},{6,5},{7,7},{8,8},{9,10},{10,9... | collective-permute-start | bytes 3932168 | tf_op jit(solution)/shard_map/ppermute | solution.py:529
  81.7 122.9 %collective-permute-start.24 = (f32[2560,128]{1,0:T(8,128)S(1)}, f32[2560,128]{1,0:T(8,128)S(1)}, u32[]{:S(2)}, u32[]{:S(2)}) collective-permute-start(f32[2560,128]{1,0:T(8,128)S(1)} %bitcast.24), channel_id=1, source_target_pairs={{0,1},{1,0},{2,3},{3,2},{4,5},{5,4},{6,7},{7,6},{8,9},{9,8},{10,11... | collective-permute-start | bytes 3932168 | tf_op jit(solution)/shard_map/ppermute | solution.py:528
  103.2 1.9 collective-permute-start.7
  103.3 5.2 %collective-permute-start.8 = (f32[10,16,128]{2,1,0:T(8,128)S(1)}, f32[10,16,128]{2,1,0:T(8,128)S(1)}, u32[]{:S(2)}, u32[]{:S(2)}) collective-permute-start(f32[10,16,128]{2,1,0:T(8,128)S(1)} %get-tuple-element.17), channel_id=1, source_target_pairs={{0,8},{4,12},{8,0},{12,4},{16,24},{20,28},{24,16},{28,20},{1,9},{5... | collective-permute-start | bytes 245768 | tf_op jit(solution)/shard_map/ppermute | solution.py:469
  104.8 4.7 %collective-permute-start.9 = (f32[10,16,128]{2,1,0:T(8,128)S(1)}, f32[10,16,128]{2,1,0:T(8,128)S(1)}, u32[]{:S(2)}, u32[]{:S(2)}) collective-permute-start(f32[10,16,128]{2,1,0:T(8,128)S(1)} %get-tuple-element.18), channel_id=1, source_target_pairs={{0,12},{4,8},{8,4},{12,0},{16,28},{20,24},{24,20},{28,16},{1,13},{... | collective-permute-start | bytes 245768 | tf_op jit(solution)/shard_map/ppermute | solution.py:469
  105.2 6.6 %collective-permute-start.10 = (f32[10,16,128]{2,1,0:T(8,128)S(1)}, f32[10,16,128]{2,1,0:T(8,128)S(1)}, u32[]{:S(2)}, u32[]{:S(2)}) collective-permute-start(f32[10,16,128]{2,1,0:T(8,128)S(1)} %get-tuple-element.19), channel_id=1, source_target_pairs={{0,16},{4,20},{8,24},{12,28},{16,0},{20,4},{24,8},{28,12},{1,17},{... | collective-permute-start | bytes 245768 | tf_op jit(solution)/shard_map/ppermute | solution.py:469
  108.5 4.7 %collective-permute-start.11 = (f32[10,16,128]{2,1,0:T(8,128)S(1)}, f32[10,16,128]{2,1,0:T(8,128)S(1)}, u32[]{:S(2)}, u32[]{:S(2)}) collective-permute-start(f32[10,16,128]{2,1,0:T(8,128)S(1)} %get-tuple-element.20), channel_id=1, source_target_pairs={{0,20},{4,16},{8,28},{12,24},{16,4},{20,0},{24,12},{28,8},{1,21},{... | collective-permute-start | bytes 245768 | tf_op jit(solution)/shard_map/ppermute | solution.py:469
  109.6 5.8 %collective-permute-start.12 = (f32[10,16,128]{2,1,0:T(8,128)S(1)}, f32[10,16,128]{2,1,0:T(8,128)S(1)}, u32[]{:S(2)}, u32[]{:S(2)}) collective-permute-start(f32[10,16,128]{2,1,0:T(8,128)S(1)} %get-tuple-element.21), channel_id=1, source_target_pairs={{0,24},{4,28},{8,16},{12,20},{16,8},{20,12},{24,0},{28,4},{1,25},{... | collective-permute-start | bytes 245768 | tf_op jit(solution)/shard_map/ppermute | solution.py:469
  111.8 5.1 %collective-permute-start.13 = (f32[10,16,128]{2,1,0:T(8,128)S(1)}, f32[10,16,128]{2,1,0:T(8,128)S(1)}, u32[]{:S(2)}, u32[]{:S(2)}) collective-permute-start(f32[10,16,128]{2,1,0:T(8,128)S(1)} %get-tuple-element.22), channel_id=1, source_target_pairs={{0,28},{4,24},{8,20},{12,16},{16,12},{20,8},{24,4},{28,0},{1,29},{... | collective-permute-start | bytes 245768 | tf_op jit(solution)/shard_map/ppermute | solution.py:469
  113.2 91.4 %collective-permute-start.26 = (f32[1536,128]{1,0:T(8,128)S(1)}, f32[1536,128]{1,0:T(8,128)}, u32[]{:S(2)}, u32[]{:S(2)}) collective-permute-start(f32[1536,128]{1,0:T(8,128)S(1)} %bitcast.28), channel_id=1, source_target_pairs={{0,0},{1,2},{2,1},{3,3},{4,4},{5,6},{6,5},{7,7},{8,8},{9,10},{10,9... | collective-permute-start | bytes 2359304 | tf_op jit(solution)/shard_map/ppermute | solution.py:529
  115.4 89.1 %collective-permute-start.23 = (f32[1536,128]{1,0:T(8,128)S(1)}, f32[1536,128]{1,0:T(8,128)}, u32[]{:S(2)}, u32[]{:S(2)}) collective-permute-start(f32[1536,128]{1,0:T(8,128)S(1)} %bitcast.29), channel_id=1, source_target_pairs={{0,1},{1,0},{2,3},{3,2},{4,5},{5,4},{6,7},{7,6},{8,9},{9,8},{10,11... | collective-permute-start | bytes 2359304 | tf_op jit(solution)/shard_map/ppermute | solution.py:528
  116.9 25.2 %collective-permute-start.14 = (f32[10,16,128]{2,1,0:T(8,128)S(1)}, f32[10,16,128]{2,1,0:T(8,128)S(1)}, u32[]{:S(2)}, u32[]{:S(2)}) collective-permute-start(f32[10,16,128]{2,1,0:T(8,128)S(1)} %add_add_fusion.1), channel_id=1, source_target_pairs={{0,1},{1,0},{2,3},{3,2},{4,5},{5,4},{6,7},{7,6},{8,9},{9,8},{10,11... | collective-permute-start | bytes 245768 | tf_op jit(solution)/shard_map/ppermute | solution.py:533
  142.1 6.9 %collective-permute-start.15 = (f32[10,16,128]{2,1,0:T(8,128)S(1)}, f32[10,16,128]{2,1,0:T(8,128)S(1)}, u32[]{:S(2)}, u32[]{:S(2)}) collective-permute-start(f32[10,16,128]{2,1,0:T(8,128)S(1)} %add.315), channel_id=1, source_target_pairs={{0,2},{1,3},{2,0},{3,1},{4,6},{5,7},{6,4},{7,5},{8,10},{9,11},{10,... | collective-permute-start | bytes 245768 | tf_op jit(solution)/shard_map/ppermute | solution.py:533
  149.0 5.6 %collective-permute-start.22 = (f32[10,16,128]{2,1,0:T(8,128)S(1)}, f32[10,16,128]{2,1,0:T(8,128)S(1)}, u32[]{:S(2)}, u32[]{:S(2)}) collective-permute-start(f32[10,16,128]{2,1,0:T(8,128)S(1)} %add.316.refs_0_), channel_id=1, source_target_pairs={{0,28},{4,24},{8,20},{12,16},{16,12},{20,8},{24,4},{28,0},{1,29},{... | collective-permute-start | bytes 245768 | tf_op jit(solution)/shard_map/ppermute | solution.py:469
  154.6 0.6 copy-start
  155.3 5.4 %collective-permute-start.21 = (f32[10,16,128]{2,1,0:T(8,128)S(1)}, f32[10,16,128]{2,1,0:T(8,128)S(1)}, u32[]{:S(2)}, u32[]{:S(2)}) collective-permute-start(f32[10,16,128]{2,1,0:T(8,128)S(1)} %add.316.refs_0_), channel_id=1, source_target_pairs={{0,24},{4,28},{8,16},{12,20},{16,8},{20,12},{24,0},{28,4},{1,25},{... | collective-permute-start | bytes 245768 | tf_op jit(solution)/shard_map/ppermute | solution.py:469
  160.6 0.6 copy-start.2
  161.2 4.6 %collective-permute-start.20 = (f32[10,16,128]{2,1,0:T(8,128)S(1)}, f32[10,16,128]{2,1,0:T(8,128)S(1)}, u32[]{:S(2)}, u32[]{:S(2)}) collective-permute-start(f32[10,16,128]{2,1,0:T(8,128)S(1)} %add.316.refs_0_), channel_id=1, source_target_pairs={{0,20},{4,16},{8,28},{12,24},{16,4},{20,0},{24,12},{28,8},{1,21},{... | collective-permute-start | bytes 245768 | tf_op jit(solution)/shard_map/ppermute | solution.py:469
  165.9 0.6 copy-start.4
  166.5 4.5 %collective-permute-start.19 = (f32[10,16,128]{2,1,0:T(8,128)S(1)}, f32[10,16,128]{2,1,0:T(8,128)S(1)}, u32[]{:S(2)}, u32[]{:S(2)}) collective-permute-start(f32[10,16,128]{2,1,0:T(8,128)S(1)} %add.316.refs_0_), channel_id=1, source_target_pairs={{0,16},{4,20},{8,24},{12,28},{16,0},{20,4},{24,8},{28,12},{1,17},{... | collective-permute-start | bytes 245768 | tf_op jit(solution)/shard_map/ppermute | solution.py:469
  171.0 0.6 copy-start.6
  171.6 4.6 %collective-permute-start.18 = (f32[10,16,128]{2,1,0:T(8,128)S(1)}, f32[10,16,128]{2,1,0:T(8,128)S(1)}, u32[]{:S(2)}, u32[]{:S(2)}) collective-permute-start(f32[10,16,128]{2,1,0:T(8,128)S(1)} %add.316.refs_0_), channel_id=1, source_target_pairs={{0,12},{4,8},{8,4},{12,0},{16,28},{20,24},{24,20},{28,16},{1,13},{... | collective-permute-start | bytes 245768 | tf_op jit(solution)/shard_map/ppermute | solution.py:469
  176.2 0.6 copy-start.8
  176.8 4.5 %collective-permute-start.17 = (f32[10,16,128]{2,1,0:T(8,128)S(1)}, f32[10,16,128]{2,1,0:T(8,128)S(1)}, u32[]{:S(2)}, u32[]{:S(2)}) collective-permute-start(f32[10,16,128]{2,1,0:T(8,128)S(1)} %add.316.refs_0_), channel_id=1, source_target_pairs={{0,8},{4,12},{8,0},{12,4},{16,24},{20,28},{24,16},{28,20},{1,9},{5... | collective-permute-start | bytes 245768 | tf_op jit(solution)/shard_map/ppermute | solution.py:469
  181.3 0.6 copy-start.10
  181.9 1.4 collective-permute-start.16
  183.3 0.9 copy-start.1
  184.2 0.9 copy-start.3
  185.1 0.9 copy-start.5
  186.0 0.9 copy-start.7
  186.8 0.9 copy-start.9
  187.7 0.9 copy-start.11
  209.4 11.4 %collective-permute-start.28 = (f32[128,8,128]{2,1,0:T(8,128)S(1)}, f32[128,8,128]{2,1,0:T(8,128)S(1)}, u32[]{:S(2)}, u32[]{:S(2)}) collective-permute-start(f32[128,8,128]{2,1,0:T(8,128)S(1)} %get-tuple-element.23), channel_id=1, source_target_pairs={{0,0},{1,2},{2,1},{3,3},{4,4},{5,6},{6,5},{7,7},{8,8},{9,10},{10,9... | collective-permute-start | bytes 1572872 | tf_op jit(solution)/shard_map/ppermute | solution.py:545
  210.1 25.5 %collective-permute-start.29 = (f32[128,8,128]{2,1,0:T(8,128)S(1)}, f32[128,8,128]{2,1,0:T(8,128)S(1)}, u32[]{:S(2)}, u32[]{:S(2)}) collective-permute-start(f32[128,8,128]{2,1,0:T(8,128)S(1)} %get-tuple-element.24), channel_id=1, source_target_pairs={{0,1},{1,0},{2,3},{3,2},{4,5},{5,4},{6,7},{7,6},{8,9},{9,8},{10,11... | collective-permute-start | bytes 1572872 | tf_op jit(solution)/shard_map/ppermute | solution.py:546
  214.8 20.8 %collective-permute-start.25 = (f32[128,8,128]{2,1,0:T(8,128)S(1)}, f32[128,8,128]{2,1,0:T(8,128)S(1)}, u32[]{:S(2)}, u32[]{:S(2)}) collective-permute-start(f32[128,8,128]{2,1,0:T(8,128)S(1)} %rotate_far.2), channel_id=1, source_target_pairs={{0,1},{1,3},{2,0},{3,2},{4,5},{5,7},{6,4},{7,6},{8,9},{9,11},{10,8... | collective-permute-start | bytes 1572872 | tf_op jit(solution)/shard_map/ppermute | solution.py:544

commit v9 on v7

--- a/solution.py
+++ b/solution.py
@@ -77,7 +77,8 @@
     def apply(v):
         high, low = split(v)
         near = mm(xy_ref[...], high) + mm(xy_ref[...], low)
-        near = near + (mm(high, z_ref[...]) + mm(low, z_ref[...]))
+        along_z = mm(jnp.concatenate([high, low], axis=0), z_ref[...])
+        near = near + (along_z[:flat] + along_z[flat:])
         return diag[...] * v + scale * near
 
     for q in range(0, orbs, pair):
@@ -365,11 +366,19 @@
 
 def skip_kernel(spec, layer_ref, v_ref, *refs):
     *twin, skip, high, low = refs
-    gather_cells(spec, twin, high, low)
     _, rows, cols = skip.shape
     layer = layer_ref[0]
-    to = jnp.clip(layer + 2 * twin_side(layer), 0, v_ref.shape[0] - 1)
-    put_rows(skip, product(v_ref[to], high[...], low[...]), rows, cols)
+    inner = (layer > 0) & (layer < v_ref.shape[0] - 1)
+
+    @pl.when(inner)
+    def _():
+        gather_cells(spec, twin, high, low)
+        to = jnp.clip(layer + 2 * twin_side(layer), 0, v_ref.shape[0] - 1)
+        put_rows(skip, product(v_ref[to], high[...], low[...]), rows, cols)
+
+    @pl.when(jnp.logical_not(inner))
+    def _():
+        skip[...] = jnp.zeros(skip.shape, f32)
 
 
 def step_kernel(spec, layer_ref, v_ref, *refs):
@@ -379,10 +388,19 @@
     _, rows, cols = step.shape
     layer = layer_ref[0]
     side = twin_side(layer)
-    for out, parts, to in ((step, twin, layer + side), (back, facing, layer - side)):
-        gather_cells(spec, parts, high, low)
-        to = jnp.clip(to, 0, v_ref.shape[0] - 1)
-        put_rows(out, product(v_ref[to], high[...], low[...]), rows, cols)
+    inner = (layer > 0) & (layer < v_ref.shape[0] - 1)
+
+    @pl.when(inner)
+    def _():
+        for out, parts, to in ((step, twin, layer + side), (back, facing, layer - side)):
+            gather_cells(spec, parts, high, low)
+            to = jnp.clip(to, 0, v_ref.shape[0] - 1)
+            put_rows(out, product(v_ref[to], high[...], low[...]), rows, cols)
+
+    @pl.when(jnp.logical_not(inner))
+    def _():
+        step[...] = jnp.zeros(step.shape, f32)
+        back[...] = jnp.zeros(back.shape, f32)
 
 
 def rotate_for_others(kernel, outs, layer, v, spec, parts):

time: 228 us -> 228 us (level)
  Pallas kernels: 39.3 us -> 35.1 us
  starting transfers between devices: 40.7 us -> 44.7 us
    pallas_call x2, Pallas kernels: 7.26 us -> 3.04 us  [rotate_for_others(): pl.pallas_call(functools.partial(kernel, spec), out_shape=[jax.ShapeDtype...]
    ppermute x1, starting transfers between devices: 2.85 us -> 5.62 us  [orthonormalized(): back = lax.ppermute(back, 'orb', [(0, 1), (1, 0), (2, 3), (3, 2)])]
where the time goes in v9:
time: 228 us
  waiting for transfers between devices  96.3 us (42%)
  starting transfers between devices  44.7 us (20%)
  blocking collectives  37 us (16%)
  Pallas kernels  35.1 us (15%)
  local copies, waits for them, and re-layouts  11.8 us (5%)
    ppermute x24, waiting for transfers between devices, swap_all(): lax.ppermute(pieces[s], axis, [(i, i ^ s) for i in range(count)])  68.3 us
    all_to_all x1, blocking collectives, orthonormalized(): lax.all_to_all(filtered, everyone, split_axis=0, concat_axis=0, tiled=True)  37 us
    ppermute x24, starting transfers between devices, swap_all(): lax.ppermute(pieces[s], axis, [(i, i ^ s) for i in range(count)])  21.6 us
    pallas_call x1, Pallas kernels, inverse_rows(): pl.pallas_call(functools.partial(inverse_kernel, factor), out_shape=jax.S...  15.9 us
    all_to_all x1, waiting for transfers between devices, orthonormalized(): lax.all_to_all(first, 'grid', split_axis=0, concat_axis=0, tiled=True)  12.9 us
    ppermute x1, waiting for transfers between devices, orthonormalized(): skip = lax.ppermute(skip, 'orb', [(0, 1), (1, 3), (2, 0), (3, 2)])  11.1 us
    unnamed x24, local copies, waits for them, and re-layouts  9.1 us
    pallas_call x2, Pallas kernels, filter_orbitals(): pl.pallas_call(functools.partial(filter_kernel, orbs), out_shape=jax.Shap...  7.17 us
  transfers between devices with their start and end apart: 33, of which 21 were waited for; matrix products, arithmetic and copies ran while one was open for 1% of the time, Pallas kernels for 12%

profile of v9, /device:TPU:0, one launch (start us, length us, event | category | flops | bytes accessed | tf_op | source)
XLA Modules:
  0.0 227.5 jit_solution(7929197531290333597)
XLA Ops:
  1.1 1.0 pad_maximum_fusion
  2.2 5.2 %all-to-all-start = ((f32[8,7,4,8,128]{4,3,2,1,0:T(8,128)}), f32[8,7,4,8,128]{4,3,2,1,0:T(8,128)S(1)}, u32[]{:S(2)}, u32[]{:S(2)}) async-start(f32[8,7,4,8,128]{4,3,2,1,0:T(8,128)} %pad_maximum_fusion), calls=%async_computation | async-start | bytes 1835008 | tf_op jit(solution)/shard_map/all_to_all | solution.py:514
  8.5 12.9 %all-to-all-done.pot_ref.refs_0_ = f32[8,7,4,8,128]{4,3,2,1,0:T(8,128)S(1)} async-done(((f32[8,7,4,8,128]{4,3,2,1,0:T(8,128)}), f32[8,7,4,8,128]{4,3,2,1,0:T(8,128)S(1)}, u32[]{:S(2)}, u32[]{:S(2)}) %all-to-all-start) | async-done | bytes 917536 | tf_op jit(solution)/shard_map/all_to_all | solution.py:514
  21.3 3.3 %filter.2 = f32[4,8,6,8,128]{4,3,2,1,0:T(8,128)} custom-call(s32[1]{0:T(128)} %bitcast.1.place_ref, bf16[256,256]{1,0:T(8,128)(2,1)S(1)} %fusion.6.xy_ref, bf16[256,256]{1,0:T(8,128)(2,1)S(1)} %select_convert_fusion.z_ref, f32[8,7,4,8,128]{4,3,2,1,0:T(8,128)S(1)} %all-to-all-done.pot_ref.refs_0_, f32[8,7,4,8,128]{4,3,2,1,0:T(8,128)S(1)} %all-to-all-done.pot_ref.refs_0_), custom_call_target="tpu_custom_call" | custom-call | tf_op jit(solution)/shard_map/filter/pallas_call | solution.py:103
  24.7 4.0 %all-to-all-start.1 = ((f32[32,6,8,128]{3,2,1,0:T(8,128)}), f32[32,6,8,128]{3,2,1,0:T(8,128)S(1)}, u32[]{:S(2)}, u32[]{:S(2)}) async-start(f32[32,6,8,128]{3,2,1,0:T(8,128)} %bitcast.3), calls=%async_computation.1 | async-start | bytes 1572864 | tf_op jit(solution)/shard_map/all_to_all | solution.py:535
  28.7 1.6 dynamic-slice_bitcast_fusion
  30.3 2.5 %collective-permute-start.6 = (f32[1,10,4,8,128]{4,3,2,1,0:T(8,128)S(1)}, f32[1,10,4,8,128]{4,3,2,1,0:T(8,128)S(1)}, u32[]{:S(2)}, u32[]{:S(2)}) collective-permute-start(f32[1,10,4,8,128]{4,3,2,1,0:T(8,128)S(1)} %get-tuple-element.25), channel_id=1, source_target_pairs={{0,28},{4,24},{8,20},{12,16},{16,12},{20,8},{24,4},{28,0},{1,29},{... | collective-permute-start | bytes 491528 | tf_op jit(solution)/shard_map/ppermute | solution.py:487
  33.3 1.5 collective-permute-start.3
  34.8 1.5 collective-permute-start.1
  36.2 6.1 %collective-permute-done.6.refs_7_ = f32[1,10,4,8,128]{4,3,2,1,0:T(8,128)S(1)} collective-permute-done((f32[1,10,4,8,128]{4,3,2,1,0:T(8,128)S(1)}, f32[1,10,4,8,128]{4,3,2,1,0:T(8,128)S(1)}, u32[]{:S(2)}, u32[]{:S(2)}) %collective-permute-start.6) | collective-permute-done | bytes 163872 | tf_op jit(solution)/shard_map/ppermute | solution.py:487
  42.3 1.4 collective-permute-start
  43.7 2.4 %collective-permute-done.4.refs_5_ = f32[1,10,4,8,128]{4,3,2,1,0:T(8,128)S(1)} collective-permute-done((f32[1,10,4,8,128]{4,3,2,1,0:T(8,128)S(1)}, f32[1,10,4,8,128]{4,3,2,1,0:T(8,128)S(1)}, u32[]{:S(2)}, u32[]{:S(2)}) %collective-permute-start.4) | collective-permute-done | bytes 163872 | tf_op jit(solution)/shard_map/ppermute | solution.py:487
  46.9 4.1 %collective-permute-done.3.refs_4_ = f32[1,10,4,8,128]{4,3,2,1,0:T(8,128)S(1)} collective-permute-done((f32[1,10,4,8,128]{4,3,2,1,0:T(8,128)S(1)}, f32[1,10,4,8,128]{4,3,2,1,0:T(8,128)S(1)}, u32[]{:S(2)}, u32[]{:S(2)}) %collective-permute-start.3) | collective-permute-done | bytes 163872 | tf_op jit(solution)/shard_map/ppermute | solution.py:487
  51.0 4.1 %collective-permute-done.5.refs_6_ = f32[1,10,4,8,128]{4,3,2,1,0:T(8,128)S(1)} collective-permute-done((f32[1,10,4,8,128]{4,3,2,1,0:T(8,128)S(1)}, f32[1,10,4,8,128]{4,3,2,1,0:T(8,128)S(1)}, u32[]{:S(2)}, u32[]{:S(2)}) %collective-permute-start.5) | collective-permute-done | bytes 163872 | tf_op jit(solution)/shard_map/ppermute | solution.py:487
  55.2 3.8 %filter.3 = f32[4,8,10,8,128]{4,3,2,1,0:T(8,128)S(1)} custom-call(s32[1]{0:T(128)} %bitcast.1.place_ref, bf16[256,256]{1,0:T(8,128)(2,1)S(1)} %fusion.6.xy_ref, bf16[256,256]{1,0:T(8,128)(2,1)S(1)} %select_convert_fusion.z_ref, f32[8,7,4,8,128]{4,3,2,1,0:T(8,128)S(1)} %all-to-all-done.pot_ref.refs_0_, f32[1,10,4,8,128]{4,3,2,1,0:T(8,128)S(1)} %get-tuple-element.31.refs_0_, ...), custom_call_target="tpu_custom_call" | custom-call | tf_op jit(solution)/shard_map/filter/pallas_call | solution.py:103
  59.0 37.0 %all_to_all.15 = f32[32,10,8,128]{3,2,1,0:T(8,128)S(1)} all-to-all(f32[32,10,8,128]{3,2,1,0:T(8,128)S(1)} %bitcast.31), channel_id=1, replica_groups=mesh['grid'=8,'orb'=4] {'orb','grid'}, dimensions={0} | all-to-all | bytes 2621440 | tf_op jit(solution)/shard_map/all_to_all | solution.py:535
  96.1 2.1 margin.1
  98.3 1.8 collective-permute-start.28
  100.1 1.4 collective-permute-start.25
  103.2 3.5 %collective-permute-done.8 = f32[10,16,128]{2,1,0:T(8,128)S(1)} collective-permute-done((f32[10,16,128]{2,1,0:T(8,128)S(1)}, f32[10,16,128]{2,1,0:T(8,128)S(1)}, u32[]{:S(2)}, u32[]{:S(2)}) %collective-permute-start.8) | collective-permute-done | bytes 81952 | tf_op jit(solution)/shard_map/ppermute | solution.py:487
  106.9 1.3 collective-permute-start.12
  108.1 1.9 collective-permute-start.13
  110.6 2.5 %collective-permute-done.12 = f32[10,16,128]{2,1,0:T(8,128)S(1)} collective-permute-done((f32[10,16,128]{2,1,0:T(8,128)S(1)}, f32[10,16,128]{2,1,0:T(8,128)S(1)}, u32[]{:S(2)}, u32[]{:S(2)}) %collective-permute-start.12) | collective-permute-done | bytes 81952 | tf_op jit(solution)/shard_map/ppermute | solution.py:487
  113.1 1.6 collective-permute-done.13
  114.8 2.6 %collective-permute-start.16 = (f32[10,16,128]{2,1,0:T(8,128)S(1)}, f32[10,16,128]{2,1,0:T(8,128)S(1)}, u32[]{:S(2)}, u32[]{:S(2)}) collective-permute-start(f32[10,16,128]{2,1,0:T(8,128)S(1)} %add_add_fusion.2), channel_id=1, source_target_pairs={{0,3},{1,2},{2,1},{3,0},{4,7},{5,6},{6,5},{7,4},{8,11},{9,10},{10,... | collective-permute-start | bytes 245768 | tf_op jit(solution)/shard_map/ppermute | solution.py:487
  117.3 1.9 collective-permute-start.14
  119.2 16.2 %collective-permute-done.16 = f32[10,16,128]{2,1,0:T(8,128)S(1)} collective-permute-done((f32[10,16,128]{2,1,0:T(8,128)S(1)}, f32[10,16,128]{2,1,0:T(8,128)S(1)}, u32[]{:S(2)}, u32[]{:S(2)}) %collective-permute-start.16) | collective-permute-done | bytes 81952 | tf_op jit(solution)/shard_map/ppermute | solution.py:487
  135.4 1.5 collective-permute-start.27
  136.9 2.0 collective-permute-done.15
  139.0 1.5 collective-permute-start.24
  140.6 4.8 %collective-permute-done.23.refs_7_ = f32[10,16,128]{2,1,0:T(8,128)S(1)} collective-permute-done((f32[10,16,128]{2,1,0:T(8,128)S(1)}, f32[10,16,128]{2,1,0:T(8,128)S(1)}, u32[]{:S(2)}, u32[]{:S(2)}) %collective-permute-start.23) | collective-permute-done | bytes 81952 | tf_op jit(solution)/shard_map/ppermute | solution.py:487
  146.0 1.5 collective-permute-start.22
  147.4 3.9 %collective-permute-done.22.refs_6_ = f32[10,16,128]{2,1,0:T(8,128)S(1)} collective-permute-done((f32[10,16,128]{2,1,0:T(8,128)S(1)}, f32[10,16,128]{2,1,0:T(8,128)S(1)}, u32[]{:S(2)}, u32[]{:S(2)}) %collective-permute-start.22) | collective-permute-done | bytes 81952 | tf_op jit(solution)/shard_map/ppermute | solution.py:487
  151.9 4.0 %collective-permute-done.21.refs_5_ = f32[10,16,128]{2,1,0:T(8,128)S(1)} collective-permute-done((f32[10,16,128]{2,1,0:T(8,128)S(1)}, f32[10,16,128]{2,1,0:T(8,128)S(1)}, u32[]{:S(2)}, u32[]{:S(2)}) %collective-permute-start.21) | collective-permute-done | bytes 81952 | tf_op jit(solution)/shard_map/ppermute | solution.py:487
  156.5 1.4 collective-permute-start.20
  157.9 3.1 %collective-permute-done.20.refs_4_ = f32[10,16,128]{2,1,0:T(8,128)S(1)} collective-permute-done((f32[10,16,128]{2,1,0:T(8,128)S(1)}, f32[10,16,128]{2,1,0:T(8,128)S(1)}, u32[]{:S(2)}, u32[]{:S(2)}) %collective-permute-start.20) | collective-permute-done | bytes 81952 | tf_op jit(solution)/shard_map/ppermute | solution.py:487
  161.9 4.4 %collective-permute-done.19.refs_3_ = f32[10,16,128]{2,1,0:T(8,128)S(1)} collective-permute-done((f32[10,16,128]{2,1,0:T(8,128)S(1)}, f32[10,16,128]{2,1,0:T(8,128)S(1)}, u32[]{:S(2)}, u32[]{:S(2)}) %collective-permute-start.19) | collective-permute-done | bytes 81952 | tf_op jit(solution)/shard_map/ppermute | solution.py:487
  167.8 3.5 %collective-permute-done.18.refs_2_ = f32[10,16,128]{2,1,0:T(8,128)S(1)} collective-permute-done((f32[10,16,128]{2,1,0:T(8,128)S(1)}, f32[10,16,128]{2,1,0:T(8,128)S(1)}, u32[]{:S(2)}, u32[]{:S(2)}) %collective-permute-start.18) | collective-permute-done | bytes 81952 | tf_op jit(solution)/shard_map/ppermute | solution.py:487
  172.0 1.4 collective-permute-done.17.refs_1_
  178.7 15.9 %inverse.1.v_ref = f32[4,128,512]{2,1,0:T(8,128)S(1)} custom-call(s32[1]{0:T(128)} %bitcast.1.place_ref, f32[10,16,128]{2,1,0:T(8,128)S(1)} %add_add_fusion.1.refs_0_, f32[10,16,128]{2,1,0:T(8,128)} %collective-permute-done.17.refs_1_, f32[10,16,128]{2,1,0:T(8,128)S(1)} %copy-done.11, f32[10,16,128]{2,1,0:T(8,128)S(1)} %copy-done.9, ...), custom_call_target="tpu_custom_call" | custom-call | tf_op jit(solution)/shard_map/inverse/pallas_call | solution.py:312
  194.7 1.9 rotate_far.3
  197.2 5.6 %collective-permute-start.30 = (f32[128,8,128]{2,1,0:T(8,128)S(1)}, f32[128,8,128]{2,1,0:T(8,128)S(1)}, u32[]{:S(2)}, u32[]{:S(2)}) collective-permute-start(f32[128,8,128]{2,1,0:T(8,128)S(1)} %get-tuple-element.24), channel_id=1, source_target_pairs={{0,1},{1,0},{2,3},{3,2},{4,5},{5,4},{6,7},{7,6},{8,9},{9,8},{10,11... | collective-permute-start | bytes 1572872 | tf_op jit(solution)/shard_map/ppermute | solution.py:561
  202.9 1.2 rotate_far.2
  204.0 1.3 collective-permute-start.26
  205.4 5.9 %rotate_near.1.near_ref = f32[128,4,8,128]{3,2,1,0:T(8,128)} custom-call(s32[1]{0:T(128)} %bitcast.layer_ref, f32[4,128,512]{2,1,0:T(8,128)S(1)} %inverse.1.v_ref, f32[1536,128]{1,0:T(8,128)S(1)} %bitcast.30, f32[2560,128]{1,0:T(8,128)S(1)} %bitcast.26, f32[1536,128]{1,0:T(8,128)} %collective-permute-done.24.refs_0_.refs_2_, ...), custom_call_target="tpu_custom_call" | custom-call | tf_op jit(solution)/shard_map/rotate_near/pallas_call | solution.py:445
  211.3 4.1 %collective-permute-done.30.back = f32[128,8,128]{2,1,0:T(8,128)S(1)} collective-permute-done((f32[128,8,128]{2,1,0:T(8,128)S(1)}, f32[128,8,128]{2,1,0:T(8,128)S(1)}, u32[]{:S(2)}, u32[]{:S(2)}) %collective-permute-start.30) | collective-permute-done | bytes 524320 | tf_op jit(solution)/shard_map/ppermute | solution.py:561
  215.3 11.1 %collective-permute-done.26.skip = f32[128,8,128]{2,1,0:T(8,128)S(1)} collective-permute-done((f32[128,8,128]{2,1,0:T(8,128)S(1)}, f32[128,8,128]{2,1,0:T(8,128)S(1)}, u32[]{:S(2)}, u32[]{:S(2)}) %collective-permute-start.26) | collective-permute-done | bytes 524320 | tf_op jit(solution)/shard_map/ppermute | solution.py:559
  226.4 1.0 join.1
  (65 shorter events, 17.3 us)
Async XLA Ops:
  0.0 1.1 slice-start
  2.2 19.2 %all-to-all-start = ((f32[8,7,4,8,128]{4,3,2,1,0:T(8,128)}), f32[8,7,4,8,128]{4,3,2,1,0:T(8,128)S(1)}, u32[]{:S(2)}, u32[]{:S(2)}) async-start(f32[8,7,4,8,128]{4,3,2,1,0:T(8,128)} %pad_maximum_fusion), calls=%async_computation | async-start | bytes 1835008 | tf_op jit(solution)/shard_map/all_to_all | solution.py:514
  24.7 34.4 %all-to-all-start.1 = ((f32[32,6,8,128]{3,2,1,0:T(8,128)}), f32[32,6,8,128]{3,2,1,0:T(8,128)S(1)}, u32[]{:S(2)}, u32[]{:S(2)}) async-start(f32[32,6,8,128]{3,2,1,0:T(8,128)} %bitcast.3), calls=%async_computation.1 | async-start | bytes 1572864 | tf_op jit(solution)/shard_map/all_to_all | solution.py:535
  30.3 12.0 %collective-permute-start.6 = (f32[1,10,4,8,128]{4,3,2,1,0:T(8,128)S(1)}, f32[1,10,4,8,128]{4,3,2,1,0:T(8,128)S(1)}, u32[]{:S(2)}, u32[]{:S(2)}) collective-permute-start(f32[1,10,4,8,128]{4,3,2,1,0:T(8,128)S(1)} %get-tuple-element.25), channel_id=1, source_target_pairs={{0,28},{4,24},{8,20},{12,16},{16,12},{20,8},{24,4},{28,0},{1,29},{... | collective-permute-start | bytes 491528 | tf_op jit(solution)/shard_map/ppermute | solution.py:487
  32.7 13.4 %collective-permute-start.4 = (f32[1,10,4,8,128]{4,3,2,1,0:T(8,128)S(1)}, f32[1,10,4,8,128]{4,3,2,1,0:T(8,128)S(1)}, u32[]{:S(2)}, u32[]{:S(2)}) collective-permute-start(f32[1,10,4,8,128]{4,3,2,1,0:T(8,128)S(1)} %get-tuple-element.26), channel_id=1, source_target_pairs={{0,20},{4,16},{8,28},{12,24},{16,4},{20,0},{24,12},{28,8},{1,21},{... | collective-permute-start | bytes 491528 | tf_op jit(solution)/shard_map/ppermute | solution.py:487
  33.3 17.7 %collective-permute-start.3 = (f32[1,10,4,8,128]{4,3,2,1,0:T(8,128)S(1)}, f32[1,10,4,8,128]{4,3,2,1,0:T(8,128)S(1)}, u32[]{:S(2)}, u32[]{:S(2)}) collective-permute-start(f32[1,10,4,8,128]{4,3,2,1,0:T(8,128)S(1)} %get-tuple-element.27), channel_id=1, source_target_pairs={{0,16},{4,20},{8,24},{12,28},{16,0},{20,4},{24,8},{28,12},{1,17},{... | collective-permute-start | bytes 491528 | tf_op jit(solution)/shard_map/ppermute | solution.py:487
  34.8 16.3 %collective-permute-start.2 = (f32[1,10,4,8,128]{4,3,2,1,0:T(8,128)S(1)}, f32[1,10,4,8,128]{4,3,2,1,0:T(8,128)S(1)}, u32[]{:S(2)}, u32[]{:S(2)}) collective-permute-start(f32[1,10,4,8,128]{4,3,2,1,0:T(8,128)S(1)} %get-tuple-element.28), channel_id=1, source_target_pairs={{0,12},{4,8},{8,4},{12,0},{16,28},{20,24},{24,20},{28,16},{1,13},{... | collective-permute-start | bytes 491528 | tf_op jit(solution)/shard_map/ppermute | solution.py:487
  34.8 16.3 %collective-permute-start.1 = (f32[1,10,4,8,128]{4,3,2,1,0:T(8,128)S(1)}, f32[1,10,4,8,128]{4,3,2,1,0:T(8,128)S(1)}, u32[]{:S(2)}, u32[]{:S(2)}) collective-permute-start(f32[1,10,4,8,128]{4,3,2,1,0:T(8,128)S(1)} %get-tuple-element.29), channel_id=1, source_target_pairs={{0,8},{4,12},{8,0},{12,4},{16,24},{20,28},{24,16},{28,20},{1,9},{5... | collective-permute-start | bytes 491528 | tf_op jit(solution)/shard_map/ppermute | solution.py:487
  42.3 8.7 %collective-permute-start = (f32[1,10,4,8,128]{4,3,2,1,0:T(8,128)S(1)}, f32[1,10,4,8,128]{4,3,2,1,0:T(8,128)S(1)}, u32[]{:S(2)}, u32[]{:S(2)}) collective-permute-start(f32[1,10,4,8,128]{4,3,2,1,0:T(8,128)S(1)} %get-tuple-element.30), channel_id=1, source_target_pairs={{0,4},{4,0},{8,12},{12,8},{16,20},{20,16},{24,28},{28,24},{1,5},{5... | collective-permute-start | bytes 491528 | tf_op jit(solution)/shard_map/ppermute | solution.py:487
  46.1 9.1 %collective-permute-start.5 = (f32[1,10,4,8,128]{4,3,2,1,0:T(8,128)S(1)}, f32[1,10,4,8,128]{4,3,2,1,0:T(8,128)S(1)}, u32[]{:S(2)}, u32[]{:S(2)}) collective-permute-start(f32[1,10,4,8,128]{4,3,2,1,0:T(8,128)S(1)} %get-tuple-element.32), channel_id=1, source_target_pairs={{0,24},{4,28},{8,16},{12,20},{16,8},{20,12},{24,0},{28,4},{1,25},{... | collective-permute-start | bytes 491528 | tf_op jit(solution)/shard_map/ppermute | solution.py:487
  98.2 4.4 %collective-permute-start.7 = (f32[10,16,128]{2,1,0:T(8,128)S(1)}, f32[10,16,128]{2,1,0:T(8,128)S(1)}, u32[]{:S(2)}, u32[]{:S(2)}) collective-permute-start(f32[10,16,128]{2,1,0:T(8,128)S(1)} %get-tuple-element.16), channel_id=1, source_target_pairs={{0,4},{4,0},{8,12},{12,8},{16,20},{20,16},{24,28},{28,24},{1,5},{5... | collective-permute-start | bytes 245768 | tf_op jit(solution)/shard_map/ppermute | solution.py:487
  98.3 96.3 %collective-permute-start.28 = (f32[2560,128]{1,0:T(8,128)S(1)}, f32[2560,128]{1,0:T(8,128)}, u32[]{:S(2)}, u32[]{:S(2)}) collective-permute-start(f32[2560,128]{1,0:T(8,128)S(1)} %bitcast.24), channel_id=1, source_target_pairs={{0,0},{1,2},{2,1},{3,3},{4,4},{5,6},{6,5},{7,7},{8,8},{9,10},{10,9... | collective-permute-start | bytes 3932168 | tf_op jit(solution)/shard_map/ppermute | solution.py:547
  100.1 94.6 %collective-permute-start.25 = (f32[2560,128]{1,0:T(8,128)S(1)}, f32[2560,128]{1,0:T(8,128)S(1)}, u32[]{:S(2)}, u32[]{:S(2)}) collective-permute-start(f32[2560,128]{1,0:T(8,128)S(1)} %bitcast.25), channel_id=1, source_target_pairs={{0,1},{1,0},{2,3},{3,2},{4,5},{5,4},{6,7},{7,6},{8,9},{9,8},{10,11... | collective-permute-start | bytes 3932168 | tf_op jit(solution)/shard_map/ppermute | solution.py:546
  101.5 5.2 %collective-permute-start.8 = (f32[10,16,128]{2,1,0:T(8,128)S(1)}, f32[10,16,128]{2,1,0:T(8,128)S(1)}, u32[]{:S(2)}, u32[]{:S(2)}) collective-permute-start(f32[10,16,128]{2,1,0:T(8,128)S(1)} %get-tuple-element.17), channel_id=1, source_target_pairs={{0,8},{4,12},{8,0},{12,4},{16,24},{20,28},{24,16},{28,20},{1,9},{5... | collective-permute-start | bytes 245768 | tf_op jit(solution)/shard_map/ppermute | solution.py:487
  102.1 4.7 %collective-permute-start.9 = (f32[10,16,128]{2,1,0:T(8,128)S(1)}, f32[10,16,128]{2,1,0:T(8,128)S(1)}, u32[]{:S(2)}, u32[]{:S(2)}) collective-permute-start(f32[10,16,128]{2,1,0:T(8,128)S(1)} %get-tuple-element.18), channel_id=1, source_target_pairs={{0,12},{4,8},{8,4},{12,0},{16,28},{20,24},{24,20},{28,16},{1,13},{... | collective-permute-start | bytes 245768 | tf_op jit(solution)/shard_map/ppermute | solution.py:487
  102.6 5.5 %collective-permute-start.10 = (f32[10,16,128]{2,1,0:T(8,128)S(1)}, f32[10,16,128]{2,1,0:T(8,128)S(1)}, u32[]{:S(2)}, u32[]{:S(2)}) collective-permute-start(f32[10,16,128]{2,1,0:T(8,128)S(1)} %get-tuple-element.19), channel_id=1, source_target_pairs={{0,16},{4,20},{8,24},{12,28},{16,0},{20,4},{24,8},{28,12},{1,17},{... | collective-permute-start | bytes 245768 | tf_op jit(solution)/shard_map/ppermute | solution.py:487
  106.7 3.9 %collective-permute-start.11 = (f32[10,16,128]{2,1,0:T(8,128)S(1)}, f32[10,16,128]{2,1,0:T(8,128)S(1)}, u32[]{:S(2)}, u32[]{:S(2)}) collective-permute-start(f32[10,16,128]{2,1,0:T(8,128)S(1)} %get-tuple-element.20), channel_id=1, source_target_pairs={{0,20},{4,16},{8,28},{12,24},{16,4},{20,0},{24,12},{28,8},{1,21},{... | collective-permute-start | bytes 245768 | tf_op jit(solution)/shard_map/ppermute | solution.py:487
  106.9 6.2 %collective-permute-start.12 = (f32[10,16,128]{2,1,0:T(8,128)S(1)}, f32[10,16,128]{2,1,0:T(8,128)S(1)}, u32[]{:S(2)}, u32[]{:S(2)}) collective-permute-start(f32[10,16,128]{2,1,0:T(8,128)S(1)} %get-tuple-element.21), channel_id=1, source_target_pairs={{0,24},{4,28},{8,16},{12,20},{16,8},{20,12},{24,0},{28,4},{1,25},{... | collective-permute-start | bytes 245768 | tf_op jit(solution)/shard_map/ppermute | solution.py:487
  108.1 6.6 %collective-permute-start.13 = (f32[10,16,128]{2,1,0:T(8,128)S(1)}, f32[10,16,128]{2,1,0:T(8,128)S(1)}, u32[]{:S(2)}, u32[]{:S(2)}) collective-permute-start(f32[10,16,128]{2,1,0:T(8,128)S(1)} %get-tuple-element.22), channel_id=1, source_target_pairs={{0,28},{4,24},{8,20},{12,16},{16,12},{20,8},{24,4},{28,0},{1,29},{... | collective-permute-start | bytes 245768 | tf_op jit(solution)/shard_map/ppermute | solution.py:487
  114.8 20.7 %collective-permute-start.16 = (f32[10,16,128]{2,1,0:T(8,128)S(1)}, f32[10,16,128]{2,1,0:T(8,128)S(1)}, u32[]{:S(2)}, u32[]{:S(2)}) collective-permute-start(f32[10,16,128]{2,1,0:T(8,128)S(1)} %add_add_fusion.2), channel_id=1, source_target_pairs={{0,3},{1,2},{2,1},{3,0},{4,7},{5,6},{6,5},{7,4},{8,11},{9,10},{10,... | collective-permute-start | bytes 245768 | tf_op jit(solution)/shard_map/ppermute | solution.py:487
  117.3 21.6 %collective-permute-start.15 = (f32[10,16,128]{2,1,0:T(8,128)S(1)}, f32[10,16,128]{2,1,0:T(8,128)S(1)}, u32[]{:S(2)}, u32[]{:S(2)}) collective-permute-start(f32[10,16,128]{2,1,0:T(8,128)S(1)} %add_add_fusion.2), channel_id=1, source_target_pairs={{0,2},{1,3},{2,0},{3,1},{4,6},{5,7},{6,4},{7,5},{8,10},{9,11},{10,... | collective-permute-start | bytes 245768 | tf_op jit(solution)/shard_map/ppermute | solution.py:487
  117.3 23.1 %collective-permute-start.14 = (f32[10,16,128]{2,1,0:T(8,128)S(1)}, f32[10,16,128]{2,1,0:T(8,128)S(1)}, u32[]{:S(2)}, u32[]{:S(2)}) collective-permute-start(f32[10,16,128]{2,1,0:T(8,128)S(1)} %add_add_fusion.2), channel_id=1, source_target_pairs={{0,1},{1,0},{2,3},{3,2},{4,5},{5,4},{6,7},{7,6},{8,9},{9,8},{10,11... | collective-permute-start | bytes 245768 | tf_op jit(solution)/shard_map/ppermute | solution.py:487
  135.4 59.2 %collective-permute-start.27 = (f32[1536,128]{1,0:T(8,128)S(1)}, f32[1536,128]{1,0:T(8,128)}, u32[]{:S(2)}, u32[]{:S(2)}) collective-permute-start(f32[1536,128]{1,0:T(8,128)S(1)} %bitcast.28), channel_id=1, source_target_pairs={{0,0},{1,2},{2,1},{3,3},{4,4},{5,6},{6,5},{7,7},{8,8},{9,10},{10,9... | collective-permute-start | bytes 2359304 | tf_op jit(solution)/shard_map/ppermute | solution.py:547
  139.0 55.7 %collective-permute-start.24 = (f32[1536,128]{1,0:T(8,128)S(1)}, f32[1536,128]{1,0:T(8,128)}, u32[]{:S(2)}, u32[]{:S(2)}) collective-permute-start(f32[1536,128]{1,0:T(8,128)S(1)} %bitcast.29), channel_id=1, source_target_pairs={{0,1},{1,0},{2,3},{3,2},{4,5},{5,4},{6,7},{7,6},{8,9},{9,8},{10,11... | collective-permute-start | bytes 2359304 | tf_op jit(solution)/shard_map/ppermute | solution.py:546
  140.5 4.8 %collective-permute-start.23 = (f32[10,16,128]{2,1,0:T(8,128)S(1)}, f32[10,16,128]{2,1,0:T(8,128)S(1)}, u32[]{:S(2)}, u32[]{:S(2)}) collective-permute-start(f32[10,16,128]{2,1,0:T(8,128)S(1)} %add_add_fusion.1.refs_0_), channel_id=1, source_target_pairs={{0,28},{4,24},{8,20},{12,16},{16,12},{20,8},{24,4},{28,0},{1,29},{... | collective-permute-start | bytes 245768 | tf_op jit(solution)/shard_map/ppermute | solution.py:487
  145.3 0.6 copy-start
  146.0 5.3 %collective-permute-start.22 = (f32[10,16,128]{2,1,0:T(8,128)S(1)}, f32[10,16,128]{2,1,0:T(8,128)S(1)}, u32[]{:S(2)}, u32[]{:S(2)}) collective-permute-start(f32[10,16,128]{2,1,0:T(8,128)S(1)} %add_add_fusion.1.refs_0_), channel_id=1, source_target_pairs={{0,24},{4,28},{8,16},{12,20},{16,8},{20,12},{24,0},{28,4},{1,25},{... | collective-permute-start | bytes 245768 | tf_op jit(solution)/shard_map/ppermute | solution.py:487
  151.3 0.6 copy-start.2
  151.9 4.0 %collective-permute-start.21 = (f32[10,16,128]{2,1,0:T(8,128)S(1)}, f32[10,16,128]{2,1,0:T(8,128)S(1)}, u32[]{:S(2)}, u32[]{:S(2)}) collective-permute-start(f32[10,16,128]{2,1,0:T(8,128)S(1)} %add_add_fusion.1.refs_0_), channel_id=1, source_target_pairs={{0,20},{4,16},{8,28},{12,24},{16,4},{20,0},{24,12},{28,8},{1,21},{... | collective-permute-start | bytes 245768 | tf_op jit(solution)/shard_map/ppermute | solution.py:487
  155.9 0.6 copy-start.4
  156.5 4.4 %collective-permute-start.20 = (f32[10,16,128]{2,1,0:T(8,128)S(1)}, f32[10,16,128]{2,1,0:T(8,128)S(1)}, u32[]{:S(2)}, u32[]{:S(2)}) collective-permute-start(f32[10,16,128]{2,1,0:T(8,128)S(1)} %add_add_fusion.1.refs_0_), channel_id=1, source_target_pairs={{0,16},{4,20},{8,24},{12,28},{16,0},{20,4},{24,8},{28,12},{1,17},{... | collective-permute-start | bytes 245768 | tf_op jit(solution)/shard_map/ppermute | solution.py:487
  160.9 0.6 copy-start.6
  161.6 4.7 %collective-permute-start.19 = (f32[10,16,128]{2,1,0:T(8,128)S(1)}, f32[10,16,128]{2,1,0:T(8,128)S(1)}, u32[]{:S(2)}, u32[]{:S(2)}) collective-permute-start(f32[10,16,128]{2,1,0:T(8,128)S(1)} %add_add_fusion.1.refs_0_), channel_id=1, source_target_pairs={{0,12},{4,8},{8,4},{12,0},{16,28},{20,24},{24,20},{28,16},{1,13},{... | collective-permute-start | bytes 245768 | tf_op jit(solution)/shard_map/ppermute | solution.py:487
  166.3 0.6 copy-start.8
  166.9 4.4 %collective-permute-start.18 = (f32[10,16,128]{2,1,0:T(8,128)S(1)}, f32[10,16,128]{2,1,0:T(8,128)S(1)}, u32[]{:S(2)}, u32[]{:S(2)}) collective-permute-start(f32[10,16,128]{2,1,0:T(8,128)S(1)} %add_add_fusion.1.refs_0_), channel_id=1, source_target_pairs={{0,8},{4,12},{8,0},{12,4},{16,24},{20,28},{24,16},{28,20},{1,9},{5... | collective-permute-start | bytes 245768 | tf_op jit(solution)/shard_map/ppermute | solution.py:487
  171.4 0.6 copy-start.10
  172.0 1.4 collective-permute-start.17
  173.4 0.9 copy-start.1
  174.3 0.9 copy-start.3
  175.2 0.9 copy-start.5
  176.1 0.9 copy-start.7
  176.9 0.9 copy-start.9
  177.8 0.9 copy-start.11
  196.5 14.7 %collective-permute-start.29 = (f32[128,8,128]{2,1,0:T(8,128)S(1)}, f32[128,8,128]{2,1,0:T(8,128)S(1)}, u32[]{:S(2)}, u32[]{:S(2)}) collective-permute-start(f32[128,8,128]{2,1,0:T(8,128)S(1)} %get-tuple-element.23), channel_id=1, source_target_pairs={{0,0},{1,2},{2,1},{3,3},{4,4},{5,6},{6,5},{7,7},{8,8},{9,10},{10,9... | collective-permute-start | bytes 1572872 | tf_op jit(solution)/shard_map/ppermute | solution.py:560
  197.2 18.1 %collective-permute-start.30 = (f32[128,8,128]{2,1,0:T(8,128)S(1)}, f32[128,8,128]{2,1,0:T(8,128)S(1)}, u32[]{:S(2)}, u32[]{:S(2)}) collective-permute-start(f32[128,8,128]{2,1,0:T(8,128)S(1)} %get-tuple-element.24), channel_id=1, source_target_pairs={{0,1},{1,0},{2,3},{3,2},{4,5},{5,4},{6,7},{7,6},{8,9},{9,8},{10,11... | collective-permute-start | bytes 1572872 | tf_op jit(solution)/shard_map/ppermute | solution.py:561
  204.0 22.3 %collective-permute-start.26 = (f32[128,8,128]{2,1,0:T(8,128)S(1)}, f32[128,8,128]{2,1,0:T(8,128)S(1)}, u32[]{:S(2)}, u32[]{:S(2)}) collective-permute-start(f32[128,8,128]{2,1,0:T(8,128)S(1)} %rotate_far.2), channel_id=1, source_target_pairs={{0,1},{1,3},{2,0},{3,2},{4,5},{5,7},{6,4},{7,6},{8,9},{9,11},{10,8... | collective-permute-start | bytes 1572872 | tf_op jit(solution)/shard_map/ppermute | solution.py:559
